TPU v7x, 256 devices: a whole 4x4x8 slice. The times are simulated.
256 devices in a mesh: freq: 8 (over z_lo, core), col: 32 (over x, y, z_hi).
Axes of the slice: x: 4, y: 4, z: 8 (z_hi: 2, z_lo: 4; z = z_hi * 4 + z_lo), core: 2. Of those that a mesh axis runs over, the one named last changes fastest.
Arguments:
- spectra: bfloat16 [2, 16, 4096, 4096], P(None, None, 'freq', 'col'), may hold values from -0.62890625 to 0.62890625
- wavelet: float32 [2, 16], P(None, 'freq'), may hold values from -1.5 to 1.5
Outputs:
- predicted: bfloat16 [2, 16, 384, 4096], P(None, 'freq', None, 'col')
All inputs are finite; a program needn't handle non-finite values.
Results may differ from a plain program's by a relative error of at most 0.001.
Values may be sent and summed in bfloat16 or wider, within the bound.
No kernel may reach another device: no remote copies, remote signals or barrier semaphores. Data moves between devices by JAX's collectives and lax.ppermute only.
A program may use at most 128 MiB of HBM per device.

v0:
```python
import jax
import jax.numpy as jnp
from jax import lax
from jax.sharding import PartitionSpec as P

NOUT = 384


def complex_product(left, right, form):
    real_part = jnp.einsum(
        form, left[0], right[0], preferred_element_type=jnp.float32
    ) - jnp.einsum(form, left[1], right[1], preferred_element_type=jnp.float32)
    imag_part = jnp.einsum(
        form, left[0], right[1], preferred_element_type=jnp.float32
    ) + jnp.einsum(form, left[1], right[0], preferred_element_type=jnp.float32)
    return jnp.stack([real_part, imag_part])


def predict(slab, window):
    upper = slab[:, :, :window, :]
    return complex_product(lax.all_gather(upper, "col", axis=3, tiled=True), slab, "fnw,fwc->fnc")


def local(spectra, wavelet):
    window = NOUT
    slab = lax.all_to_all(spectra, "freq", split_axis=1, concat_axis=2, tiled=True)
    product = predict(slab, window)
    wave_real = wavelet[0][:, None, None]
    wave_imag = wavelet[1][:, None, None]
    real_out = -(wave_real * product[0] - wave_imag * product[1])
    imag_out = -(wave_real * product[1] + wave_imag * product[0])
    return jnp.stack([real_out, imag_out]).astype(jnp.bfloat16)


def solution(mesh):
    return jax.shard_map(
        local,
        mesh=mesh,
        in_specs=(P(None, None, "freq", "col"), P(None, "freq")),
        out_specs=P(None, "freq", None, "col"),
        check_vma=False,
    )
```

profile of v0, /device:TPU:4, one launch (start us, length us, event | category | flops | bytes accessed | tf_op | source)
XLA Modules:
  0.0 409.9 jit_solution(6084486596494399329)
XLA Ops:
  6.5 0.0 all-gather.2.cloned.1.call-start
  6.5 2.5 copy.4
  9.0 99.7 %all_to_all.18 = bf16[2,16,512,128]{3,2,0,1:T(8,128)(2,1)S(1)} all-to-all(bf16[2,16,512,128]{3,2,0,1:T(8,128)(2,1)S(1)} %copy.4), channel_id=1, replica_groups=mesh['freq'=8,'col'=32] {'freq'}, dimensions={1} | all-to-all | bytes 8388608 | tf_op jit(solution)/shard_map/all_to_all | solution.py:26
  108.7 0.0 copy-start.2
  108.7 0.4 copy.8
  109.1 0.0 copy-start
  109.1 1.9 copy-done
  111.1 0.8 slice.34
  111.8 0.0 all-gather.2.cloned.1.call-update
  111.9 0.0 copy-done.2
  111.9 3.9 fusion.8
  115.8 272.8 %all-gather.2.cloned.1.call-done = bf16[2,2,384,4096]{3,2,1,0:T(8,128)(2,1)} async-done(((bf16[2,2,384,128]{3,2,1,0:T(8,128)(2,1)}), bf16[2,2,384,4096]{3,2,1,0:T(8,128)(2,1)}) %all-gather.2.cloned.1.call-update) | async-done | bytes 12582928 | tf_op jit(solution)/shard_map/all_gather | solution.py:21
  388.6 0.0 copy-start.1
  388.6 0.0 copy-start.3
  388.6 4.7 %fusion.1 = f32[2,384,128]{2,1,0:T(8,128)S(1)} fusion(bf16[2,4096,128]{2,1,0:T(8,128)(2,1)S(1)} %bitcast.36, bf16[2,2,384,4096]{3,2,1,0:T(8,128)(2,1)} %all-gather.2.cloned.1.call-done), kind=kOutput, calls=%fused_computation.3 | convolution fusion | flops 805306368 | bytes 8781824 | tf_op jit(solution)/shard_map/fnw,fwc->fnc/dot_general | solution.py:10
  393.3 0.0 copy-done.1
  393.3 5.3 %fusion = f32[2,384,128]{2,1,0:T(8,128)S(1)} fusion(bf16[2,4096,128]{2,1,0:T(8,128)(2,1)S(1)} %bitcast.38, bf16[2,2,384,4096]{3,2,1,0:T(8,128)(2,1)} %all-gather.2.cloned.1.call-done), kind=kOutput, calls=%fused_computation.2 | convolution fusion | flops 805306368 | bytes 8781824 | tf_op jit(solution)/shard_map/fnw,fwc->fnc/dot_general | solution.py:13
  398.7 0.0 copy-done.3
  398.7 1.8 fusion.4
  400.5 1.8 fusion.6
  402.3 0.8 pad_maximum_fusion
  (1 shorter events, 0.0 us)
Async XLA Ops:
  6.5 382.1 %all-gather.2.cloned.1.call-start = ((), (), s32[]{:S(2)}) async-start(), calls=%async_computation.1 | async-start | bytes 12976128 | tf_op jit(solution)/shard_map/all_gather | solution.py:21
  108.7 3.2 copy-start.2
  109.1 1.9 copy-start
  388.6 4.7 %copy-start.1 = (bf16[1,2,8,512,128]{4,3,2,1,0:T(8,128)(2,1)S(1)}, bf16[1,2,8,512,128]{4,3,2,1,0:T(8,128)(2,1)}, u32[]{:S(2)}) copy-start(bf16[1,2,8,512,128]{4,3,2,1,0:T(8,128)(2,1)} %get-tuple-element.5) | copy-start | bytes 6291460
  388.6 10.1 %copy-start.3 = (bf16[2,2,384,4096]{3,2,1,0:T(8,128)(2,1)S(1)}, bf16[2,2,384,4096]{3,2,1,0:T(8,128)(2,1)}, u32[]{:S(2)}) copy-start(bf16[2,2,384,4096]{3,2,1,0:T(8,128)(2,1)} %all-gather.2.cloned.1.call-done) | copy-start | bytes 37748740
Sparse Core Ops, SparseCore 0:
  112.0 276.5 all-gather.1
where the time goes:
time: 412 us; the launch traced here: 410 us
  waiting for transfers between devices  273 us (66%)
  blocking collectives  99.7 us (24%)
  matrix products  13.7 us (3%)
  between operations  13.5 us (3%)
  local copies, waits for them, and re-layouts  9.51 us (2%)
    all_gather x1, waiting for transfers between devices, predict(): lax.all_gather(upper, 'col', axis=3, tiled=True)  273 us
    all_to_all x1, blocking collectives, local(): lax.all_to_all(spectra, 'freq', split_axis=1, concat_axis=2, tiled=True)  99.7 us
  transfers between devices with their start and end apart: 1, of which 1 were waited for; matrix products, arithmetic and copies ran while one was open for 1% of the time, Pallas kernels for 0%

commit v1 on v0

v1 whole, which is shorter than its diff:
```python
import jax
import jax.numpy as jnp
from jax import lax
from jax.sharding import Mesh, PartitionSpec as P

NOUT = 384
AXES = ("zq", "zr", "core", "x", "y", "zh")
SIZES = (2, 2, 2, 4, 4, 2)


def coordinates():
    out = [()]
    for size in SIZES:
        out = [c + (i,) for c in out for i in range(size)]
    return out


def flat(c):
    index = 0
    for i, size in zip(c, SIZES):
        index = index * size + i
    return index


def moved(target):
    pairs = []
    for c in coordinates():
        t = target(*c)
        if t is not None and tuple(t) != c:
            pairs.append((flat(c), flat(t)))
    return pairs


def send(value, target):
    return lax.ppermute(value, AXES, moved(target))


def home(zq, zr, core, x, y, zh):
    return (x // 2, zr, x % 2, 2 * zq + core, y, zh)


def local(spectra, wavelet):
    zq, zr, core = lax.axis_index("zq"), lax.axis_index("zr"), lax.axis_index("core")
    y, zh = lax.axis_index("y"), lax.axis_index("zh")
    window = NOUT * spectra.shape[2] // 512
    lanes = spectra.shape[3]

    back = [(b, a) for a, b in moved(home)]
    stay = (zq == lax.axis_index("x") // 2) & (core == lax.axis_index("x") % 2)
    wave = jnp.where(stay, wavelet, lax.ppermute(wavelet, AXES, back))

    parted = spectra.reshape((2, 2, 2, 2, 2) + spectra.shape[2:])
    parted = parted.transpose(4, 1, 3, 2, 0, 5, 6).reshape((2, 8, 2) + spectra.shape[2:])

    def exchange(block):
        return lax.all_to_all(block, ("x", "zr"), split_axis=0, concat_axis=0, tiled=True)

    upper = [exchange(parted[g, :, :, :window]) for g in range(2)]
    lower = exchange(parted[:, :, :, window:].transpose(1, 0, 2, 3, 4))

    outs = []
    for g in range(2):
        shots = upper[g].reshape((4, 2) + upper[g].shape[1:])[:, 0]
        near, far = shots[:2], shots[2:]
        source = (zq == 0) & (core == 0)
        here = source & (y < 2)
        own = jnp.where(here, near, 0) + send(
            near, lambda q, r, c, x, y, h: (0, r, y // 2, x, y, h) if q == 0 and c == 0 and y >= 2 else None
        ) + send(far, lambda q, r, c, x, y, h: (1, r, y // 2, x, y, h) if q == 0 and c == 0 else None)
        other = send(
            near, lambda q, r, c, x, y, h: (0, r, y // 2, x, y, 1 - h) if q == 0 and c == 0 else None
        ) + send(far, lambda q, r, c, x, y, h: (1, r, y // 2, x, y, 1 - h) if q == 0 and c == 0 else None)
        pieces = []
        for piece in (own, other):
            turned = [piece] + [
                send(piece, lambda q, r, c, x, y, h: (q, r, c, x, (y + s) % 4, h) if y // 2 == c else None)
                for s in (1, 2, 3)
            ]
            pieces.append(
                [
                    lax.select_n((y - 2 * core - low) % 4, *turned)
                    for low in range(2)
                ]
            )
        blocks = []
        for low in range(2):
            a, b = pieces[0][low], pieces[1][low]
            blocks.append(jnp.where(zh == 0, a, b))
            blocks.append(jnp.where(zh == 0, b, a))
        left = jnp.stack(blocks, 1)
        right = jnp.concatenate([upper[g], lower[:, g]], 2).reshape(4, 2, 2, 4, lanes, lanes)

        def dot(i, j):
            return jnp.einsum(
                "rbmk,xrbkc->xmc", left[:, :, i], right[:, :, j], preferred_element_type=jnp.float32
            )

        partial = jnp.stack([dot(0, 0) - dot(1, 1), dot(0, 1) + dot(1, 0)], 1)
        partial = partial.reshape((2, 2) + partial.shape[1:])
        even, odd = partial[:, 0], partial[:, 1]
        kept = jnp.where(core == 0, even, odd) + send(
            jnp.where(core == 0, odd, even), lambda q, r, c, x, y, h: (q, r, 1 - c, x, y, h)
        )
        product = jnp.where(zq == 0, kept[0], kept[1]) + send(
            jnp.where(zq == 0, kept[1], kept[0]), lambda q, r, c, x, y, h: (1 - q, r, c, x, y, h)
        )
        real_out = -(wave[0, g] * product[0] - wave[1, g] * product[1])
        imag_out = -(wave[0, g] * product[1] + wave[1, g] * product[0])
        done = jnp.stack([real_out, imag_out]).astype(jnp.bfloat16)
        outs.append(jnp.where(stay, done, send(done, home)))
    return jnp.stack(outs, 1)


def solution(mesh):
    fine = Mesh(mesh.devices.reshape(SIZES), AXES)
    freq, col = AXES[:3], AXES[3:]
    return jax.shard_map(
        local,
        mesh=fine,
        in_specs=(P(None, None, freq, col), P(None, freq)),
        out_specs=P(None, freq, None, col),
        check_vma=False,
    )
```

time: 412 us -> 233 us (0.57)
  waiting for transfers between devices: 273 us -> 51.3 us
  starting transfers between devices: 0.01 us -> 96.3 us
  blocking collectives: 99.7 us -> 24.5 us
  local copies, waits for them, and re-layouts: 9.51 us -> 27.6 us
  other arithmetic: 0.78 us -> 18.8 us
  between operations: 13.5 us -> 0.61 us
    all_gather x1 -> x0, waiting for transfers between devices: 273 us -> none  [predict(): lax.all_gather(upper, 'col', axis=3, tiled=True)]
    ppermute x0 -> x27, starting transfers between devices: none -> 84.2 us  [the longest x26 79.2 us: send(): return lax.ppermute(value, AXES, moved(target))]
    all_to_all x1, blocking collectives: 99.7 us -> 24.5 us  [exchange(): lax.all_to_all(block, ('x', 'zr'), split_axis=0, concat_axis=0, tiled=True)]
    ppermute x0 -> x27, waiting for transfers between devices: none -> 41.6 us  [the longest x26 41.6 us: send(): return lax.ppermute(value, AXES, moved(target))]
    all_to_all x0 -> x2, starting transfers between devices: none -> 12.1 us  [exchange(): lax.all_to_all(block, ('x', 'zr'), split_axis=0, concat_axis=0, tiled=True)]
    all_to_all x0 -> x2, waiting for transfers between devices: none -> 9.68 us  [exchange(): lax.all_to_all(block, ('x', 'zr'), split_axis=0, concat_axis=0, tiled=True)]
    add x0 -> x8, other arithmetic: none -> 9.15 us  [the longest x2 3.87 us: local(): send(near, lambda q, r, c, x, y, h: (0, r, y // 2, x, y, 1 - h) if q == 0...]
    unnamed x9 -> x52, local copies, waits for them, and re-layouts: 4.4 us -> 11.9 us
  transfers between devices with their start and end apart: 1 -> 29, of which waited for: 1 -> 7; matrix products, arithmetic and copies ran while one was open for 1% -> 21% of each run, Pallas kernels for 0% -> 0%
where the time goes in v1:
time: 233 us; the launch traced here: 232 us
  starting transfers between devices  96.3 us (41%)
  waiting for transfers between devices  51.3 us (22%)
  local copies, waits for them, and re-layouts  27.6 us (12%)
  blocking collectives  24.5 us (11%)
  other arithmetic  18.8 us (8%)
  matrix products  13 us (6%)
    ppermute x26, starting transfers between devices, send(): return lax.ppermute(value, AXES, moved(target))  79.2 us
    ppermute x26, waiting for transfers between devices, send(): return lax.ppermute(value, AXES, moved(target))  41.6 us
    all_to_all x1, blocking collectives, exchange(): lax.all_to_all(block, ('x', 'zr'), split_axis=0, concat_axis=0, tiled=True)  24.5 us
    dot_general x8, matrix products, dot(): jnp.einsum('rbmk,xrbkc->xmc', left[:, :, i], right[:, :, j], preferred_el...  13 us
    all_to_all x2, starting transfers between devices, exchange(): lax.all_to_all(block, ('x', 'zr'), split_axis=0, concat_axis=0, tiled=True)  12.1 us
    unnamed x52, local copies, waits for them, and re-layouts  11.9 us
    all_to_all x2, waiting for transfers between devices, exchange(): lax.all_to_all(block, ('x', 'zr'), split_axis=0, concat_axis=0, tiled=True)  9.68 us
    another operation x4, local copies, waits for them, and re-layouts, local(): partial = jnp.stack([dot(0, 0) - dot(1, 1), dot(0, 1) + dot(1, 0)], 1)  5.55 us
  transfers between devices with their start and end apart: 29, of which 7 were waited for; matrix products, arithmetic and copies ran while one was open for 21% of the time, Pallas kernels for 0%

profile of v1, /device:TPU:4, one launch (start us, length us, event | category | flops | bytes accessed | tf_op | source)
XLA Modules:
  0.0 232.1 jit_solution(11122719156065367694)
XLA Ops:
  0.0 2.5 %copy.44 = bf16[2,2,2,2,2,512,128]{6,5,4,3,2,1,0:T(8,128)(2,1)S(1)} copy(bf16[2,2,2,2,2,512,128]{6,5,0,2,3,1,4:T(8,128)(2,1)} %bitcast.192) | data formatting | bytes 8388608 | tf_op jit(solution)/shard_map/transpose | solution.py:53
  2.5 2.0 copy-done
  5.6 6.2 %all-to-all-start.1 = ((bf16[8,2,2,128,128]{4,3,2,1,0:T(8,128)(2,1)}), bf16[8,2,2,128,128]{4,3,2,1,0:T(8,128)(2,1)S(1)}, u32[]{:S(2)}, u32[]{:S(2)}) async-start(bf16[8,2,2,128,128]{4,3,2,1,0:T(8,128)(2,1)} %copy.45), calls=%async_computation.1 | async-start | bytes 2097152 | tf_op jit(solution)/shard_map/all_to_all | solution.py:56
  11.7 3.3 %slice_bitcast_fusion.1 = (bf16[8,2,384,128]{3,2,1,0:T(8,128)(2,1)}, bf16[8,2,384,128]{3,2,1,0:T(8,128)(2,1)S(1)}) fusion(bf16[2,8,2,512,128]{4,3,2,1,0:T(8,128)(2,1)} %bitcast.187), kind=kLoop, calls=%fused_computation.3 | loop fusion | bytes 6291456 | tf_op jit(solution)/shard_map/squeeze | solution.py:58
  15.1 9.7 %all-to-all-done.1 = bf16[8,2,2,128,128]{4,3,2,1,0:T(8,128)(2,1)S(1)} async-done(((bf16[8,2,2,128,128]{4,3,2,1,0:T(8,128)(2,1)}), bf16[8,2,2,128,128]{4,3,2,1,0:T(8,128)(2,1)S(1)}, u32[]{:S(2)}, u32[]{:S(2)}) %all-to-all-start.1) | async-done | bytes 1048608 | tf_op jit(solution)/shard_map/all_to_all | solution.py:56
  25.8 24.5 %all_to_all.15 = bf16[8,2,384,128]{3,2,1,0:T(8,128)(2,1)S(1)} all-to-all(bf16[8,2,384,128]{3,2,1,0:T(8,128)(2,1)S(1)} %get-tuple-element.18), channel_id=1, replica_groups=mesh['zq'=2,'zr'=2,'core'=2,'x'=4,'y'=4,'zh'=2] {'x','zr'}, dimensions={0} | all-to-all | bytes 3145728 | tf_op jit(solution)/shard_map/all_to_all | solution.py:56
  50.3 5.9 %all-to-all-start = ((bf16[8,2,384,128]{3,2,1,0:T(8,128)(2,1)}), bf16[8,2,384,128]{3,2,1,0:T(8,128)(2,1)S(1)}, u32[]{:S(2)}, u32[]{:S(2)}) async-start(bf16[8,2,384,128]{3,2,1,0:T(8,128)(2,1)} %get-tuple-element.17), calls=%async_computation | async-start | bytes 3145728 | tf_op jit(solution)/shard_map/all_to_all | solution.py:56
  57.0 5.9 %collective-permute-start.15 = (bf16[2,2,384,128]{3,2,0,1:T(8,128)(2,1)}, bf16[2,2,384,128]{3,2,0,1:T(8,128)(2,1)}, u32[]{:S(2)}, u32[]{:S(2)}) collective-permute-start(bf16[2,2,384,128]{3,2,0,1:T(8,128)(2,1)} %bitcast.182), channel_id=1, source_target_pairs={{0,128},{1,129},{2,130},{3,131},{4,164},{5,165},{6,166},{7,167},{8... | collective-permute-start | bytes 1179656 | tf_op jit(solution)/shard_map/ppermute | solution.py:35
  66.2 6.4 %collective-permute-start.19 = (bf16[2,2,384,128]{3,2,0,1:T(8,128)(2,1)}, bf16[2,2,384,128]{3,2,0,1:T(8,128)(2,1)}, u32[]{:S(2)}, u32[]{:S(2)}) collective-permute-start(bf16[2,2,384,128]{3,2,0,1:T(8,128)(2,1)} %bitcast.183), channel_id=1, source_target_pairs={{0,1},{1,0},{2,3},{3,2},{4,37},{5,36},{6,39},{7,38},{8,9},{9,8},{1... | collective-permute-start | bytes 1179656 | tf_op jit(solution)/shard_map/ppermute | solution.py:35
  72.6 2.0 collective-permute-start.20
  76.3 8.2 %collective-permute-start.6 = (bf16[2,2,384,128]{3,2,0,1:T(8,128)(2,1)S(1)}, bf16[2,2,384,128]{3,2,0,1:T(8,128)(2,1)S(1)}, u32[]{:S(2)}, u32[]{:S(2)}) collective-permute-start(bf16[2,2,384,128]{3,2,0,1:T(8,128)(2,1)S(1)} %bitcast.200), channel_id=1, source_target_pairs={{0,1},{1,0},{2,3},{3,2},{4,37},{5,36},{6,39},{7,38},{8,9},{9,8},{1... | collective-permute-start | bytes 1179656 | tf_op jit(solution)/shard_map/ppermute | solution.py:35
  84.5 2.9 %collective-permute-start.2 = (bf16[2,2,384,128]{3,2,0,1:T(8,128)(2,1)S(1)}, bf16[2,2,384,128]{3,2,0,1:T(8,128)(2,1)S(1)}, u32[]{:S(2)}, u32[]{:S(2)}) collective-permute-start(bf16[2,2,384,128]{3,2,0,1:T(8,128)(2,1)S(1)} %bitcast.197), channel_id=1, source_target_pairs={{0,128},{1,129},{2,130},{3,131},{4,164},{5,165},{6,166},{7,167},{8... | collective-permute-start | bytes 1179656 | tf_op jit(solution)/shard_map/ppermute | solution.py:35
  91.7 3.0 %collective-permute-start.17 = (bf16[2,2,384,128]{3,2,0,1:T(8,128)(2,1)}, bf16[2,2,384,128]{3,2,0,1:T(8,128)(2,1)S(1)}, u32[]{:S(2)}, u32[]{:S(2)}) collective-permute-start(bf16[2,2,384,128]{3,2,0,1:T(8,128)(2,1)} %add_add_fusion), channel_id=1, source_target_pairs={{0,4},{1,5},{2,6},{3,7},{8,12},{9,13},{10,14},{11,15},{16,20},{17,... | collective-permute-start | bytes 1179656 | tf_op jit(solution)/shard_map/ppermute | solution.py:35
  95.5 2.0 add.81
  99.4 5.4 %collective-permute-start.16 = (bf16[2,2,384,128]{3,2,0,1:T(8,128)(2,1)}, bf16[2,2,384,128]{3,2,0,1:T(8,128)(2,1)}, u32[]{:S(2)}, u32[]{:S(2)}) collective-permute-start(bf16[2,2,384,128]{3,2,0,1:T(8,128)(2,1)} %add_add_fusion), channel_id=1, source_target_pairs={{0,2},{1,3},{2,4},{3,5},{8,10},{9,11},{10,12},{11,13},{16,18},{17,... | collective-permute-start | bytes 1179656 | tf_op jit(solution)/shard_map/ppermute | solution.py:35
  104.8 2.0 collective-permute-start.22
  108.8 5.4 %collective-permute-start.21 = (bf16[2,2,384,128]{3,2,0,1:T(8,128)(2,1)}, bf16[2,2,384,128]{3,2,0,1:T(8,128)(2,1)}, u32[]{:S(2)}, u32[]{:S(2)}) collective-permute-start(bf16[2,2,384,128]{3,2,0,1:T(8,128)(2,1)} %add.81), channel_id=1, source_target_pairs={{0,2},{1,3},{2,4},{3,5},{8,10},{9,11},{10,12},{11,13},{16,18},{17,... | collective-permute-start | bytes 1179656 | tf_op jit(solution)/shard_map/ppermute | solution.py:35
  123.8 2.0 collective-permute-start.4
  127.8 5.5 %collective-permute-start.3 = (bf16[2,2,384,128]{3,2,0,1:T(8,128)(2,1)}, bf16[2,2,384,128]{3,2,0,1:T(8,128)(2,1)}, u32[]{:S(2)}, u32[]{:S(2)}) collective-permute-start(bf16[2,2,384,128]{3,2,0,1:T(8,128)(2,1)} %add_add_fusion.1), channel_id=1, source_target_pairs={{0,2},{1,3},{2,4},{3,5},{8,10},{9,11},{10,12},{11,13},{16,18},{17,... | collective-permute-start | bytes 1179656 | tf_op jit(solution)/shard_map/ppermute | solution.py:35
  133.3 2.1 collective-permute-start.9
  137.3 1.9 select_bitcast_fusion.6
  144.8 2.0 convolution_bitcast_fusion.2
  146.8 5.4 %collective-permute-start.8 = (bf16[2,2,384,128]{3,2,0,1:T(8,128)(2,1)}, bf16[2,2,384,128]{3,2,0,1:T(8,128)(2,1)}, u32[]{:S(2)}, u32[]{:S(2)}) collective-permute-start(bf16[2,2,384,128]{3,2,0,1:T(8,128)(2,1)} %add.72), channel_id=1, source_target_pairs={{0,2},{1,3},{2,4},{3,5},{8,10},{9,11},{10,12},{11,13},{16,18},{17,... | collective-permute-start | bytes 1179656 | tf_op jit(solution)/shard_map/ppermute | solution.py:35
  156.2 5.0 %collective-permute-start = (f32[2,2]{1,0:T(2,128)S(1)}, f32[2,2]{1,0:T(2,128)S(1)}, u32[]{:S(2)}, u32[]{:S(2)}) collective-permute-start(f32[2,2]{1,0:T(2,128)S(1)} %copy-done.21), channel_id=1, source_target_pairs={{32,8},{33,9},{34,10},{35,11},{36,12},{37,13},{38,14},{39,15},{128... | collective-permute-start | bytes 56 | tf_op jit(solution)/shard_map/ppermute | solution.py:50
  161.6 2.0 select_bitcast_fusion.11
  170.4 3.0 %fusion = f32[4,128,384]{2,1,0:T(8,128)} fusion(f32[4,128,384]{2,1,0:T(8,128)} %convolution_bitcast_fusion.6, bf16[4,2,1,4,128,128]{4,5,1,0,3,2:T(8,128)(2,1)S(1)} %copy.77, bf16[2,4,2,384,128]{4,3,0,1,2:T(8,128)(2,1)} %copy-done.1), kind=kOutput, calls=%fused_computation.18 | convolution fusion | flops 402849792 | bytes 3407872 | tf_op jit(solution)/shard_map/rbmk,xrbkc->xmc/dot_general | solution.py:94
  177.7 3.0 %collective-permute-start.12 = (f32[2,384,128]{2,1,0:T(8,128)S(1)}, f32[2,384,128]{2,1,0:T(8,128)S(1)}, u32[]{:S(2)}, u32[]{:S(2)}) collective-permute-start(f32[2,384,128]{2,1,0:T(8,128)S(1)} %select_bitcast_fusion.7), channel_id=1, source_target_pairs={{0,128},{1,129},{2,130},{3,131},{4,132},{5,133},{6,134},{7,135},{8... | collective-permute-start | bytes 1179656 | tf_op jit(solution)/shard_map/ppermute | solution.py:35
  180.7 26.6 %collective-permute-done.25 = f32[2,384,128]{2,1,0:T(8,128)S(1)} collective-permute-done((f32[2,384,128]{2,1,0:T(8,128)S(1)}, f32[2,384,128]{2,1,0:T(8,128)S(1)}, u32[]{:S(2)}, u32[]{:S(2)}) %collective-permute-start.25) | collective-permute-done | bytes 393248 | tf_op jit(solution)/shard_map/ppermute | solution.py:35
  208.7 1.9 collective-permute-start.26
  210.7 4.1 %collective-permute-done.12 = f32[2,384,128]{2,1,0:T(8,128)S(1)} collective-permute-done((f32[2,384,128]{2,1,0:T(8,128)S(1)}, f32[2,384,128]{2,1,0:T(8,128)S(1)}, u32[]{:S(2)}, u32[]{:S(2)}) %collective-permute-start.12) | collective-permute-done | bytes 393248 | tf_op jit(solution)/shard_map/ppermute | solution.py:35
  216.2 5.9 %collective-permute-start.13 = (bf16[2,384,128]{2,1,0:T(8,128)(2,1)S(1)}, bf16[2,384,128]{2,1,0:T(8,128)(2,1)S(1)}, u32[]{:S(2)}, u32[]{:S(2)}) collective-permute-start(bf16[2,384,128]{2,1,0:T(8,128)(2,1)S(1)} %pad_maximum_fusion.7), channel_id=1, source_target_pairs={{8,32},{9,33},{10,34},{11,35},{12,36},{13,37},{14,38},{15,39},{16,... | collective-permute-start | bytes 589832 | tf_op jit(solution)/shard_map/ppermute | solution.py:35
  223.7 7.6 %collective-permute-done.13 = bf16[2,384,128]{2,1,0:T(8,128)(2,1)S(1)} collective-permute-done((bf16[2,384,128]{2,1,0:T(8,128)(2,1)S(1)}, bf16[2,384,128]{2,1,0:T(8,128)(2,1)S(1)}, u32[]{:S(2)}, u32[]{:S(2)}) %collective-permute-start.13) | collective-permute-done | bytes 196640 | tf_op jit(solution)/shard_map/ppermute | solution.py:35
  (128 shorter events, 56.1 us)
Async XLA Ops:
  5.6 19.2 %all-to-all-start.1 = ((bf16[8,2,2,128,128]{4,3,2,1,0:T(8,128)(2,1)}), bf16[8,2,2,128,128]{4,3,2,1,0:T(8,128)(2,1)S(1)}, u32[]{:S(2)}, u32[]{:S(2)}) async-start(bf16[8,2,2,128,128]{4,3,2,1,0:T(8,128)(2,1)} %copy.45), calls=%async_computation.1 | async-start | bytes 2097152 | tf_op jit(solution)/shard_map/all_to_all | solution.py:56
  50.3 24.4 %all-to-all-start = ((bf16[8,2,384,128]{3,2,1,0:T(8,128)(2,1)}), bf16[8,2,384,128]{3,2,1,0:T(8,128)(2,1)S(1)}, u32[]{:S(2)}, u32[]{:S(2)}) async-start(bf16[8,2,384,128]{3,2,1,0:T(8,128)(2,1)} %get-tuple-element.17), calls=%async_computation | async-start | bytes 3145728 | tf_op jit(solution)/shard_map/all_to_all | solution.py:56
  57.0 19.3 %collective-permute-start.15 = (bf16[2,2,384,128]{3,2,0,1:T(8,128)(2,1)}, bf16[2,2,384,128]{3,2,0,1:T(8,128)(2,1)}, u32[]{:S(2)}, u32[]{:S(2)}) collective-permute-start(bf16[2,2,384,128]{3,2,0,1:T(8,128)(2,1)} %bitcast.182), channel_id=1, source_target_pairs={{0,128},{1,129},{2,130},{3,131},{4,164},{5,165},{6,166},{7,167},{8... | collective-permute-start | bytes 1179656 | tf_op jit(solution)/shard_map/ppermute | solution.py:35
  63.7 20.8 %collective-permute-start.14 = (bf16[2,2,384,128]{3,2,0,1:T(8,128)(2,1)}, bf16[2,2,384,128]{3,2,0,1:T(8,128)(2,1)}, u32[]{:S(2)}, u32[]{:S(2)}) collective-permute-start(bf16[2,2,384,128]{3,2,0,1:T(8,128)(2,1)} %bitcast.183), channel_id=1, source_target_pairs={{4,36},{5,37},{6,38},{7,39},{12,44},{13,45},{14,46},{15,47},{20,52... | collective-permute-start | bytes 1179656 | tf_op jit(solution)/shard_map/ppermute | solution.py:35
  66.2 23.1 %collective-permute-start.19 = (bf16[2,2,384,128]{3,2,0,1:T(8,128)(2,1)}, bf16[2,2,384,128]{3,2,0,1:T(8,128)(2,1)}, u32[]{:S(2)}, u32[]{:S(2)}) collective-permute-start(bf16[2,2,384,128]{3,2,0,1:T(8,128)(2,1)} %bitcast.183), channel_id=1, source_target_pairs={{0,1},{1,0},{2,3},{3,2},{4,37},{5,36},{6,39},{7,38},{8,9},{9,8},{1... | collective-permute-start | bytes 1179656 | tf_op jit(solution)/shard_map/ppermute | solution.py:35
  72.6 19.1 %collective-permute-start.20 = (bf16[2,2,384,128]{3,2,0,1:T(8,128)(2,1)}, bf16[2,2,384,128]{3,2,0,1:T(8,128)(2,1)}, u32[]{:S(2)}, u32[]{:S(2)}) collective-permute-start(bf16[2,2,384,128]{3,2,0,1:T(8,128)(2,1)} %bitcast.182), channel_id=1, source_target_pairs={{0,129},{1,128},{2,131},{3,130},{4,165},{5,164},{6,167},{7,166},{8... | collective-permute-start | bytes 1179656 | tf_op jit(solution)/shard_map/ppermute | solution.py:35
  74.7 20.0 %copy-start.11 = (bf16[8,2,128,128]{3,2,1,0:T(8,128)(2,1)S(1)}, bf16[8,2,128,128]{3,2,1,0:T(8,128)(2,1)}, u32[]{:S(2)}) copy-start(bf16[8,2,128,128]{3,2,1,0:T(8,128)(2,1)} %get-tuple-element.33) | copy-start | bytes 1572868
  74.7 20.0 %copy-start.12 = (bf16[8,2,128,128]{3,2,1,0:T(8,128)(2,1)S(1)}, bf16[8,2,128,128]{3,2,1,0:T(8,128)(2,1)}, u32[]{:S(2)}) copy-start(bf16[8,2,128,128]{3,2,1,0:T(8,128)(2,1)} %get-tuple-element.34) | copy-start | bytes 1572868
  74.8 24.6 %collective-permute-start.1 = (bf16[2,2,384,128]{3,2,0,1:T(8,128)(2,1)S(1)}, bf16[2,2,384,128]{3,2,0,1:T(8,128)(2,1)S(1)}, u32[]{:S(2)}, u32[]{:S(2)}) collective-permute-start(bf16[2,2,384,128]{3,2,0,1:T(8,128)(2,1)S(1)} %bitcast.199), channel_id=1, source_target_pairs={{4,36},{5,37},{6,38},{7,39},{12,44},{13,45},{14,46},{15,47},{20,52... | collective-permute-start | bytes 1179656 | tf_op jit(solution)/shard_map/ppermute | solution.py:35
  76.3 28.5 %collective-permute-start.6 = (bf16[2,2,384,128]{3,2,0,1:T(8,128)(2,1)S(1)}, bf16[2,2,384,128]{3,2,0,1:T(8,128)(2,1)S(1)}, u32[]{:S(2)}, u32[]{:S(2)}) collective-permute-start(bf16[2,2,384,128]{3,2,0,1:T(8,128)(2,1)S(1)} %bitcast.200), channel_id=1, source_target_pairs={{0,1},{1,0},{2,3},{3,2},{4,37},{5,36},{6,39},{7,38},{8,9},{9,8},{1... | collective-permute-start | bytes 1179656 | tf_op jit(solution)/shard_map/ppermute | solution.py:35
  84.5 12.9 %collective-permute-start.2 = (bf16[2,2,384,128]{3,2,0,1:T(8,128)(2,1)S(1)}, bf16[2,2,384,128]{3,2,0,1:T(8,128)(2,1)S(1)}, u32[]{:S(2)}, u32[]{:S(2)}) collective-permute-start(bf16[2,2,384,128]{3,2,0,1:T(8,128)(2,1)S(1)} %bitcast.197), channel_id=1, source_target_pairs={{0,128},{1,129},{2,130},{3,131},{4,164},{5,165},{6,166},{7,167},{8... | collective-permute-start | bytes 1179656 | tf_op jit(solution)/shard_map/ppermute | solution.py:35
  89.3 17.5 %collective-permute-start.7 = (bf16[2,2,384,128]{3,2,0,1:T(8,128)(2,1)S(1)}, bf16[2,2,384,128]{3,2,0,1:T(8,128)(2,1)S(1)}, u32[]{:S(2)}, u32[]{:S(2)}) collective-permute-start(bf16[2,2,384,128]{3,2,0,1:T(8,128)(2,1)S(1)} %bitcast.198), channel_id=1, source_target_pairs={{0,129},{1,128},{2,131},{3,130},{4,165},{5,164},{6,167},{7,166},{8... | collective-permute-start | bytes 1179656 | tf_op jit(solution)/shard_map/ppermute | solution.py:35
  91.7 17.0 %collective-permute-start.17 = (bf16[2,2,384,128]{3,2,0,1:T(8,128)(2,1)}, bf16[2,2,384,128]{3,2,0,1:T(8,128)(2,1)S(1)}, u32[]{:S(2)}, u32[]{:S(2)}) collective-permute-start(bf16[2,2,384,128]{3,2,0,1:T(8,128)(2,1)} %add_add_fusion), channel_id=1, source_target_pairs={{0,4},{1,5},{2,6},{3,7},{8,12},{9,13},{10,14},{11,15},{16,20},{17,... | collective-permute-start | bytes 1179656 | tf_op jit(solution)/shard_map/ppermute | solution.py:35
  97.4 17.9 %copy-start.19 = (bf16[2,2,384,128]{3,2,0,1:T(8,128)(2,1)}, bf16[2,2,384,128]{3,2,0,1:T(8,128)(2,1)S(1)}, u32[]{:S(2)}) copy-start(bf16[2,2,384,128]{3,2,0,1:T(8,128)(2,1)S(1)} %collective-permute-done.2) | copy-start | bytes 1179652
  97.4 26.4 %collective-permute-start.18 = (bf16[2,2,384,128]{3,2,0,1:T(8,128)(2,1)}, bf16[2,2,384,128]{3,2,0,1:T(8,128)(2,1)}, u32[]{:S(2)}, u32[]{:S(2)}) collective-permute-start(bf16[2,2,384,128]{3,2,0,1:T(8,128)(2,1)} %add_add_fusion), channel_id=1, source_target_pairs={{0,6},{1,7},{2,0},{3,1},{8,14},{9,15},{10,8},{11,9},{16,22},{17,23... | collective-permute-start | bytes 1179656 | tf_op jit(solution)/shard_map/ppermute | solution.py:35
  99.4 26.5 %collective-permute-start.16 = (bf16[2,2,384,128]{3,2,0,1:T(8,128)(2,1)}, bf16[2,2,384,128]{3,2,0,1:T(8,128)(2,1)}, u32[]{:S(2)}, u32[]{:S(2)}) collective-permute-start(bf16[2,2,384,128]{3,2,0,1:T(8,128)(2,1)} %add_add_fusion), channel_id=1, source_target_pairs={{0,2},{1,3},{2,4},{3,5},{8,10},{9,11},{10,12},{11,13},{16,18},{17,... | collective-permute-start | bytes 1179656 | tf_op jit(solution)/shard_map/ppermute | solution.py:35
  104.8 23.0 %collective-permute-start.22 = (bf16[2,2,384,128]{3,2,0,1:T(8,128)(2,1)}, bf16[2,2,384,128]{3,2,0,1:T(8,128)(2,1)}, u32[]{:S(2)}, u32[]{:S(2)}) collective-permute-start(bf16[2,2,384,128]{3,2,0,1:T(8,128)(2,1)} %add.81), channel_id=1, source_target_pairs={{0,4},{1,5},{2,6},{3,7},{8,12},{9,13},{10,14},{11,15},{16,20},{17,... | collective-permute-start | bytes 1179656 | tf_op jit(solution)/shard_map/ppermute | solution.py:35
  106.8 26.5 %collective-permute-start.23 = (bf16[2,2,384,128]{3,2,0,1:T(8,128)(2,1)}, bf16[2,2,384,128]{3,2,0,1:T(8,128)(2,1)}, u32[]{:S(2)}, u32[]{:S(2)}) collective-permute-start(bf16[2,2,384,128]{3,2,0,1:T(8,128)(2,1)} %add.81), channel_id=1, source_target_pairs={{0,6},{1,7},{2,0},{3,1},{8,14},{9,15},{10,8},{11,9},{16,22},{17,23... | collective-permute-start | bytes 1179656 | tf_op jit(solution)/shard_map/ppermute | solution.py:35
  108.8 26.6 %collective-permute-start.21 = (bf16[2,2,384,128]{3,2,0,1:T(8,128)(2,1)}, bf16[2,2,384,128]{3,2,0,1:T(8,128)(2,1)}, u32[]{:S(2)}, u32[]{:S(2)}) collective-permute-start(bf16[2,2,384,128]{3,2,0,1:T(8,128)(2,1)} %add.81), channel_id=1, source_target_pairs={{0,2},{1,3},{2,4},{3,5},{8,10},{9,11},{10,12},{11,13},{16,18},{17,... | collective-permute-start | bytes 1179656 | tf_op jit(solution)/shard_map/ppermute | solution.py:35
  123.8 23.0 %collective-permute-start.4 = (bf16[2,2,384,128]{3,2,0,1:T(8,128)(2,1)}, bf16[2,2,384,128]{3,2,0,1:T(8,128)(2,1)}, u32[]{:S(2)}, u32[]{:S(2)}) collective-permute-start(bf16[2,2,384,128]{3,2,0,1:T(8,128)(2,1)} %add_add_fusion.1), channel_id=1, source_target_pairs={{0,4},{1,5},{2,6},{3,7},{8,12},{9,13},{10,14},{11,15},{16,20},{17,... | collective-permute-start | bytes 1179656 | tf_op jit(solution)/shard_map/ppermute | solution.py:35
  125.8 30.4 %collective-permute-start.5 = (bf16[2,2,384,128]{3,2,0,1:T(8,128)(2,1)}, bf16[2,2,384,128]{3,2,0,1:T(8,128)(2,1)}, u32[]{:S(2)}, u32[]{:S(2)}) collective-permute-start(bf16[2,2,384,128]{3,2,0,1:T(8,128)(2,1)} %add_add_fusion.1), channel_id=1, source_target_pairs={{0,6},{1,7},{2,0},{3,1},{8,14},{9,15},{10,8},{11,9},{16,22},{17,23... | collective-permute-start | bytes 1179656 | tf_op jit(solution)/shard_map/ppermute | solution.py:35
  127.8 33.5 %collective-permute-start.3 = (bf16[2,2,384,128]{3,2,0,1:T(8,128)(2,1)}, bf16[2,2,384,128]{3,2,0,1:T(8,128)(2,1)}, u32[]{:S(2)}, u32[]{:S(2)}) collective-permute-start(bf16[2,2,384,128]{3,2,0,1:T(8,128)(2,1)} %add_add_fusion.1), channel_id=1, source_target_pairs={{0,2},{1,3},{2,4},{3,5},{8,10},{9,11},{10,12},{11,13},{16,18},{17,... | collective-permute-start | bytes 1179656 | tf_op jit(solution)/shard_map/ppermute | solution.py:35
  133.3 28.3 %collective-permute-start.9 = (bf16[2,2,384,128]{3,2,0,1:T(8,128)(2,1)}, bf16[2,2,384,128]{3,2,0,1:T(8,128)(2,1)}, u32[]{:S(2)}, u32[]{:S(2)}) collective-permute-start(bf16[2,2,384,128]{3,2,0,1:T(8,128)(2,1)} %add.72), channel_id=1, source_target_pairs={{0,4},{1,5},{2,6},{3,7},{8,12},{9,13},{10,14},{11,15},{16,20},{17,... | collective-permute-start | bytes 1179656 | tf_op jit(solution)/shard_map/ppermute | solution.py:35
  135.3 26.2 %collective-permute-start.10 = (bf16[2,2,384,128]{3,2,0,1:T(8,128)(2,1)}, bf16[2,2,384,128]{3,2,0,1:T(8,128)(2,1)}, u32[]{:S(2)}, u32[]{:S(2)}) collective-permute-start(bf16[2,2,384,128]{3,2,0,1:T(8,128)(2,1)} %add.72), channel_id=1, source_target_pairs={{0,6},{1,7},{2,0},{3,1},{8,14},{9,15},{10,8},{11,9},{16,22},{17,23... | collective-permute-start | bytes 1179656 | tf_op jit(solution)/shard_map/ppermute | solution.py:35
  146.8 14.7 %collective-permute-start.8 = (bf16[2,2,384,128]{3,2,0,1:T(8,128)(2,1)}, bf16[2,2,384,128]{3,2,0,1:T(8,128)(2,1)}, u32[]{:S(2)}, u32[]{:S(2)}) collective-permute-start(bf16[2,2,384,128]{3,2,0,1:T(8,128)(2,1)} %add.72), channel_id=1, source_target_pairs={{0,2},{1,3},{2,4},{3,5},{8,10},{9,11},{10,12},{11,13},{16,18},{17,... | collective-permute-start | bytes 1179656 | tf_op jit(solution)/shard_map/ppermute | solution.py:35
  156.2 19.2 %collective-permute-start = (f32[2,2]{1,0:T(2,128)S(1)}, f32[2,2]{1,0:T(2,128)S(1)}, u32[]{:S(2)}, u32[]{:S(2)}) collective-permute-start(f32[2,2]{1,0:T(2,128)S(1)} %copy-done.21), channel_id=1, source_target_pairs={{32,8},{33,9},{34,10},{35,11},{36,12},{37,13},{38,14},{39,15},{128... | collective-permute-start | bytes 56 | tf_op jit(solution)/shard_map/ppermute | solution.py:50
  161.3 14.9 %collective-permute-start.24 = (f32[2,2,384,128]{3,2,1,0:T(8,128)}, f32[2,2,384,128]{3,2,1,0:T(8,128)}, u32[]{:S(2)}, u32[]{:S(2)}) collective-permute-start(f32[2,2,384,128]{3,2,1,0:T(8,128)} %select_bitcast_fusion), channel_id=1, source_target_pairs={{0,32},{1,33},{2,34},{3,35},{4,36},{5,37},{6,38},{7,39},{8,40},{9,... | collective-permute-start | bytes 2359304 | tf_op jit(solution)/shard_map/ppermute | solution.py:35
  174.9 2.6 %collective-permute-start.11 = (f32[2,2,384,128]{3,2,1,0:T(8,128)S(1)}, f32[2,2,384,128]{3,2,1,0:T(8,128)S(1)}, u32[]{:S(2)}, u32[]{:S(2)}) collective-permute-start(f32[2,2,384,128]{3,2,1,0:T(8,128)S(1)} %select_bitcast_fusion.1), channel_id=1, source_target_pairs={{0,32},{1,33},{2,34},{3,35},{4,36},{5,37},{6,38},{7,39},{8,40},{9,... | collective-permute-start | bytes 2359304 | tf_op jit(solution)/shard_map/ppermute | solution.py:35
  177.4 29.8 %collective-permute-start.25 = (f32[2,384,128]{2,1,0:T(8,128)S(1)}, f32[2,384,128]{2,1,0:T(8,128)S(1)}, u32[]{:S(2)}, u32[]{:S(2)}) collective-permute-start(f32[2,384,128]{2,1,0:T(8,128)S(1)} %select_bitcast_fusion.2), channel_id=1, source_target_pairs={{0,128},{1,129},{2,130},{3,131},{4,132},{5,133},{6,134},{7,135},{8... | collective-permute-start | bytes 1179656 | tf_op jit(solution)/shard_map/ppermute | solution.py:35
  177.7 37.0 %collective-permute-start.12 = (f32[2,384,128]{2,1,0:T(8,128)S(1)}, f32[2,384,128]{2,1,0:T(8,128)S(1)}, u32[]{:S(2)}, u32[]{:S(2)}) collective-permute-start(f32[2,384,128]{2,1,0:T(8,128)S(1)} %select_bitcast_fusion.7), channel_id=1, source_target_pairs={{0,128},{1,129},{2,130},{3,131},{4,132},{5,133},{6,134},{7,135},{8... | collective-permute-start | bytes 1179656 | tf_op jit(solution)/shard_map/ppermute | solution.py:35
  208.7 14.9 %collective-permute-start.26 = (bf16[2,384,128]{2,1,0:T(8,128)(2,1)S(1)}, bf16[2,384,128]{2,1,0:T(8,128)(2,1)S(1)}, u32[]{:S(2)}, u32[]{:S(2)}) collective-permute-start(bf16[2,384,128]{2,1,0:T(8,128)(2,1)S(1)} %pad_maximum_fusion.8), channel_id=1, source_target_pairs={{8,32},{9,33},{10,34},{11,35},{12,36},{13,37},{14,38},{15,39},{16,... | collective-permute-start | bytes 589832 | tf_op jit(solution)/shard_map/ppermute | solution.py:35
  216.2 15.1 %collective-permute-start.13 = (bf16[2,384,128]{2,1,0:T(8,128)(2,1)S(1)}, bf16[2,384,128]{2,1,0:T(8,128)(2,1)S(1)}, u32[]{:S(2)}, u32[]{:S(2)}) collective-permute-start(bf16[2,384,128]{2,1,0:T(8,128)(2,1)S(1)} %pad_maximum_fusion.7), channel_id=1, source_target_pairs={{8,32},{9,33},{10,34},{11,35},{12,36},{13,37},{14,38},{15,39},{16,... | collective-permute-start | bytes 589832 | tf_op jit(solution)/shard_map/ppermute | solution.py:35
  (19 other events, 112.5 us)

commit v2 on v1

v2 whole, which is shorter than its diff:
```python
import jax
import jax.numpy as jnp
from jax import lax
from jax.experimental import pallas as pl
from jax.experimental.pallas import tpu as pltpu
from jax.sharding import Mesh, PartitionSpec as P

NOUT = 384
AXES = ("zq", "zr", "core", "x", "y", "zh")
SIZES = (2, 2, 2, 4, 4, 2)


def coordinates():
    out = [()]
    for size in SIZES:
        out = [c + (i,) for c in out for i in range(size)]
    return out


def flat(c):
    index = 0
    for i, size in zip(c, SIZES):
        index = index * size + i
    return index


def moved(target):
    pairs = []
    for c in coordinates():
        t = target(*c)
        if t is not None:
            pairs.append((flat(c), flat(t)))
    return pairs


def send(value, target):
    return lax.ppermute(value, AXES, moved(target))


def swap_core(value):
    return lax.ppermute(value, "core", [(0, 1), (1, 0)])


def contract(place, shots, a_own, a_peer, b_own, b_peer):
    half, lanes = shots.shape[-2:]
    depth = 16 * lanes

    def kernel(place_ref, u_ref, ao_ref, ap_ref, bo_ref, bp_ref, sent_ref, kept_ref, left):
        core, zh, zq = place_ref[0], place_ref[1], place_ref[2]
        for xl in range(2):
            for ys in range(4):
                for zs in range(2):
                    start = ((xl * 4 + ys) * 2 + zs) * lanes
                    for part in range(2):
                        left[part * half : (part + 1) * half, start : start + lanes] = u_ref[ys, zs ^ zh, xl, part]

        first = core == 0
        for side, out in ((1, sent_ref), (0, kept_ref)):
            for low in range(2):
                x = 2 * (zq ^ side) + low
                rows = []
                for zr in range(2):
                    i = 2 * x + zr
                    parts = []
                    for part in range(2):
                        ao, ap, bo, bp = ao_ref[i, part], ap_ref[i, part], bo_ref[i, part], bp_ref[i, part]
                        parts.append(
                            jnp.concatenate(
                                [
                                    jnp.where(first, ao, ap),
                                    jnp.where(first, ap, ao),
                                    jnp.where(first, bo, bp),
                                    jnp.where(first, bp, bo),
                                ],
                                0,
                            )
                        )
                    rows.append(jnp.concatenate(parts, 1))
                right = jnp.concatenate(rows, 0)
                both = jnp.dot(left[...], right, preferred_element_type=jnp.float32)
                out[low, 0] = both[:half, :lanes] - both[half:, lanes:]
                out[low, 1] = both[:half, lanes:] + both[half:, :lanes]

    vmem = pl.BlockSpec(memory_space=pltpu.VMEM)
    result = jax.ShapeDtypeStruct((2, 2, half, lanes), jnp.float32)
    return pl.pallas_call(
        kernel,
        out_shape=(result, result),
        in_specs=[pl.BlockSpec(memory_space=pltpu.SMEM)] + [vmem] * 5,
        out_specs=(vmem, vmem),
        scratch_shapes=[pltpu.VMEM((2 * half, depth), jnp.bfloat16)],
        cost_estimate=pl.CostEstimate(
            flops=2 * 2 * half * depth * 8 * lanes, bytes_accessed=7 << 20, transcendentals=0
        ),
        compiler_params=pltpu.CompilerParams(vmem_limit_bytes=40 << 20),
    )(place, shots, a_own, a_peer, b_own, b_peer)


def local(spectra, wavelet):
    zq, core, x = lax.axis_index("zq"), lax.axis_index("core"), lax.axis_index("x")
    zh = lax.axis_index("zh")
    place = jnp.stack([core, zh, zq]).astype(jnp.int32)
    rows, lanes = spectra.shape[2:]
    window = NOUT * rows // 512
    half = window // 2
    first = core == 0

    wave = send(wavelet, lambda q, r, c, x, y, h: (x // 2, r, x % 2, 2 * q + c, y, h))

    def ordered(block):
        block = block.reshape((2, 2, 2, 2, 2) + block.shape[2:])
        return block.transpose(4, 1, 3, 2, 0, 5, 6).reshape((2, 8, 2) + block.shape[5:])

    low, mid, rest = spectra[:, :, :half], spectra[:, :, half:window], spectra[:, :, window:]
    passed = swap_core(jnp.where(first, mid, low))
    a = ordered(jnp.where(first, low, passed))
    b = ordered(
        jnp.where(first, jnp.concatenate([rest, passed], 2), spectra[:, :, half:])
    )

    def exchange(block):
        return lax.all_to_all(block, ("x", "zr"), split_axis=0, concat_axis=0, tiled=True)

    a_own = [exchange(a[g]) for g in range(2)]
    b_own = [exchange(b[g]) for g in range(2)]

    outs = []
    for g in range(2):
        shots = a_own[g].reshape((4, 2) + a_own[g].shape[1:])[:, 0]
        near, far = shots[:2], shots[2:]
        own = jnp.where(zq == 0, near, send(far, lambda q, r, c, x, y, h: (1, r, c, x, y, h) if q == 0 else None))
        other = send(near, lambda q, r, c, x, y, h: (0, r, c, x, y, 1 - h) if q == 0 else None) + send(
            far, lambda q, r, c, x, y, h: (1, r, c, x, y, 1 - h) if q == 0 else None
        )
        pieces = jnp.stack([own, other])
        pieces = jnp.broadcast_to(pieces[None], (4,) + pieces.shape)
        spread = lax.all_to_all(pieces, "y", split_axis=0, concat_axis=0, tiled=True)
        a_peer, b_peer = swap_core(a_own[g]), swap_core(b_own[g])
        sent, kept = contract(place, spread, a_own[g], a_peer, b_own[g], b_peer)
        product = kept + send(sent, lambda q, r, c, x, y, h: (1 - q, r, c, x, y, h))
        real_out = -(wave[0, g] * product[:, 0] - wave[1, g] * product[:, 1])
        imag_out = -(wave[0, g] * product[:, 1] + wave[1, g] * product[:, 0])
        done = jnp.stack([real_out, imag_out], 1).astype(jnp.bfloat16)
        same, cross = jnp.where(first, done[0], done[1]), jnp.where(first, done[1], done[0])
        same = send(same, lambda q, r, c, x, y, h: (x // 2, r, x % 2, 2 * q + c, y, h))
        cross = send(cross, lambda q, r, c, x, y, h: (x // 2, r, x % 2, 2 * q + 1 - c, y, h))
        even = x % 2 == 0
        outs.append(
            jnp.concatenate([jnp.where(even, same, cross), jnp.where(even, cross, same)], 1)
        )
    return jnp.stack(outs, 1)


def solution(mesh):
    fine = Mesh(mesh.devices.reshape(SIZES), AXES)
    freq, col = AXES[:3], AXES[3:]
    return jax.shard_map(
        local,
        mesh=fine,
        in_specs=(P(None, None, freq, col), P(None, freq)),
        out_specs=P(None, freq, None, col),
        check_vma=False,
    )
```

time: 233 us -> 188 us (0.81)
  starting transfers between devices: 96.3 us -> 62.5 us
  local copies, waits for them, and re-layouts: 27.6 us -> 13.8 us
  matrix products: 13 us -> 0 us
  blocking collectives: 24.5 us -> 36.9 us
  other arithmetic: 18.8 us -> 9.04 us
  Pallas kernels: 0 us -> 6.97 us
  waiting for transfers between devices: 51.3 us -> 57 us
    ppermute x26 -> x13, starting transfers between devices: 79.2 us -> 40.1 us  [send(): return lax.ppermute(value, AXES, moved(target))]
    dot_general x8 -> x0, matrix products: 13 us -> none  [dot(): jnp.einsum('rbmk,xrbkc->xmc', left[:, :, i], right[:, :, j], preferred_el...]
    all_to_all x1 -> x2, blocking collectives: 24.5 us -> 36.9 us  [exchange(): lax.all_to_all(block, ('x', 'zr'), split_axis=0, concat_axis=0, tiled=True)]
    all_to_all x0 -> x2, starting transfers between devices: none -> 9.26 us  [local(): lax.all_to_all(pieces, 'y', split_axis=0, concat_axis=0, tiled=True)]
    add x8 -> x2, other arithmetic: 9.15 us -> 0.08 us  [local(): product = kept + send(sent, lambda q, r, c, x, y, h: (1 - q, r, c, x, y, h))]
    pallas_call x0 -> x2, Pallas kernels: none -> 6.97 us  [contract(): pl.pallas_call(kernel, out_shape=(result, result), in_specs=[pl.BlockSpec...]
    all_to_all x2, waiting for transfers between devices: 9.68 us -> 3.8 us  [exchange(): lax.all_to_all(block, ('x', 'zr'), split_axis=0, concat_axis=0, tiled=True)]
    ppermute x26 -> x13, waiting for transfers between devices: 41.6 us -> 47.4 us  [send(): return lax.ppermute(value, AXES, moved(target))]
  transfers between devices with their start and end apart: 29 -> 22, of which waited for: 7 -> 11; matrix products, arithmetic and copies ran while one was open for 21% -> 6% of each run, Pallas kernels for 0% -> 4%
where the time goes in v2:
time: 188 us; the launch traced here: 187 us
  starting transfers between devices  62.5 us (33%)
  waiting for transfers between devices  57 us (30%)
  blocking collectives  36.9 us (20%)
  local copies, waits for them, and re-layouts  13.8 us (7%)
  other arithmetic  9.04 us (5%)
  Pallas kernels  6.97 us (4%)
    ppermute x13, waiting for transfers between devices, send(): return lax.ppermute(value, AXES, moved(target))  47.4 us
    ppermute x13, starting transfers between devices, send(): return lax.ppermute(value, AXES, moved(target))  40.1 us
    all_to_all x2, blocking collectives, exchange(): lax.all_to_all(block, ('x', 'zr'), split_axis=0, concat_axis=0, tiled=True)  36.9 us
    all_to_all x2, starting transfers between devices, exchange(): lax.all_to_all(block, ('x', 'zr'), split_axis=0, concat_axis=0, tiled=True)  11.9 us
    all_to_all x2, starting transfers between devices, local(): lax.all_to_all(pieces, 'y', split_axis=0, concat_axis=0, tiled=True)  9.26 us
    pallas_call x2, Pallas kernels, contract(): pl.pallas_call(kernel, out_shape=(result, result), in_specs=[pl.BlockSpec...  6.97 us
    unnamed x18, local copies, waits for them, and re-layouts  6.48 us
    ppermute x5, waiting for transfers between devices, swap_core(): return lax.ppermute(value, 'core', [(0, 1), (1, 0)])  5.23 us
  transfers between devices with their start and end apart: 22, of which 11 were waited for; matrix products, arithmetic and copies ran while one was open for 6% of the time, Pallas kernels for 4%

profile of v2, /device:TPU:4, one launch (start us, length us, event | category | flops | bytes accessed | tf_op | source)
XLA Modules:
  0.0 186.7 jit_solution(11667879736134119879)
XLA Ops:
  0.0 2.2 %slice_select_fusion = bf16[2,16,192,128]{3,2,1,0:T(8,128)(2,1)S(1)} fusion(bf16[2,16,512,128]{3,2,1,0:T(8,128)(2,1)} %param.2, pred[]{:T(512)S(6)} %eq.15), kind=kLoop, calls=%fused_computation.3 | loop fusion | flops 786432 | bytes 4718593 | tf_op jit(solution)/shard_map/jit(_where)/select_n | solution.py:115
  2.3 3.4 %collective-permute-done.1 = bf16[2,16,192,128]{3,2,1,0:T(8,128)(2,1)S(1)} collective-permute-done((bf16[2,16,192,128]{3,2,1,0:T(8,128)(2,1)S(1)}, bf16[2,16,192,128]{3,2,1,0:T(8,128)(2,1)S(1)}, u32[]{:S(2)}, u32[]{:S(2)}) %collective-permute-start.1) | collective-permute-done | bytes 1572896 | tf_op jit(solution)/shard_map/ppermute | solution.py:41
  8.0 16.7 %all_to_all.30.ao_ref = bf16[8,2,192,128]{3,2,1,0:T(8,128)(2,1)S(1)} all-to-all(bf16[8,2,192,128]{3,2,1,0:T(8,128)(2,1)S(1)} %bitcast.69), channel_id=1, replica_groups=mesh['zq'=2,'zr'=2,'core'=2,'x'=4,'y'=4,'zh'=2] {'x','zr'}, dimensions={0} | all-to-all | bytes 1572864 | tf_op jit(solution)/shard_map/all_to_all | solution.py:122
  24.8 6.0 %all-to-all-start.3 = ((bf16[8,2,192,128]{3,2,1,0:T(8,128)(2,1)}), bf16[8,2,192,128]{3,2,1,0:T(8,128)(2,1)S(1)}, u32[]{:S(2)}, u32[]{:S(2)}) async-start(bf16[8,2,192,128]{3,2,1,0:T(8,128)(2,1)} %bitcast.20), calls=%async_computation.3 | async-start | bytes 1572864 | tf_op jit(solution)/shard_map/all_to_all | solution.py:122
  30.8 1.4 copy-done.7
  32.2 2.7 %maximum_select_fusion = bf16[2,16,320,128]{3,2,1,0:T(8,128)(2,1)S(1)} fusion(bf16[2,16,192,128]{3,2,1,0:T(8,128)(2,1)S(1)} %copy-done.7, bf16[2,16,128,128]{3,2,1,0:T(8,128)(2,1)S(1)} %slice-done, bf16[2,16,512,128]{3,2,1,0:T(8,128)(2,1)} %param.2, pred[]{:T(512)S(6)} %eq.15), kind=kLoop, calls=%fused_computation | loop fusion | flops 6553600 | bytes 7864321 | tf_op jit(solution)/shard_map/jit(_where)/select_n | solution.py:118
  36.4 3.8 %all-to-all-done.3.ao_ref = bf16[8,2,192,128]{3,2,1,0:T(8,128)(2,1)S(1)} async-done(((bf16[8,2,192,128]{3,2,1,0:T(8,128)(2,1)}), bf16[8,2,192,128]{3,2,1,0:T(8,128)(2,1)S(1)}, u32[]{:S(2)}, u32[]{:S(2)}) %all-to-all-start.3) | async-done | bytes 786464 | tf_op jit(solution)/shard_map/all_to_all | solution.py:122
  40.2 20.2 %all_to_all.31.bo_ref = bf16[8,2,320,128]{3,2,1,0:T(8,128)(2,1)} all-to-all(bf16[8,2,320,128]{3,2,1,0:T(8,128)(2,1)S(1)} %bitcast.68), channel_id=1, replica_groups=mesh['zq'=2,'zr'=2,'core'=2,'x'=4,'y'=4,'zh'=2] {'x','zr'}, dimensions={0} | all-to-all | bytes 2621440 | tf_op jit(solution)/shard_map/all_to_all | solution.py:122
  60.4 5.9 %all-to-all-start.5 = ((bf16[8,2,320,128]{3,2,1,0:T(8,128)(2,1)}), bf16[8,2,320,128]{3,2,1,0:T(8,128)(2,1)S(1)}, u32[]{:S(2)}, u32[]{:S(2)}) async-start(bf16[8,2,320,128]{3,2,1,0:T(8,128)(2,1)} %bitcast.67), calls=%async_computation.5 | async-start | bytes 2621440 | tf_op jit(solution)/shard_map/all_to_all | solution.py:122
  66.4 8.2 %collective-permute-start.3 = (bf16[2,2,192,128]{3,2,1,0:T(8,128)(2,1)S(1)}, bf16[2,2,192,128]{3,2,1,0:T(8,128)(2,1)S(1)}, u32[]{:S(2)}, u32[]{:S(2)}) collective-permute-start(bf16[2,2,192,128]{3,2,1,0:T(8,128)(2,1)S(1)} %get-tuple-element.18), channel_id=1, source_target_pairs={{0,1},{1,0},{2,3},{3,2},{4,5},{5,4},{6,7},{7,6},{8,9},{9,8},{10,11... | collective-permute-start | bytes 589832 | tf_op jit(solution)/shard_map/ppermute | solution.py:37
  74.6 2.0 %collective-permute-start.4 = (bf16[2,2,192,128]{3,2,1,0:T(8,128)(2,1)S(1)}, bf16[2,2,192,128]{3,2,1,0:T(8,128)(2,1)}, u32[]{:S(2)}, u32[]{:S(2)}) collective-permute-start(bf16[2,2,192,128]{3,2,1,0:T(8,128)(2,1)S(1)} %get-tuple-element.17), channel_id=1, source_target_pairs={{0,129},{1,128},{2,131},{3,130},{4,133},{5,132},{6,135},{7,134},{8... | collective-permute-start | bytes 589832 | tf_op jit(solution)/shard_map/ppermute | solution.py:37
  77.9 13.1 %collective-permute-done.3 = bf16[2,2,192,128]{3,2,1,0:T(8,128)(2,1)S(1)} collective-permute-done((bf16[2,2,192,128]{3,2,1,0:T(8,128)(2,1)S(1)}, bf16[2,2,192,128]{3,2,1,0:T(8,128)(2,1)S(1)}, u32[]{:S(2)}, u32[]{:S(2)}) %collective-permute-start.3) | collective-permute-done | bytes 196640 | tf_op jit(solution)/shard_map/ppermute | solution.py:37
  92.1 1.6 broadcast_in_dim.4
  93.6 4.5 %all-to-all-start.1 = ((bf16[4,2,2,2,192,128]{5,4,3,2,1,0:T(8,128)(2,1)}), bf16[4,2,2,2,192,128]{5,4,3,2,1,0:T(8,128)(2,1)S(1)}, u32[]{:S(2)}, u32[]{:S(2)}) async-start(bf16[4,2,2,2,192,128]{5,4,3,2,1,0:T(8,128)(2,1)} %broadcast_in_dim.4), calls=%async_computation.1 | async-start | bytes 3145728 | tf_op jit(solution)/shard_map/all_to_all | solution.py:137
  99.4 3.6 %collective-permute-start.12 = (bf16[2,2,192,128]{3,2,1,0:T(8,128)(2,1)S(1)}, bf16[2,2,192,128]{3,2,1,0:T(8,128)(2,1)S(1)}, u32[]{:S(2)}, u32[]{:S(2)}) collective-permute-start(bf16[2,2,192,128]{3,2,1,0:T(8,128)(2,1)S(1)} %get-tuple-element.19), channel_id=1, source_target_pairs={{0,129},{1,128},{2,131},{3,130},{4,133},{5,132},{6,135},{7,134},{8... | collective-permute-start | bytes 589832 | tf_op jit(solution)/shard_map/ppermute | solution.py:37
  103.0 4.3 %collective-permute-start.11 = (bf16[2,2,192,128]{3,2,1,0:T(8,128)(2,1)S(1)}, bf16[2,2,192,128]{3,2,1,0:T(8,128)(2,1)S(1)}, u32[]{:S(2)}, u32[]{:S(2)}) collective-permute-start(bf16[2,2,192,128]{3,2,1,0:T(8,128)(2,1)S(1)} %get-tuple-element.20), channel_id=1, source_target_pairs={{0,1},{1,0},{2,3},{3,2},{4,5},{5,4},{6,7},{7,6},{8,9},{9,8},{10,11... | collective-permute-start | bytes 589832 | tf_op jit(solution)/shard_map/ppermute | solution.py:37
  108.0 6.5 %collective-permute-done.11 = bf16[2,2,192,128]{3,2,1,0:T(8,128)(2,1)S(1)} collective-permute-done((bf16[2,2,192,128]{3,2,1,0:T(8,128)(2,1)S(1)}, bf16[2,2,192,128]{3,2,1,0:T(8,128)(2,1)S(1)}, u32[]{:S(2)}, u32[]{:S(2)}) %collective-permute-start.11) | collective-permute-done | bytes 196640 | tf_op jit(solution)/shard_map/ppermute | solution.py:37
  114.6 1.6 broadcast_in_dim.5
  116.2 4.8 %all-to-all-start.4 = ((bf16[4,2,2,2,192,128]{5,4,3,2,1,0:T(8,128)(2,1)}), bf16[4,2,2,2,192,128]{5,4,3,2,1,0:T(8,128)(2,1)S(1)}, u32[]{:S(2)}, u32[]{:S(2)}) async-start(bf16[4,2,2,2,192,128]{5,4,3,2,1,0:T(8,128)(2,1)} %broadcast_in_dim.5), calls=%async_computation.4 | async-start | bytes 3145728 | tf_op jit(solution)/shard_map/all_to_all | solution.py:137
  121.6 1.8 collective-permute-done.5.ap_ref
  123.4 1.4 copy-done.1
  126.2 3.5 %shard_map.28 = (f32[2,2,192,128]{3,2,1,0:T(8,128)}, f32[2,2,192,128]{3,2,1,0:T(8,128)S(1)}) custom-call(s32[3]{0:T(128)S(1)} %pad_add_fusion.place_ref, bf16[4,2,2,2,192,128]{5,4,3,2,1,0:T(8,128)(2,1)S(1)} %copy-done.1, bf16[8,2,192,128]{3,2,1,0:T(8,128)(2,1)S(1)} %all_to_all.30.ao_ref, bf16[8,2,192,128]{3,2,1,0:T(8,128)(2,1)} %collective-permute-done.5.ap_ref, ...), custom_call_target="tpu_custom_call" | custom-call | flops 1610612736 | bytes 7340032 | tf_op jit(solution)/shard_map/pallas_call | solution.py:86
  129.8 6.8 %collective-permute-start = (f32[2,2]{1,0:T(2,128)S(1)}, f32[2,2]{1,0:T(2,128)S(1)}, u32[]{:S(2)}, u32[]{:S(2)}) collective-permute-start(f32[2,2]{1,0:T(2,128)S(1)} %copy-done.8), channel_id=1, source_target_pairs={{0,0},{1,1},{2,2},{3,3},{4,4},{5,5},{6,6},{7,7},{8,32},{9,33},{10,... | collective-permute-start | bytes 56 | tf_op jit(solution)/shard_map/ppermute | solution.py:37
  138.4 3.5 %shard_map.29 = (f32[2,2,192,128]{3,2,1,0:T(8,128)S(1)}, f32[2,2,192,128]{3,2,1,0:T(8,128)S(1)}) custom-call(s32[3]{0:T(128)S(1)} %pad_add_fusion.place_ref, bf16[4,2,2,2,192,128]{5,4,3,2,1,0:T(8,128)(2,1)S(1)} %all-to-all-done.4.u_ref, bf16[8,2,192,128]{3,2,1,0:T(8,128)(2,1)S(1)} %all-to-all-done.3.ao_ref, ...), custom_call_target="tpu_custom_call" | custom-call | flops 1610612736 | bytes 7340032 | tf_op jit(solution)/shard_map/pallas_call | solution.py:86
  142.0 19.0 %collective-permute-done = f32[2,2]{1,0:T(2,128)S(1)} collective-permute-done((f32[2,2]{1,0:T(2,128)S(1)}, f32[2,2]{1,0:T(2,128)S(1)}, u32[]{:S(2)}, u32[]{:S(2)}) %collective-permute-start) | collective-permute-done | bytes 48 | tf_op jit(solution)/shard_map/ppermute | solution.py:37
  163.0 1.9 %collective-permute-start.8 = (bf16[2,192,128]{2,1,0:T(8,128)(2,1)S(1)}, bf16[2,192,128]{2,1,0:T(8,128)(2,1)S(1)}, u32[]{:S(2)}, u32[]{:S(2)}) collective-permute-start(bf16[2,192,128]{2,1,0:T(8,128)(2,1)S(1)} %get-tuple-element.27), channel_id=1, source_target_pairs={{0,0},{1,1},{2,2},{3,3},{4,4},{5,5},{6,6},{7,7},{8,32},{9,33},{10,... | collective-permute-start | bytes 294920 | tf_op jit(solution)/shard_map/ppermute | solution.py:37
  164.9 2.0 %collective-permute-start.9 = (bf16[2,192,128]{2,1,0:T(8,128)(2,1)S(1)}, bf16[2,192,128]{2,1,0:T(8,128)(2,1)S(1)}, u32[]{:S(2)}, u32[]{:S(2)}) collective-permute-start(bf16[2,192,128]{2,1,0:T(8,128)(2,1)S(1)} %get-tuple-element.28), channel_id=1, source_target_pairs={{0,8},{1,9},{2,10},{3,11},{4,12},{5,13},{6,14},{7,15},{8,40},{9,41... | collective-permute-start | bytes 294920 | tf_op jit(solution)/shard_map/ppermute | solution.py:37
  168.7 5.7 %collective-permute-start.16 = (bf16[2,192,128]{2,1,0:T(8,128)(2,1)S(1)}, bf16[2,192,128]{2,1,0:T(8,128)(2,1)S(1)}, u32[]{:S(2)}, u32[]{:S(2)}) collective-permute-start(bf16[2,192,128]{2,1,0:T(8,128)(2,1)S(1)} %get-tuple-element.31), channel_id=1, source_target_pairs={{0,0},{1,1},{2,2},{3,3},{4,4},{5,5},{6,6},{7,7},{8,32},{9,33},{10,... | collective-permute-start | bytes 294920 | tf_op jit(solution)/shard_map/ppermute | solution.py:37
  174.4 2.9 %collective-permute-start.17 = (bf16[2,192,128]{2,1,0:T(8,128)(2,1)S(1)}, bf16[2,192,128]{2,1,0:T(8,128)(2,1)S(1)}, u32[]{:S(2)}, u32[]{:S(2)}) collective-permute-start(bf16[2,192,128]{2,1,0:T(8,128)(2,1)S(1)} %get-tuple-element.32), channel_id=1, source_target_pairs={{0,8},{1,9},{2,10},{3,11},{4,12},{5,13},{6,14},{7,15},{8,40},{9,41... | collective-permute-start | bytes 294920 | tf_op jit(solution)/shard_map/ppermute | solution.py:37
  177.3 2.2 %collective-permute-done.9 = bf16[2,192,128]{2,1,0:T(8,128)(2,1)S(1)} collective-permute-done((bf16[2,192,128]{2,1,0:T(8,128)(2,1)S(1)}, bf16[2,192,128]{2,1,0:T(8,128)(2,1)S(1)}, u32[]{:S(2)}, u32[]{:S(2)}) %collective-permute-start.9) | collective-permute-done | bytes 98336 | tf_op jit(solution)/shard_map/ppermute | solution.py:37
  179.5 5.0 %collective-permute-done.16 = bf16[2,192,128]{2,1,0:T(8,128)(2,1)S(1)} collective-permute-done((bf16[2,192,128]{2,1,0:T(8,128)(2,1)S(1)}, bf16[2,192,128]{2,1,0:T(8,128)(2,1)S(1)}, u32[]{:S(2)}, u32[]{:S(2)}) %collective-permute-start.16) | collective-permute-done | bytes 98336 | tf_op jit(solution)/shard_map/ppermute | solution.py:37
  184.5 1.3 collective-permute-done.17
  (66 shorter events, 16.9 us)
Async XLA Ops:
  0.0 5.7 %copy-start.5 = (bf16[2,16,512,128]{3,2,1,0:T(8,128)(2,1)S(1)}, bf16[2,16,512,128]{3,2,1,0:T(8,128)(2,1)}, u32[]{:S(2)}) copy-start(bf16[2,16,512,128]{3,2,1,0:T(8,128)(2,1)} %param.2) | copy-start | bytes 12582916
  2.2 3.5 %collective-permute-start.1 = (bf16[2,16,192,128]{3,2,1,0:T(8,128)(2,1)S(1)}, bf16[2,16,192,128]{3,2,1,0:T(8,128)(2,1)S(1)}, u32[]{:S(2)}, u32[]{:S(2)}) collective-permute-start(bf16[2,16,192,128]{3,2,1,0:T(8,128)(2,1)S(1)} %slice_select_fusion), channel_id=1, source_target_pairs={{0,32},{32,0},{1,33},{33,1},{2,34},{34,2},{3,35},{35,3},{4,36},{36... | collective-permute-start | bytes 4718600 | tf_op jit(solution)/shard_map/ppermute | solution.py:41
  5.7 1.2 copy-start.6
  24.8 6.0 %slice-start = ((bf16[2,16,512,128]{3,2,1,0:T(8,128)(2,1)}), bf16[2,16,128,128]{3,2,1,0:T(8,128)(2,1)S(1)}, s32[]{:S(2)}) async-start(bf16[2,16,512,128]{3,2,1,0:T(8,128)(2,1)} %param.2), calls=%async_computation.6 | async-start | bytes 2097152 | tf_op jit(solution)/shard_map/slice | solution.py:114
  24.8 15.5 %all-to-all-start.3 = ((bf16[8,2,192,128]{3,2,1,0:T(8,128)(2,1)}), bf16[8,2,192,128]{3,2,1,0:T(8,128)(2,1)S(1)}, u32[]{:S(2)}, u32[]{:S(2)}) async-start(bf16[8,2,192,128]{3,2,1,0:T(8,128)(2,1)} %bitcast.20), calls=%async_computation.3 | async-start | bytes 1572864 | tf_op jit(solution)/shard_map/all_to_all | solution.py:122
  30.8 1.4 copy-start.7
  60.4 31.6 %all-to-all-start.5 = ((bf16[8,2,320,128]{3,2,1,0:T(8,128)(2,1)}), bf16[8,2,320,128]{3,2,1,0:T(8,128)(2,1)S(1)}, u32[]{:S(2)}, u32[]{:S(2)}) async-start(bf16[8,2,320,128]{3,2,1,0:T(8,128)(2,1)} %bitcast.67), calls=%async_computation.5 | async-start | bytes 2621440 | tf_op jit(solution)/shard_map/all_to_all | solution.py:122
  66.4 24.6 %collective-permute-start.3 = (bf16[2,2,192,128]{3,2,1,0:T(8,128)(2,1)S(1)}, bf16[2,2,192,128]{3,2,1,0:T(8,128)(2,1)S(1)}, u32[]{:S(2)}, u32[]{:S(2)}) collective-permute-start(bf16[2,2,192,128]{3,2,1,0:T(8,128)(2,1)S(1)} %get-tuple-element.18), channel_id=1, source_target_pairs={{0,1},{1,0},{2,3},{3,2},{4,5},{5,4},{6,7},{7,6},{8,9},{9,8},{10,11... | collective-permute-start | bytes 589832 | tf_op jit(solution)/shard_map/ppermute | solution.py:37
  74.6 16.4 %collective-permute-start.4 = (bf16[2,2,192,128]{3,2,1,0:T(8,128)(2,1)S(1)}, bf16[2,2,192,128]{3,2,1,0:T(8,128)(2,1)}, u32[]{:S(2)}, u32[]{:S(2)}) collective-permute-start(bf16[2,2,192,128]{3,2,1,0:T(8,128)(2,1)S(1)} %get-tuple-element.17), channel_id=1, source_target_pairs={{0,129},{1,128},{2,131},{3,130},{4,133},{5,132},{6,135},{7,134},{8... | collective-permute-start | bytes 589832 | tf_op jit(solution)/shard_map/ppermute | solution.py:37
  76.6 15.4 %collective-permute-start.2 = (bf16[2,2,192,128]{3,2,1,0:T(8,128)(2,1)S(1)}, bf16[2,2,192,128]{3,2,1,0:T(8,128)(2,1)S(1)}, u32[]{:S(2)}, u32[]{:S(2)}) collective-permute-start(bf16[2,2,192,128]{3,2,1,0:T(8,128)(2,1)S(1)} %get-tuple-element.17), channel_id=1, source_target_pairs={{0,128},{1,129},{2,130},{3,131},{4,132},{5,133},{6,134},{7,135},{8... | collective-permute-start | bytes 589832 | tf_op jit(solution)/shard_map/ppermute | solution.py:37
  92.1 1.6 copy-start.2
  93.6 20.9 %all-to-all-start.1 = ((bf16[4,2,2,2,192,128]{5,4,3,2,1,0:T(8,128)(2,1)}), bf16[4,2,2,2,192,128]{5,4,3,2,1,0:T(8,128)(2,1)S(1)}, u32[]{:S(2)}, u32[]{:S(2)}) async-start(bf16[4,2,2,2,192,128]{5,4,3,2,1,0:T(8,128)(2,1)} %broadcast_in_dim.4), calls=%async_computation.1 | async-start | bytes 3145728 | tf_op jit(solution)/shard_map/all_to_all | solution.py:137
  98.1 9.3 %collective-permute-start.10 = (bf16[2,2,192,128]{3,2,1,0:T(8,128)(2,1)S(1)}, bf16[2,2,192,128]{3,2,1,0:T(8,128)(2,1)S(1)}, u32[]{:S(2)}, u32[]{:S(2)}) collective-permute-start(bf16[2,2,192,128]{3,2,1,0:T(8,128)(2,1)S(1)} %get-tuple-element.19), channel_id=1, source_target_pairs={{0,128},{1,129},{2,130},{3,131},{4,132},{5,133},{6,134},{7,135},{8... | collective-permute-start | bytes 589832 | tf_op jit(solution)/shard_map/ppermute | solution.py:37
  99.4 15.0 %collective-permute-start.12 = (bf16[2,2,192,128]{3,2,1,0:T(8,128)(2,1)S(1)}, bf16[2,2,192,128]{3,2,1,0:T(8,128)(2,1)S(1)}, u32[]{:S(2)}, u32[]{:S(2)}) collective-permute-start(bf16[2,2,192,128]{3,2,1,0:T(8,128)(2,1)S(1)} %get-tuple-element.19), channel_id=1, source_target_pairs={{0,129},{1,128},{2,131},{3,130},{4,133},{5,132},{6,135},{7,134},{8... | collective-permute-start | bytes 589832 | tf_op jit(solution)/shard_map/ppermute | solution.py:37
  103.0 11.5 %collective-permute-start.11 = (bf16[2,2,192,128]{3,2,1,0:T(8,128)(2,1)S(1)}, bf16[2,2,192,128]{3,2,1,0:T(8,128)(2,1)S(1)}, u32[]{:S(2)}, u32[]{:S(2)}) collective-permute-start(bf16[2,2,192,128]{3,2,1,0:T(8,128)(2,1)S(1)} %get-tuple-element.20), channel_id=1, source_target_pairs={{0,1},{1,0},{2,3},{3,2},{4,5},{5,4},{6,7},{7,6},{8,9},{9,8},{10,11... | collective-permute-start | bytes 589832 | tf_op jit(solution)/shard_map/ppermute | solution.py:37
  107.3 16.1 %collective-permute-start.6 = (bf16[8,2,320,128]{3,2,1,0:T(8,128)(2,1)}, bf16[8,2,320,128]{3,2,1,0:T(8,128)(2,1)}, u32[]{:S(2)}, u32[]{:S(2)}) collective-permute-start(bf16[8,2,320,128]{3,2,1,0:T(8,128)(2,1)} %all_to_all.31.bo_ref), channel_id=1, source_target_pairs={{0,32},{32,0},{1,33},{33,1},{2,34},{34,2},{3,35},{35,3},{4,36},{36... | collective-permute-start | bytes 3932168 | tf_op jit(solution)/shard_map/ppermute | solution.py:41
  107.4 29.7 %collective-permute-start.14 = (bf16[8,2,320,128]{3,2,1,0:T(8,128)(2,1)}, bf16[8,2,320,128]{3,2,1,0:T(8,128)(2,1)}, u32[]{:S(2)}, u32[]{:S(2)}) collective-permute-start(bf16[8,2,320,128]{3,2,1,0:T(8,128)(2,1)} %copy-done.2), channel_id=1, source_target_pairs={{0,32},{32,0},{1,33},{33,1},{2,34},{34,2},{3,35},{35,3},{4,36},{36... | collective-permute-start | bytes 3932168 | tf_op jit(solution)/shard_map/ppermute | solution.py:41
  114.6 1.7 copy-start
  116.2 20.9 %all-to-all-start.4 = ((bf16[4,2,2,2,192,128]{5,4,3,2,1,0:T(8,128)(2,1)}), bf16[4,2,2,2,192,128]{5,4,3,2,1,0:T(8,128)(2,1)S(1)}, u32[]{:S(2)}, u32[]{:S(2)}) async-start(bf16[4,2,2,2,192,128]{5,4,3,2,1,0:T(8,128)(2,1)} %broadcast_in_dim.5), calls=%async_computation.4 | async-start | bytes 3145728 | tf_op jit(solution)/shard_map/all_to_all | solution.py:137
  121.0 2.4 %collective-permute-start.5 = (bf16[8,2,192,128]{3,2,1,0:T(8,128)(2,1)S(1)}, bf16[8,2,192,128]{3,2,1,0:T(8,128)(2,1)}, u32[]{:S(2)}, u32[]{:S(2)}) collective-permute-start(bf16[8,2,192,128]{3,2,1,0:T(8,128)(2,1)S(1)} %all_to_all.30.ao_ref), channel_id=1, source_target_pairs={{0,32},{32,0},{1,33},{33,1},{2,34},{34,2},{3,35},{35,3},{4,36},{36... | collective-permute-start | bytes 2359304 | tf_op jit(solution)/shard_map/ppermute | solution.py:41
  121.0 15.5 %collective-permute-start.13 = (bf16[8,2,192,128]{3,2,1,0:T(8,128)(2,1)S(1)}, bf16[8,2,192,128]{3,2,1,0:T(8,128)(2,1)}, u32[]{:S(2)}, u32[]{:S(2)}) collective-permute-start(bf16[8,2,192,128]{3,2,1,0:T(8,128)(2,1)S(1)} %all-to-all-done.3.ao_ref), channel_id=1, source_target_pairs={{0,32},{32,0},{1,33},{33,1},{2,34},{34,2},{3,35},{35,3},{4,36},{36... | collective-permute-start | bytes 2359304 | tf_op jit(solution)/shard_map/ppermute | solution.py:41
  121.5 8.2 %copy-start.8 = (f32[2,2]{1,0:T(2,128)S(1)}, f32[2,2]{1,0:T(2,128)}, u32[]{:S(2)}) copy-start(f32[2,2]{1,0:T(2,128)} %param.3) | copy-start | bytes 52
  123.4 1.4 copy-start.1
  124.8 1.3 copy-start.4
  129.6 32.0 %collective-permute-start.7 = (f32[2,2,192,128]{3,2,1,0:T(8,128)}, f32[2,2,192,128]{3,2,1,0:T(8,128)S(1)}, u32[]{:S(2)}, u32[]{:S(2)}) collective-permute-start(f32[2,2,192,128]{3,2,1,0:T(8,128)} %get-tuple-element.10), channel_id=1, source_target_pairs={{0,128},{1,129},{2,130},{3,131},{4,132},{5,133},{6,134},{7,135},{8... | collective-permute-start | bytes 1179656 | tf_op jit(solution)/shard_map/ppermute | solution.py:37
  129.8 31.3 %collective-permute-start = (f32[2,2]{1,0:T(2,128)S(1)}, f32[2,2]{1,0:T(2,128)S(1)}, u32[]{:S(2)}, u32[]{:S(2)}) collective-permute-start(f32[2,2]{1,0:T(2,128)S(1)} %copy-done.8), channel_id=1, source_target_pairs={{0,0},{1,1},{2,2},{3,3},{4,4},{5,5},{6,6},{7,7},{8,32},{9,33},{10,... | collective-permute-start | bytes 56 | tf_op jit(solution)/shard_map/ppermute | solution.py:37
  137.1 1.3 copy-start.3
  141.9 25.3 %collective-permute-start.15 = (f32[2,2,192,128]{3,2,1,0:T(8,128)S(1)}, f32[2,2,192,128]{3,2,1,0:T(8,128)S(1)}, u32[]{:S(2)}, u32[]{:S(2)}) collective-permute-start(f32[2,2,192,128]{3,2,1,0:T(8,128)S(1)} %get-tuple-element.12), channel_id=1, source_target_pairs={{0,128},{1,129},{2,130},{3,131},{4,132},{5,133},{6,134},{7,135},{8... | collective-permute-start | bytes 1179656 | tf_op jit(solution)/shard_map/ppermute | solution.py:37
  163.0 14.3 %collective-permute-start.8 = (bf16[2,192,128]{2,1,0:T(8,128)(2,1)S(1)}, bf16[2,192,128]{2,1,0:T(8,128)(2,1)S(1)}, u32[]{:S(2)}, u32[]{:S(2)}) collective-permute-start(bf16[2,192,128]{2,1,0:T(8,128)(2,1)S(1)} %get-tuple-element.27), channel_id=1, source_target_pairs={{0,0},{1,1},{2,2},{3,3},{4,4},{5,5},{6,6},{7,7},{8,32},{9,33},{10,... | collective-permute-start | bytes 294920 | tf_op jit(solution)/shard_map/ppermute | solution.py:37
  164.9 14.6 %collective-permute-start.9 = (bf16[2,192,128]{2,1,0:T(8,128)(2,1)S(1)}, bf16[2,192,128]{2,1,0:T(8,128)(2,1)S(1)}, u32[]{:S(2)}, u32[]{:S(2)}) collective-permute-start(bf16[2,192,128]{2,1,0:T(8,128)(2,1)S(1)} %get-tuple-element.28), channel_id=1, source_target_pairs={{0,8},{1,9},{2,10},{3,11},{4,12},{5,13},{6,14},{7,15},{8,40},{9,41... | collective-permute-start | bytes 294920 | tf_op jit(solution)/shard_map/ppermute | solution.py:37
  168.7 15.8 %collective-permute-start.16 = (bf16[2,192,128]{2,1,0:T(8,128)(2,1)S(1)}, bf16[2,192,128]{2,1,0:T(8,128)(2,1)S(1)}, u32[]{:S(2)}, u32[]{:S(2)}) collective-permute-start(bf16[2,192,128]{2,1,0:T(8,128)(2,1)S(1)} %get-tuple-element.31), channel_id=1, source_target_pairs={{0,0},{1,1},{2,2},{3,3},{4,4},{5,5},{6,6},{7,7},{8,32},{9,33},{10,... | collective-permute-start | bytes 294920 | tf_op jit(solution)/shard_map/ppermute | solution.py:37
  174.4 11.4 %collective-permute-start.17 = (bf16[2,192,128]{2,1,0:T(8,128)(2,1)S(1)}, bf16[2,192,128]{2,1,0:T(8,128)(2,1)S(1)}, u32[]{:S(2)}, u32[]{:S(2)}) collective-permute-start(bf16[2,192,128]{2,1,0:T(8,128)(2,1)S(1)} %get-tuple-element.32), channel_id=1, source_target_pairs={{0,8},{1,9},{2,10},{3,11},{4,12},{5,13},{6,14},{7,15},{8,40},{9,41... | collective-permute-start | bytes 294920 | tf_op jit(solution)/shard_map/ppermute | solution.py:37

commit v3 on v2

v3 whole, which is shorter than its diff:
```python
import jax
import jax.numpy as jnp
from jax import lax
from jax.experimental import pallas as pl
from jax.experimental.pallas import tpu as pltpu
from jax.sharding import Mesh, PartitionSpec as P


NOUT = 384
AXES = ("zq", "zr", "core", "x", "y", "zh")
SIZES = (2, 2, 2, 4, 4, 2)


def coordinates():
    out = [()]
    for size in SIZES:
        out = [c + (i,) for c in out for i in range(size)]
    return out


def flat(c):
    index = 0
    for i, size in zip(c, SIZES):
        index = index * size + i
    return index


def moved(target):
    pairs = []
    for c in coordinates():
        t = target(*c)
        if t is not None:
            pairs.append((flat(c), flat(t)))
    return pairs


def send(value, target):
    return lax.ppermute(value, AXES, moved(target))


def swap_core(value):
    return lax.ppermute(value, "core", [(0, 1), (1, 0)])


def contract(g, place, turned, a_own, a_peer, b_own, b_peer):
    half, lanes = turned[0].shape[-2:]
    depth = 16 * lanes

    def kernel(place_ref, u0, u1, u2, u3, ao_ref, ap_ref, bo_ref, bp_ref, sent_ref, kept_ref, left):
        core, zh, zq, y = place_ref[0], place_ref[1], place_ref[2], place_ref[3]
        for step, u_ref in enumerate((u0, u1, u2, u3)):
            ys = (y + 4 - step) % 4
            for xl in range(2):
                for piece in range(2):
                    start = pl.multiple_of(((xl * 4 + ys) * 2 + (piece ^ zh)) * lanes, lanes)
                    for part in range(2):
                        left[part * half : (part + 1) * half, pl.ds(start, lanes)] = u_ref[piece, xl, part]

        first = core == 0
        for side, out in ((1, sent_ref), (0, kept_ref)):
            for low in range(2):
                x = 2 * (zq ^ side) + low
                rows = []
                for zr in range(2):
                    i = 2 * x + zr
                    parts = []
                    for part in range(2):
                        ao, ap = ao_ref[i, g, part], ap_ref[i, g, part]
                        bo, bp = bo_ref[i, part], bp_ref[i, part]
                        parts.append(
                            jnp.concatenate(
                                [
                                    jnp.where(first, ao, ap),
                                    jnp.where(first, ap, ao),
                                    jnp.where(first, bo, bp),
                                    jnp.where(first, bp, bo),
                                ],
                                0,
                            )
                        )
                    rows.append(jnp.concatenate(parts, 1))
                right = jnp.concatenate(rows, 0)
                both = jnp.dot(left[...], right, preferred_element_type=jnp.float32)
                out[low, 0] = both[:half, :lanes] - both[half:, lanes:]
                out[low, 1] = both[:half, lanes:] + both[half:, :lanes]

    vmem = pl.BlockSpec(memory_space=pltpu.VMEM)
    result = jax.ShapeDtypeStruct((2, 2, half, lanes), jnp.float32)
    return pl.pallas_call(
        kernel,
        out_shape=(result, result),
        in_specs=[pl.BlockSpec(memory_space=pltpu.SMEM)] + [vmem] * 8,
        out_specs=(vmem, vmem),
        scratch_shapes=[pltpu.VMEM((2 * half, depth), jnp.bfloat16)],
        cost_estimate=pl.CostEstimate(
            flops=2 * 2 * half * depth * 8 * lanes, bytes_accessed=7 << 20, transcendentals=0
        ),
        compiler_params=pltpu.CompilerParams(vmem_limit_bytes=40 << 20),
    )(place, *turned, a_own, a_peer, b_own, b_peer)


def step(spectra, wavelet):
    zq, core, x = lax.axis_index("zq"), lax.axis_index("core"), lax.axis_index("x")
    y, zh = lax.axis_index("y"), lax.axis_index("zh")
    place = jnp.stack([core, zh, zq, y]).astype(jnp.int32)
    rows, _ = spectra.shape[2:]
    window = NOUT * rows // 512
    half = window // 2
    first = core == 0

    wave = send(wavelet, lambda q, r, c, x, y, h: (x // 2, r, x % 2, 2 * q + c, y, h))

    def ordered(block):
        return block.reshape((2, 2, 2, 2, 2) + block.shape[2:])

    low, mid, rest = spectra[:, :, :half], spectra[:, :, half:window], spectra[:, :, window:]
    passed = swap_core(jnp.where(first, mid, low))
    a = ordered(jnp.where(first, low, passed)).transpose(1, 3, 2, 4, 0, 5, 6)
    a = a.reshape((8, 2, 2) + a.shape[5:])
    b = ordered(
        jnp.where(first, jnp.concatenate([rest, passed], 2), spectra[:, :, half:])
    ).transpose(4, 1, 3, 2, 0, 5, 6)
    b = b.reshape((2, 8, 2) + b.shape[5:])

    def exchange(block):
        return lax.all_to_all(block, ("x", "zr"), split_axis=0, concat_axis=0, tiled=True)

    a_own = exchange(a)
    a_own, b = lax.optimization_barrier((a_own, b))
    a_peer = swap_core(a_own)
    b_own, b_peer = [], []
    for g in range(2):
        b_own.append(exchange(b[g]))
        b_peer.append(swap_core(b_own[g]))

    outs = []
    for g in range(2):
        shots = a_own.reshape((4, 2) + a_own.shape[1:])[:, 0, g]
        near, far = shots[:2], shots[2:]
        across = send(near, lambda q, r, c, x, y, h: (0, r, c, x, y, 1 - h) if q == 0 else None)
        up = send(far, lambda q, r, c, x, y, h: (1, r, c, x, y, h) if q == 0 else None)
        down = send(far, lambda q, r, c, x, y, h: (1, r, c, x, y, 1 - h) if q == 0 else None)
        near, across, up, down = lax.optimization_barrier((near, across, up, down))
        pieces = jnp.stack([jnp.where(zq == 0, near, up), jnp.where(zq == 0, across, down)])
        turned = [pieces] + [
            lax.ppermute(pieces, "y", [(i, (i + s) % 4) for i in range(4)]) for s in (1, 3, 2)
        ]
        turned = [turned[0], turned[1], turned[3], turned[2]]
        sent, kept = contract(g, place, turned, a_own, a_peer, b_own[g], b_peer[g])
        product = kept + send(sent, lambda q, r, c, x, y, h: (1 - q, r, c, x, y, h))
        real_out = -(wave[0, g] * product[:, 0] - wave[1, g] * product[:, 1])
        imag_out = -(wave[0, g] * product[:, 1] + wave[1, g] * product[:, 0])
        done = jnp.stack([real_out, imag_out], 1).astype(jnp.bfloat16)
        same, cross = jnp.where(first, done[0], done[1]), jnp.where(first, done[1], done[0])
        same = send(same, lambda q, r, c, x, y, h: (x // 2, r, x % 2, 2 * q + c, y, h))
        cross = send(cross, lambda q, r, c, x, y, h: (x // 2, r, x % 2, 2 * q + 1 - c, y, h))
        even = x % 2 == 0
        outs.append(
            jnp.concatenate([jnp.where(even, same, cross), jnp.where(even, cross, same)], 1)
        )
    return jnp.stack(outs, 1)


def solution(mesh):
    fine = Mesh(mesh.devices.reshape(SIZES), AXES)
    freq, col = AXES[:3], AXES[3:]
    return jax.shard_map(
        step,
        mesh=fine,
        in_specs=(P(None, None, freq, col), P(None, freq)),
        out_specs=P(None, freq, None, col),
        check_vma=False,
    )
```

time: 188 us -> 200 us (1.064); the launches traced: 187 us -> 196 us
  waiting for transfers between devices: 57 us -> 73.4 us
  blocking collectives: 36.9 us -> 21.5 us
  starting transfers between devices: 62.5 us -> 67.9 us
  other arithmetic: 9.04 us -> 11.8 us
    all_to_all x2 -> x1, blocking collectives: 36.9 us -> 21.5 us  [exchange(): lax.all_to_all(block, ('x', 'zr'), split_axis=0, concat_axis=0, tiled=True)]
    ppermute x0 -> x6, waiting for transfers between devices: none -> 15.3 us  [step(): lax.ppermute(pieces, 'y', [(i, (i + s) % 4) for i in range(4)])]
    ppermute x0 -> x6, starting transfers between devices: none -> 11 us  [step(): lax.ppermute(pieces, 'y', [(i, (i + s) % 4) for i in range(4)])]
    all_to_all x2, waiting for transfers between devices: 3.8 us -> 13.4 us  [exchange(): lax.all_to_all(block, ('x', 'zr'), split_axis=0, concat_axis=0, tiled=True)]
    all_to_all x2 -> x0, starting transfers between devices: 9.26 us -> none  [local(): lax.all_to_all(pieces, 'y', split_axis=0, concat_axis=0, tiled=True)]
    ppermute x13, waiting for transfers between devices: 47.4 us -> 41.3 us  [send(): return lax.ppermute(value, AXES, moved(target))]
    unnamed x18 -> x14, local copies, waits for them, and re-layouts: 6.48 us -> 2.53 us
    ppermute x13, starting transfers between devices: 40.1 us -> 43.8 us  [send(): return lax.ppermute(value, AXES, moved(target))]
  transfers between devices with their start and end apart: 22 -> 25, of which waited for: 11 -> 11; matrix products, arithmetic and copies ran while one was open for 6% -> 6% of each run, Pallas kernels for 4% -> 5%
where the time goes in v3:
time: 200 us; the launch traced here: 196 us
  waiting for transfers between devices  73.4 us (37%)
  starting transfers between devices  67.9 us (34%)
  blocking collectives  21.5 us (11%)
  local copies, waits for them, and re-layouts  12 us (6%)
  other arithmetic  11.8 us (6%)
  Pallas kernels  8.88 us (4%)
    ppermute x13, starting transfers between devices, send(): return lax.ppermute(value, AXES, moved(target))  43.8 us
    ppermute x13, waiting for transfers between devices, send(): return lax.ppermute(value, AXES, moved(target))  41.3 us
    all_to_all x1, blocking collectives, exchange(): lax.all_to_all(block, ('x', 'zr'), split_axis=0, concat_axis=0, tiled=True)  21.5 us
    ppermute x6, waiting for transfers between devices, step(): lax.ppermute(pieces, 'y', [(i, (i + s) % 4) for i in range(4)])  15.3 us
    all_to_all x2, waiting for transfers between devices, exchange(): lax.all_to_all(block, ('x', 'zr'), split_axis=0, concat_axis=0, tiled=True)  13.4 us
    all_to_all x2, starting transfers between devices, exchange(): lax.all_to_all(block, ('x', 'zr'), split_axis=0, concat_axis=0, tiled=True)  12.7 us
    ppermute x6, starting transfers between devices, step(): lax.ppermute(pieces, 'y', [(i, (i + s) % 4) for i in range(4)])  11 us
    pallas_call x2, Pallas kernels, contract(): pl.pallas_call(kernel, out_shape=(result, result), in_specs=[pl.BlockSpec...  8.88 us
  transfers between devices with their start and end apart: 25, of which 11 were waited for; matrix products, arithmetic and copies ran while one was open for 6% of the time, Pallas kernels for 5%

profile of v3, /device:TPU:4, one launch (start us, length us, event | category | flops | bytes accessed | tf_op | source)
XLA Modules:
  0.0 195.8 jit_solution(3332017444214077275)
XLA Ops:
  0.0 2.2 %slice_select_fusion = bf16[2,16,192,128]{3,2,1,0:T(8,128)(2,1)S(1)} fusion(bf16[2,16,512,128]{3,2,1,0:T(8,128)(2,1)} %param.2, pred[]{:T(512)S(6)} %eq.17), kind=kLoop, calls=%fused_computation.1 | loop fusion | flops 786432 | bytes 4718593 | tf_op jit(solution)/shard_map/jit(_where)/select_n | solution.py:117
  2.3 3.4 %collective-permute-done.1 = bf16[2,16,192,128]{3,2,1,0:T(8,128)(2,1)S(1)} collective-permute-done((bf16[2,16,192,128]{3,2,1,0:T(8,128)(2,1)S(1)}, bf16[2,16,192,128]{3,2,1,0:T(8,128)(2,1)S(1)}, u32[]{:S(2)}, u32[]{:S(2)}) %collective-permute-start.1) | collective-permute-done | bytes 1572896 | tf_op jit(solution)/shard_map/ppermute | solution.py:42
  7.2 6.2 %all-to-all-start = ((bf16[8,2,2,192,128]{4,3,2,1,0:T(8,128)(2,1)}), bf16[8,2,2,192,128]{4,3,2,1,0:T(8,128)(2,1)S(1)}, u32[]{:S(2)}, u32[]{:S(2)}) async-start(bf16[8,2,2,192,128]{4,3,2,1,0:T(8,128)(2,1)} %bitcast.7), calls=%async_computation | async-start | bytes 3145728 | tf_op jit(solution)/shard_map/all_to_all | solution.py:126
  14.6 2.7 %maximum_select_fusion = bf16[2,16,320,128]{3,2,1,0:T(8,128)(2,1)S(1)} fusion(bf16[2,16,192,128]{3,2,1,0:T(8,128)(2,1)S(1)} %collective-permute-done.1, bf16[2,16,128,128]{3,2,1,0:T(8,128)(2,1)S(1)} %slice-done, bf16[2,16,512,128]{3,2,1,0:T(8,128)(2,1)} %param.2, pred[]{:T(512)S(6)} %eq.17), kind=kLoop, calls=%fused_computation | loop fusion | flops 6553600 | bytes 7864321 | tf_op jit(solution)/shard_map/jit(_where)/select_n | solution.py:121
  17.3 1.7 copy.4
  19.0 13.4 %all-to-all-done.ao_ref = bf16[8,2,2,192,128]{4,3,2,1,0:T(8,128)(2,1)S(1)} async-done(((bf16[8,2,2,192,128]{4,3,2,1,0:T(8,128)(2,1)}), bf16[8,2,2,192,128]{4,3,2,1,0:T(8,128)(2,1)S(1)}, u32[]{:S(2)}, u32[]{:S(2)}) %all-to-all-start) | async-done | bytes 1572896 | tf_op jit(solution)/shard_map/all_to_all | solution.py:126
  32.4 3.0 %slice_bitcast_fusion.1 = (bf16[8,2,320,128]{3,2,1,0:T(8,128)(2,1)}, bf16[8,2,320,128]{3,2,1,0:T(8,128)(2,1)S(1)}) fusion(bf16[2,8,2,320,128]{4,3,2,1,0:T(8,128)(2,1)} %bitcast.58), kind=kLoop, calls=%fused_computation.4 | loop fusion | bytes 5242880 | tf_op jit(solution)/shard_map/squeeze | solution.py:133
  35.4 21.5 %all_to_all.15.bo_ref = bf16[8,2,320,128]{3,2,1,0:T(8,128)(2,1)} all-to-all(bf16[8,2,320,128]{3,2,1,0:T(8,128)(2,1)S(1)} %get-tuple-element.34), channel_id=1, replica_groups=mesh['zq'=2,'zr'=2,'core'=2,'x'=4,'y'=4,'zh'=2] {'x','zr'}, dimensions={0} | all-to-all | bytes 2621440 | tf_op jit(solution)/shard_map/all_to_all | solution.py:126
  56.9 6.6 %all-to-all-start.1 = ((bf16[8,2,320,128]{3,2,1,0:T(8,128)(2,1)}), bf16[8,2,320,128]{3,2,1,0:T(8,128)(2,1)}, u32[]{:S(2)}, u32[]{:S(2)}) async-start(bf16[8,2,320,128]{3,2,1,0:T(8,128)(2,1)} %get-tuple-element.33), calls=%async_computation.1 | async-start | bytes 2621440 | tf_op jit(solution)/shard_map/all_to_all | solution.py:126
  64.3 8.2 %collective-permute-start.13 = (bf16[2,2,192,128]{3,2,1,0:T(8,128)(2,1)S(1)}, bf16[2,2,192,128]{3,2,1,0:T(8,128)(2,1)}, u32[]{:S(2)}, u32[]{:S(2)}) collective-permute-start(bf16[2,2,192,128]{3,2,1,0:T(8,128)(2,1)S(1)} %get-tuple-element.27), channel_id=1, source_target_pairs={{0,1},{1,0},{2,3},{3,2},{4,5},{5,4},{6,7},{7,6},{8,9},{9,8},{10,11... | collective-permute-start | bytes 589832 | tf_op jit(solution)/shard_map/ppermute | solution.py:38
  72.5 2.0 %collective-permute-start.14 = (bf16[2,2,192,128]{3,2,1,0:T(8,128)(2,1)}, bf16[2,2,192,128]{3,2,1,0:T(8,128)(2,1)}, u32[]{:S(2)}, u32[]{:S(2)}) collective-permute-start(bf16[2,2,192,128]{3,2,1,0:T(8,128)(2,1)} %get-tuple-element.38), channel_id=1, source_target_pairs={{0,128},{1,129},{2,130},{3,131},{4,132},{5,133},{6,134},{7,135},{8... | collective-permute-start | bytes 589832 | tf_op jit(solution)/shard_map/ppermute | solution.py:38
  74.5 2.0 %collective-permute-start.15 = (bf16[2,2,192,128]{3,2,1,0:T(8,128)(2,1)}, bf16[2,2,192,128]{3,2,1,0:T(8,128)(2,1)}, u32[]{:S(2)}, u32[]{:S(2)}) collective-permute-start(bf16[2,2,192,128]{3,2,1,0:T(8,128)(2,1)} %get-tuple-element.38), channel_id=1, source_target_pairs={{0,129},{1,128},{2,131},{3,130},{4,133},{5,132},{6,135},{7,134},{8... | collective-permute-start | bytes 589832 | tf_op jit(solution)/shard_map/ppermute | solution.py:38
  76.7 12.8 %collective-permute-done.13 = bf16[2,2,192,128]{3,2,1,0:T(8,128)(2,1)} collective-permute-done((bf16[2,2,192,128]{3,2,1,0:T(8,128)(2,1)S(1)}, bf16[2,2,192,128]{3,2,1,0:T(8,128)(2,1)}, u32[]{:S(2)}, u32[]{:S(2)}) %collective-permute-start.13) | collective-permute-done | bytes 196640 | tf_op jit(solution)/shard_map/ppermute | solution.py:38
  89.5 1.9 collective-permute-start.2
  91.4 2.0 %collective-permute-start.3 = (bf16[2,2,192,128]{3,2,1,0:T(8,128)(2,1)}, bf16[2,2,192,128]{3,2,1,0:T(8,128)(2,1)}, u32[]{:S(2)}, u32[]{:S(2)}) collective-permute-start(bf16[2,2,192,128]{3,2,1,0:T(8,128)(2,1)} %get-tuple-element.35), channel_id=1, source_target_pairs={{0,128},{1,129},{2,130},{3,131},{4,132},{5,133},{6,134},{7,135},{8... | collective-permute-start | bytes 589832 | tf_op jit(solution)/shard_map/ppermute | solution.py:38
  95.2 5.9 %collective-permute-done.2 = bf16[2,2,192,128]{3,2,1,0:T(8,128)(2,1)} collective-permute-done((bf16[2,2,192,128]{3,2,1,0:T(8,128)(2,1)S(1)}, bf16[2,2,192,128]{3,2,1,0:T(8,128)(2,1)}, u32[]{:S(2)}, u32[]{:S(2)}) %collective-permute-start.2) | collective-permute-done | bytes 196640 | tf_op jit(solution)/shard_map/ppermute | solution.py:38
  101.1 1.6 collective-permute-start.16
  102.7 3.0 %collective-permute-start.4 = (bf16[2,2,192,128]{3,2,1,0:T(8,128)(2,1)S(1)}, bf16[2,2,192,128]{3,2,1,0:T(8,128)(2,1)S(1)}, u32[]{:S(2)}, u32[]{:S(2)}) collective-permute-start(bf16[2,2,192,128]{3,2,1,0:T(8,128)(2,1)S(1)} %copy-done.5), channel_id=1, source_target_pairs={{0,129},{1,128},{2,131},{3,130},{4,133},{5,132},{6,135},{7,134},{8... | collective-permute-start | bytes 589832 | tf_op jit(solution)/shard_map/ppermute | solution.py:38
  105.7 7.4 %collective-permute-done.4 = bf16[2,2,192,128]{3,2,1,0:T(8,128)(2,1)S(1)} collective-permute-done((bf16[2,2,192,128]{3,2,1,0:T(8,128)(2,1)S(1)}, bf16[2,2,192,128]{3,2,1,0:T(8,128)(2,1)S(1)}, u32[]{:S(2)}, u32[]{:S(2)}) %collective-permute-start.4) | collective-permute-done | bytes 196640 | tf_op jit(solution)/shard_map/ppermute | solution.py:38
  113.1 3.2 %collective-permute-start.17 = (bf16[2,2,2,192,128]{4,3,2,1,0:T(8,128)(2,1)}, bf16[2,2,2,192,128]{4,3,2,1,0:T(8,128)(2,1)}, u32[]{:S(2)}, u32[]{:S(2)}) collective-permute-start(bf16[2,2,2,192,128]{4,3,2,1,0:T(8,128)(2,1)} %pad_maximum_fusion.1.u0), channel_id=1, source_target_pairs={{0,4},{2,6},{4,0},{6,2},{1,5},{3,7},{5,1},{7,3},{8,12},{10,14},{12... | collective-permute-start | bytes 1179656 | tf_op jit(solution)/shard_map/ppermute | solution.py:146
  119.2 7.9 %collective-permute-done.17.u2 = bf16[2,2,2,192,128]{4,3,2,1,0:T(8,128)(2,1)} collective-permute-done((bf16[2,2,2,192,128]{4,3,2,1,0:T(8,128)(2,1)}, bf16[2,2,2,192,128]{4,3,2,1,0:T(8,128)(2,1)}, u32[]{:S(2)}, u32[]{:S(2)}) %collective-permute-start.17) | collective-permute-done | bytes 393248 | tf_op jit(solution)/shard_map/ppermute | solution.py:146
  127.4 7.4 %collective-permute-done.18.u3 = bf16[2,2,2,192,128]{4,3,2,1,0:T(8,128)(2,1)} collective-permute-done((bf16[2,2,2,192,128]{4,3,2,1,0:T(8,128)(2,1)}, bf16[2,2,2,192,128]{4,3,2,1,0:T(8,128)(2,1)}, u32[]{:S(2)}, u32[]{:S(2)}) %collective-permute-start.18) | collective-permute-done | bytes 393248 | tf_op jit(solution)/shard_map/ppermute | solution.py:146
  134.8 1.7 collective-permute-start.6
  136.5 3.1 %collective-permute-start.7 = (bf16[2,2,2,192,128]{4,3,2,1,0:T(8,128)(2,1)S(1)}, bf16[2,2,2,192,128]{4,3,2,1,0:T(8,128)(2,1)}, u32[]{:S(2)}, u32[]{:S(2)}) collective-permute-start(bf16[2,2,2,192,128]{4,3,2,1,0:T(8,128)(2,1)S(1)} %pad_maximum_fusion.u0), channel_id=1, source_target_pairs={{0,6},{2,0},{4,2},{6,4},{1,7},{3,1},{5,3},{7,5},{8,14},{10,8},{12,... | collective-permute-start | bytes 1179656 | tf_op jit(solution)/shard_map/ppermute | solution.py:146
  140.7 4.4 %shard_map.29 = (f32[2,2,192,128]{3,2,1,0:T(8,128)}, f32[2,2,192,128]{3,2,1,0:T(8,128)S(1)}) custom-call(s32[4]{0:T(128)S(1)} %pad_add_fusion.place_ref, bf16[2,2,2,192,128]{4,3,2,1,0:T(8,128)(2,1)} %pad_maximum_fusion.1.u0, bf16[2,2,2,192,128]{4,3,2,1,0:T(8,128)(2,1)S(1)} %copy-done.3, bf16[2,2,2,192,128]{4,3,2,1,0:T(8,128)(2,1)} %collective-permute-done.17.u2, ...), custom_call_target="tpu_custom_call" | custom-call | flops 1610612736 | bytes 7340032 | tf_op jit(solution)/shard_map/pallas_call | solution.py:89
  145.9 4.8 %collective-permute-start = (f32[2,2]{1,0:T(2,128)S(1)}, f32[2,2]{1,0:T(2,128)S(1)}, u32[]{:S(2)}, u32[]{:S(2)}) collective-permute-start(f32[2,2]{1,0:T(2,128)S(1)} %copy-done.6), channel_id=1, source_target_pairs={{0,0},{1,1},{2,2},{3,3},{4,4},{5,5},{6,6},{7,7},{8,32},{9,33},{10,... | collective-permute-start | bytes 56 | tf_op jit(solution)/shard_map/ppermute | solution.py:38
  150.8 4.4 %shard_map.28 = (f32[2,2,192,128]{3,2,1,0:T(8,128)S(1)}, f32[2,2,192,128]{3,2,1,0:T(8,128)S(1)}) custom-call(s32[4]{0:T(128)S(1)} %pad_add_fusion.place_ref, bf16[2,2,2,192,128]{4,3,2,1,0:T(8,128)(2,1)S(1)} %pad_maximum_fusion.u0, bf16[2,2,2,192,128]{4,3,2,1,0:T(8,128)(2,1)} %collective-permute-done.5.u1, ...), custom_call_target="tpu_custom_call" | custom-call | flops 1610612736 | bytes 7340032 | tf_op jit(solution)/shard_map/pallas_call | solution.py:89
  155.3 5.8 %collective-permute-done = f32[2,2]{1,0:T(2,128)S(1)} collective-permute-done((f32[2,2]{1,0:T(2,128)S(1)}, f32[2,2]{1,0:T(2,128)S(1)}, u32[]{:S(2)}, u32[]{:S(2)}) %collective-permute-start) | collective-permute-done | bytes 48 | tf_op jit(solution)/shard_map/ppermute | solution.py:38
  164.2 1.9 collective-permute-start.21
  166.1 14.6 %collective-permute-start.22 = (bf16[2,192,128]{2,1,0:T(8,128)(2,1)S(1)}, bf16[2,192,128]{2,1,0:T(8,128)(2,1)S(1)}, u32[]{:S(2)}, u32[]{:S(2)}) collective-permute-start(bf16[2,192,128]{2,1,0:T(8,128)(2,1)S(1)} %get-tuple-element.50), channel_id=1, source_target_pairs={{0,8},{1,9},{2,10},{3,11},{4,12},{5,13},{6,14},{7,15},{8,40},{9,41... | collective-permute-start | bytes 294920 | tf_op jit(solution)/shard_map/ppermute | solution.py:38
  182.1 3.2 %collective-permute-start.11 = (bf16[2,192,128]{2,1,0:T(8,128)(2,1)S(1)}, bf16[2,192,128]{2,1,0:T(8,128)(2,1)S(1)}, u32[]{:S(2)}, u32[]{:S(2)}) collective-permute-start(bf16[2,192,128]{2,1,0:T(8,128)(2,1)S(1)} %get-tuple-element.45), channel_id=1, source_target_pairs={{0,0},{1,1},{2,2},{3,3},{4,4},{5,5},{6,6},{7,7},{8,32},{9,33},{10,... | collective-permute-start | bytes 294920 | tf_op jit(solution)/shard_map/ppermute | solution.py:38
  187.0 7.7 %collective-permute-done.11 = bf16[2,192,128]{2,1,0:T(8,128)(2,1)S(1)} collective-permute-done((bf16[2,192,128]{2,1,0:T(8,128)(2,1)S(1)}, bf16[2,192,128]{2,1,0:T(8,128)(2,1)S(1)}, u32[]{:S(2)}, u32[]{:S(2)}) %collective-permute-start.11) | collective-permute-done | bytes 98336 | tf_op jit(solution)/shard_map/ppermute | solution.py:38
  (62 shorter events, 17.9 us)
Async XLA Ops:
  0.0 5.7 %copy-start.4 = (bf16[2,16,512,128]{3,2,1,0:T(8,128)(2,1)S(1)}, bf16[2,16,512,128]{3,2,1,0:T(8,128)(2,1)}, u32[]{:S(2)}) copy-start(bf16[2,16,512,128]{3,2,1,0:T(8,128)(2,1)} %param.2) | copy-start | bytes 12582916
  2.2 3.5 %collective-permute-start.1 = (bf16[2,16,192,128]{3,2,1,0:T(8,128)(2,1)S(1)}, bf16[2,16,192,128]{3,2,1,0:T(8,128)(2,1)S(1)}, u32[]{:S(2)}, u32[]{:S(2)}) collective-permute-start(bf16[2,16,192,128]{3,2,1,0:T(8,128)(2,1)S(1)} %slice_select_fusion), channel_id=1, source_target_pairs={{0,32},{32,0},{1,33},{33,1},{2,34},{34,2},{3,35},{35,3},{4,36},{36... | collective-permute-start | bytes 4718600 | tf_op jit(solution)/shard_map/ppermute | solution.py:42
  7.2 25.1 %all-to-all-start = ((bf16[8,2,2,192,128]{4,3,2,1,0:T(8,128)(2,1)}), bf16[8,2,2,192,128]{4,3,2,1,0:T(8,128)(2,1)S(1)}, u32[]{:S(2)}, u32[]{:S(2)}) async-start(bf16[8,2,2,192,128]{4,3,2,1,0:T(8,128)(2,1)} %bitcast.7), calls=%async_computation | async-start | bytes 3145728 | tf_op jit(solution)/shard_map/all_to_all | solution.py:126
  13.4 1.2 slice-start
  56.9 36.4 %all-to-all-start.1 = ((bf16[8,2,320,128]{3,2,1,0:T(8,128)(2,1)}), bf16[8,2,320,128]{3,2,1,0:T(8,128)(2,1)}, u32[]{:S(2)}, u32[]{:S(2)}) async-start(bf16[8,2,320,128]{3,2,1,0:T(8,128)(2,1)} %get-tuple-element.33), calls=%async_computation.1 | async-start | bytes 2621440 | tf_op jit(solution)/shard_map/all_to_all | solution.py:126
  63.5 73.0 %collective-permute-start.8 = (bf16[8,2,2,192,128]{4,3,2,1,0:T(8,128)(2,1)S(1)}, bf16[8,2,2,192,128]{4,3,2,1,0:T(8,128)(2,1)S(1)}, u32[]{:S(2)}, u32[]{:S(2)}) collective-permute-start(bf16[8,2,2,192,128]{4,3,2,1,0:T(8,128)(2,1)S(1)} %all-to-all-done.ao_ref), channel_id=1, source_target_pairs={{0,32},{32,0},{1,33},{33,1},{2,34},{34,2},{3,35},{35,3},{4,36},{36... | collective-permute-start | bytes 4718600 | tf_op jit(solution)/shard_map/ppermute | solution.py:42
  64.3 25.1 %collective-permute-start.13 = (bf16[2,2,192,128]{3,2,1,0:T(8,128)(2,1)S(1)}, bf16[2,2,192,128]{3,2,1,0:T(8,128)(2,1)}, u32[]{:S(2)}, u32[]{:S(2)}) collective-permute-start(bf16[2,2,192,128]{3,2,1,0:T(8,128)(2,1)S(1)} %get-tuple-element.27), channel_id=1, source_target_pairs={{0,1},{1,0},{2,3},{3,2},{4,5},{5,4},{6,7},{7,6},{8,9},{9,8},{10,11... | collective-permute-start | bytes 589832 | tf_op jit(solution)/shard_map/ppermute | solution.py:38
  72.5 18.9 %collective-permute-start.14 = (bf16[2,2,192,128]{3,2,1,0:T(8,128)(2,1)}, bf16[2,2,192,128]{3,2,1,0:T(8,128)(2,1)}, u32[]{:S(2)}, u32[]{:S(2)}) collective-permute-start(bf16[2,2,192,128]{3,2,1,0:T(8,128)(2,1)} %get-tuple-element.38), channel_id=1, source_target_pairs={{0,128},{1,129},{2,130},{3,131},{4,132},{5,133},{6,134},{7,135},{8... | collective-permute-start | bytes 589832 | tf_op jit(solution)/shard_map/ppermute | solution.py:38
  74.5 18.9 %collective-permute-start.15 = (bf16[2,2,192,128]{3,2,1,0:T(8,128)(2,1)}, bf16[2,2,192,128]{3,2,1,0:T(8,128)(2,1)}, u32[]{:S(2)}, u32[]{:S(2)}) collective-permute-start(bf16[2,2,192,128]{3,2,1,0:T(8,128)(2,1)} %get-tuple-element.38), channel_id=1, source_target_pairs={{0,129},{1,128},{2,131},{3,130},{4,133},{5,132},{6,135},{7,134},{8... | collective-permute-start | bytes 589832 | tf_op jit(solution)/shard_map/ppermute | solution.py:38
  76.5 63.2 %collective-permute-start.19 = (bf16[8,2,320,128]{3,2,1,0:T(8,128)(2,1)}, bf16[8,2,320,128]{3,2,1,0:T(8,128)(2,1)}, u32[]{:S(2)}, u32[]{:S(2)}) collective-permute-start(bf16[8,2,320,128]{3,2,1,0:T(8,128)(2,1)} %all_to_all.15.bo_ref), channel_id=1, source_target_pairs={{0,32},{32,0},{1,33},{33,1},{2,34},{34,2},{3,35},{35,3},{4,36},{36... | collective-permute-start | bytes 3932168 | tf_op jit(solution)/shard_map/ppermute | solution.py:42
  89.5 11.7 %collective-permute-start.2 = (bf16[2,2,192,128]{3,2,1,0:T(8,128)(2,1)S(1)}, bf16[2,2,192,128]{3,2,1,0:T(8,128)(2,1)}, u32[]{:S(2)}, u32[]{:S(2)}) collective-permute-start(bf16[2,2,192,128]{3,2,1,0:T(8,128)(2,1)S(1)} %get-tuple-element.20), channel_id=1, source_target_pairs={{0,1},{1,0},{2,3},{3,2},{4,5},{5,4},{6,7},{7,6},{8,9},{9,8},{10,11... | collective-permute-start | bytes 589832 | tf_op jit(solution)/shard_map/ppermute | solution.py:38
  91.4 11.3 %collective-permute-start.3 = (bf16[2,2,192,128]{3,2,1,0:T(8,128)(2,1)}, bf16[2,2,192,128]{3,2,1,0:T(8,128)(2,1)}, u32[]{:S(2)}, u32[]{:S(2)}) collective-permute-start(bf16[2,2,192,128]{3,2,1,0:T(8,128)(2,1)} %get-tuple-element.35), channel_id=1, source_target_pairs={{0,128},{1,129},{2,130},{3,131},{4,132},{5,133},{6,134},{7,135},{8... | collective-permute-start | bytes 589832 | tf_op jit(solution)/shard_map/ppermute | solution.py:38
  93.4 9.3 %copy-start.5 = (bf16[2,2,192,128]{3,2,1,0:T(8,128)(2,1)S(1)}, bf16[2,2,192,128]{3,2,1,0:T(8,128)(2,1)}, u32[]{:S(2)}) copy-start(bf16[2,2,192,128]{3,2,1,0:T(8,128)(2,1)} %get-tuple-element.35) | copy-start | bytes 589828
  93.4 57.4 %collective-permute-start.9 = (bf16[8,2,320,128]{3,2,1,0:T(8,128)(2,1)}, bf16[8,2,320,128]{3,2,1,0:T(8,128)(2,1)}, u32[]{:S(2)}, u32[]{:S(2)}) collective-permute-start(bf16[8,2,320,128]{3,2,1,0:T(8,128)(2,1)} %all-to-all-done.1.bo_ref), channel_id=1, source_target_pairs={{0,32},{32,0},{1,33},{33,1},{2,34},{34,2},{3,35},{35,3},{4,36},{36... | collective-permute-start | bytes 3932168 | tf_op jit(solution)/shard_map/ppermute | solution.py:42
  101.1 15.2 %collective-permute-start.16 = (bf16[2,2,2,192,128]{4,3,2,1,0:T(8,128)(2,1)}, bf16[2,2,2,192,128]{4,3,2,1,0:T(8,128)(2,1)S(1)}, u32[]{:S(2)}, u32[]{:S(2)}) collective-permute-start(bf16[2,2,2,192,128]{4,3,2,1,0:T(8,128)(2,1)} %pad_maximum_fusion.1.u0), channel_id=1, source_target_pairs={{0,2},{2,4},{4,6},{6,0},{1,3},{3,5},{5,7},{7,1},{8,10},{10,12},{12... | collective-permute-start | bytes 1179656 | tf_op jit(solution)/shard_map/ppermute | solution.py:146
  102.7 10.4 %collective-permute-start.4 = (bf16[2,2,192,128]{3,2,1,0:T(8,128)(2,1)S(1)}, bf16[2,2,192,128]{3,2,1,0:T(8,128)(2,1)S(1)}, u32[]{:S(2)}, u32[]{:S(2)}) collective-permute-start(bf16[2,2,192,128]{3,2,1,0:T(8,128)(2,1)S(1)} %copy-done.5), channel_id=1, source_target_pairs={{0,129},{1,128},{2,131},{3,130},{4,133},{5,132},{6,135},{7,134},{8... | collective-permute-start | bytes 589832 | tf_op jit(solution)/shard_map/ppermute | solution.py:38
  113.1 13.9 %collective-permute-start.17 = (bf16[2,2,2,192,128]{4,3,2,1,0:T(8,128)(2,1)}, bf16[2,2,2,192,128]{4,3,2,1,0:T(8,128)(2,1)}, u32[]{:S(2)}, u32[]{:S(2)}) collective-permute-start(bf16[2,2,2,192,128]{4,3,2,1,0:T(8,128)(2,1)} %pad_maximum_fusion.1.u0), channel_id=1, source_target_pairs={{0,4},{2,6},{4,0},{6,2},{1,5},{3,7},{5,1},{7,3},{8,12},{10,14},{12... | collective-permute-start | bytes 1179656 | tf_op jit(solution)/shard_map/ppermute | solution.py:146
  116.3 0.8 copy-start.2
  117.1 17.7 %collective-permute-start.18 = (bf16[2,2,2,192,128]{4,3,2,1,0:T(8,128)(2,1)}, bf16[2,2,2,192,128]{4,3,2,1,0:T(8,128)(2,1)}, u32[]{:S(2)}, u32[]{:S(2)}) collective-permute-start(bf16[2,2,2,192,128]{4,3,2,1,0:T(8,128)(2,1)} %pad_maximum_fusion.1.u0), channel_id=1, source_target_pairs={{0,6},{2,0},{4,2},{6,4},{1,7},{3,1},{5,3},{7,5},{8,14},{10,8},{12,... | collective-permute-start | bytes 1179656 | tf_op jit(solution)/shard_map/ppermute | solution.py:146
  127.0 18.9 %collective-permute-start.5 = (bf16[2,2,2,192,128]{4,3,2,1,0:T(8,128)(2,1)S(1)}, bf16[2,2,2,192,128]{4,3,2,1,0:T(8,128)(2,1)}, u32[]{:S(2)}, u32[]{:S(2)}) collective-permute-start(bf16[2,2,2,192,128]{4,3,2,1,0:T(8,128)(2,1)S(1)} %pad_maximum_fusion.u0), channel_id=1, source_target_pairs={{0,2},{2,4},{4,6},{6,0},{1,3},{3,5},{5,7},{7,1},{8,10},{10,12},{12... | collective-permute-start | bytes 1179656 | tf_op jit(solution)/shard_map/ppermute | solution.py:146
  134.8 16.0 %collective-permute-start.6 = (bf16[2,2,2,192,128]{4,3,2,1,0:T(8,128)(2,1)S(1)}, bf16[2,2,2,192,128]{4,3,2,1,0:T(8,128)(2,1)}, u32[]{:S(2)}, u32[]{:S(2)}) collective-permute-start(bf16[2,2,2,192,128]{4,3,2,1,0:T(8,128)(2,1)S(1)} %pad_maximum_fusion.u0), channel_id=1, source_target_pairs={{0,4},{2,6},{4,0},{6,2},{1,5},{3,7},{5,1},{7,3},{8,12},{10,14},{12... | collective-permute-start | bytes 1179656 | tf_op jit(solution)/shard_map/ppermute | solution.py:146
  136.5 14.3 %collective-permute-start.7 = (bf16[2,2,2,192,128]{4,3,2,1,0:T(8,128)(2,1)S(1)}, bf16[2,2,2,192,128]{4,3,2,1,0:T(8,128)(2,1)}, u32[]{:S(2)}, u32[]{:S(2)}) collective-permute-start(bf16[2,2,2,192,128]{4,3,2,1,0:T(8,128)(2,1)S(1)} %pad_maximum_fusion.u0), channel_id=1, source_target_pairs={{0,6},{2,0},{4,2},{6,4},{1,7},{3,1},{5,3},{7,5},{8,14},{10,8},{12,... | collective-permute-start | bytes 1179656 | tf_op jit(solution)/shard_map/ppermute | solution.py:146
  139.7 1.0 copy-start.3
  140.7 5.2 %copy-start.6 = (f32[2,2]{1,0:T(2,128)S(1)}, f32[2,2]{1,0:T(2,128)}, u32[]{:S(2)}) copy-start(f32[2,2]{1,0:T(2,128)} %param.3) | copy-start | bytes 52
  145.9 15.9 %collective-permute-start.20 = (f32[2,2,192,128]{3,2,1,0:T(8,128)}, f32[2,2,192,128]{3,2,1,0:T(8,128)}, u32[]{:S(2)}, u32[]{:S(2)}) collective-permute-start(f32[2,2,192,128]{3,2,1,0:T(8,128)} %get-tuple-element.32), channel_id=1, source_target_pairs={{0,128},{1,129},{2,130},{3,131},{4,132},{5,133},{6,134},{7,135},{8... | collective-permute-start | bytes 1179656 | tf_op jit(solution)/shard_map/ppermute | solution.py:38
  145.9 15.9 %copy-start.1 = (f32[2,2,192,128]{3,2,1,0:T(8,128)S(1)}, f32[2,2,192,128]{3,2,1,0:T(8,128)}, u32[]{:S(2)}) copy-start(f32[2,2,192,128]{3,2,1,0:T(8,128)} %copy-done) | copy-start | bytes 1179652
  145.9 15.2 %collective-permute-start = (f32[2,2]{1,0:T(2,128)S(1)}, f32[2,2]{1,0:T(2,128)S(1)}, u32[]{:S(2)}, u32[]{:S(2)}) collective-permute-start(f32[2,2]{1,0:T(2,128)S(1)} %copy-done.6), channel_id=1, source_target_pairs={{0,0},{1,1},{2,2},{3,3},{4,4},{5,5},{6,6},{7,7},{8,32},{9,33},{10,... | collective-permute-start | bytes 56 | tf_op jit(solution)/shard_map/ppermute | solution.py:38
  155.2 25.5 %collective-permute-start.10 = (f32[2,2,192,128]{3,2,1,0:T(8,128)S(1)}, f32[2,2,192,128]{3,2,1,0:T(8,128)S(1)}, u32[]{:S(2)}, u32[]{:S(2)}) collective-permute-start(f32[2,2,192,128]{3,2,1,0:T(8,128)S(1)} %get-tuple-element.26), channel_id=1, source_target_pairs={{0,128},{1,129},{2,130},{3,131},{4,132},{5,133},{6,134},{7,135},{8... | collective-permute-start | bytes 1179656 | tf_op jit(solution)/shard_map/ppermute | solution.py:38
  164.2 21.2 %collective-permute-start.21 = (bf16[2,192,128]{2,1,0:T(8,128)(2,1)S(1)}, bf16[2,192,128]{2,1,0:T(8,128)(2,1)S(1)}, u32[]{:S(2)}, u32[]{:S(2)}) collective-permute-start(bf16[2,192,128]{2,1,0:T(8,128)(2,1)S(1)} %get-tuple-element.49), channel_id=1, source_target_pairs={{0,0},{1,1},{2,2},{3,3},{4,4},{5,5},{6,6},{7,7},{8,32},{9,33},{10,... | collective-permute-start | bytes 294920 | tf_op jit(solution)/shard_map/ppermute | solution.py:38
  166.1 20.9 %collective-permute-start.22 = (bf16[2,192,128]{2,1,0:T(8,128)(2,1)S(1)}, bf16[2,192,128]{2,1,0:T(8,128)(2,1)S(1)}, u32[]{:S(2)}, u32[]{:S(2)}) collective-permute-start(bf16[2,192,128]{2,1,0:T(8,128)(2,1)S(1)} %get-tuple-element.50), channel_id=1, source_target_pairs={{0,8},{1,9},{2,10},{3,11},{4,12},{5,13},{6,14},{7,15},{8,40},{9,41... | collective-permute-start | bytes 294920 | tf_op jit(solution)/shard_map/ppermute | solution.py:38
  182.1 12.6 %collective-permute-start.11 = (bf16[2,192,128]{2,1,0:T(8,128)(2,1)S(1)}, bf16[2,192,128]{2,1,0:T(8,128)(2,1)S(1)}, u32[]{:S(2)}, u32[]{:S(2)}) collective-permute-start(bf16[2,192,128]{2,1,0:T(8,128)(2,1)S(1)} %get-tuple-element.45), channel_id=1, source_target_pairs={{0,0},{1,1},{2,2},{3,3},{4,4},{5,5},{6,6},{7,7},{8,32},{9,33},{10,... | collective-permute-start | bytes 294920 | tf_op jit(solution)/shard_map/ppermute | solution.py:38
  185.3 9.6 %collective-permute-start.12 = (bf16[2,192,128]{2,1,0:T(8,128)(2,1)S(1)}, bf16[2,192,128]{2,1,0:T(8,128)(2,1)S(1)}, u32[]{:S(2)}, u32[]{:S(2)}) collective-permute-start(bf16[2,192,128]{2,1,0:T(8,128)(2,1)S(1)} %get-tuple-element.46), channel_id=1, source_target_pairs={{0,8},{1,9},{2,10},{3,11},{4,12},{5,13},{6,14},{7,15},{8,40},{9,41... | collective-permute-start | bytes 294920 | tf_op jit(solution)/shard_map/ppermute | solution.py:38
  (1 other events, 0.7 us)

commit v4 on v3

v4 whole, which is shorter than its diff:
```python
import jax
import jax.numpy as jnp
from jax import lax
from jax.experimental import pallas as pl
from jax.experimental.pallas import tpu as pltpu
from jax.sharding import Mesh, PartitionSpec as P


NOUT = 384
AXES = ("zq", "zr", "core", "x", "yq", "yr", "zh")
SIZES = (2, 2, 2, 4, 2, 2, 2)


def coordinates():
    out = [()]
    for size in SIZES:
        out = [c + (i,) for c in out for i in range(size)]
    return out


def flat(c):
    index = 0
    for i, size in zip(c, SIZES):
        index = index * size + i
    return index


def moved(target):
    pairs = []
    for c in coordinates():
        t = target(*c)
        if t is not None:
            pairs.append((flat(c), flat(t)))
    return pairs


def send(value, target):
    return lax.ppermute(value, AXES, moved(target))


def swap_core(value):
    return lax.ppermute(value, "core", [(0, 1), (1, 0)])


def contract(turn, place, mine, theirs, a_own, a_peer, b_own, b_peer):
    half, lanes = mine[0].shape[-2:]
    depth = 16 * lanes

    def kernel(place_ref, m0, m1, t0, t1, ao_ref, ap_ref, bo_ref, bp_ref, sent_ref, kept_ref, left):
        core, zh, zq, yq, yr = (place_ref[i] for i in range(5))
        for far, refs in enumerate(((m0, m1), (t0, t1))):
            for piece, u_ref in enumerate(refs):
                for xl in range(2):
                    for yl in range(2):
                        block = (xl * 4 + 2 * (yq ^ far) + yl) * 2 + (piece ^ zh)
                        start = pl.multiple_of(block * lanes, lanes)
                        for part in range(2):
                            left[part * half : (part + 1) * half, pl.ds(start, lanes)] = u_ref[xl, yl, part]

        first = core == 0
        for side, out in ((1, sent_ref), (0, kept_ref)):
            for low in range(2):
                x = 2 * (zq ^ side) + low
                rows = []
                for zr in range(2):
                    i = 4 * x + 2 * (yr ^ turn) + zr
                    parts = []
                    for part in range(2):
                        ao, ap = ao_ref[i, part], ap_ref[i, part]
                        bo, bp = bo_ref[i, part], bp_ref[i, part]
                        parts.append(
                            jnp.concatenate(
                                [
                                    jnp.where(first, ao, ap),
                                    jnp.where(first, ap, ao),
                                    jnp.where(first, bo, bp),
                                    jnp.where(first, bp, bo),
                                ],
                                0,
                            )
                        )
                    rows.append(jnp.concatenate(parts, 1))
                right = jnp.concatenate(rows, 0)
                both = jnp.dot(left[...], right, preferred_element_type=jnp.float32)
                out[low, 0] = both[:half, :lanes] - both[half:, lanes:]
                out[low, 1] = both[:half, lanes:] + both[half:, :lanes]

    vmem = pl.BlockSpec(memory_space=pltpu.VMEM)
    result = jax.ShapeDtypeStruct((2, 2, half, lanes), jnp.float32)
    return pl.pallas_call(
        kernel,
        out_shape=(result, result),
        in_specs=[pl.BlockSpec(memory_space=pltpu.SMEM)] + [vmem] * 8,
        out_specs=(vmem, vmem),
        scratch_shapes=[pltpu.VMEM((2 * half, depth), jnp.bfloat16)],
        cost_estimate=pl.CostEstimate(
            flops=2 * 2 * half * depth * 8 * lanes, bytes_accessed=7 << 20, transcendentals=0
        ),
        compiler_params=pltpu.CompilerParams(vmem_limit_bytes=40 << 20),
    )(place, *mine, *theirs, a_own, a_peer, b_own, b_peer)


def step(spectra, wavelet):
    zq, core, x = lax.axis_index("zq"), lax.axis_index("core"), lax.axis_index("x")
    yq, yr, zh = lax.axis_index("yq"), lax.axis_index("yr"), lax.axis_index("zh")
    place = jnp.stack([core, zh, zq, yq, yr]).astype(jnp.int32)
    rows, _ = spectra.shape[2:]
    window = NOUT * rows // 512
    half = window // 2
    first = core == 0

    wave = send(wavelet, lambda q, r, c, x, a, b, h: (x // 2, r, x % 2, 2 * q + c, a, b, h))
    wave = jnp.where(yr == 0, wave[:, 0], wave[:, 1])

    def ordered(block):
        block = block.reshape((2, 2, 2, 2, 2) + block.shape[2:])
        return block.transpose(1, 3, 4, 2, 0, 5, 6).reshape((16, 2) + block.shape[5:])

    low, mid, rest = spectra[:, :, :half], spectra[:, :, half:window], spectra[:, :, window:]
    passed = swap_core(jnp.where(first, mid, low))
    a = ordered(jnp.where(first, low, passed))
    b = ordered(jnp.where(first, jnp.concatenate([rest, passed], 2), spectra[:, :, half:]))

    def exchange(block):
        return lax.all_to_all(block, ("x", "yr", "zr"), split_axis=0, concat_axis=0, tiled=True)

    a_own = exchange(a)
    a_own, b = lax.optimization_barrier((a_own, b))
    b_own = exchange(b)
    a_peer = swap_core(a_own)
    b_peer = swap_core(b_own)

    shots = a_own.reshape((4, 2, 2) + a_own.shape[1:])[:, :, 0]
    near, far = shots[:2], shots[2:]
    up = send(far, lambda q, r, c, x, a, b, h: (1, r, c, x, a, b, h) if q == 0 else None)
    across = send(near, lambda q, r, c, x, a, b, h: (0, r, c, x, a, b, 1 - h) if q == 0 else None)
    down = send(far, lambda q, r, c, x, a, b, h: (1, r, c, x, a, b, 1 - h) if q == 0 else None)
    mine = [jnp.where(zq == 0, near, up), jnp.where(zq == 0, across, down)]
    theirs = [lax.ppermute(piece, "yq", [(0, 1), (1, 0)]) for piece in mine]

    def homeward(turn, same, cross):
        same = send(
            same, lambda q, r, c, x, a, b, h: (x // 2, r, x % 2, 2 * q + c, a, b ^ turn, h)
        )
        cross = send(
            cross, lambda q, r, c, x, a, b, h: (x // 2, r, x % 2, 2 * q + 1 - c, a, b ^ turn, h)
        )
        even = x % 2 == 0
        same, cross = jnp.where(even, same, cross), jnp.where(even, cross, same)
        return jnp.concatenate([same, cross], 1)

    arrived = []
    for turn in range(2):
        sent, kept = contract(turn, place, mine, theirs, a_own, a_peer, b_own, b_peer)
        other = send(sent, lambda q, r, c, x, a, b, h: (1 - q, r, c, x, a, b, h))
        if turn:
            other, kept, early = lax.optimization_barrier((other, kept, homeward(0, same, cross)))
            arrived.append(early)
        product = kept + lax.optimization_barrier(other)
        real_out = -(wave[0] * product[:, 0] - wave[1] * product[:, 1])
        imag_out = -(wave[0] * product[:, 1] + wave[1] * product[:, 0])
        done = jnp.stack([real_out, imag_out], 1).astype(jnp.bfloat16)
        same, cross = jnp.where(first, done[0], done[1]), jnp.where(first, done[1], done[0])
        same, cross = lax.optimization_barrier((same, cross))
    arrived.append(homeward(1, same, cross))
    return jnp.stack(
        [jnp.where(yr == 0, arrived[0], arrived[1]), jnp.where(yr == 0, arrived[1], arrived[0])], 1
    )


def solution(mesh):
    fine = Mesh(mesh.devices.reshape(SIZES), AXES)
    freq, col = AXES[:3], AXES[3:]
    return jax.shard_map(
        step,
        mesh=fine,
        in_specs=(P(None, None, freq, col), P(None, freq)),
        out_specs=P(None, freq, None, col),
        check_vma=False,
    )
```

time: 200 us -> 205 us (1.025); the launches traced: 196 us -> 204 us
  starting transfers between devices: 67.9 us -> 40 us
  waiting for transfers between devices: 73.4 us -> 97.4 us
  blocking collectives: 21.5 us -> 35.2 us
  local copies, waits for them, and re-layouts: 12 us -> 7.08 us
    ppermute x13 -> x10, waiting for transfers between devices: 41.3 us -> 61.3 us  [send(): return lax.ppermute(value, AXES, moved(target))]
    ppermute x13 -> x10, starting transfers between devices: 43.8 us -> 28.4 us  [send(): return lax.ppermute(value, AXES, moved(target))]
    all_to_all x1, blocking collectives: 21.5 us -> 35.2 us  [exchange(): lax.all_to_all(block, ('x', 'yr', 'zr'), split_axis=0, concat_axis=0, til...]
    ppermute x6 -> x2, starting transfers between devices: 11 us -> 3.7 us  [step(): theirs = [lax.ppermute(piece, 'yq', [(0, 1), (1, 0)]) for piece in mine]]
    all_to_all x2 -> x1, starting transfers between devices: 12.7 us -> 7.32 us  [exchange(): lax.all_to_all(block, ('x', 'yr', 'zr'), split_axis=0, concat_axis=0, til...]
    select_n x5 -> x8, other arithmetic: 0.28 us -> 4.01 us  [the longest x2 2.08 us: step(): mine = [jnp.where(zq == 0, near, up), jnp.where(zq == 0, across, down)]]
    all_to_all x2 -> x1, waiting for transfers between devices: 13.4 us -> 16.8 us  [exchange(): lax.all_to_all(block, ('x', 'yr', 'zr'), split_axis=0, concat_axis=0, til...]
    squeeze x1 -> x0, local copies, waits for them, and re-layouts: 3.03 us -> none  [step(): b_own.append(exchange(b[g]))]
  transfers between devices with their start and end apart: 25 -> 16, of which waited for: 11 -> 11; matrix products, arithmetic and copies ran while one was open for 6% -> 5% of each run, Pallas kernels for 5% -> 3%
where the time goes in v4:
time: 205 us; the launch traced here: 204 us
  waiting for transfers between devices  97.4 us (48%)
  starting transfers between devices  40 us (20%)
  blocking collectives  35.2 us (17%)
  other arithmetic  13.8 us (7%)
  Pallas kernels  10.6 us (5%)
  local copies, waits for them, and re-layouts  7.08 us (3%)
    ppermute x10, waiting for transfers between devices, send(): return lax.ppermute(value, AXES, moved(target))  61.3 us
    all_to_all x1, blocking collectives, exchange(): lax.all_to_all(block, ('x', 'yr', 'zr'), split_axis=0, concat_axis=0, til...  35.2 us
    ppermute x10, starting transfers between devices, send(): return lax.ppermute(value, AXES, moved(target))  28.4 us
    all_to_all x1, waiting for transfers between devices, exchange(): lax.all_to_all(block, ('x', 'yr', 'zr'), split_axis=0, concat_axis=0, til...  16.8 us
    ppermute x2, waiting for transfers between devices, step(): theirs = [lax.ppermute(piece, 'yq', [(0, 1), (1, 0)]) for piece in mine]  15.9 us
    pallas_call x2, Pallas kernels, contract(): pl.pallas_call(kernel, out_shape=(result, result), in_specs=[pl.BlockSpec...  10.6 us
    all_to_all x1, starting transfers between devices, exchange(): lax.all_to_all(block, ('x', 'yr', 'zr'), split_axis=0, concat_axis=0, til...  7.32 us
  transfers between devices with their start and end apart: 16, of which 11 were waited for; matrix products, arithmetic and copies ran while one was open for 5% of the time, Pallas kernels for 3%

profile of v4, /device:TPU:4, one launch (start us, length us, event | category | flops | bytes accessed | tf_op | source)
XLA Modules:
  0.0 204.3 jit_solution(9104307296047936917)
XLA Ops:
  0.0 2.2 %slice_select_fusion = bf16[2,16,192,128]{3,2,1,0:T(8,128)(2,1)S(1)} fusion(bf16[2,16,512,128]{3,2,1,0:T(8,128)(2,1)} %param.2, pred[]{:T(512)S(6)} %eq.21), kind=kLoop, calls=%fused_computation.1 | loop fusion | flops 786432 | bytes 4718593 | tf_op jit(solution)/shard_map/jit(_where)/select_n | solution.py:120
  2.3 3.4 %collective-permute-done = bf16[2,16,192,128]{3,2,1,0:T(8,128)(2,1)S(1)} collective-permute-done((bf16[2,16,192,128]{3,2,1,0:T(8,128)(2,1)S(1)}, bf16[2,16,192,128]{3,2,1,0:T(8,128)(2,1)S(1)}, u32[]{:S(2)}, u32[]{:S(2)}) %collective-permute-start) | collective-permute-done | bytes 1572896 | tf_op jit(solution)/shard_map/ppermute | solution.py:42
  5.9 1.3 copy.3
  7.2 7.3 %all-to-all-start = ((bf16[16,2,192,128]{3,2,1,0:T(8,128)(2,1)}), bf16[16,2,192,128]{3,2,1,0:T(8,128)(2,1)}, u32[]{:S(2)}, u32[]{:S(2)}) async-start(bf16[16,2,192,128]{3,2,1,0:T(8,128)(2,1)} %bitcast.7), calls=%async_computation | async-start | bytes 3145728 | tf_op jit(solution)/shard_map/all_to_all | solution.py:125
  14.5 2.7 %maximum_select_fusion = bf16[2,16,320,128]{3,2,1,0:T(8,128)(2,1)S(1)} fusion(bf16[2,16,192,128]{3,2,1,0:T(8,128)(2,1)S(1)} %collective-permute-done, bf16[2,16,128,128]{3,2,1,0:T(8,128)(2,1)S(1)} %slice-done, bf16[2,16,512,128]{3,2,1,0:T(8,128)(2,1)} %param.2, pred[]{:T(512)S(6)} %eq.21), kind=kLoop, calls=%fused_computation | loop fusion | flops 6553600 | bytes 7864321 | tf_op jit(solution)/shard_map/jit(_where)/select_n | solution.py:122
  17.2 1.7 copy.4
  18.9 16.8 %all-to-all-done.ao_ref = bf16[16,2,192,128]{3,2,1,0:T(8,128)(2,1)} async-done(((bf16[16,2,192,128]{3,2,1,0:T(8,128)(2,1)}), bf16[16,2,192,128]{3,2,1,0:T(8,128)(2,1)}, u32[]{:S(2)}, u32[]{:S(2)}) %all-to-all-start) | async-done | bytes 1572896 | tf_op jit(solution)/shard_map/all_to_all | solution.py:125
  35.7 35.2 %all_to_all.10.bo_ref = bf16[16,2,320,128]{3,2,1,0:T(8,128)(2,1)S(1)} all-to-all(bf16[16,2,320,128]{3,2,1,0:T(8,128)(2,1)} %bitcast.38), channel_id=1, replica_groups=mesh['zq'=2,'zr'=2,'core'=2,'x'=4,'yq'=2,'yr'=2,'zh'=2] {'x','yr','zr'}, dimensions={0} | all-to-all | bytes 5242880 | tf_op jit(solution)/shard_map/all_to_all | solution.py:125
  71.4 1.2 slice_bitcast_fusion.1
  72.6 8.1 %collective-permute-start.3 = (bf16[2,2,2,192,128]{4,3,2,1,0:T(8,128)(2,1)S(1)}, bf16[2,2,2,192,128]{4,3,2,1,0:T(8,128)(2,1)}, u32[]{:S(2)}, u32[]{:S(2)}) collective-permute-start(bf16[2,2,2,192,128]{4,3,2,1,0:T(8,128)(2,1)S(1)} %get-tuple-element.32), channel_id=1, source_target_pairs={{0,129},{1,128},{2,131},{3,130},{4,133},{5,132},{6,135},{7,134},{8... | collective-permute-start | bytes 1179656 | tf_op jit(solution)/shard_map/ppermute | solution.py:38
  80.6 3.3 %collective-permute-start.2 = (bf16[2,2,2,192,128]{4,3,2,1,0:T(8,128)(2,1)S(1)}, bf16[2,2,2,192,128]{4,3,2,1,0:T(8,128)(2,1)}, u32[]{:S(2)}, u32[]{:S(2)}) collective-permute-start(bf16[2,2,2,192,128]{4,3,2,1,0:T(8,128)(2,1)S(1)} %get-tuple-element.31), channel_id=1, source_target_pairs={{0,1},{1,0},{2,3},{3,2},{4,5},{5,4},{6,7},{7,6},{8,9},{9,8},{10,11... | collective-permute-start | bytes 1179656 | tf_op jit(solution)/shard_map/ppermute | solution.py:38
  84.0 2.1 %collective-permute-start.1 = (bf16[2,2,2,192,128]{4,3,2,1,0:T(8,128)(2,1)S(1)}, bf16[2,2,2,192,128]{4,3,2,1,0:T(8,128)(2,1)}, u32[]{:S(2)}, u32[]{:S(2)}) collective-permute-start(bf16[2,2,2,192,128]{4,3,2,1,0:T(8,128)(2,1)S(1)} %get-tuple-element.32), channel_id=1, source_target_pairs={{0,128},{1,129},{2,130},{3,131},{4,132},{5,133},{6,134},{7,135},{8... | collective-permute-start | bytes 1179656 | tf_op jit(solution)/shard_map/ppermute | solution.py:38
  86.1 19.2 %collective-permute-done.3 = bf16[2,2,2,192,128]{4,3,2,1,0:T(8,128)(2,1)} collective-permute-done((bf16[2,2,2,192,128]{4,3,2,1,0:T(8,128)(2,1)S(1)}, bf16[2,2,2,192,128]{4,3,2,1,0:T(8,128)(2,1)}, u32[]{:S(2)}, u32[]{:S(2)}) %collective-permute-start.3) | collective-permute-done | bytes 393248 | tf_op jit(solution)/shard_map/ppermute | solution.py:38
  105.3 1.0 broadcast_select_fusion.1.m1
  106.3 3.0 %collective-permute-start.5 = (bf16[2,2,2,192,128]{4,3,2,1,0:T(8,128)(2,1)S(1)}, bf16[2,2,2,192,128]{4,3,2,1,0:T(8,128)(2,1)}, u32[]{:S(2)}, u32[]{:S(2)}) collective-permute-start(bf16[2,2,2,192,128]{4,3,2,1,0:T(8,128)(2,1)S(1)} %broadcast_select_fusion.1.m1), channel_id=1, source_target_pairs={{0,4},{4,0},{1,5},{5,1},{2,6},{6,2},{3,7},{7,3},{8,12},{12,8},{9,1... | collective-permute-start | bytes 1179656 | tf_op jit(solution)/shard_map/ppermute | solution.py:139
  111.2 8.8 %collective-permute-done.5.t1 = bf16[2,2,2,192,128]{4,3,2,1,0:T(8,128)(2,1)} collective-permute-done((bf16[2,2,2,192,128]{4,3,2,1,0:T(8,128)(2,1)S(1)}, bf16[2,2,2,192,128]{4,3,2,1,0:T(8,128)(2,1)}, u32[]{:S(2)}, u32[]{:S(2)}) %collective-permute-start.5) | collective-permute-done | bytes 393248 | tf_op jit(solution)/shard_map/ppermute | solution.py:139
  120.0 7.1 %collective-permute-done.4.t0 = bf16[2,2,2,192,128]{4,3,2,1,0:T(8,128)(2,1)} collective-permute-done((bf16[2,2,2,192,128]{4,3,2,1,0:T(8,128)(2,1)S(1)}, bf16[2,2,2,192,128]{4,3,2,1,0:T(8,128)(2,1)}, u32[]{:S(2)}, u32[]{:S(2)}) %collective-permute-start.4) | collective-permute-done | bytes 393248 | tf_op jit(solution)/shard_map/ppermute | solution.py:139
  127.1 5.3 %shard_map.29 = (f32[2,2,192,128]{3,2,1,0:T(8,128)}, f32[2,2,192,128]{3,2,1,0:T(8,128)S(1)}) custom-call(s32[5]{0:T(128)S(1)} %stack.44.place_ref, bf16[2,2,2,192,128]{4,3,2,1,0:T(8,128)(2,1)S(1)} %broadcast_select_fusion.2.m0, bf16[2,2,2,192,128]{4,3,2,1,0:T(8,128)(2,1)S(1)} %broadcast_select_fusion.1.m1, ...), custom_call_target="tpu_custom_call" | custom-call | flops 1610612736 | bytes 7340032 | tf_op jit(solution)/shard_map/pallas_call | solution.py:90
  133.1 2.6 %collective-permute-start.10 = (f32[2,2,192,128]{3,2,1,0:T(8,128)}, f32[2,2,192,128]{3,2,1,0:T(8,128)}, u32[]{:S(2)}, u32[]{:S(2)}) collective-permute-start(f32[2,2,192,128]{3,2,1,0:T(8,128)} %get-tuple-element.23), channel_id=1, source_target_pairs={{0,128},{1,129},{2,130},{3,131},{4,132},{5,133},{6,134},{7,135},{8... | collective-permute-start | bytes 1179656 | tf_op jit(solution)/shard_map/ppermute | solution.py:38
  135.7 2.9 %collective-permute-start.9 = (f32[2,2]{1,0:T(2,128)S(1)}, f32[2,2]{1,0:T(2,128)S(1)}, u32[]{:S(2)}, u32[]{:S(2)}) collective-permute-start(f32[2,2]{1,0:T(2,128)S(1)} %copy-done.3), channel_id=1, source_target_pairs={{0,0},{1,1},{2,2},{3,3},{4,4},{5,5},{6,6},{7,7},{8,32},{9,33},{10,... | collective-permute-start | bytes 56 | tf_op jit(solution)/shard_map/ppermute | solution.py:38
  138.6 13.0 %collective-permute-done.9 = f32[2,2]{1,0:T(2,128)S(1)} collective-permute-done((f32[2,2]{1,0:T(2,128)S(1)}, f32[2,2]{1,0:T(2,128)S(1)}, u32[]{:S(2)}, u32[]{:S(2)}) %collective-permute-start.9) | collective-permute-done | bytes 48 | tf_op jit(solution)/shard_map/ppermute | solution.py:38
  152.3 1.2 add.20
  153.4 1.3 negate_convert_fusion.3
  155.4 1.9 collective-permute-start.11
  157.3 2.7 %collective-permute-start.12 = (bf16[2,192,128]{2,1,0:T(8,128)(2,1)S(1)}, bf16[2,192,128]{2,1,0:T(8,128)(2,1)}, u32[]{:S(2)}, u32[]{:S(2)}) collective-permute-start(bf16[2,192,128]{2,1,0:T(8,128)(2,1)S(1)} %get-tuple-element.25), channel_id=1, source_target_pairs={{0,8},{1,9},{2,10},{3,11},{4,12},{5,13},{6,14},{7,15},{8,40},{9,41... | collective-permute-start | bytes 294920 | tf_op jit(solution)/shard_map/ppermute | solution.py:38
  160.0 5.3 %shard_map.28 = (f32[2,2,192,128]{3,2,1,0:T(8,128)}, f32[2,2,192,128]{3,2,1,0:T(8,128)S(1)}) custom-call(s32[5]{0:T(128)S(1)} %stack.44.place_ref, bf16[2,2,2,192,128]{4,3,2,1,0:T(8,128)(2,1)S(1)} %broadcast_select_fusion.2.m0, bf16[2,2,2,192,128]{4,3,2,1,0:T(8,128)(2,1)S(1)} %broadcast_select_fusion.1.m1, ...), custom_call_target="tpu_custom_call" | custom-call | flops 1610612736 | bytes 7340032 | tf_op jit(solution)/shard_map/pallas_call | solution.py:90
  166.8 4.0 %collective-permute-done.12 = bf16[2,192,128]{2,1,0:T(8,128)(2,1)} collective-permute-done((bf16[2,192,128]{2,1,0:T(8,128)(2,1)S(1)}, bf16[2,192,128]{2,1,0:T(8,128)(2,1)}, u32[]{:S(2)}, u32[]{:S(2)}) %collective-permute-start.12) | collective-permute-done | bytes 98336 | tf_op jit(solution)/shard_map/ppermute | solution.py:38
  171.8 15.2 %collective-permute-done.8 = f32[2,2,192,128]{3,2,1,0:T(8,128)S(1)} collective-permute-done((f32[2,2,192,128]{3,2,1,0:T(8,128)}, f32[2,2,192,128]{3,2,1,0:T(8,128)S(1)}, u32[]{:S(2)}, u32[]{:S(2)}) %collective-permute-start.8) | collective-permute-done | bytes 393248 | tf_op jit(solution)/shard_map/ppermute | solution.py:38
  188.0 1.3 negate_convert_fusion.1
  190.2 4.0 %collective-permute-start.14 = (bf16[2,192,128]{2,1,0:T(8,128)(2,1)S(1)}, bf16[2,192,128]{2,1,0:T(8,128)(2,1)S(1)}, u32[]{:S(2)}, u32[]{:S(2)}) collective-permute-start(bf16[2,192,128]{2,1,0:T(8,128)(2,1)S(1)} %get-tuple-element.30), channel_id=1, source_target_pairs={{0,10},{1,11},{2,8},{3,9},{4,14},{5,15},{6,12},{7,13},{8,42},{9,43... | collective-permute-start | bytes 294920 | tf_op jit(solution)/shard_map/ppermute | solution.py:38
  194.2 5.1 %collective-permute-done.13 = bf16[2,192,128]{2,1,0:T(8,128)(2,1)S(1)} collective-permute-done((bf16[2,192,128]{2,1,0:T(8,128)(2,1)S(1)}, bf16[2,192,128]{2,1,0:T(8,128)(2,1)S(1)}, u32[]{:S(2)}, u32[]{:S(2)}) %collective-permute-start.13) | collective-permute-done | bytes 98336 | tf_op jit(solution)/shard_map/ppermute | solution.py:38
  199.3 4.1 %collective-permute-done.14 = bf16[2,192,128]{2,1,0:T(8,128)(2,1)S(1)} collective-permute-done((bf16[2,192,128]{2,1,0:T(8,128)(2,1)S(1)}, bf16[2,192,128]{2,1,0:T(8,128)(2,1)S(1)}, u32[]{:S(2)}, u32[]{:S(2)}) %collective-permute-start.14) | collective-permute-done | bytes 98336 | tf_op jit(solution)/shard_map/ppermute | solution.py:38
  (36 shorter events, 10.0 us)
Async XLA Ops:
  0.0 5.7 %copy-start.2 = (bf16[2,16,512,128]{3,2,1,0:T(8,128)(2,1)S(1)}, bf16[2,16,512,128]{3,2,1,0:T(8,128)(2,1)}, u32[]{:S(2)}) copy-start(bf16[2,16,512,128]{3,2,1,0:T(8,128)(2,1)} %param.2) | copy-start | bytes 12582916
  2.2 3.5 %collective-permute-start = (bf16[2,16,192,128]{3,2,1,0:T(8,128)(2,1)S(1)}, bf16[2,16,192,128]{3,2,1,0:T(8,128)(2,1)S(1)}, u32[]{:S(2)}, u32[]{:S(2)}) collective-permute-start(bf16[2,16,192,128]{3,2,1,0:T(8,128)(2,1)S(1)} %slice_select_fusion), channel_id=1, source_target_pairs={{0,32},{32,0},{1,33},{33,1},{2,34},{34,2},{3,35},{35,3},{4,36},{36... | collective-permute-start | bytes 4718600 | tf_op jit(solution)/shard_map/ppermute | solution.py:42
  7.2 7.3 %slice-start = ((bf16[2,16,512,128]{3,2,1,0:T(8,128)(2,1)}), bf16[2,16,128,128]{3,2,1,0:T(8,128)(2,1)S(1)}, s32[]{:S(2)}) async-start(bf16[2,16,512,128]{3,2,1,0:T(8,128)(2,1)} %param.2), calls=%async_computation.2 | async-start | bytes 2097152 | tf_op jit(solution)/shard_map/slice | solution.py:119
  7.2 28.5 %all-to-all-start = ((bf16[16,2,192,128]{3,2,1,0:T(8,128)(2,1)}), bf16[16,2,192,128]{3,2,1,0:T(8,128)(2,1)}, u32[]{:S(2)}, u32[]{:S(2)}) async-start(bf16[16,2,192,128]{3,2,1,0:T(8,128)(2,1)} %bitcast.7), calls=%async_computation | async-start | bytes 3145728 | tf_op jit(solution)/shard_map/all_to_all | solution.py:125
  70.9 56.2 %collective-permute-start.7 = (bf16[16,2,320,128]{3,2,1,0:T(8,128)(2,1)S(1)}, bf16[16,2,320,128]{3,2,1,0:T(8,128)(2,1)}, u32[]{:S(2)}, u32[]{:S(2)}) collective-permute-start(bf16[16,2,320,128]{3,2,1,0:T(8,128)(2,1)S(1)} %all_to_all.10.bo_ref), channel_id=1, source_target_pairs={{0,32},{32,0},{1,33},{33,1},{2,34},{34,2},{3,35},{35,3},{4,36},{36... | collective-permute-start | bytes 7864328 | tf_op jit(solution)/shard_map/ppermute | solution.py:42
  70.9 56.2 %collective-permute-start.6 = (bf16[16,2,192,128]{3,2,1,0:T(8,128)(2,1)}, bf16[16,2,192,128]{3,2,1,0:T(8,128)(2,1)}, u32[]{:S(2)}, u32[]{:S(2)}) collective-permute-start(bf16[16,2,192,128]{3,2,1,0:T(8,128)(2,1)} %all-to-all-done.ao_ref), channel_id=1, source_target_pairs={{0,32},{32,0},{1,33},{33,1},{2,34},{34,2},{3,35},{35,3},{4,36},{36... | collective-permute-start | bytes 4718600 | tf_op jit(solution)/shard_map/ppermute | solution.py:42
  72.6 32.7 %collective-permute-start.3 = (bf16[2,2,2,192,128]{4,3,2,1,0:T(8,128)(2,1)S(1)}, bf16[2,2,2,192,128]{4,3,2,1,0:T(8,128)(2,1)}, u32[]{:S(2)}, u32[]{:S(2)}) collective-permute-start(bf16[2,2,2,192,128]{4,3,2,1,0:T(8,128)(2,1)S(1)} %get-tuple-element.32), channel_id=1, source_target_pairs={{0,129},{1,128},{2,131},{3,130},{4,133},{5,132},{6,135},{7,134},{8... | collective-permute-start | bytes 1179656 | tf_op jit(solution)/shard_map/ppermute | solution.py:38
  80.6 24.6 %collective-permute-start.2 = (bf16[2,2,2,192,128]{4,3,2,1,0:T(8,128)(2,1)S(1)}, bf16[2,2,2,192,128]{4,3,2,1,0:T(8,128)(2,1)}, u32[]{:S(2)}, u32[]{:S(2)}) collective-permute-start(bf16[2,2,2,192,128]{4,3,2,1,0:T(8,128)(2,1)S(1)} %get-tuple-element.31), channel_id=1, source_target_pairs={{0,1},{1,0},{2,3},{3,2},{4,5},{5,4},{6,7},{7,6},{8,9},{9,8},{10,11... | collective-permute-start | bytes 1179656 | tf_op jit(solution)/shard_map/ppermute | solution.py:38
  84.0 25.3 %collective-permute-start.1 = (bf16[2,2,2,192,128]{4,3,2,1,0:T(8,128)(2,1)S(1)}, bf16[2,2,2,192,128]{4,3,2,1,0:T(8,128)(2,1)}, u32[]{:S(2)}, u32[]{:S(2)}) collective-permute-start(bf16[2,2,2,192,128]{4,3,2,1,0:T(8,128)(2,1)S(1)} %get-tuple-element.32), channel_id=1, source_target_pairs={{0,128},{1,129},{2,130},{3,131},{4,132},{5,133},{6,134},{7,135},{8... | collective-permute-start | bytes 1179656 | tf_op jit(solution)/shard_map/ppermute | solution.py:38
  106.3 13.7 %collective-permute-start.5 = (bf16[2,2,2,192,128]{4,3,2,1,0:T(8,128)(2,1)S(1)}, bf16[2,2,2,192,128]{4,3,2,1,0:T(8,128)(2,1)}, u32[]{:S(2)}, u32[]{:S(2)}) collective-permute-start(bf16[2,2,2,192,128]{4,3,2,1,0:T(8,128)(2,1)S(1)} %broadcast_select_fusion.1.m1), channel_id=1, source_target_pairs={{0,4},{4,0},{1,5},{5,1},{2,6},{6,2},{3,7},{7,3},{8,12},{12,8},{9,1... | collective-permute-start | bytes 1179656 | tf_op jit(solution)/shard_map/ppermute | solution.py:139
  110.3 16.7 %collective-permute-start.4 = (bf16[2,2,2,192,128]{4,3,2,1,0:T(8,128)(2,1)S(1)}, bf16[2,2,2,192,128]{4,3,2,1,0:T(8,128)(2,1)}, u32[]{:S(2)}, u32[]{:S(2)}) collective-permute-start(bf16[2,2,2,192,128]{4,3,2,1,0:T(8,128)(2,1)S(1)} %broadcast_select_fusion.2.m0), channel_id=1, source_target_pairs={{0,4},{4,0},{1,5},{5,1},{2,6},{6,2},{3,7},{7,3},{8,12},{12,8},{9,1... | collective-permute-start | bytes 1179656 | tf_op jit(solution)/shard_map/ppermute | solution.py:139
  111.1 24.6 %copy-start.3 = (f32[2,2]{1,0:T(2,128)S(1)}, f32[2,2]{1,0:T(2,128)}, u32[]{:S(2)}) copy-start(f32[2,2]{1,0:T(2,128)} %param.3) | copy-start | bytes 52
  132.4 0.8 copy-start.1
  133.1 19.1 %collective-permute-start.10 = (f32[2,2,192,128]{3,2,1,0:T(8,128)}, f32[2,2,192,128]{3,2,1,0:T(8,128)}, u32[]{:S(2)}, u32[]{:S(2)}) collective-permute-start(f32[2,2,192,128]{3,2,1,0:T(8,128)} %get-tuple-element.23), channel_id=1, source_target_pairs={{0,128},{1,129},{2,130},{3,131},{4,132},{5,133},{6,134},{7,135},{8... | collective-permute-start | bytes 1179656 | tf_op jit(solution)/shard_map/ppermute | solution.py:38
  135.7 15.9 %collective-permute-start.9 = (f32[2,2]{1,0:T(2,128)S(1)}, f32[2,2]{1,0:T(2,128)S(1)}, u32[]{:S(2)}, u32[]{:S(2)}) collective-permute-start(f32[2,2]{1,0:T(2,128)S(1)} %copy-done.3), channel_id=1, source_target_pairs={{0,0},{1,1},{2,2},{3,3},{4,4},{5,5},{6,6},{7,7},{8,32},{9,33},{10,... | collective-permute-start | bytes 56 | tf_op jit(solution)/shard_map/ppermute | solution.py:38
  155.4 11.4 %collective-permute-start.11 = (bf16[2,192,128]{2,1,0:T(8,128)(2,1)}, bf16[2,192,128]{2,1,0:T(8,128)(2,1)}, u32[]{:S(2)}, u32[]{:S(2)}) collective-permute-start(bf16[2,192,128]{2,1,0:T(8,128)(2,1)} %get-tuple-element.24), channel_id=1, source_target_pairs={{0,0},{1,1},{2,2},{3,3},{4,4},{5,5},{6,6},{7,7},{8,32},{9,33},{10,... | collective-permute-start | bytes 294920 | tf_op jit(solution)/shard_map/ppermute | solution.py:38
  157.3 13.6 %collective-permute-start.12 = (bf16[2,192,128]{2,1,0:T(8,128)(2,1)S(1)}, bf16[2,192,128]{2,1,0:T(8,128)(2,1)}, u32[]{:S(2)}, u32[]{:S(2)}) collective-permute-start(bf16[2,192,128]{2,1,0:T(8,128)(2,1)S(1)} %get-tuple-element.25), channel_id=1, source_target_pairs={{0,8},{1,9},{2,10},{3,11},{4,12},{5,13},{6,14},{7,15},{8,40},{9,41... | collective-permute-start | bytes 294920 | tf_op jit(solution)/shard_map/ppermute | solution.py:38
  165.3 0.7 copy-start
  166.1 20.9 %collective-permute-start.8 = (f32[2,2,192,128]{3,2,1,0:T(8,128)}, f32[2,2,192,128]{3,2,1,0:T(8,128)S(1)}, u32[]{:S(2)}, u32[]{:S(2)}) collective-permute-start(f32[2,2,192,128]{3,2,1,0:T(8,128)} %get-tuple-element.20), channel_id=1, source_target_pairs={{0,128},{1,129},{2,130},{3,131},{4,132},{5,133},{6,134},{7,135},{8... | collective-permute-start | bytes 1179656 | tf_op jit(solution)/shard_map/ppermute | solution.py:38
  189.4 10.0 %collective-permute-start.13 = (bf16[2,192,128]{2,1,0:T(8,128)(2,1)S(1)}, bf16[2,192,128]{2,1,0:T(8,128)(2,1)S(1)}, u32[]{:S(2)}, u32[]{:S(2)}) collective-permute-start(bf16[2,192,128]{2,1,0:T(8,128)(2,1)S(1)} %get-tuple-element.29), channel_id=1, source_target_pairs={{0,2},{1,3},{2,0},{3,1},{4,6},{5,7},{6,4},{7,5},{8,34},{9,35},{10,... | collective-permute-start | bytes 294920 | tf_op jit(solution)/shard_map/ppermute | solution.py:38
  190.2 13.2 %collective-permute-start.14 = (bf16[2,192,128]{2,1,0:T(8,128)(2,1)S(1)}, bf16[2,192,128]{2,1,0:T(8,128)(2,1)S(1)}, u32[]{:S(2)}, u32[]{:S(2)}) collective-permute-start(bf16[2,192,128]{2,1,0:T(8,128)(2,1)S(1)} %get-tuple-element.30), channel_id=1, source_target_pairs={{0,10},{1,11},{2,8},{3,9},{4,14},{5,15},{6,12},{7,13},{8,42},{9,43... | collective-permute-start | bytes 294920 | tf_op jit(solution)/shard_map/ppermute | solution.py:38

commit v5 on v3

v5 whole, which is shorter than its diff:
```python
import jax
import jax.numpy as jnp
from jax import lax
from jax.experimental import pallas as pl
from jax.experimental.pallas import tpu as pltpu
from jax.sharding import Mesh, PartitionSpec as P


NOUT = 384
AXES = ("zq", "zr", "core", "x", "y", "zh")
SIZES = (2, 2, 2, 4, 4, 2)


def coordinates():
    out = [()]
    for size in SIZES:
        out = [c + (i,) for c in out for i in range(size)]
    return out


def flat(c):
    index = 0
    for i, size in zip(c, SIZES):
        index = index * size + i
    return index


def moved(target):
    pairs = []
    for c in coordinates():
        t = target(*c)
        if t is not None:
            pairs.append((flat(c), flat(t)))
    return pairs


def send(value, target):
    return lax.ppermute(value, AXES, moved(target))


def swap_core(value):
    return lax.ppermute(value, "core", [(0, 1), (1, 0)])


def contract(g, place, turned, a_own, a_peer, b_own, b_peer):
    half, lanes = turned[0].shape[-2:]
    depth = 16 * lanes

    def kernel(place_ref, u0, u1, u2, u3, ao_ref, ap_ref, bo_ref, bp_ref, o0, o1, o2, o3, left):
        core, zh, zq, y = place_ref[0], place_ref[1], place_ref[2], place_ref[3]
        for step, u_ref in enumerate((u0, u1, u2, u3)):
            ys = (y + 4 - step) % 4
            for xl in range(2):
                for piece in range(2):
                    start = pl.multiple_of(((xl * 4 + ys) * 2 + (piece ^ zh)) * lanes, lanes)
                    for part in range(2):
                        left[part * half : (part + 1) * half, pl.ds(start, lanes)] = u_ref[piece, xl, part]

        first = core == 0
        for t, out in enumerate((o0, o1, o2, o3)):
            x = (2 * zq + core) ^ t
            rows = []
            for zr in range(2):
                i = 2 * x + zr
                parts = []
                for part in range(2):
                    ao, ap = ao_ref[i, g, part], ap_ref[i, g, part]
                    bo, bp = bo_ref[i, part], bp_ref[i, part]
                    parts.append(
                        jnp.concatenate(
                            [
                                jnp.where(first, ao, ap),
                                jnp.where(first, ap, ao),
                                jnp.where(first, bo, bp),
                                jnp.where(first, bp, bo),
                            ],
                            0,
                        )
                    )
                rows.append(jnp.concatenate(parts, 1))
            right = jnp.concatenate(rows, 0)
            both = jnp.dot(left[...], right, preferred_element_type=jnp.float32)
            out[0] = both[:half, :lanes] - both[half:, lanes:]
            out[1] = both[:half, lanes:] + both[half:, :lanes]

    vmem = pl.BlockSpec(memory_space=pltpu.VMEM)
    result = jax.ShapeDtypeStruct((2, half, lanes), jnp.float32)
    return pl.pallas_call(
        kernel,
        out_shape=(result,) * 4,
        in_specs=[pl.BlockSpec(memory_space=pltpu.SMEM)] + [vmem] * 8,
        out_specs=(vmem,) * 4,
        scratch_shapes=[pltpu.VMEM((2 * half, depth), jnp.bfloat16)],
        cost_estimate=pl.CostEstimate(
            flops=2 * 2 * half * depth * 8 * lanes, bytes_accessed=7 << 20, transcendentals=0
        ),
        compiler_params=pltpu.CompilerParams(vmem_limit_bytes=40 << 20),
    )(place, *turned, a_own, a_peer, b_own, b_peer)


def step(spectra, wavelet):
    zq, core, x = lax.axis_index("zq"), lax.axis_index("core"), lax.axis_index("x")
    y, zh = lax.axis_index("y"), lax.axis_index("zh")
    place = jnp.stack([core, zh, zq, y]).astype(jnp.int32)
    rows, _ = spectra.shape[2:]
    window = NOUT * rows // 512
    half = window // 2
    first = core == 0

    def ordered(block):
        return block.reshape((2, 2, 2, 2, 2) + block.shape[2:])

    passed = swap_core(lax.dynamic_slice_in_dim(spectra, (1 - core) * half, half, 2))
    a = ordered(jnp.where(first, spectra[:, :, :half], passed)).transpose(1, 3, 2, 4, 0, 5, 6)
    a = a.reshape((8, 2, 2) + a.shape[5:])
    b = jnp.where(first, jnp.concatenate([spectra[:, :, window:], passed], 2), spectra[:, :, half:])
    b = [ordered(b)[:, :, :, :, g].transpose(1, 3, 2, 0, 4, 5) for g in range(2)]
    b = [b[g].reshape((8, 2) + b[g].shape[4:]) for g in range(2)]
    b = lax.optimization_barrier(b)

    def exchange(block):
        return lax.all_to_all(block, ("x", "zr"), split_axis=0, concat_axis=0, tiled=True)

    a_own = exchange(a)
    a_own, *b = lax.optimization_barrier((a_own, *b))
    a_peer = swap_core(a_own)
    b_own, b_peer = [], []
    for g in range(2):
        b_own.append(exchange(b[g]))
        b_peer.append(swap_core(b_own[g]))

    shots = a_own.reshape((4, 2) + a_own.shape[1:])[:, 0]
    near, far = shots[:2], shots[2:]
    near, far = lax.optimization_barrier((near, far))
    across = send(near, lambda q, r, c, x, y, h: (0, r, c, x, y, 1 - h) if q == 0 else None)
    up = send(far, lambda q, r, c, x, y, h: (1, r, c, x, y, h) if q == 0 else None)
    down = send(far, lambda q, r, c, x, y, h: (1, r, c, x, y, 1 - h) if q == 0 else None)
    mine, others = jnp.where(zq == 0, near, up), jnp.where(zq == 0, across, down)
    pieces = [jnp.stack([mine[:, g], others[:, g]]) for g in range(2)]

    def turn(g):
        plus, minus, two = (
            lax.ppermute(pieces[g], "y", [(i, (i + s) % 4) for i in range(4)]) for s in (1, 3, 2)
        )
        return pieces[g], plus, two, minus

    turned = [turn(g) for g in range(2)]

    def homeward(blocks):
        return [
            send(
                block,
                lambda q, r, c, x, y, h: (x // 2, r, x % 2, (2 * q + c) ^ t, y, h),
            )
            for t, block in enumerate(blocks)
        ]

    def finish(g, blocks):
        pair = [blocks[0] + blocks[2], blocks[1] + blocks[3]]
        pair = [
            jnp.stack(
                [
                    -(wavelet[0, g] * p[0] - wavelet[1, g] * p[1]),
                    -(wavelet[0, g] * p[1] + wavelet[1, g] * p[0]),
                ]
            ).astype(jnp.bfloat16)
            for p in pair
        ]
        even = x % 2 == 0
        return jnp.concatenate(
            [jnp.where(even, pair[0], pair[1]), jnp.where(even, pair[1], pair[0])], 1
        )

    blocks = []
    for g in range(2):
        partial = contract(g, place, turned[g], a_own, a_peer, b_own[g], b_peer[g])
        blocks.append(homeward(partial))
    early = finish(0, blocks[0])
    late, early = lax.optimization_barrier((blocks[1], early))
    return jnp.stack([early, finish(1, late)], 1)


def solution(mesh):
    fine = Mesh(mesh.devices.reshape(SIZES), AXES)
    freq, col = AXES[:3], AXES[3:]
    return jax.shard_map(
        step,
        mesh=fine,
        in_specs=(P(None, None, freq, col), P(None, freq)),
        out_specs=P(None, freq, None, col),
        check_vma=False,
    )
```

time: 200 us -> 226 us (1.13)
  waiting for transfers between devices: 73.4 us -> 105 us
  starting transfers between devices: 67.9 us -> 57.4 us
  local copies, waits for them, and re-layouts: 12 us -> 17.6 us
    ppermute x13 -> x11, waiting for transfers between devices: 41.3 us -> 73 us  [send(): return lax.ppermute(value, AXES, moved(target))]
    ppermute x13 -> x11, starting transfers between devices: 43.8 us -> 24.4 us  [send(): return lax.ppermute(value, AXES, moved(target))]
    ppermute x6, starting transfers between devices: 11 us -> 19.6 us  [turn(): lax.ppermute(pieces[g], 'y', [(i, (i + s) % 4) for i in range(4)])]
    unnamed x14 -> x28, local copies, waits for them, and re-layouts: 2.53 us -> 10.2 us
    squeeze x1 -> x0, local copies, waits for them, and re-layouts: 3.03 us -> none  [step(): b_own.append(exchange(b[g]))]
    another operation x9 -> x8, other arithmetic: 5.49 us -> 6.24 us  [the longest x4 2.77 us: step(): jnp.stack([jnp.where(zq == 0, near, up), jnp.where(zq == 0, across, down)])]
    select_n x7 -> x6, other arithmetic: 5.17 us -> 5.39 us  [the longest x1 2.68 us: step(): jnp.where(first, jnp.concatenate([spectra[:, :, window:], passed], 2), sp...]
  transfers between devices with their start and end apart: 25 -> 23, of which waited for: 11 -> 12; matrix products, arithmetic and copies ran while one was open for 6% -> 6% of each run, Pallas kernels for 5% -> 4%
where the time goes in v5:
time: 226 us; the launch traced here: 223 us
  waiting for transfers between devices  105 us (46%)
  starting transfers between devices  57.4 us (25%)
  blocking collectives  21.5 us (10%)
  local copies, waits for them, and re-layouts  17.6 us (8%)
  other arithmetic  12.8 us (6%)
  Pallas kernels  8.78 us (4%)
    ppermute x11, waiting for transfers between devices, send(): return lax.ppermute(value, AXES, moved(target))  73 us
    ppermute x11, starting transfers between devices, send(): return lax.ppermute(value, AXES, moved(target))  24.4 us
    all_to_all x1, blocking collectives, exchange(): lax.all_to_all(block, ('x', 'zr'), split_axis=0, concat_axis=0, tiled=True)  21.5 us
    ppermute x6, starting transfers between devices, turn(): lax.ppermute(pieces[g], 'y', [(i, (i + s) % 4) for i in range(4)])  19.6 us
    ppermute x6, waiting for transfers between devices, turn(): lax.ppermute(pieces[g], 'y', [(i, (i + s) % 4) for i in range(4)])  14.7 us
    all_to_all x2, waiting for transfers between devices, exchange(): lax.all_to_all(block, ('x', 'zr'), split_axis=0, concat_axis=0, tiled=True)  13.6 us
    all_to_all x2, starting transfers between devices, exchange(): lax.all_to_all(block, ('x', 'zr'), split_axis=0, concat_axis=0, tiled=True)  12.7 us
    unnamed x28, local copies, waits for them, and re-layouts  10.2 us
  transfers between devices with their start and end apart: 23, of which 12 were waited for; matrix products, arithmetic and copies ran while one was open for 6% of the time, Pallas kernels for 4%

profile of v5, /device:TPU:4, one launch (start us, length us, event | category | flops | bytes accessed | tf_op | source)
XLA Modules:
  0.0 223.1 jit_solution(7515899496247900330)
XLA Ops:
  0.0 1.5 constant_dynamic-slice_fusion
  1.6 3.4 %collective-permute-done = bf16[2,16,192,128]{3,2,1,0:T(8,128)(2,1)S(1)} collective-permute-done((bf16[2,16,192,128]{3,2,1,0:T(8,128)(2,1)S(1)}, bf16[2,16,192,128]{3,2,1,0:T(8,128)(2,1)S(1)}, u32[]{:S(2)}, u32[]{:S(2)}) %collective-permute-start) | collective-permute-done | bytes 1572896 | tf_op jit(solution)/shard_map/ppermute | solution.py:42
  5.0 1.6 slice_select_fusion
  6.6 1.3 copy.3
  7.9 6.2 %all-to-all-start = ((bf16[8,2,2,192,128]{4,3,2,1,0:T(8,128)(2,1)}), bf16[8,2,2,192,128]{4,3,2,1,0:T(8,128)(2,1)S(1)}, u32[]{:S(2)}, u32[]{:S(2)}) async-start(bf16[8,2,2,192,128]{4,3,2,1,0:T(8,128)(2,1)} %bitcast.6), calls=%async_computation | async-start | bytes 3145728 | tf_op jit(solution)/shard_map/all_to_all | solution.py:122
  15.3 2.7 %maximum_select_fusion = bf16[2,16,320,128]{3,2,1,0:T(8,128)(2,1)S(1)} fusion(bf16[2,16,192,128]{3,2,1,0:T(8,128)(2,1)S(1)} %collective-permute-done, bf16[2,16,128,128]{3,2,1,0:T(8,128)(2,1)S(1)} %slice-done, bf16[2,16,512,128]{3,2,1,0:T(8,128)(2,1)} %param.2, pred[]{:T(512)S(6)} %eq.15), kind=kLoop, calls=%fused_computation | loop fusion | flops 6553600 | bytes 7864321 | tf_op jit(solution)/shard_map/jit(_where)/select_n | solution.py:116
  19.5 13.6 %all-to-all-done.ao_ref = bf16[8,2,2,192,128]{4,3,2,1,0:T(8,128)(2,1)S(1)} async-done(((bf16[8,2,2,192,128]{4,3,2,1,0:T(8,128)(2,1)}), bf16[8,2,2,192,128]{4,3,2,1,0:T(8,128)(2,1)S(1)}, u32[]{:S(2)}, u32[]{:S(2)}) %all-to-all-start) | async-done | bytes 1572896 | tf_op jit(solution)/shard_map/all_to_all | solution.py:122
  33.1 21.5 %all_to_all.15.bo_ref = bf16[8,2,320,128]{3,2,1,0:T(8,128)(2,1)} all-to-all(bf16[8,2,320,128]{3,2,1,0:T(8,128)(2,1)S(1)} %bitcast.42), channel_id=1, replica_groups=mesh['zq'=2,'zr'=2,'core'=2,'x'=4,'y'=4,'zh'=2] {'x','zr'}, dimensions={0} | all-to-all | bytes 2621440 | tf_op jit(solution)/shard_map/all_to_all | solution.py:122
  54.6 6.6 %all-to-all-start.1 = ((bf16[8,2,320,128]{3,2,1,0:T(8,128)(2,1)}), bf16[8,2,320,128]{3,2,1,0:T(8,128)(2,1)}, u32[]{:S(2)}, u32[]{:S(2)}) async-start(bf16[8,2,320,128]{3,2,1,0:T(8,128)(2,1)} %bitcast.13), calls=%async_computation.1 | async-start | bytes 2621440 | tf_op jit(solution)/shard_map/all_to_all | solution.py:122
  62.0 5.9 %collective-permute-start.1 = (bf16[2,2,2,192,128]{4,3,2,0,1:T(8,128)(2,1)}, bf16[2,2,2,192,128]{4,3,2,0,1:T(8,128)(2,1)}, u32[]{:S(2)}, u32[]{:S(2)}) collective-permute-start(bf16[2,2,2,192,128]{4,3,2,0,1:T(8,128)(2,1)} %get-tuple-element.29), channel_id=1, source_target_pairs={{0,128},{1,129},{2,130},{3,131},{4,132},{5,133},{6,134},{7,135},{8... | collective-permute-start | bytes 1179656 | tf_op jit(solution)/shard_map/ppermute | solution.py:38
  68.0 6.4 %collective-permute-start.2 = (bf16[2,2,2,192,128]{4,3,2,0,1:T(8,128)(2,1)S(1)}, bf16[2,2,2,192,128]{4,3,2,0,1:T(8,128)(2,1)}, u32[]{:S(2)}, u32[]{:S(2)}) collective-permute-start(bf16[2,2,2,192,128]{4,3,2,0,1:T(8,128)(2,1)S(1)} %get-tuple-element.28), channel_id=1, source_target_pairs={{0,1},{1,0},{2,3},{3,2},{4,5},{5,4},{6,7},{7,6},{8,9},{9,8},{10,11... | collective-permute-start | bytes 1179656 | tf_op jit(solution)/shard_map/ppermute | solution.py:38
  74.4 2.0 collective-permute-start.3
  76.4 8.7 %collective-permute-done.1 = bf16[2,2,2,192,128]{4,3,2,0,1:T(8,128)(2,1)} collective-permute-done((bf16[2,2,2,192,128]{4,3,2,0,1:T(8,128)(2,1)}, bf16[2,2,2,192,128]{4,3,2,0,1:T(8,128)(2,1)}, u32[]{:S(2)}, u32[]{:S(2)}) %collective-permute-start.1) | collective-permute-done | bytes 393248 | tf_op jit(solution)/shard_map/ppermute | solution.py:38
  85.1 12.4 %collective-permute-done.2 = bf16[2,2,2,192,128]{4,3,2,0,1:T(8,128)(2,1)} collective-permute-done((bf16[2,2,2,192,128]{4,3,2,0,1:T(8,128)(2,1)S(1)}, bf16[2,2,2,192,128]{4,3,2,0,1:T(8,128)(2,1)}, u32[]{:S(2)}, u32[]{:S(2)}) %collective-permute-start.2) | collective-permute-done | bytes 393248 | tf_op jit(solution)/shard_map/ppermute | solution.py:38
  102.2 1.7 collective-permute-start.13
  103.9 2.9 %collective-permute-start.14 = (bf16[2,2,2,192,128]{4,3,2,1,0:T(8,128)(2,1)S(1)}, bf16[2,2,2,192,128]{4,3,2,1,0:T(8,128)(2,1)S(1)}, u32[]{:S(2)}, u32[]{:S(2)}) collective-permute-start(bf16[2,2,2,192,128]{4,3,2,1,0:T(8,128)(2,1)S(1)} %pad_maximum_fusion.1.u0), channel_id=1, source_target_pairs={{0,4},{2,6},{4,0},{6,2},{1,5},{3,7},{5,1},{7,3},{8,12},{10,14},{12... | collective-permute-start | bytes 1179656 | tf_op jit(solution)/shard_map/ppermute | solution.py:143
  106.8 7.9 %collective-permute-done.13.u1 = bf16[2,2,2,192,128]{4,3,2,1,0:T(8,128)(2,1)S(1)} collective-permute-done((bf16[2,2,2,192,128]{4,3,2,1,0:T(8,128)(2,1)S(1)}, bf16[2,2,2,192,128]{4,3,2,1,0:T(8,128)(2,1)S(1)}, u32[]{:S(2)}, u32[]{:S(2)}) %collective-permute-start.13) | collective-permute-done | bytes 393248 | tf_op jit(solution)/shard_map/ppermute | solution.py:143
  115.4 2.7 %collective-permute-start.15 = (bf16[2,2,2,192,128]{4,3,2,1,0:T(8,128)(2,1)S(1)}, bf16[2,2,2,192,128]{4,3,2,1,0:T(8,128)(2,1)S(1)}, u32[]{:S(2)}, u32[]{:S(2)}) collective-permute-start(bf16[2,2,2,192,128]{4,3,2,1,0:T(8,128)(2,1)S(1)} %pad_maximum_fusion.1.u0), channel_id=1, source_target_pairs={{0,6},{2,0},{4,2},{6,4},{1,7},{3,1},{5,3},{7,5},{8,14},{10,8},{12,... | collective-permute-start | bytes 1179656 | tf_op jit(solution)/shard_map/ppermute | solution.py:143
  118.1 6.1 %collective-permute-done.14.u2 = bf16[2,2,2,192,128]{4,3,2,1,0:T(8,128)(2,1)S(1)} collective-permute-done((bf16[2,2,2,192,128]{4,3,2,1,0:T(8,128)(2,1)S(1)}, bf16[2,2,2,192,128]{4,3,2,1,0:T(8,128)(2,1)S(1)}, u32[]{:S(2)}, u32[]{:S(2)}) %collective-permute-start.14) | collective-permute-done | bytes 393248 | tf_op jit(solution)/shard_map/ppermute | solution.py:143
  126.5 11.1 %collective-permute-start.5 = (bf16[2,2,2,192,128]{4,3,2,1,0:T(8,128)(2,1)S(1)}, bf16[2,2,2,192,128]{4,3,2,1,0:T(8,128)(2,1)}, u32[]{:S(2)}, u32[]{:S(2)}) collective-permute-start(bf16[2,2,2,192,128]{4,3,2,1,0:T(8,128)(2,1)S(1)} %pad_maximum_fusion.u0), channel_id=1, source_target_pairs={{0,4},{2,6},{4,0},{6,2},{1,5},{3,7},{5,1},{7,3},{8,12},{10,14},{12... | collective-permute-start | bytes 1179656 | tf_op jit(solution)/shard_map/ppermute | solution.py:143
  139.0 1.3 copy-done
  144.3 4.4 %shard_map.29 = (f32[2,192,128]{2,1,0:T(8,128)}, f32[2,192,128]{2,1,0:T(8,128)S(1)}, f32[2,192,128]{2,1,0:T(8,128)}, f32[2,192,128]{2,1,0:T(8,128)S(1)}) custom-call(s32[4]{0:T(128)S(1)} %pad_add_fusion.place_ref, bf16[2,2,2,192,128]{4,3,2,1,0:T(8,128)(2,1)S(1)} %copy-done.2, bf16[2,2,2,192,128]{4,3,2,1,0:T(8,128)(2,1)S(1)} %copy-done.4, ...), custom_call_target="tpu_custom_call" | custom-call | flops 1610612736 | bytes 7340032 | tf_op jit(solution)/shard_map/pallas_call | solution.py:88
  150.0 4.5 %collective-permute-start.17 = (f32[2,192,128]{2,1,0:T(8,128)}, f32[2,192,128]{2,1,0:T(8,128)}, u32[]{:S(2)}, u32[]{:S(2)}) collective-permute-start(f32[2,192,128]{2,1,0:T(8,128)} %get-tuple-element.36), channel_id=1, source_target_pairs={{0,0},{1,1},{2,2},{3,3},{4,4},{5,5},{6,6},{7,7},{8,32},{9,33},{10,... | collective-permute-start | bytes 589832 | tf_op jit(solution)/shard_map/ppermute | solution.py:38
  156.8 1.9 collective-permute-start.20
  158.7 4.4 %shard_map.28 = (f32[2,192,128]{2,1,0:T(8,128)S(1)}, f32[2,192,128]{2,1,0:T(8,128)S(1)}, f32[2,192,128]{2,1,0:T(8,128)S(1)}, f32[2,192,128]{2,1,0:T(8,128)S(1)}) custom-call(s32[4]{0:T(128)S(1)} %pad_add_fusion.place_ref, bf16[2,2,2,192,128]{4,3,2,1,0:T(8,128)(2,1)S(1)} %pad_maximum_fusion.u0, bf16[2,2,2,192,128]{4,3,2,1,0:T(8,128)(2,1)} %collective-permute-done.4.u1, ...), custom_call_target="tpu_custom_call" | custom-call | flops 1610612736 | bytes 7340032 | tf_op jit(solution)/shard_map/pallas_call | solution.py:88
  163.2 17.7 %collective-permute-done.17 = f32[2,192,128]{2,1,0:T(8,128)} collective-permute-done((f32[2,192,128]{2,1,0:T(8,128)}, f32[2,192,128]{2,1,0:T(8,128)}, u32[]{:S(2)}, u32[]{:S(2)}) %collective-permute-start.17) | collective-permute-done | bytes 196640 | tf_op jit(solution)/shard_map/ppermute | solution.py:38
  183.2 13.2 %collective-permute-done.19 = f32[2,192,128]{2,1,0:T(8,128)S(1)} collective-permute-done((f32[2,192,128]{2,1,0:T(8,128)}, f32[2,192,128]{2,1,0:T(8,128)S(1)}, u32[]{:S(2)}, u32[]{:S(2)}) %collective-permute-start.19) | collective-permute-done | bytes 196640 | tf_op jit(solution)/shard_map/ppermute | solution.py:38
  196.4 1.9 collective-permute-start.9
  199.7 7.1 %collective-permute-done.10 = f32[2,192,128]{2,1,0:T(8,128)S(1)} collective-permute-done((f32[2,192,128]{2,1,0:T(8,128)S(1)}, f32[2,192,128]{2,1,0:T(8,128)S(1)}, u32[]{:S(2)}, u32[]{:S(2)}) %collective-permute-start.10) | collective-permute-done | bytes 196640 | tf_op jit(solution)/shard_map/ppermute | solution.py:38
  206.9 12.7 %collective-permute-done.9 = f32[2,192,128]{2,1,0:T(8,128)S(1)} collective-permute-done((f32[2,192,128]{2,1,0:T(8,128)S(1)}, f32[2,192,128]{2,1,0:T(8,128)S(1)}, u32[]{:S(2)}, u32[]{:S(2)}) %collective-permute-start.9) | collective-permute-done | bytes 196640 | tf_op jit(solution)/shard_map/ppermute | solution.py:38
  219.6 1.3 negate_convert_fusion.3
  220.9 1.3 negate_convert_fusion.1
  (76 shorter events, 25.0 us)
Async XLA Ops:
  1.5 3.5 %collective-permute-start = (bf16[2,16,192,128]{3,2,1,0:T(8,128)(2,1)S(1)}, bf16[2,16,192,128]{3,2,1,0:T(8,128)(2,1)S(1)}, u32[]{:S(2)}, u32[]{:S(2)}) collective-permute-start(bf16[2,16,192,128]{3,2,1,0:T(8,128)(2,1)S(1)} %constant_dynamic-slice_fusion), channel_id=1, source_target_pairs={{0,32},{32,0},{1,33},{33,1},{2,34},{34,2},{3,35},{35,3},{4,36},{36... | collective-permute-start | bytes 4718600 | tf_op jit(solution)/shard_map/ppermute | solution.py:42
  7.9 25.1 %all-to-all-start = ((bf16[8,2,2,192,128]{4,3,2,1,0:T(8,128)(2,1)}), bf16[8,2,2,192,128]{4,3,2,1,0:T(8,128)(2,1)S(1)}, u32[]{:S(2)}, u32[]{:S(2)}) async-start(bf16[8,2,2,192,128]{4,3,2,1,0:T(8,128)(2,1)} %bitcast.6), calls=%async_computation | async-start | bytes 3145728 | tf_op jit(solution)/shard_map/all_to_all | solution.py:122
  14.1 1.2 slice-start
  54.6 46.1 %all-to-all-start.1 = ((bf16[8,2,320,128]{3,2,1,0:T(8,128)(2,1)}), bf16[8,2,320,128]{3,2,1,0:T(8,128)(2,1)}, u32[]{:S(2)}, u32[]{:S(2)}) async-start(bf16[8,2,320,128]{3,2,1,0:T(8,128)(2,1)} %bitcast.13), calls=%async_computation.1 | async-start | bytes 2621440 | tf_op jit(solution)/shard_map/all_to_all | solution.py:122
  62.0 23.1 %collective-permute-start.1 = (bf16[2,2,2,192,128]{4,3,2,0,1:T(8,128)(2,1)}, bf16[2,2,2,192,128]{4,3,2,0,1:T(8,128)(2,1)}, u32[]{:S(2)}, u32[]{:S(2)}) collective-permute-start(bf16[2,2,2,192,128]{4,3,2,0,1:T(8,128)(2,1)} %get-tuple-element.29), channel_id=1, source_target_pairs={{0,128},{1,129},{2,130},{3,131},{4,132},{5,133},{6,134},{7,135},{8... | collective-permute-start | bytes 1179656 | tf_op jit(solution)/shard_map/ppermute | solution.py:38
  68.0 29.6 %collective-permute-start.2 = (bf16[2,2,2,192,128]{4,3,2,0,1:T(8,128)(2,1)S(1)}, bf16[2,2,2,192,128]{4,3,2,0,1:T(8,128)(2,1)}, u32[]{:S(2)}, u32[]{:S(2)}) collective-permute-start(bf16[2,2,2,192,128]{4,3,2,0,1:T(8,128)(2,1)S(1)} %get-tuple-element.28), channel_id=1, source_target_pairs={{0,1},{1,0},{2,3},{3,2},{4,5},{5,4},{6,7},{7,6},{8,9},{9,8},{10,11... | collective-permute-start | bytes 1179656 | tf_op jit(solution)/shard_map/ppermute | solution.py:38
  74.4 24.4 %collective-permute-start.3 = (bf16[2,2,2,192,128]{4,3,2,0,1:T(8,128)(2,1)}, bf16[2,2,2,192,128]{4,3,2,0,1:T(8,128)(2,1)}, u32[]{:S(2)}, u32[]{:S(2)}) collective-permute-start(bf16[2,2,2,192,128]{4,3,2,0,1:T(8,128)(2,1)} %get-tuple-element.29), channel_id=1, source_target_pairs={{0,129},{1,128},{2,131},{3,130},{4,133},{5,132},{6,135},{7,134},{8... | collective-permute-start | bytes 1179656 | tf_op jit(solution)/shard_map/ppermute | solution.py:38
  76.4 61.2 %collective-permute-start.7 = (bf16[8,2,2,192,128]{4,3,2,1,0:T(8,128)(2,1)S(1)}, bf16[8,2,2,192,128]{4,3,2,1,0:T(8,128)(2,1)S(1)}, u32[]{:S(2)}, u32[]{:S(2)}) collective-permute-start(bf16[8,2,2,192,128]{4,3,2,1,0:T(8,128)(2,1)S(1)} %all-to-all-done.ao_ref), channel_id=1, source_target_pairs={{0,32},{32,0},{1,33},{33,1},{2,34},{34,2},{3,35},{35,3},{4,36},{36... | collective-permute-start | bytes 4718600 | tf_op jit(solution)/shard_map/ppermute | solution.py:42
  99.9 39.1 %collective-permute-start.16 = (bf16[8,2,320,128]{3,2,1,0:T(8,128)(2,1)}, bf16[8,2,320,128]{3,2,1,0:T(8,128)(2,1)}, u32[]{:S(2)}, u32[]{:S(2)}) collective-permute-start(bf16[8,2,320,128]{3,2,1,0:T(8,128)(2,1)} %all_to_all.15.bo_ref), channel_id=1, source_target_pairs={{0,32},{32,0},{1,33},{33,1},{2,34},{34,2},{3,35},{35,3},{4,36},{36... | collective-permute-start | bytes 3932168 | tf_op jit(solution)/shard_map/ppermute | solution.py:42
  100.7 17.4 %copy-start.11 = (bf16[1,2,2,192,128]{4,3,2,1,0:T(8,128)(2,1)S(1)}, bf16[1,2,2,192,128]{4,3,2,1,0:T(8,128)(2,1)}, u32[]{:S(2)}) copy-start(bf16[1,2,2,192,128]{4,3,2,1,0:T(8,128)(2,1)} %get-tuple-element.50) | copy-start | bytes 589828
  100.7 58.0 %collective-permute-start.8 = (bf16[8,2,320,128]{3,2,1,0:T(8,128)(2,1)}, bf16[8,2,320,128]{3,2,1,0:T(8,128)(2,1)}, u32[]{:S(2)}, u32[]{:S(2)}) collective-permute-start(bf16[8,2,320,128]{3,2,1,0:T(8,128)(2,1)} %all-to-all-done.1.bo_ref), channel_id=1, source_target_pairs={{0,32},{32,0},{1,33},{33,1},{2,34},{34,2},{3,35},{35,3},{4,36},{36... | collective-permute-start | bytes 3932168 | tf_op jit(solution)/shard_map/ppermute | solution.py:42
  102.2 35.4 %copy-start.1 = (bf16[2,2,2,192,128]{4,3,2,1,0:T(8,128)(2,1)}, bf16[2,2,2,192,128]{4,3,2,1,0:T(8,128)(2,1)S(1)}, u32[]{:S(2)}) copy-start(bf16[2,2,2,192,128]{4,3,2,1,0:T(8,128)(2,1)S(1)} %pad_maximum_fusion.1.u0) | copy-start | bytes 1179652
  102.2 12.4 %collective-permute-start.13 = (bf16[2,2,2,192,128]{4,3,2,1,0:T(8,128)(2,1)S(1)}, bf16[2,2,2,192,128]{4,3,2,1,0:T(8,128)(2,1)S(1)}, u32[]{:S(2)}, u32[]{:S(2)}) collective-permute-start(bf16[2,2,2,192,128]{4,3,2,1,0:T(8,128)(2,1)S(1)} %pad_maximum_fusion.1.u0), channel_id=1, source_target_pairs={{0,2},{2,4},{4,6},{6,0},{1,3},{3,5},{5,7},{7,1},{8,10},{10,12},{12... | collective-permute-start | bytes 1179656 | tf_op jit(solution)/shard_map/ppermute | solution.py:143
  103.9 20.4 %collective-permute-start.14 = (bf16[2,2,2,192,128]{4,3,2,1,0:T(8,128)(2,1)S(1)}, bf16[2,2,2,192,128]{4,3,2,1,0:T(8,128)(2,1)S(1)}, u32[]{:S(2)}, u32[]{:S(2)}) collective-permute-start(bf16[2,2,2,192,128]{4,3,2,1,0:T(8,128)(2,1)S(1)} %pad_maximum_fusion.1.u0), channel_id=1, source_target_pairs={{0,4},{2,6},{4,0},{6,2},{1,5},{3,7},{5,1},{7,3},{8,12},{10,14},{12... | collective-permute-start | bytes 1179656 | tf_op jit(solution)/shard_map/ppermute | solution.py:143
  115.4 10.3 %collective-permute-start.15 = (bf16[2,2,2,192,128]{4,3,2,1,0:T(8,128)(2,1)S(1)}, bf16[2,2,2,192,128]{4,3,2,1,0:T(8,128)(2,1)S(1)}, u32[]{:S(2)}, u32[]{:S(2)}) collective-permute-start(bf16[2,2,2,192,128]{4,3,2,1,0:T(8,128)(2,1)S(1)} %pad_maximum_fusion.1.u0), channel_id=1, source_target_pairs={{0,6},{2,0},{4,2},{6,4},{1,7},{3,1},{5,3},{7,5},{8,14},{10,8},{12,... | collective-permute-start | bytes 1179656 | tf_op jit(solution)/shard_map/ppermute | solution.py:143
  125.0 29.5 %collective-permute-start.4 = (bf16[2,2,2,192,128]{4,3,2,1,0:T(8,128)(2,1)S(1)}, bf16[2,2,2,192,128]{4,3,2,1,0:T(8,128)(2,1)}, u32[]{:S(2)}, u32[]{:S(2)}) collective-permute-start(bf16[2,2,2,192,128]{4,3,2,1,0:T(8,128)(2,1)S(1)} %pad_maximum_fusion.u0), channel_id=1, source_target_pairs={{0,2},{2,4},{4,6},{6,0},{1,3},{3,5},{5,7},{7,1},{8,10},{10,12},{12... | collective-permute-start | bytes 1179656 | tf_op jit(solution)/shard_map/ppermute | solution.py:143
  126.5 29.9 %collective-permute-start.5 = (bf16[2,2,2,192,128]{4,3,2,1,0:T(8,128)(2,1)S(1)}, bf16[2,2,2,192,128]{4,3,2,1,0:T(8,128)(2,1)}, u32[]{:S(2)}, u32[]{:S(2)}) collective-permute-start(bf16[2,2,2,192,128]{4,3,2,1,0:T(8,128)(2,1)S(1)} %pad_maximum_fusion.u0), channel_id=1, source_target_pairs={{0,4},{2,6},{4,0},{6,2},{1,5},{3,7},{5,1},{7,3},{8,12},{10,14},{12... | collective-permute-start | bytes 1179656 | tf_op jit(solution)/shard_map/ppermute | solution.py:143
  137.6 19.1 %collective-permute-start.6 = (bf16[2,2,2,192,128]{4,3,2,1,0:T(8,128)(2,1)S(1)}, bf16[2,2,2,192,128]{4,3,2,1,0:T(8,128)(2,1)}, u32[]{:S(2)}, u32[]{:S(2)}) collective-permute-start(bf16[2,2,2,192,128]{4,3,2,1,0:T(8,128)(2,1)S(1)} %pad_maximum_fusion.u0), channel_id=1, source_target_pairs={{0,6},{2,0},{4,2},{6,4},{1,7},{3,1},{5,3},{7,5},{8,14},{10,8},{12,... | collective-permute-start | bytes 1179656 | tf_op jit(solution)/shard_map/ppermute | solution.py:143
  139.0 1.3 copy-start
  140.3 1.0 copy-start.2
  141.3 1.0 copy-start.4
  142.3 1.0 copy-start.6
  143.3 1.0 copy-start.8
  144.3 11.5 %copy-start.12 = (f32[2,2]{1,0:T(2,128)S(1)}, f32[2,2]{1,0:T(2,128)}, u32[]{:S(2)}) copy-start(f32[2,2]{1,0:T(2,128)} %param.3) | copy-start | bytes 52
  150.0 30.9 %collective-permute-start.17 = (f32[2,192,128]{2,1,0:T(8,128)}, f32[2,192,128]{2,1,0:T(8,128)}, u32[]{:S(2)}, u32[]{:S(2)}) collective-permute-start(f32[2,192,128]{2,1,0:T(8,128)} %get-tuple-element.36), channel_id=1, source_target_pairs={{0,0},{1,1},{2,2},{3,3},{4,4},{5,5},{6,6},{7,7},{8,32},{9,33},{10,... | collective-permute-start | bytes 589832 | tf_op jit(solution)/shard_map/ppermute | solution.py:38
  154.5 26.4 %collective-permute-start.18 = (f32[2,192,128]{2,1,0:T(8,128)}, f32[2,192,128]{2,1,0:T(8,128)}, u32[]{:S(2)}, u32[]{:S(2)}) collective-permute-start(f32[2,192,128]{2,1,0:T(8,128)} %get-tuple-element.37), channel_id=1, source_target_pairs={{0,16},{1,17},{2,18},{3,19},{4,20},{5,21},{6,22},{7,23},{8,48},{9,... | collective-permute-start | bytes 589832 | tf_op jit(solution)/shard_map/ppermute | solution.py:38
  156.4 40.0 %collective-permute-start.19 = (f32[2,192,128]{2,1,0:T(8,128)}, f32[2,192,128]{2,1,0:T(8,128)S(1)}, u32[]{:S(2)}, u32[]{:S(2)}) collective-permute-start(f32[2,192,128]{2,1,0:T(8,128)} %copy-done.10), channel_id=1, source_target_pairs={{0,8},{1,9},{2,10},{3,11},{4,12},{5,13},{6,14},{7,15},{8,40},{9,41... | collective-permute-start | bytes 589832 | tf_op jit(solution)/shard_map/ppermute | solution.py:38
  156.8 41.6 %collective-permute-start.20 = (f32[2,192,128]{2,1,0:T(8,128)}, f32[2,192,128]{2,1,0:T(8,128)S(1)}, u32[]{:S(2)}, u32[]{:S(2)}) collective-permute-start(f32[2,192,128]{2,1,0:T(8,128)} %copy-done.9), channel_id=1, source_target_pairs={{0,24},{1,25},{2,26},{3,27},{4,28},{5,29},{6,30},{7,31},{8,56},{9,... | collective-permute-start | bytes 589832 | tf_op jit(solution)/shard_map/ppermute | solution.py:38
  163.1 43.7 %collective-permute-start.10 = (f32[2,192,128]{2,1,0:T(8,128)S(1)}, f32[2,192,128]{2,1,0:T(8,128)S(1)}, u32[]{:S(2)}, u32[]{:S(2)}) collective-permute-start(f32[2,192,128]{2,1,0:T(8,128)S(1)} %get-tuple-element.32), channel_id=1, source_target_pairs={{0,8},{1,9},{2,10},{3,11},{4,12},{5,13},{6,14},{7,15},{8,40},{9,41... | collective-permute-start | bytes 589832 | tf_op jit(solution)/shard_map/ppermute | solution.py:38
  180.9 26.0 %collective-permute-start.11 = (f32[2,192,128]{2,1,0:T(8,128)S(1)}, f32[2,192,128]{2,1,0:T(8,128)S(1)}, u32[]{:S(2)}, u32[]{:S(2)}) collective-permute-start(f32[2,192,128]{2,1,0:T(8,128)S(1)} %get-tuple-element.33), channel_id=1, source_target_pairs={{0,16},{1,17},{2,18},{3,19},{4,20},{5,21},{6,22},{7,23},{8,48},{9,... | collective-permute-start | bytes 589832 | tf_op jit(solution)/shard_map/ppermute | solution.py:38
  180.9 26.0 %collective-permute-start.12 = (f32[2,192,128]{2,1,0:T(8,128)S(1)}, f32[2,192,128]{2,1,0:T(8,128)S(1)}, u32[]{:S(2)}, u32[]{:S(2)}) collective-permute-start(f32[2,192,128]{2,1,0:T(8,128)S(1)} %get-tuple-element.34), channel_id=1, source_target_pairs={{0,24},{1,25},{2,26},{3,27},{4,28},{5,29},{6,30},{7,31},{8,56},{9,... | collective-permute-start | bytes 589832 | tf_op jit(solution)/shard_map/ppermute | solution.py:38
  196.4 23.2 %collective-permute-start.9 = (f32[2,192,128]{2,1,0:T(8,128)S(1)}, f32[2,192,128]{2,1,0:T(8,128)S(1)}, u32[]{:S(2)}, u32[]{:S(2)}) collective-permute-start(f32[2,192,128]{2,1,0:T(8,128)S(1)} %get-tuple-element.31), channel_id=1, source_target_pairs={{0,0},{1,1},{2,2},{3,3},{4,4},{5,5},{6,6},{7,7},{8,32},{9,33},{10,... | collective-permute-start | bytes 589832 | tf_op jit(solution)/shard_map/ppermute | solution.py:38
  (5 other events, 3.6 us)

commit v6 on v5

--- a/solution.py
+++ b/solution.py
@@ -108,14 +108,14 @@
     first = core == 0
 
     def ordered(block):
-        return block.reshape((2, 2, 2, 2, 2) + block.shape[2:])
+        return block.reshape((2, 2, 4, 2) + block.shape[2:])
 
     passed = swap_core(lax.dynamic_slice_in_dim(spectra, (1 - core) * half, half, 2))
-    a = ordered(jnp.where(first, spectra[:, :, :half], passed)).transpose(1, 3, 2, 4, 0, 5, 6)
-    a = a.reshape((8, 2, 2) + a.shape[5:])
+    a = ordered(jnp.where(first, spectra[:, :, :half], passed)).transpose(2, 1, 3, 0, 4, 5)
+    a = a.reshape((8, 2, 2) + a.shape[4:])
     b = jnp.where(first, jnp.concatenate([spectra[:, :, window:], passed], 2), spectra[:, :, half:])
-    b = [ordered(b)[:, :, :, :, g].transpose(1, 3, 2, 0, 4, 5) for g in range(2)]
-    b = [b[g].reshape((8, 2) + b[g].shape[4:]) for g in range(2)]
+    b = [ordered(b)[:, :, :, g].transpose(2, 1, 0, 3, 4) for g in range(2)]
+    b = [b[g].reshape((8, 2) + b[g].shape[3:]) for g in range(2)]
     b = lax.optimization_barrier(b)
 
     def exchange(block):
@@ -129,20 +129,18 @@
         b_own.append(exchange(b[g]))
         b_peer.append(swap_core(b_own[g]))
 
-    shots = a_own.reshape((4, 2) + a_own.shape[1:])[:, 0]
-    near, far = shots[:2], shots[2:]
-    near, far = lax.optimization_barrier((near, far))
-    across = send(near, lambda q, r, c, x, y, h: (0, r, c, x, y, 1 - h) if q == 0 else None)
-    up = send(far, lambda q, r, c, x, y, h: (1, r, c, x, y, h) if q == 0 else None)
-    down = send(far, lambda q, r, c, x, y, h: (1, r, c, x, y, 1 - h) if q == 0 else None)
-    mine, others = jnp.where(zq == 0, near, up), jnp.where(zq == 0, across, down)
-    pieces = [jnp.stack([mine[:, g], others[:, g]]) for g in range(2)]
-
     def turn(g):
+        shots = a_own.reshape((4, 2) + a_own.shape[1:])[:, 0, g]
+        near, far = shots[:2], shots[2:]
+        across = send(near, lambda q, r, c, x, y, h: (0, r, c, x, y, 1 - h) if q == 0 else None)
+        up = send(far, lambda q, r, c, x, y, h: (1, r, c, x, y, h) if q == 0 else None)
+        down = send(far, lambda q, r, c, x, y, h: (1, r, c, x, y, 1 - h) if q == 0 else None)
+        mine, across, up, down = lax.optimization_barrier((near, across, up, down))
+        pieces = jnp.stack([jnp.where(zq == 0, mine, up), jnp.where(zq == 0, across, down)])
         plus, minus, two = (
-            lax.ppermute(pieces[g], "y", [(i, (i + s) % 4) for i in range(4)]) for s in (1, 3, 2)
+            lax.ppermute(pieces, "y", [(i, (i + s) % 4) for i in range(4)]) for s in (1, 3, 2)
         )
-        return pieces[g], plus, two, minus
+        return pieces, plus, two, minus
 
     turned = [turn(g) for g in range(2)]
 
@@ -150,7 +148,7 @@
         return [
             send(
                 block,
-                lambda q, r, c, x, y, h: (x // 2, r, x % 2, (2 * q + c) ^ t, y, h),
+                lambda q, r, c, x, y, h: (r, x // 2, x % 2, (2 * q + c) ^ t, y, h),
             )
             for t, block in enumerate(blocks)
         ]

time: 226 us -> 193 us (0.85)
  waiting for transfers between devices: 105 us -> 58.2 us
  starting transfers between devices: 57.4 us -> 70 us
    ppermute x11 -> x14, waiting for transfers between devices: 73 us -> 36.1 us  [send(): return lax.ppermute(value, AXES, moved(target))]
    ppermute x11 -> x14, starting transfers between devices: 24.4 us -> 42.9 us  [send(): return lax.ppermute(value, AXES, moved(target))]
    ppermute x6, waiting for transfers between devices: 14.7 us -> 5.15 us  [turn(): lax.ppermute(pieces, 'y', [(i, (i + s) % 4) for i in range(4)])]
    ppermute x6, starting transfers between devices: 19.6 us -> 13.7 us  [turn(): lax.ppermute(pieces, 'y', [(i, (i + s) % 4) for i in range(4)])]
    another operation x6 -> x8, other arithmetic: 6.19 us -> 9.07 us
    unnamed x28 -> x26, local copies, waits for them, and re-layouts: 10.2 us -> 10.3 us
  transfers between devices with their start and end apart: 23 -> 26, of which waited for: 12 -> 10; matrix products, arithmetic and copies ran while one was open for 6% -> 7% of each run, Pallas kernels for 4% -> 5%
where the time goes in v6:
time: 193 us; the launch traced here: 190 us
  starting transfers between devices  70 us (36%)
  waiting for transfers between devices  58.2 us (30%)
  blocking collectives  21.5 us (11%)
  local copies, waits for them, and re-layouts  16.7 us (9%)
  other arithmetic  14.6 us (8%)
  Pallas kernels  8.8 us (5%)
    ppermute x14, starting transfers between devices, send(): return lax.ppermute(value, AXES, moved(target))  42.9 us
    ppermute x14, waiting for transfers between devices, send(): return lax.ppermute(value, AXES, moved(target))  36.1 us
    all_to_all x1, blocking collectives, exchange(): lax.all_to_all(block, ('x', 'zr'), split_axis=0, concat_axis=0, tiled=True)  21.5 us
    ppermute x6, starting transfers between devices, turn(): lax.ppermute(pieces, 'y', [(i, (i + s) % 4) for i in range(4)])  13.7 us
    all_to_all x2, waiting for transfers between devices, exchange(): lax.all_to_all(block, ('x', 'zr'), split_axis=0, concat_axis=0, tiled=True)  13.6 us
    all_to_all x2, starting transfers between devices, exchange(): lax.all_to_all(block, ('x', 'zr'), split_axis=0, concat_axis=0, tiled=True)  12.7 us
    unnamed x26, local copies, waits for them, and re-layouts  10.3 us
    pallas_call x2, Pallas kernels, contract(): pl.pallas_call(kernel, out_shape=(result,) * 4, in_specs=[pl.BlockSpec(me...  8.8 us
  transfers between devices with their start and end apart: 26, of which 10 were waited for; matrix products, arithmetic and copies ran while one was open for 7% of the time, Pallas kernels for 5%

profile of v6, /device:TPU:4, one launch (start us, length us, event | category | flops | bytes accessed | tf_op | source)
XLA Modules:
  0.0 190.1 jit_solution(13788986554081448363)
XLA Ops:
  1.6 3.4 %collective-permute-done = bf16[2,16,192,128]{3,2,1,0:T(8,128)(2,1)S(1)} collective-permute-done((bf16[2,16,192,128]{3,2,1,0:T(8,128)(2,1)S(1)}, bf16[2,16,192,128]{3,2,1,0:T(8,128)(2,1)S(1)}, u32[]{:S(2)}, u32[]{:S(2)}) %collective-permute-start) | collective-permute-done | bytes 1572896 | tf_op jit(solution)/shard_map/ppermute | solution.py:42
  5.0 1.6 slice_select_fusion
  7.9 6.2 %all-to-all-start = ((bf16[8,2,2,192,128]{4,3,2,1,0:T(8,128)(2,1)}), bf16[8,2,2,192,128]{4,3,2,1,0:T(8,128)(2,1)S(1)}, u32[]{:S(2)}, u32[]{:S(2)}) async-start(bf16[8,2,2,192,128]{4,3,2,1,0:T(8,128)(2,1)} %bitcast.6), calls=%async_computation | async-start | bytes 3145728 | tf_op jit(solution)/shard_map/all_to_all | solution.py:122
  15.3 2.7 %maximum_select_fusion = bf16[2,16,320,128]{3,2,1,0:T(8,128)(2,1)S(1)} fusion(bf16[2,16,192,128]{3,2,1,0:T(8,128)(2,1)S(1)} %collective-permute-done, bf16[2,16,128,128]{3,2,1,0:T(8,128)(2,1)S(1)} %slice-done, bf16[2,16,512,128]{3,2,1,0:T(8,128)(2,1)} %param.2, pred[]{:T(512)S(6)} %eq.17), kind=kLoop, calls=%fused_computation | loop fusion | flops 6553600 | bytes 7864321 | tf_op jit(solution)/shard_map/jit(_where)/select_n | solution.py:116
  19.5 13.6 %all-to-all-done.ao_ref = bf16[8,2,2,192,128]{4,3,2,1,0:T(8,128)(2,1)S(1)} async-done(((bf16[8,2,2,192,128]{4,3,2,1,0:T(8,128)(2,1)}), bf16[8,2,2,192,128]{4,3,2,1,0:T(8,128)(2,1)S(1)}, u32[]{:S(2)}, u32[]{:S(2)}) %all-to-all-start) | async-done | bytes 1572896 | tf_op jit(solution)/shard_map/all_to_all | solution.py:122
  33.1 21.5 %all_to_all.15.bo_ref = bf16[8,2,320,128]{3,2,1,0:T(8,128)(2,1)} all-to-all(bf16[8,2,320,128]{3,2,1,0:T(8,128)(2,1)S(1)} %bitcast.54), channel_id=1, replica_groups=mesh['zq'=2,'zr'=2,'core'=2,'x'=4,'y'=4,'zh'=2] {'x','zr'}, dimensions={0} | all-to-all | bytes 2621440 | tf_op jit(solution)/shard_map/all_to_all | solution.py:122
  54.6 6.6 %all-to-all-start.1 = ((bf16[8,2,320,128]{3,2,1,0:T(8,128)(2,1)}), bf16[8,2,320,128]{3,2,1,0:T(8,128)(2,1)}, u32[]{:S(2)}, u32[]{:S(2)}) async-start(bf16[8,2,320,128]{3,2,1,0:T(8,128)(2,1)} %bitcast.13), calls=%async_computation.1 | async-start | bytes 2621440 | tf_op jit(solution)/shard_map/all_to_all | solution.py:122
  62.0 8.2 %collective-permute-start.13 = (bf16[2,2,192,128]{3,2,1,0:T(8,128)(2,1)S(1)}, bf16[2,2,192,128]{3,2,1,0:T(8,128)(2,1)}, u32[]{:S(2)}, u32[]{:S(2)}) collective-permute-start(bf16[2,2,192,128]{3,2,1,0:T(8,128)(2,1)S(1)} %get-tuple-element.43), channel_id=1, source_target_pairs={{0,1},{1,0},{2,3},{3,2},{4,5},{5,4},{6,7},{7,6},{8,9},{9,8},{10,11... | collective-permute-start | bytes 589832 | tf_op jit(solution)/shard_map/ppermute | solution.py:38
  70.2 2.0 %collective-permute-start.14 = (bf16[2,2,192,128]{3,2,1,0:T(8,128)(2,1)}, bf16[2,2,192,128]{3,2,1,0:T(8,128)(2,1)}, u32[]{:S(2)}, u32[]{:S(2)}) collective-permute-start(bf16[2,2,192,128]{3,2,1,0:T(8,128)(2,1)} %get-tuple-element.59), channel_id=1, source_target_pairs={{0,128},{1,129},{2,130},{3,131},{4,132},{5,133},{6,134},{7,135},{8... | collective-permute-start | bytes 589832 | tf_op jit(solution)/shard_map/ppermute | solution.py:38
  72.1 2.0 %collective-permute-start.15 = (bf16[2,2,192,128]{3,2,1,0:T(8,128)(2,1)}, bf16[2,2,192,128]{3,2,1,0:T(8,128)(2,1)}, u32[]{:S(2)}, u32[]{:S(2)}) collective-permute-start(bf16[2,2,192,128]{3,2,1,0:T(8,128)(2,1)} %get-tuple-element.59), channel_id=1, source_target_pairs={{0,129},{1,128},{2,131},{3,130},{4,133},{5,132},{6,135},{7,134},{8... | collective-permute-start | bytes 589832 | tf_op jit(solution)/shard_map/ppermute | solution.py:38
  74.1 3.4 %collective-permute-start.1 = (bf16[2,2,192,128]{3,2,1,0:T(8,128)(2,1)S(1)}, bf16[2,2,192,128]{3,2,1,0:T(8,128)(2,1)}, u32[]{:S(2)}, u32[]{:S(2)}) collective-permute-start(bf16[2,2,192,128]{3,2,1,0:T(8,128)(2,1)S(1)} %get-tuple-element.34), channel_id=1, source_target_pairs={{0,1},{1,0},{2,3},{3,2},{4,5},{5,4},{6,7},{7,6},{8,9},{9,8},{10,11... | collective-permute-start | bytes 589832 | tf_op jit(solution)/shard_map/ppermute | solution.py:38
  77.5 10.2 %collective-permute-done.13 = bf16[2,2,192,128]{3,2,1,0:T(8,128)(2,1)} collective-permute-done((bf16[2,2,192,128]{3,2,1,0:T(8,128)(2,1)S(1)}, bf16[2,2,192,128]{3,2,1,0:T(8,128)(2,1)}, u32[]{:S(2)}, u32[]{:S(2)}) %collective-permute-start.13) | collective-permute-done | bytes 196640 | tf_op jit(solution)/shard_map/ppermute | solution.py:38
  87.7 2.0 %collective-permute-start.2 = (bf16[2,2,192,128]{3,2,1,0:T(8,128)(2,1)}, bf16[2,2,192,128]{3,2,1,0:T(8,128)(2,1)}, u32[]{:S(2)}, u32[]{:S(2)}) collective-permute-start(bf16[2,2,192,128]{3,2,1,0:T(8,128)(2,1)} %get-tuple-element.61), channel_id=1, source_target_pairs={{0,128},{1,129},{2,130},{3,131},{4,132},{5,133},{6,134},{7,135},{8... | collective-permute-start | bytes 589832 | tf_op jit(solution)/shard_map/ppermute | solution.py:38
  90.1 1.7 select_bitcast_fusion
  93.4 2.1 %collective-permute-done.1 = bf16[2,2,192,128]{3,2,1,0:T(8,128)(2,1)} collective-permute-done((bf16[2,2,192,128]{3,2,1,0:T(8,128)(2,1)S(1)}, bf16[2,2,192,128]{3,2,1,0:T(8,128)(2,1)}, u32[]{:S(2)}, u32[]{:S(2)}) %collective-permute-start.1) | collective-permute-done | bytes 196640 | tf_op jit(solution)/shard_map/ppermute | solution.py:38
  95.5 1.6 collective-permute-start.16
  97.1 4.6 %collective-permute-start.3 = (bf16[2,2,192,128]{3,2,1,0:T(8,128)(2,1)}, bf16[2,2,192,128]{3,2,1,0:T(8,128)(2,1)S(1)}, u32[]{:S(2)}, u32[]{:S(2)}) collective-permute-start(bf16[2,2,192,128]{3,2,1,0:T(8,128)(2,1)} %get-tuple-element.61), channel_id=1, source_target_pairs={{0,129},{1,128},{2,131},{3,130},{4,133},{5,132},{6,135},{7,134},{8... | collective-permute-start | bytes 589832 | tf_op jit(solution)/shard_map/ppermute | solution.py:38
  101.7 8.6 %collective-permute-done.3 = bf16[2,2,192,128]{3,2,1,0:T(8,128)(2,1)S(1)} collective-permute-done((bf16[2,2,192,128]{3,2,1,0:T(8,128)(2,1)}, bf16[2,2,192,128]{3,2,1,0:T(8,128)(2,1)S(1)}, u32[]{:S(2)}, u32[]{:S(2)}) %collective-permute-start.3) | collective-permute-done | bytes 196640 | tf_op jit(solution)/shard_map/ppermute | solution.py:38
  111.0 4.2 %collective-permute-start.18 = (bf16[2,2,2,192,128]{4,3,2,1,0:T(8,128)(2,1)S(1)}, bf16[2,2,2,192,128]{4,3,2,1,0:T(8,128)(2,1)S(1)}, u32[]{:S(2)}, u32[]{:S(2)}) collective-permute-start(bf16[2,2,2,192,128]{4,3,2,1,0:T(8,128)(2,1)S(1)} %pad_maximum_fusion.1.u0), channel_id=1, source_target_pairs={{0,6},{2,0},{4,2},{6,4},{1,7},{3,1},{5,3},{7,5},{8,14},{10,8},{12,... | collective-permute-start | bytes 1179656 | tf_op jit(solution)/shard_map/ppermute | solution.py:141
  116.3 4.2 %collective-permute-done.17.u2 = bf16[2,2,2,192,128]{4,3,2,1,0:T(8,128)(2,1)S(1)} collective-permute-done((bf16[2,2,2,192,128]{4,3,2,1,0:T(8,128)(2,1)S(1)}, bf16[2,2,2,192,128]{4,3,2,1,0:T(8,128)(2,1)S(1)}, u32[]{:S(2)}, u32[]{:S(2)}) %collective-permute-start.17) | collective-permute-done | bytes 393248 | tf_op jit(solution)/shard_map/ppermute | solution.py:141
  121.3 2.8 %collective-permute-start.4 = (bf16[2,2,2,192,128]{4,3,2,1,0:T(8,128)(2,1)S(1)}, bf16[2,2,2,192,128]{4,3,2,1,0:T(8,128)(2,1)}, u32[]{:S(2)}, u32[]{:S(2)}) collective-permute-start(bf16[2,2,2,192,128]{4,3,2,1,0:T(8,128)(2,1)S(1)} %pad_maximum_fusion.u0), channel_id=1, source_target_pairs={{0,2},{2,4},{4,6},{6,0},{1,3},{3,5},{5,7},{7,1},{8,10},{10,12},{12... | collective-permute-start | bytes 1179656 | tf_op jit(solution)/shard_map/ppermute | solution.py:141
  125.8 3.1 %collective-permute-start.5 = (bf16[2,2,2,192,128]{4,3,2,1,0:T(8,128)(2,1)S(1)}, bf16[2,2,2,192,128]{4,3,2,1,0:T(8,128)(2,1)}, u32[]{:S(2)}, u32[]{:S(2)}) collective-permute-start(bf16[2,2,2,192,128]{4,3,2,1,0:T(8,128)(2,1)S(1)} %pad_maximum_fusion.u0), channel_id=1, source_target_pairs={{0,4},{2,6},{4,0},{6,2},{1,5},{3,7},{5,1},{7,3},{8,12},{10,14},{12... | collective-permute-start | bytes 1179656 | tf_op jit(solution)/shard_map/ppermute | solution.py:141
  128.9 2.0 %collective-permute-start.6 = (bf16[2,2,2,192,128]{4,3,2,1,0:T(8,128)(2,1)S(1)}, bf16[2,2,2,192,128]{4,3,2,1,0:T(8,128)(2,1)}, u32[]{:S(2)}, u32[]{:S(2)}) collective-permute-start(bf16[2,2,2,192,128]{4,3,2,1,0:T(8,128)(2,1)S(1)} %pad_maximum_fusion.u0), channel_id=1, source_target_pairs={{0,6},{2,0},{4,2},{6,4},{1,7},{3,1},{5,3},{7,5},{8,14},{10,8},{12,... | collective-permute-start | bytes 1179656 | tf_op jit(solution)/shard_map/ppermute | solution.py:141
  136.3 4.4 %shard_map.29 = (f32[2,192,128]{2,1,0:T(8,128)}, f32[2,192,128]{2,1,0:T(8,128)S(1)}, f32[2,192,128]{2,1,0:T(8,128)}, f32[2,192,128]{2,1,0:T(8,128)S(1)}) custom-call(s32[4]{0:T(128)S(1)} %pad_add_fusion.place_ref, bf16[2,2,2,192,128]{4,3,2,1,0:T(8,128)(2,1)S(1)} %copy-done.2, bf16[2,2,2,192,128]{4,3,2,1,0:T(8,128)(2,1)S(1)} %copy-done.4, ...), custom_call_target="tpu_custom_call" | custom-call | flops 1610612736 | bytes 7340032 | tf_op jit(solution)/shard_map/pallas_call | solution.py:88
  142.0 6.3 %collective-permute-start.20 = (f32[2,192,128]{2,1,0:T(8,128)}, f32[2,192,128]{2,1,0:T(8,128)}, u32[]{:S(2)}, u32[]{:S(2)}) collective-permute-start(f32[2,192,128]{2,1,0:T(8,128)} %get-tuple-element.48), channel_id=1, source_target_pairs={{0,0},{1,1},{2,2},{3,3},{4,4},{5,5},{6,6},{7,7},{8,32},{9,33},{10,... | collective-permute-start | bytes 589832 | tf_op jit(solution)/shard_map/ppermute | solution.py:38
  148.3 3.7 %collective-permute-start.21 = (f32[2,192,128]{2,1,0:T(8,128)}, f32[2,192,128]{2,1,0:T(8,128)}, u32[]{:S(2)}, u32[]{:S(2)}) collective-permute-start(f32[2,192,128]{2,1,0:T(8,128)} %get-tuple-element.49), channel_id=1, source_target_pairs={{0,16},{1,17},{2,18},{3,19},{4,20},{5,21},{6,22},{7,23},{8,48},{9,... | collective-permute-start | bytes 589832 | tf_op jit(solution)/shard_map/ppermute | solution.py:38
  152.8 1.8 collective-permute-start.23
  154.6 4.4 %shard_map.28 = (f32[2,192,128]{2,1,0:T(8,128)S(1)}, f32[2,192,128]{2,1,0:T(8,128)S(1)}, f32[2,192,128]{2,1,0:T(8,128)S(1)}, f32[2,192,128]{2,1,0:T(8,128)S(1)}) custom-call(s32[4]{0:T(128)S(1)} %pad_add_fusion.place_ref, bf16[2,2,2,192,128]{4,3,2,1,0:T(8,128)(2,1)S(1)} %pad_maximum_fusion.u0, bf16[2,2,2,192,128]{4,3,2,1,0:T(8,128)(2,1)} %collective-permute-done.4.u1, ...), custom_call_target="tpu_custom_call" | custom-call | flops 1610612736 | bytes 7340032 | tf_op jit(solution)/shard_map/pallas_call | solution.py:88
  159.0 2.1 %collective-permute-start.10 = (f32[2,192,128]{2,1,0:T(8,128)S(1)}, f32[2,192,128]{2,1,0:T(8,128)S(1)}, u32[]{:S(2)}, u32[]{:S(2)}) collective-permute-start(f32[2,192,128]{2,1,0:T(8,128)S(1)} %get-tuple-element.40), channel_id=1, source_target_pairs={{0,8},{1,9},{2,10},{3,11},{4,12},{5,13},{6,14},{7,15},{8,40},{9,41... | collective-permute-start | bytes 589832 | tf_op jit(solution)/shard_map/ppermute | solution.py:38
  163.5 2.0 %collective-permute-start.12 = (f32[2,192,128]{2,1,0:T(8,128)S(1)}, f32[2,192,128]{2,1,0:T(8,128)S(1)}, u32[]{:S(2)}, u32[]{:S(2)}) collective-permute-start(f32[2,192,128]{2,1,0:T(8,128)S(1)} %get-tuple-element.42), channel_id=1, source_target_pairs={{0,24},{1,25},{2,26},{3,27},{4,28},{5,29},{6,30},{7,31},{8,56},{9,... | collective-permute-start | bytes 589832 | tf_op jit(solution)/shard_map/ppermute | solution.py:38
  167.9 3.8 %collective-permute-start.9 = (f32[2,192,128]{2,1,0:T(8,128)S(1)}, f32[2,192,128]{2,1,0:T(8,128)S(1)}, u32[]{:S(2)}, u32[]{:S(2)}) collective-permute-start(f32[2,192,128]{2,1,0:T(8,128)S(1)} %get-tuple-element.39), channel_id=1, source_target_pairs={{0,0},{1,1},{2,2},{3,3},{4,4},{5,5},{6,6},{7,7},{8,32},{9,33},{10,... | collective-permute-start | bytes 589832 | tf_op jit(solution)/shard_map/ppermute | solution.py:38
  173.1 13.4 %collective-permute-done.11 = f32[2,192,128]{2,1,0:T(8,128)S(1)} collective-permute-done((f32[2,192,128]{2,1,0:T(8,128)S(1)}, f32[2,192,128]{2,1,0:T(8,128)S(1)}, u32[]{:S(2)}, u32[]{:S(2)}) %collective-permute-start.11) | collective-permute-done | bytes 196640 | tf_op jit(solution)/shard_map/ppermute | solution.py:38
  (77 shorter events, 30.0 us)
Async XLA Ops:
  1.5 3.5 %collective-permute-start = (bf16[2,16,192,128]{3,2,1,0:T(8,128)(2,1)S(1)}, bf16[2,16,192,128]{3,2,1,0:T(8,128)(2,1)S(1)}, u32[]{:S(2)}, u32[]{:S(2)}) collective-permute-start(bf16[2,16,192,128]{3,2,1,0:T(8,128)(2,1)S(1)} %constant_dynamic-slice_fusion), channel_id=1, source_target_pairs={{0,32},{32,0},{1,33},{33,1},{2,34},{34,2},{3,35},{35,3},{4,36},{36... | collective-permute-start | bytes 4718600 | tf_op jit(solution)/shard_map/ppermute | solution.py:42
  7.9 25.1 %all-to-all-start = ((bf16[8,2,2,192,128]{4,3,2,1,0:T(8,128)(2,1)}), bf16[8,2,2,192,128]{4,3,2,1,0:T(8,128)(2,1)S(1)}, u32[]{:S(2)}, u32[]{:S(2)}) async-start(bf16[8,2,2,192,128]{4,3,2,1,0:T(8,128)(2,1)} %bitcast.6), calls=%async_computation | async-start | bytes 3145728 | tf_op jit(solution)/shard_map/all_to_all | solution.py:122
  14.1 1.2 slice-start
  54.6 37.3 %all-to-all-start.1 = ((bf16[8,2,320,128]{3,2,1,0:T(8,128)(2,1)}), bf16[8,2,320,128]{3,2,1,0:T(8,128)(2,1)}, u32[]{:S(2)}, u32[]{:S(2)}) async-start(bf16[8,2,320,128]{3,2,1,0:T(8,128)(2,1)} %bitcast.13), calls=%async_computation.1 | async-start | bytes 2621440 | tf_op jit(solution)/shard_map/all_to_all | solution.py:122
  61.2 67.7 %collective-permute-start.7 = (bf16[8,2,2,192,128]{4,3,2,1,0:T(8,128)(2,1)S(1)}, bf16[8,2,2,192,128]{4,3,2,1,0:T(8,128)(2,1)S(1)}, u32[]{:S(2)}, u32[]{:S(2)}) collective-permute-start(bf16[8,2,2,192,128]{4,3,2,1,0:T(8,128)(2,1)S(1)} %all-to-all-done.ao_ref), channel_id=1, source_target_pairs={{0,32},{32,0},{1,33},{33,1},{2,34},{34,2},{3,35},{35,3},{4,36},{36... | collective-permute-start | bytes 4718600 | tf_op jit(solution)/shard_map/ppermute | solution.py:42
  62.0 25.7 %collective-permute-start.13 = (bf16[2,2,192,128]{3,2,1,0:T(8,128)(2,1)S(1)}, bf16[2,2,192,128]{3,2,1,0:T(8,128)(2,1)}, u32[]{:S(2)}, u32[]{:S(2)}) collective-permute-start(bf16[2,2,192,128]{3,2,1,0:T(8,128)(2,1)S(1)} %get-tuple-element.43), channel_id=1, source_target_pairs={{0,1},{1,0},{2,3},{3,2},{4,5},{5,4},{6,7},{7,6},{8,9},{9,8},{10,11... | collective-permute-start | bytes 589832 | tf_op jit(solution)/shard_map/ppermute | solution.py:38
  70.2 19.5 %collective-permute-start.14 = (bf16[2,2,192,128]{3,2,1,0:T(8,128)(2,1)}, bf16[2,2,192,128]{3,2,1,0:T(8,128)(2,1)}, u32[]{:S(2)}, u32[]{:S(2)}) collective-permute-start(bf16[2,2,192,128]{3,2,1,0:T(8,128)(2,1)} %get-tuple-element.59), channel_id=1, source_target_pairs={{0,128},{1,129},{2,130},{3,131},{4,132},{5,133},{6,134},{7,135},{8... | collective-permute-start | bytes 589832 | tf_op jit(solution)/shard_map/ppermute | solution.py:38
  72.1 18.0 %collective-permute-start.15 = (bf16[2,2,192,128]{3,2,1,0:T(8,128)(2,1)}, bf16[2,2,192,128]{3,2,1,0:T(8,128)(2,1)}, u32[]{:S(2)}, u32[]{:S(2)}) collective-permute-start(bf16[2,2,192,128]{3,2,1,0:T(8,128)(2,1)} %get-tuple-element.59), channel_id=1, source_target_pairs={{0,129},{1,128},{2,131},{3,130},{4,133},{5,132},{6,135},{7,134},{8... | collective-permute-start | bytes 589832 | tf_op jit(solution)/shard_map/ppermute | solution.py:38
  74.1 21.4 %collective-permute-start.1 = (bf16[2,2,192,128]{3,2,1,0:T(8,128)(2,1)S(1)}, bf16[2,2,192,128]{3,2,1,0:T(8,128)(2,1)}, u32[]{:S(2)}, u32[]{:S(2)}) collective-permute-start(bf16[2,2,192,128]{3,2,1,0:T(8,128)(2,1)S(1)} %get-tuple-element.34), channel_id=1, source_target_pairs={{0,1},{1,0},{2,3},{3,2},{4,5},{5,4},{6,7},{7,6},{8,9},{9,8},{10,11... | collective-permute-start | bytes 589832 | tf_op jit(solution)/shard_map/ppermute | solution.py:38
  87.7 9.4 %collective-permute-start.2 = (bf16[2,2,192,128]{3,2,1,0:T(8,128)(2,1)}, bf16[2,2,192,128]{3,2,1,0:T(8,128)(2,1)}, u32[]{:S(2)}, u32[]{:S(2)}) collective-permute-start(bf16[2,2,192,128]{3,2,1,0:T(8,128)(2,1)} %get-tuple-element.61), channel_id=1, source_target_pairs={{0,128},{1,129},{2,130},{3,131},{4,132},{5,133},{6,134},{7,135},{8... | collective-permute-start | bytes 589832 | tf_op jit(solution)/shard_map/ppermute | solution.py:38
  90.1 40.8 %collective-permute-start.19 = (bf16[8,2,320,128]{3,2,1,0:T(8,128)(2,1)}, bf16[8,2,320,128]{3,2,1,0:T(8,128)(2,1)}, u32[]{:S(2)}, u32[]{:S(2)}) collective-permute-start(bf16[8,2,320,128]{3,2,1,0:T(8,128)(2,1)} %all_to_all.15.bo_ref), channel_id=1, source_target_pairs={{0,32},{32,0},{1,33},{33,1},{2,34},{34,2},{3,35},{35,3},{4,36},{36... | collective-permute-start | bytes 3932168 | tf_op jit(solution)/shard_map/ppermute | solution.py:42
  91.8 62.7 %collective-permute-start.8 = (bf16[8,2,320,128]{3,2,1,0:T(8,128)(2,1)}, bf16[8,2,320,128]{3,2,1,0:T(8,128)(2,1)}, u32[]{:S(2)}, u32[]{:S(2)}) collective-permute-start(bf16[8,2,320,128]{3,2,1,0:T(8,128)(2,1)} %all-to-all-done.1.bo_ref), channel_id=1, source_target_pairs={{0,32},{32,0},{1,33},{33,1},{2,34},{34,2},{3,35},{35,3},{4,36},{36... | collective-permute-start | bytes 3932168 | tf_op jit(solution)/shard_map/ppermute | solution.py:42
  93.4 35.5 %copy-start.1 = (bf16[2,2,2,192,128]{4,3,2,1,0:T(8,128)(2,1)}, bf16[2,2,2,192,128]{4,3,2,1,0:T(8,128)(2,1)S(1)}, u32[]{:S(2)}) copy-start(bf16[2,2,2,192,128]{4,3,2,1,0:T(8,128)(2,1)S(1)} %pad_maximum_fusion.1.u0) | copy-start | bytes 1179652
  95.5 14.7 %collective-permute-start.16 = (bf16[2,2,2,192,128]{4,3,2,1,0:T(8,128)(2,1)S(1)}, bf16[2,2,2,192,128]{4,3,2,1,0:T(8,128)(2,1)S(1)}, u32[]{:S(2)}, u32[]{:S(2)}) collective-permute-start(bf16[2,2,2,192,128]{4,3,2,1,0:T(8,128)(2,1)S(1)} %pad_maximum_fusion.1.u0), channel_id=1, source_target_pairs={{0,2},{2,4},{4,6},{6,0},{1,3},{3,5},{5,7},{7,1},{8,10},{10,12},{12... | collective-permute-start | bytes 1179656 | tf_op jit(solution)/shard_map/ppermute | solution.py:141
  97.1 13.2 %collective-permute-start.3 = (bf16[2,2,192,128]{3,2,1,0:T(8,128)(2,1)}, bf16[2,2,192,128]{3,2,1,0:T(8,128)(2,1)S(1)}, u32[]{:S(2)}, u32[]{:S(2)}) collective-permute-start(bf16[2,2,192,128]{3,2,1,0:T(8,128)(2,1)} %get-tuple-element.61), channel_id=1, source_target_pairs={{0,129},{1,128},{2,131},{3,130},{4,133},{5,132},{6,135},{7,134},{8... | collective-permute-start | bytes 589832 | tf_op jit(solution)/shard_map/ppermute | solution.py:38
  110.3 10.3 %collective-permute-start.17 = (bf16[2,2,2,192,128]{4,3,2,1,0:T(8,128)(2,1)S(1)}, bf16[2,2,2,192,128]{4,3,2,1,0:T(8,128)(2,1)S(1)}, u32[]{:S(2)}, u32[]{:S(2)}) collective-permute-start(bf16[2,2,2,192,128]{4,3,2,1,0:T(8,128)(2,1)S(1)} %pad_maximum_fusion.1.u0), channel_id=1, source_target_pairs={{0,4},{2,6},{4,0},{6,2},{1,5},{3,7},{5,1},{7,3},{8,12},{10,14},{12... | collective-permute-start | bytes 1179656 | tf_op jit(solution)/shard_map/ppermute | solution.py:141
  111.0 14.0 %collective-permute-start.18 = (bf16[2,2,2,192,128]{4,3,2,1,0:T(8,128)(2,1)S(1)}, bf16[2,2,2,192,128]{4,3,2,1,0:T(8,128)(2,1)S(1)}, u32[]{:S(2)}, u32[]{:S(2)}) collective-permute-start(bf16[2,2,2,192,128]{4,3,2,1,0:T(8,128)(2,1)S(1)} %pad_maximum_fusion.1.u0), channel_id=1, source_target_pairs={{0,6},{2,0},{4,2},{6,4},{1,7},{3,1},{5,3},{7,5},{8,14},{10,8},{12,... | collective-permute-start | bytes 1179656 | tf_op jit(solution)/shard_map/ppermute | solution.py:141
  121.3 27.0 %collective-permute-start.4 = (bf16[2,2,2,192,128]{4,3,2,1,0:T(8,128)(2,1)S(1)}, bf16[2,2,2,192,128]{4,3,2,1,0:T(8,128)(2,1)}, u32[]{:S(2)}, u32[]{:S(2)}) collective-permute-start(bf16[2,2,2,192,128]{4,3,2,1,0:T(8,128)(2,1)S(1)} %pad_maximum_fusion.u0), channel_id=1, source_target_pairs={{0,2},{2,4},{4,6},{6,0},{1,3},{3,5},{5,7},{7,1},{8,10},{10,12},{12... | collective-permute-start | bytes 1179656 | tf_op jit(solution)/shard_map/ppermute | solution.py:141
  125.8 26.8 %collective-permute-start.5 = (bf16[2,2,2,192,128]{4,3,2,1,0:T(8,128)(2,1)S(1)}, bf16[2,2,2,192,128]{4,3,2,1,0:T(8,128)(2,1)}, u32[]{:S(2)}, u32[]{:S(2)}) collective-permute-start(bf16[2,2,2,192,128]{4,3,2,1,0:T(8,128)(2,1)S(1)} %pad_maximum_fusion.u0), channel_id=1, source_target_pairs={{0,4},{2,6},{4,0},{6,2},{1,5},{3,7},{5,1},{7,3},{8,12},{10,14},{12... | collective-permute-start | bytes 1179656 | tf_op jit(solution)/shard_map/ppermute | solution.py:141
  128.9 23.9 %collective-permute-start.6 = (bf16[2,2,2,192,128]{4,3,2,1,0:T(8,128)(2,1)S(1)}, bf16[2,2,2,192,128]{4,3,2,1,0:T(8,128)(2,1)}, u32[]{:S(2)}, u32[]{:S(2)}) collective-permute-start(bf16[2,2,2,192,128]{4,3,2,1,0:T(8,128)(2,1)S(1)} %pad_maximum_fusion.u0), channel_id=1, source_target_pairs={{0,6},{2,0},{4,2},{6,4},{1,7},{3,1},{5,3},{7,5},{8,14},{10,8},{12,... | collective-permute-start | bytes 1179656 | tf_op jit(solution)/shard_map/ppermute | solution.py:141
  131.0 1.3 copy-start
  132.3 1.0 copy-start.2
  135.3 1.0 copy-start.8
  136.3 15.7 %copy-start.11 = (f32[2,2]{1,0:T(2,128)S(1)}, f32[2,2]{1,0:T(2,128)}, u32[]{:S(2)}) copy-start(f32[2,2]{1,0:T(2,128)} %param.3) | copy-start | bytes 52
  142.0 19.1 %collective-permute-start.20 = (f32[2,192,128]{2,1,0:T(8,128)}, f32[2,192,128]{2,1,0:T(8,128)}, u32[]{:S(2)}, u32[]{:S(2)}) collective-permute-start(f32[2,192,128]{2,1,0:T(8,128)} %get-tuple-element.48), channel_id=1, source_target_pairs={{0,0},{1,1},{2,2},{3,3},{4,4},{5,5},{6,6},{7,7},{8,32},{9,33},{10,... | collective-permute-start | bytes 589832 | tf_op jit(solution)/shard_map/ppermute | solution.py:38
  148.3 15.2 %collective-permute-start.21 = (f32[2,192,128]{2,1,0:T(8,128)}, f32[2,192,128]{2,1,0:T(8,128)}, u32[]{:S(2)}, u32[]{:S(2)}) collective-permute-start(f32[2,192,128]{2,1,0:T(8,128)} %get-tuple-element.49), channel_id=1, source_target_pairs={{0,16},{1,17},{2,18},{3,19},{4,20},{5,21},{6,22},{7,23},{8,48},{9,... | collective-permute-start | bytes 589832 | tf_op jit(solution)/shard_map/ppermute | solution.py:38
  152.6 15.3 %collective-permute-start.22 = (f32[2,192,128]{2,1,0:T(8,128)}, f32[2,192,128]{2,1,0:T(8,128)S(1)}, u32[]{:S(2)}, u32[]{:S(2)}) collective-permute-start(f32[2,192,128]{2,1,0:T(8,128)} %copy-done.10), channel_id=1, source_target_pairs={{0,8},{1,9},{2,10},{3,11},{4,12},{5,13},{6,14},{7,15},{8,40},{9,41... | collective-permute-start | bytes 589832 | tf_op jit(solution)/shard_map/ppermute | solution.py:38
  152.8 18.9 %collective-permute-start.23 = (f32[2,192,128]{2,1,0:T(8,128)}, f32[2,192,128]{2,1,0:T(8,128)S(1)}, u32[]{:S(2)}, u32[]{:S(2)}) collective-permute-start(f32[2,192,128]{2,1,0:T(8,128)} %copy-done.9), channel_id=1, source_target_pairs={{0,24},{1,25},{2,26},{3,27},{4,28},{5,29},{6,30},{7,31},{8,56},{9,... | collective-permute-start | bytes 589832 | tf_op jit(solution)/shard_map/ppermute | solution.py:38
  159.0 14.1 %collective-permute-start.10 = (f32[2,192,128]{2,1,0:T(8,128)S(1)}, f32[2,192,128]{2,1,0:T(8,128)S(1)}, u32[]{:S(2)}, u32[]{:S(2)}) collective-permute-start(f32[2,192,128]{2,1,0:T(8,128)S(1)} %get-tuple-element.40), channel_id=1, source_target_pairs={{0,8},{1,9},{2,10},{3,11},{4,12},{5,13},{6,14},{7,15},{8,40},{9,41... | collective-permute-start | bytes 589832 | tf_op jit(solution)/shard_map/ppermute | solution.py:38
  161.1 25.4 %collective-permute-start.11 = (f32[2,192,128]{2,1,0:T(8,128)S(1)}, f32[2,192,128]{2,1,0:T(8,128)S(1)}, u32[]{:S(2)}, u32[]{:S(2)}) collective-permute-start(f32[2,192,128]{2,1,0:T(8,128)S(1)} %get-tuple-element.41), channel_id=1, source_target_pairs={{0,16},{1,17},{2,18},{3,19},{4,20},{5,21},{6,22},{7,23},{8,48},{9,... | collective-permute-start | bytes 589832 | tf_op jit(solution)/shard_map/ppermute | solution.py:38
  163.5 23.0 %collective-permute-start.12 = (f32[2,192,128]{2,1,0:T(8,128)S(1)}, f32[2,192,128]{2,1,0:T(8,128)S(1)}, u32[]{:S(2)}, u32[]{:S(2)}) collective-permute-start(f32[2,192,128]{2,1,0:T(8,128)S(1)} %get-tuple-element.42), channel_id=1, source_target_pairs={{0,24},{1,25},{2,26},{3,27},{4,28},{5,29},{6,30},{7,31},{8,56},{9,... | collective-permute-start | bytes 589832 | tf_op jit(solution)/shard_map/ppermute | solution.py:38
  167.9 18.6 %collective-permute-start.9 = (f32[2,192,128]{2,1,0:T(8,128)S(1)}, f32[2,192,128]{2,1,0:T(8,128)S(1)}, u32[]{:S(2)}, u32[]{:S(2)}) collective-permute-start(f32[2,192,128]{2,1,0:T(8,128)S(1)} %get-tuple-element.39), channel_id=1, source_target_pairs={{0,0},{1,1},{2,2},{3,3},{4,4},{5,5},{6,6},{7,7},{8,32},{9,33},{10,... | collective-permute-start | bytes 589832 | tf_op jit(solution)/shard_map/ppermute | solution.py:38
  (7 other events, 5.7 us)

commit v7 on v6

--- a/solution.py
+++ b/solution.py
@@ -98,6 +98,29 @@
     )(place, *turned, a_own, a_peer, b_own, b_peer)
 
 
+def finish(odd, wavelet, *blocks):
+    half, lanes = blocks[0].shape[1:]
+
+    def kernel(odd_ref, wave_ref, *refs):
+        for g in range(2):
+            wave_real, wave_imag = wave_ref[0, g], wave_ref[1, g]
+            for t in range(2):
+                start = pl.multiple_of((odd_ref[0] ^ t) * half, half)
+                one, two = refs[4 * g + t], refs[4 * g + t + 2]
+                real, imag = one[0] + two[0], one[1] + two[1]
+                refs[8][0, g, pl.ds(start, half)] = (-(wave_real * real - wave_imag * imag)).astype(jnp.bfloat16)
+                refs[8][1, g, pl.ds(start, half)] = (-(wave_real * imag + wave_imag * real)).astype(jnp.bfloat16)
+
+    smem, vmem = pl.BlockSpec(memory_space=pltpu.SMEM), pl.BlockSpec(memory_space=pltpu.VMEM)
+    return pl.pallas_call(
+        kernel,
+        out_shape=jax.ShapeDtypeStruct((2, 2, 2 * half, lanes), jnp.bfloat16),
+        in_specs=[smem, smem] + [vmem] * 8,
+        out_specs=vmem,
+        cost_estimate=pl.CostEstimate(flops=8 * 4 * half * lanes, bytes_accessed=2 << 20, transcendentals=0),
+    )(odd, wavelet, *blocks)
+
+
 def step(spectra, wavelet):
     zq, core, x = lax.axis_index("zq"), lax.axis_index("core"), lax.axis_index("x")
     y, zh = lax.axis_index("y"), lax.axis_index("zh")
@@ -153,29 +176,11 @@
             for t, block in enumerate(blocks)
         ]
 
-    def finish(g, blocks):
-        pair = [blocks[0] + blocks[2], blocks[1] + blocks[3]]
-        pair = [
-            jnp.stack(
-                [
-                    -(wavelet[0, g] * p[0] - wavelet[1, g] * p[1]),
-                    -(wavelet[0, g] * p[1] + wavelet[1, g] * p[0]),
-                ]
-            ).astype(jnp.bfloat16)
-            for p in pair
-        ]
-        even = x % 2 == 0
-        return jnp.concatenate(
-            [jnp.where(even, pair[0], pair[1]), jnp.where(even, pair[1], pair[0])], 1
-        )
-
     blocks = []
     for g in range(2):
         partial = contract(g, place, turned[g], a_own, a_peer, b_own[g], b_peer[g])
         blocks.append(homeward(partial))
-    early = finish(0, blocks[0])
-    late, early = lax.optimization_barrier((blocks[1], early))
-    return jnp.stack([early, finish(1, late)], 1)
+    return finish(jnp.stack([x % 2]).astype(jnp.int32), wavelet, *blocks[0], *blocks[1])
 
 
 def solution(mesh):

time: 193 us -> 191 us (0.990)
  the two profiles are of different devices: /device:TPU:4 before, /device:TPU:213 now
where the time goes in v7:
time: 191 us; the launch traced here: 190 us
  waiting for transfers between devices  82.9 us (43%)
  starting transfers between devices  51.2 us (27%)
  blocking collectives  20.6 us (11%)
  local copies, waits for them, and re-layouts  15.3 us (8%)
  Pallas kernels  11.9 us (6%)
  other arithmetic  8.23 us (4%)
    ppermute x14, waiting for transfers between devices, send(): return lax.ppermute(value, AXES, moved(target))  53 us
    ppermute x14, starting transfers between devices, send(): return lax.ppermute(value, AXES, moved(target))  31.2 us
    all_to_all x1, blocking collectives, exchange(): lax.all_to_all(block, ('x', 'zr'), split_axis=0, concat_axis=0, tiled=True)  20.6 us
    ppermute x6, waiting for transfers between devices, turn(): lax.ppermute(pieces, 'y', [(i, (i + s) % 4) for i in range(4)])  13.9 us
    all_to_all x2, waiting for transfers between devices, exchange(): lax.all_to_all(block, ('x', 'zr'), split_axis=0, concat_axis=0, tiled=True)  13 us
    all_to_all x2, starting transfers between devices, exchange(): lax.all_to_all(block, ('x', 'zr'), split_axis=0, concat_axis=0, tiled=True)  11.2 us
    unnamed x34, local copies, waits for them, and re-layouts  10.2 us
    pallas_call x2, Pallas kernels, contract(): pl.pallas_call(kernel, out_shape=(result,) * 4, in_specs=[pl.BlockSpec(me...  9.59 us
  transfers between devices with their start and end apart: 26, of which 10 were waited for; matrix products, arithmetic and copies ran while one was open for 5% of the time, Pallas kernels for 5%

profile of v7, /device:TPU:213, one launch (start us, length us, event | category | flops | bytes accessed | tf_op | source)
XLA Modules:
  0.0 190.4 jit_solution(9762611764358809385)
XLA Ops:
  0.0 1.5 constant_dynamic-slice_fusion
  2.3 3.0 %collective-permute-done = bf16[2,16,192,128]{3,2,1,0:T(8,128)(2,1)S(1)} collective-permute-done((bf16[2,16,192,128]{3,2,1,0:T(8,128)(2,1)S(1)}, bf16[2,16,192,128]{3,2,1,0:T(8,128)(2,1)S(1)}, u32[]{:S(2)}, u32[]{:S(2)}) %collective-permute-start) | collective-permute-done | bytes 1572896 | tf_op jit(solution)/shard_map/ppermute | solution.py:42
  5.3 1.6 slice_select_fusion
  6.9 1.3 copy.3
  8.2 4.7 %all-to-all-start = ((bf16[8,2,2,192,128]{4,3,2,1,0:T(8,128)(2,1)}), bf16[8,2,2,192,128]{4,3,2,1,0:T(8,128)(2,1)S(1)}, u32[]{:S(2)}, u32[]{:S(2)}) async-start(bf16[8,2,2,192,128]{4,3,2,1,0:T(8,128)(2,1)} %bitcast.7), calls=%async_computation | async-start | bytes 3145728 | tf_op jit(solution)/shard_map/all_to_all | solution.py:145
  14.1 2.7 %maximum_select_fusion = bf16[2,16,320,128]{3,2,1,0:T(8,128)(2,1)S(1)} fusion(bf16[2,16,192,128]{3,2,1,0:T(8,128)(2,1)S(1)} %collective-permute-done, bf16[2,16,128,128]{3,2,1,0:T(8,128)(2,1)S(1)} %slice-done, bf16[2,16,512,128]{3,2,1,0:T(8,128)(2,1)} %param.2, pred[]{:T(512)S(6)} %eq.12), kind=kLoop, calls=%fused_computation | loop fusion | flops 6553600 | bytes 7864321 | tf_op jit(solution)/shard_map/jit(_where)/select_n | solution.py:139
  18.3 13.0 %all-to-all-done.ao_ref = bf16[8,2,2,192,128]{4,3,2,1,0:T(8,128)(2,1)S(1)} async-done(((bf16[8,2,2,192,128]{4,3,2,1,0:T(8,128)(2,1)}), bf16[8,2,2,192,128]{4,3,2,1,0:T(8,128)(2,1)S(1)}, u32[]{:S(2)}, u32[]{:S(2)}) %all-to-all-start) | async-done | bytes 1572896 | tf_op jit(solution)/shard_map/all_to_all | solution.py:145
  31.3 20.6 %all_to_all.15.bo_ref = bf16[8,2,320,128]{3,2,1,0:T(8,128)(2,1)} all-to-all(bf16[8,2,320,128]{3,2,1,0:T(8,128)(2,1)S(1)} %bitcast.48), channel_id=1, replica_groups=mesh['zq'=2,'zr'=2,'core'=2,'x'=4,'y'=4,'zh'=2] {'x','zr'}, dimensions={0} | all-to-all | bytes 2621440 | tf_op jit(solution)/shard_map/all_to_all | solution.py:145
  52.0 6.5 %all-to-all-start.1 = ((bf16[8,2,320,128]{3,2,1,0:T(8,128)(2,1)}), bf16[8,2,320,128]{3,2,1,0:T(8,128)(2,1)}, u32[]{:S(2)}, u32[]{:S(2)}) async-start(bf16[8,2,320,128]{3,2,1,0:T(8,128)(2,1)} %bitcast.11), calls=%async_computation.1 | async-start | bytes 2621440 | tf_op jit(solution)/shard_map/all_to_all | solution.py:145
  58.4 2.5 %collective-permute-start.7 = (bf16[8,2,2,192,128]{4,3,2,1,0:T(8,128)(2,1)S(1)}, bf16[8,2,2,192,128]{4,3,2,1,0:T(8,128)(2,1)S(1)}, u32[]{:S(2)}, u32[]{:S(2)}) collective-permute-start(bf16[8,2,2,192,128]{4,3,2,1,0:T(8,128)(2,1)S(1)} %all-to-all-done.ao_ref), channel_id=1, source_target_pairs={{0,32},{32,0},{1,33},{33,1},{2,34},{34,2},{3,35},{35,3},{4,36},{36... | collective-permute-start | bytes 4718600 | tf_op jit(solution)/shard_map/ppermute | solution.py:42
  61.8 1.3 collective-permute-start.13
  65.7 1.3 collective-permute-start.1
  68.3 12.7 %collective-permute-done.14 = bf16[2,2,192,128]{3,2,1,0:T(8,128)(2,1)} collective-permute-done((bf16[2,2,192,128]{3,2,1,0:T(8,128)(2,1)}, bf16[2,2,192,128]{3,2,1,0:T(8,128)(2,1)}, u32[]{:S(2)}, u32[]{:S(2)}) %collective-permute-start.14) | collective-permute-done | bytes 196640 | tf_op jit(solution)/shard_map/ppermute | solution.py:38
  81.0 7.4 %collective-permute-done.15 = bf16[2,2,192,128]{3,2,1,0:T(8,128)(2,1)} collective-permute-done((bf16[2,2,192,128]{3,2,1,0:T(8,128)(2,1)}, bf16[2,2,192,128]{3,2,1,0:T(8,128)(2,1)}, u32[]{:S(2)}, u32[]{:S(2)}) %collective-permute-start.15) | collective-permute-done | bytes 196640 | tf_op jit(solution)/shard_map/ppermute | solution.py:38
  89.1 1.8 select_bitcast_fusion
  94.4 8.6 %collective-permute-done.3 = bf16[2,2,192,128]{3,2,1,0:T(8,128)(2,1)S(1)} collective-permute-done((bf16[2,2,192,128]{3,2,1,0:T(8,128)(2,1)}, bf16[2,2,192,128]{3,2,1,0:T(8,128)(2,1)S(1)}, u32[]{:S(2)}, u32[]{:S(2)}) %collective-permute-start.3) | collective-permute-done | bytes 196640 | tf_op jit(solution)/shard_map/ppermute | solution.py:38
  106.1 5.0 %collective-permute-done.17.u2 = bf16[2,2,2,192,128]{4,3,2,1,0:T(8,128)(2,1)S(1)} collective-permute-done((bf16[2,2,2,192,128]{4,3,2,1,0:T(8,128)(2,1)S(1)}, bf16[2,2,2,192,128]{4,3,2,1,0:T(8,128)(2,1)S(1)}, u32[]{:S(2)}, u32[]{:S(2)}) %collective-permute-start.17) | collective-permute-done | bytes 393248 | tf_op jit(solution)/shard_map/ppermute | solution.py:164
  112.1 8.9 %collective-permute-done.18.u3 = bf16[2,2,2,192,128]{4,3,2,1,0:T(8,128)(2,1)S(1)} collective-permute-done((bf16[2,2,2,192,128]{4,3,2,1,0:T(8,128)(2,1)S(1)}, bf16[2,2,2,192,128]{4,3,2,1,0:T(8,128)(2,1)S(1)}, u32[]{:S(2)}, u32[]{:S(2)}) %collective-permute-start.18) | collective-permute-done | bytes 393248 | tf_op jit(solution)/shard_map/ppermute | solution.py:164
  121.7 2.3 %collective-permute-start.6 = (bf16[2,2,2,192,128]{4,3,2,1,0:T(8,128)(2,1)S(1)}, bf16[2,2,2,192,128]{4,3,2,1,0:T(8,128)(2,1)}, u32[]{:S(2)}, u32[]{:S(2)}) collective-permute-start(bf16[2,2,2,192,128]{4,3,2,1,0:T(8,128)(2,1)S(1)} %pad_maximum_fusion.u0), channel_id=1, source_target_pairs={{0,6},{2,0},{4,2},{6,4},{1,7},{3,1},{5,3},{7,5},{8,14},{10,8},{12,... | collective-permute-start | bytes 1179656 | tf_op jit(solution)/shard_map/ppermute | solution.py:164
  124.1 1.3 copy-done
  129.4 4.4 %shard_map.29 = (f32[2,192,128]{2,1,0:T(8,128)S(1)}, f32[2,192,128]{2,1,0:T(8,128)S(1)}, f32[2,192,128]{2,1,0:T(8,128)S(1)}, f32[2,192,128]{2,1,0:T(8,128)}) custom-call(s32[4]{0:T(128)S(1)} %pad_add_fusion.place_ref, bf16[2,2,2,192,128]{4,3,2,1,0:T(8,128)(2,1)S(1)} %copy-done.2, bf16[2,2,2,192,128]{4,3,2,1,0:T(8,128)(2,1)S(1)} %copy-done.4, ...), custom_call_target="tpu_custom_call" | custom-call | flops 1610612736 | bytes 7340032 | tf_op jit(solution)/shard_map/pallas_call | solution.py:88
  133.8 7.1 %collective-permute-start.20 = (f32[2,192,128]{2,1,0:T(8,128)S(1)}, f32[2,192,128]{2,1,0:T(8,128)S(1)}, u32[]{:S(2)}, u32[]{:S(2)}) collective-permute-start(f32[2,192,128]{2,1,0:T(8,128)S(1)} %get-tuple-element.43), channel_id=1, source_target_pairs={{0,0},{1,1},{2,2},{3,3},{4,4},{5,5},{6,6},{7,7},{8,32},{9,33},{10,... | collective-permute-start | bytes 589832 | tf_op jit(solution)/shard_map/ppermute | solution.py:38
  140.9 4.7 %collective-permute-start.21 = (f32[2,192,128]{2,1,0:T(8,128)S(1)}, f32[2,192,128]{2,1,0:T(8,128)S(1)}, u32[]{:S(2)}, u32[]{:S(2)}) collective-permute-start(f32[2,192,128]{2,1,0:T(8,128)S(1)} %get-tuple-element.44), channel_id=1, source_target_pairs={{0,8},{1,9},{2,10},{3,11},{4,12},{5,13},{6,14},{7,15},{8,40},{9,41... | collective-permute-start | bytes 589832 | tf_op jit(solution)/shard_map/ppermute | solution.py:38
  145.6 4.1 %collective-permute-start.23 = (f32[2,192,128]{2,1,0:T(8,128)}, f32[2,192,128]{2,1,0:T(8,128)}, u32[]{:S(2)}, u32[]{:S(2)}) collective-permute-start(f32[2,192,128]{2,1,0:T(8,128)} %get-tuple-element.46), channel_id=1, source_target_pairs={{0,24},{1,25},{2,26},{3,27},{4,28},{5,29},{6,30},{7,31},{8,56},{9,... | collective-permute-start | bytes 589832 | tf_op jit(solution)/shard_map/ppermute | solution.py:38
  149.7 5.2 %shard_map.28 = (f32[2,192,128]{2,1,0:T(8,128)}, f32[2,192,128]{2,1,0:T(8,128)}, f32[2,192,128]{2,1,0:T(8,128)}, f32[2,192,128]{2,1,0:T(8,128)}) custom-call(s32[4]{0:T(128)S(1)} %pad_add_fusion.place_ref, bf16[2,2,2,192,128]{4,3,2,1,0:T(8,128)(2,1)S(1)} %pad_maximum_fusion.u0, bf16[2,2,2,192,128]{4,3,2,1,0:T(8,128)(2,1)} %collective-permute-done.4.u1, ...), custom_call_target="tpu_custom_call" | custom-call | flops 1610612736 | bytes 7340032 | tf_op jit(solution)/shard_map/pallas_call | solution.py:88
  154.9 2.3 %collective-permute-start.10 = (f32[2,192,128]{2,1,0:T(8,128)}, f32[2,192,128]{2,1,0:T(8,128)S(1)}, u32[]{:S(2)}, u32[]{:S(2)}) collective-permute-start(f32[2,192,128]{2,1,0:T(8,128)} %get-tuple-element.35), channel_id=1, source_target_pairs={{0,8},{1,9},{2,10},{3,11},{4,12},{5,13},{6,14},{7,15},{8,40},{9,41... | collective-permute-start | bytes 589832 | tf_op jit(solution)/shard_map/ppermute | solution.py:38
  157.3 3.3 %collective-permute-start.12 = (f32[2,192,128]{2,1,0:T(8,128)}, f32[2,192,128]{2,1,0:T(8,128)S(1)}, u32[]{:S(2)}, u32[]{:S(2)}) collective-permute-start(f32[2,192,128]{2,1,0:T(8,128)} %get-tuple-element.37), channel_id=1, source_target_pairs={{0,24},{1,25},{2,26},{3,27},{4,28},{5,29},{6,30},{7,31},{8,56},{9,... | collective-permute-start | bytes 589832 | tf_op jit(solution)/shard_map/ppermute | solution.py:38
  161.3 1.9 %collective-permute-start.9 = (f32[2,192,128]{2,1,0:T(8,128)}, f32[2,192,128]{2,1,0:T(8,128)S(1)}, u32[]{:S(2)}, u32[]{:S(2)}) collective-permute-start(f32[2,192,128]{2,1,0:T(8,128)} %get-tuple-element.34), channel_id=1, source_target_pairs={{0,0},{1,1},{2,2},{3,3},{4,4},{5,5},{6,6},{7,7},{8,32},{9,33},{10,... | collective-permute-start | bytes 589832 | tf_op jit(solution)/shard_map/ppermute | solution.py:38
  163.2 8.3 %collective-permute-done.10.refs_1_ = f32[2,192,128]{2,1,0:T(8,128)S(1)} collective-permute-done((f32[2,192,128]{2,1,0:T(8,128)}, f32[2,192,128]{2,1,0:T(8,128)S(1)}, u32[]{:S(2)}, u32[]{:S(2)}) %collective-permute-start.10) | collective-permute-done | bytes 196640 | tf_op jit(solution)/shard_map/ppermute | solution.py:38
  171.5 5.5 %collective-permute-done.12.refs_3_ = f32[2,192,128]{2,1,0:T(8,128)S(1)} collective-permute-done((f32[2,192,128]{2,1,0:T(8,128)}, f32[2,192,128]{2,1,0:T(8,128)S(1)}, u32[]{:S(2)}, u32[]{:S(2)}) %collective-permute-start.12) | collective-permute-done | bytes 196640 | tf_op jit(solution)/shard_map/ppermute | solution.py:38
  177.0 10.4 %collective-permute-done.9.refs_0_ = f32[2,192,128]{2,1,0:T(8,128)S(1)} collective-permute-done((f32[2,192,128]{2,1,0:T(8,128)}, f32[2,192,128]{2,1,0:T(8,128)S(1)}, u32[]{:S(2)}, u32[]{:S(2)}) %collective-permute-start.9) | collective-permute-done | bytes 196640 | tf_op jit(solution)/shard_map/ppermute | solution.py:38
  188.1 2.4 %shard_map.30 = bf16[2,2,384,128]{3,2,1,0:T(8,128)(2,1)} custom-call(s32[1]{0:T(128)} %bitcast.odd_ref, f32[2,2]{1,0:T(2,128)} %wave_ref.1, f32[2,192,128]{2,1,0:T(8,128)} %copy-done.15, f32[2,192,128]{2,1,0:T(8,128)} %copy-done.12, f32[2,192,128]{2,1,0:T(8,128)} %copy-done.13, f32[2,192,128]{2,1,0:T(8,128)} %copy-done.14, f32[2,192,128]{2,1,0:T(8,128)} %copy-done.9, ...), custom_call_target="tpu_custom_call" | custom-call | flops 786432 | bytes 2097152 | tf_op jit(solution)/shard_map/pallas_call | solution.py:115
  (71 shorter events, 22.5 us)
Async XLA Ops:
  1.5 3.8 %collective-permute-start = (bf16[2,16,192,128]{3,2,1,0:T(8,128)(2,1)S(1)}, bf16[2,16,192,128]{3,2,1,0:T(8,128)(2,1)S(1)}, u32[]{:S(2)}, u32[]{:S(2)}) collective-permute-start(bf16[2,16,192,128]{3,2,1,0:T(8,128)(2,1)S(1)} %constant_dynamic-slice_fusion), channel_id=1, source_target_pairs={{0,32},{32,0},{1,33},{33,1},{2,34},{34,2},{3,35},{35,3},{4,36},{36... | collective-permute-start | bytes 4718600 | tf_op jit(solution)/shard_map/ppermute | solution.py:42
  8.2 23.1 %all-to-all-start = ((bf16[8,2,2,192,128]{4,3,2,1,0:T(8,128)(2,1)}), bf16[8,2,2,192,128]{4,3,2,1,0:T(8,128)(2,1)S(1)}, u32[]{:S(2)}, u32[]{:S(2)}) async-start(bf16[8,2,2,192,128]{4,3,2,1,0:T(8,128)(2,1)} %bitcast.7), calls=%async_computation | async-start | bytes 3145728 | tf_op jit(solution)/shard_map/all_to_all | solution.py:145
  52.0 39.0 %all-to-all-start.1 = ((bf16[8,2,320,128]{3,2,1,0:T(8,128)(2,1)}), bf16[8,2,320,128]{3,2,1,0:T(8,128)(2,1)}, u32[]{:S(2)}, u32[]{:S(2)}) async-start(bf16[8,2,320,128]{3,2,1,0:T(8,128)(2,1)} %bitcast.11), calls=%async_computation.1 | async-start | bytes 2621440 | tf_op jit(solution)/shard_map/all_to_all | solution.py:145
  58.4 63.3 %collective-permute-start.7 = (bf16[8,2,2,192,128]{4,3,2,1,0:T(8,128)(2,1)S(1)}, bf16[8,2,2,192,128]{4,3,2,1,0:T(8,128)(2,1)S(1)}, u32[]{:S(2)}, u32[]{:S(2)}) collective-permute-start(bf16[8,2,2,192,128]{4,3,2,1,0:T(8,128)(2,1)S(1)} %all-to-all-done.ao_ref), channel_id=1, source_target_pairs={{0,32},{32,0},{1,33},{33,1},{2,34},{34,2},{3,35},{35,3},{4,36},{36... | collective-permute-start | bytes 4718600 | tf_op jit(solution)/shard_map/ppermute | solution.py:42
  61.8 5.3 %collective-permute-start.13 = (bf16[2,2,192,128]{3,2,1,0:T(8,128)(2,1)S(1)}, bf16[2,2,192,128]{3,2,1,0:T(8,128)(2,1)}, u32[]{:S(2)}, u32[]{:S(2)}) collective-permute-start(bf16[2,2,192,128]{3,2,1,0:T(8,128)(2,1)S(1)} %get-tuple-element.38), channel_id=1, source_target_pairs={{0,1},{1,0},{2,3},{3,2},{4,5},{5,4},{6,7},{7,6},{8,9},{9,8},{10,11... | collective-permute-start | bytes 589832 | tf_op jit(solution)/shard_map/ppermute | solution.py:38
  63.1 17.9 %collective-permute-start.14 = (bf16[2,2,192,128]{3,2,1,0:T(8,128)(2,1)}, bf16[2,2,192,128]{3,2,1,0:T(8,128)(2,1)}, u32[]{:S(2)}, u32[]{:S(2)}) collective-permute-start(bf16[2,2,192,128]{3,2,1,0:T(8,128)(2,1)} %get-tuple-element.49), channel_id=1, source_target_pairs={{0,128},{1,129},{2,130},{3,131},{4,132},{5,133},{6,134},{7,135},{8... | collective-permute-start | bytes 589832 | tf_op jit(solution)/shard_map/ppermute | solution.py:38
  64.4 24.1 %collective-permute-start.15 = (bf16[2,2,192,128]{3,2,1,0:T(8,128)(2,1)}, bf16[2,2,192,128]{3,2,1,0:T(8,128)(2,1)}, u32[]{:S(2)}, u32[]{:S(2)}) collective-permute-start(bf16[2,2,192,128]{3,2,1,0:T(8,128)(2,1)} %get-tuple-element.49), channel_id=1, source_target_pairs={{0,129},{1,128},{2,131},{3,130},{4,133},{5,132},{6,135},{7,134},{8... | collective-permute-start | bytes 589832 | tf_op jit(solution)/shard_map/ppermute | solution.py:38
  65.7 26.3 %collective-permute-start.1 = (bf16[2,2,192,128]{3,2,1,0:T(8,128)(2,1)S(1)}, bf16[2,2,192,128]{3,2,1,0:T(8,128)(2,1)}, u32[]{:S(2)}, u32[]{:S(2)}) collective-permute-start(bf16[2,2,192,128]{3,2,1,0:T(8,128)(2,1)S(1)} %get-tuple-element.29), channel_id=1, source_target_pairs={{0,1},{1,0},{2,3},{3,2},{4,5},{5,4},{6,7},{7,6},{8,9},{9,8},{10,11... | collective-permute-start | bytes 589832 | tf_op jit(solution)/shard_map/ppermute | solution.py:38
  67.0 26.0 %collective-permute-start.2 = (bf16[2,2,192,128]{3,2,1,0:T(8,128)(2,1)}, bf16[2,2,192,128]{3,2,1,0:T(8,128)(2,1)}, u32[]{:S(2)}, u32[]{:S(2)}) collective-permute-start(bf16[2,2,192,128]{3,2,1,0:T(8,128)(2,1)} %get-tuple-element.51), channel_id=1, source_target_pairs={{0,128},{1,129},{2,130},{3,131},{4,132},{5,133},{6,134},{7,135},{8... | collective-permute-start | bytes 589832 | tf_op jit(solution)/shard_map/ppermute | solution.py:38
  88.5 35.6 %collective-permute-start.19 = (bf16[8,2,320,128]{3,2,1,0:T(8,128)(2,1)}, bf16[8,2,320,128]{3,2,1,0:T(8,128)(2,1)}, u32[]{:S(2)}, u32[]{:S(2)}) collective-permute-start(bf16[8,2,320,128]{3,2,1,0:T(8,128)(2,1)} %all_to_all.15.bo_ref), channel_id=1, source_target_pairs={{0,32},{32,0},{1,33},{33,1},{2,34},{34,2},{3,35},{35,3},{4,36},{36... | collective-permute-start | bytes 3932168 | tf_op jit(solution)/shard_map/ppermute | solution.py:42
  90.9 58.8 %collective-permute-start.8 = (bf16[8,2,320,128]{3,2,1,0:T(8,128)(2,1)}, bf16[8,2,320,128]{3,2,1,0:T(8,128)(2,1)}, u32[]{:S(2)}, u32[]{:S(2)}) collective-permute-start(bf16[8,2,320,128]{3,2,1,0:T(8,128)(2,1)} %all-to-all-done.1.bo_ref), channel_id=1, source_target_pairs={{0,32},{32,0},{1,33},{33,1},{2,34},{34,2},{3,35},{35,3},{4,36},{36... | collective-permute-start | bytes 3932168 | tf_op jit(solution)/shard_map/ppermute | solution.py:42
  92.0 29.7 %copy-start.1 = (bf16[2,2,2,192,128]{4,3,2,1,0:T(8,128)(2,1)}, bf16[2,2,2,192,128]{4,3,2,1,0:T(8,128)(2,1)S(1)}, u32[]{:S(2)}) copy-start(bf16[2,2,2,192,128]{4,3,2,1,0:T(8,128)(2,1)S(1)} %pad_maximum_fusion.1.u0) | copy-start | bytes 1179652
  92.0 11.3 %collective-permute-start.16 = (bf16[2,2,2,192,128]{4,3,2,1,0:T(8,128)(2,1)S(1)}, bf16[2,2,2,192,128]{4,3,2,1,0:T(8,128)(2,1)S(1)}, u32[]{:S(2)}, u32[]{:S(2)}) collective-permute-start(bf16[2,2,2,192,128]{4,3,2,1,0:T(8,128)(2,1)S(1)} %pad_maximum_fusion.1.u0), channel_id=1, source_target_pairs={{0,2},{2,4},{4,6},{6,0},{1,3},{3,5},{5,7},{7,1},{8,10},{10,12},{12... | collective-permute-start | bytes 1179656 | tf_op jit(solution)/shard_map/ppermute | solution.py:164
  93.1 9.9 %collective-permute-start.3 = (bf16[2,2,192,128]{3,2,1,0:T(8,128)(2,1)}, bf16[2,2,192,128]{3,2,1,0:T(8,128)(2,1)S(1)}, u32[]{:S(2)}, u32[]{:S(2)}) collective-permute-start(bf16[2,2,192,128]{3,2,1,0:T(8,128)(2,1)} %get-tuple-element.51), channel_id=1, source_target_pairs={{0,129},{1,128},{2,131},{3,130},{4,133},{5,132},{6,135},{7,134},{8... | collective-permute-start | bytes 589832 | tf_op jit(solution)/shard_map/ppermute | solution.py:38
  103.0 8.1 %collective-permute-start.17 = (bf16[2,2,2,192,128]{4,3,2,1,0:T(8,128)(2,1)S(1)}, bf16[2,2,2,192,128]{4,3,2,1,0:T(8,128)(2,1)S(1)}, u32[]{:S(2)}, u32[]{:S(2)}) collective-permute-start(bf16[2,2,2,192,128]{4,3,2,1,0:T(8,128)(2,1)S(1)} %pad_maximum_fusion.1.u0), channel_id=1, source_target_pairs={{0,4},{2,6},{4,0},{6,2},{1,5},{3,7},{5,1},{7,3},{8,12},{10,14},{12... | collective-permute-start | bytes 1179656 | tf_op jit(solution)/shard_map/ppermute | solution.py:164
  104.1 16.9 %collective-permute-start.18 = (bf16[2,2,2,192,128]{4,3,2,1,0:T(8,128)(2,1)S(1)}, bf16[2,2,2,192,128]{4,3,2,1,0:T(8,128)(2,1)S(1)}, u32[]{:S(2)}, u32[]{:S(2)}) collective-permute-start(bf16[2,2,2,192,128]{4,3,2,1,0:T(8,128)(2,1)S(1)} %pad_maximum_fusion.1.u0), channel_id=1, source_target_pairs={{0,6},{2,0},{4,2},{6,4},{1,7},{3,1},{5,3},{7,5},{8,14},{10,8},{12,... | collective-permute-start | bytes 1179656 | tf_op jit(solution)/shard_map/ppermute | solution.py:164
  111.9 29.1 %collective-permute-start.4 = (bf16[2,2,2,192,128]{4,3,2,1,0:T(8,128)(2,1)S(1)}, bf16[2,2,2,192,128]{4,3,2,1,0:T(8,128)(2,1)}, u32[]{:S(2)}, u32[]{:S(2)}) collective-permute-start(bf16[2,2,2,192,128]{4,3,2,1,0:T(8,128)(2,1)S(1)} %pad_maximum_fusion.u0), channel_id=1, source_target_pairs={{0,2},{2,4},{4,6},{6,0},{1,3},{3,5},{5,7},{7,1},{8,10},{10,12},{12... | collective-permute-start | bytes 1179656 | tf_op jit(solution)/shard_map/ppermute | solution.py:164
  121.7 23.9 %collective-permute-start.5 = (bf16[2,2,2,192,128]{4,3,2,1,0:T(8,128)(2,1)S(1)}, bf16[2,2,2,192,128]{4,3,2,1,0:T(8,128)(2,1)}, u32[]{:S(2)}, u32[]{:S(2)}) collective-permute-start(bf16[2,2,2,192,128]{4,3,2,1,0:T(8,128)(2,1)S(1)} %pad_maximum_fusion.u0), channel_id=1, source_target_pairs={{0,4},{2,6},{4,0},{6,2},{1,5},{3,7},{5,1},{7,3},{8,12},{10,14},{12... | collective-permute-start | bytes 1179656 | tf_op jit(solution)/shard_map/ppermute | solution.py:164
  121.7 23.9 %collective-permute-start.6 = (bf16[2,2,2,192,128]{4,3,2,1,0:T(8,128)(2,1)S(1)}, bf16[2,2,2,192,128]{4,3,2,1,0:T(8,128)(2,1)}, u32[]{:S(2)}, u32[]{:S(2)}) collective-permute-start(bf16[2,2,2,192,128]{4,3,2,1,0:T(8,128)(2,1)S(1)} %pad_maximum_fusion.u0), channel_id=1, source_target_pairs={{0,6},{2,0},{4,2},{6,4},{1,7},{3,1},{5,3},{7,5},{8,14},{10,8},{12,... | collective-permute-start | bytes 1179656 | tf_op jit(solution)/shard_map/ppermute | solution.py:164
  133.8 23.5 %collective-permute-start.20 = (f32[2,192,128]{2,1,0:T(8,128)S(1)}, f32[2,192,128]{2,1,0:T(8,128)S(1)}, u32[]{:S(2)}, u32[]{:S(2)}) collective-permute-start(f32[2,192,128]{2,1,0:T(8,128)S(1)} %get-tuple-element.43), channel_id=1, source_target_pairs={{0,0},{1,1},{2,2},{3,3},{4,4},{5,5},{6,6},{7,7},{8,32},{9,33},{10,... | collective-permute-start | bytes 589832 | tf_op jit(solution)/shard_map/ppermute | solution.py:38
  140.9 16.3 %collective-permute-start.21 = (f32[2,192,128]{2,1,0:T(8,128)S(1)}, f32[2,192,128]{2,1,0:T(8,128)S(1)}, u32[]{:S(2)}, u32[]{:S(2)}) collective-permute-start(f32[2,192,128]{2,1,0:T(8,128)S(1)} %get-tuple-element.44), channel_id=1, source_target_pairs={{0,8},{1,9},{2,10},{3,11},{4,12},{5,13},{6,14},{7,15},{8,40},{9,41... | collective-permute-start | bytes 589832 | tf_op jit(solution)/shard_map/ppermute | solution.py:38
  145.6 14.9 %collective-permute-start.22 = (f32[2,192,128]{2,1,0:T(8,128)S(1)}, f32[2,192,128]{2,1,0:T(8,128)S(1)}, u32[]{:S(2)}, u32[]{:S(2)}) collective-permute-start(f32[2,192,128]{2,1,0:T(8,128)S(1)} %get-tuple-element.45), channel_id=1, source_target_pairs={{0,16},{1,17},{2,18},{3,19},{4,20},{5,21},{6,22},{7,23},{8,48},{9,... | collective-permute-start | bytes 589832 | tf_op jit(solution)/shard_map/ppermute | solution.py:38
  145.6 17.5 %collective-permute-start.23 = (f32[2,192,128]{2,1,0:T(8,128)}, f32[2,192,128]{2,1,0:T(8,128)}, u32[]{:S(2)}, u32[]{:S(2)}) collective-permute-start(f32[2,192,128]{2,1,0:T(8,128)} %get-tuple-element.46), channel_id=1, source_target_pairs={{0,24},{1,25},{2,26},{3,27},{4,28},{5,29},{6,30},{7,31},{8,56},{9,... | collective-permute-start | bytes 589832 | tf_op jit(solution)/shard_map/ppermute | solution.py:38
  154.9 16.6 %collective-permute-start.10 = (f32[2,192,128]{2,1,0:T(8,128)}, f32[2,192,128]{2,1,0:T(8,128)S(1)}, u32[]{:S(2)}, u32[]{:S(2)}) collective-permute-start(f32[2,192,128]{2,1,0:T(8,128)} %get-tuple-element.35), channel_id=1, source_target_pairs={{0,8},{1,9},{2,10},{3,11},{4,12},{5,13},{6,14},{7,15},{8,40},{9,41... | collective-permute-start | bytes 589832 | tf_op jit(solution)/shard_map/ppermute | solution.py:38
  157.3 3.3 %copy-start.9 = (f32[2,192,128]{2,1,0:T(8,128)}, f32[2,192,128]{2,1,0:T(8,128)S(1)}, u32[]{:S(2)}) copy-start(f32[2,192,128]{2,1,0:T(8,128)S(1)} %collective-permute-done.20.refs_4_) | copy-start | bytes 589828
  157.3 14.2 %collective-permute-start.11 = (f32[2,192,128]{2,1,0:T(8,128)}, f32[2,192,128]{2,1,0:T(8,128)S(1)}, u32[]{:S(2)}, u32[]{:S(2)}) collective-permute-start(f32[2,192,128]{2,1,0:T(8,128)} %get-tuple-element.36), channel_id=1, source_target_pairs={{0,16},{1,17},{2,18},{3,19},{4,20},{5,21},{6,22},{7,23},{8,48},{9,... | collective-permute-start | bytes 589832 | tf_op jit(solution)/shard_map/ppermute | solution.py:38
  157.3 3.3 %copy-start.10 = (f32[2,192,128]{2,1,0:T(8,128)}, f32[2,192,128]{2,1,0:T(8,128)S(1)}, u32[]{:S(2)}) copy-start(f32[2,192,128]{2,1,0:T(8,128)S(1)} %collective-permute-done.21.refs_5_) | copy-start | bytes 589828
  157.3 19.7 %collective-permute-start.12 = (f32[2,192,128]{2,1,0:T(8,128)}, f32[2,192,128]{2,1,0:T(8,128)S(1)}, u32[]{:S(2)}, u32[]{:S(2)}) collective-permute-start(f32[2,192,128]{2,1,0:T(8,128)} %get-tuple-element.37), channel_id=1, source_target_pairs={{0,24},{1,25},{2,26},{3,27},{4,28},{5,29},{6,30},{7,31},{8,56},{9,... | collective-permute-start | bytes 589832 | tf_op jit(solution)/shard_map/ppermute | solution.py:38
  161.3 26.2 %collective-permute-start.9 = (f32[2,192,128]{2,1,0:T(8,128)}, f32[2,192,128]{2,1,0:T(8,128)S(1)}, u32[]{:S(2)}, u32[]{:S(2)}) collective-permute-start(f32[2,192,128]{2,1,0:T(8,128)} %get-tuple-element.34), channel_id=1, source_target_pairs={{0,0},{1,1},{2,2},{3,3},{4,4},{5,5},{6,6},{7,7},{8,32},{9,33},{10,... | collective-permute-start | bytes 589832 | tf_op jit(solution)/shard_map/ppermute | solution.py:38
  171.5 15.9 %copy-start.12 = (f32[2,192,128]{2,1,0:T(8,128)}, f32[2,192,128]{2,1,0:T(8,128)S(1)}, u32[]{:S(2)}) copy-start(f32[2,192,128]{2,1,0:T(8,128)S(1)} %collective-permute-done.10.refs_1_) | copy-start | bytes 589828
  171.5 15.9 %copy-start.13 = (f32[2,192,128]{2,1,0:T(8,128)}, f32[2,192,128]{2,1,0:T(8,128)S(1)}, u32[]{:S(2)}) copy-start(f32[2,192,128]{2,1,0:T(8,128)S(1)} %collective-permute-done.11.refs_2_) | copy-start | bytes 589828
  177.0 10.4 %copy-start.14 = (f32[2,192,128]{2,1,0:T(8,128)}, f32[2,192,128]{2,1,0:T(8,128)S(1)}, u32[]{:S(2)}) copy-start(f32[2,192,128]{2,1,0:T(8,128)S(1)} %collective-permute-done.12.refs_3_) | copy-start | bytes 589828
  (11 other events, 10.2 us)

commit v8 on v7

--- a/solution.py
+++ b/solution.py
@@ -42,11 +42,14 @@
     return lax.ppermute(value, "core", [(0, 1), (1, 0)])
 
 
-def contract(g, place, turned, a_own, a_peer, b_own, b_peer):
+def contract(g, place, turned, a_own, a_peer, b_own, b_peer, near=False, far=()):
     half, lanes = turned[0].shape[-2:]
     depth = 16 * lanes
-
-    def kernel(place_ref, u0, u1, u2, u3, ao_ref, ap_ref, bo_ref, bp_ref, o0, o1, o2, o3, left):
+    given = (a_own, a_peer, b_own, b_peer)
+    operands = given if not (near or far) else (given[:3] if near else (b_peer, *far))
+
+    def kernel(place_ref, u0, u1, u2, u3, *refs):
+        refs, outs, left = refs[: len(operands)], refs[len(operands) : -1], refs[-1]
         core, zh, zq, y = place_ref[0], place_ref[1], place_ref[2], place_ref[3]
         for step, u_ref in enumerate((u0, u1, u2, u3)):
             ys = (y + 4 - step) % 4
@@ -57,45 +60,64 @@
                         left[part * half : (part + 1) * half, pl.ds(start, lanes)] = u_ref[piece, xl, part]
 
         first = core == 0
-        for t, out in enumerate((o0, o1, o2, o3)):
+        gap = 3 * lanes - (8 * lanes - 2 * half) // 2
+        blank = jnp.zeros((gap, lanes), jnp.bfloat16)
+
+        def window(ref, i, part, early):
+            value = ref[i, part]
+            return jnp.where(early, jnp.concatenate([value, blank], 0), jnp.concatenate([blank, value], 0))
+
+        for t, out in enumerate(outs):
             x = (2 * zq + core) ^ t
-            rows = []
+            both = None
             for zr in range(2):
                 i = 2 * x + zr
-                parts = []
-                for part in range(2):
-                    ao, ap = ao_ref[i, g, part], ap_ref[i, g, part]
-                    bo, bp = bo_ref[i, part], bp_ref[i, part]
-                    parts.append(
-                        jnp.concatenate(
-                            [
-                                jnp.where(first, ao, ap),
-                                jnp.where(first, ap, ao),
-                                jnp.where(first, bo, bp),
-                                jnp.where(first, bp, bo),
-                            ],
-                            0,
-                        )
-                    )
-                rows.append(jnp.concatenate(parts, 1))
-            right = jnp.concatenate(rows, 0)
-            both = jnp.dot(left[...], right, preferred_element_type=jnp.float32)
-            out[0] = both[:half, :lanes] - both[half:, lanes:]
-            out[1] = both[:half, lanes:] + both[half:, :lanes]
+                base = 8 * zr * lanes
+                columns = []
+                if not far:
+                    ao_ref, ap_ref, bo_ref = refs[:3]
+                    top = []
+                    for part in range(2):
+                        ao, ap = ao_ref[i, g, part], ap_ref[i, g, part]
+                        top.append([jnp.where(first, ao, ap), jnp.where(first, ap, ao)])
+                if not (near or far):
+                    bp_ref = refs[3]
+                    for part in range(2):
+                        bo, bp = bo_ref[i, part], bp_ref[i, part]
+                        top[part] += [jnp.where(first, bo, bp), jnp.where(first, bp, bo)]
+                    columns.append((left[:, base : base + 8 * lanes], top))
+                elif near:
+                    columns.append((left[:, base : base + 3 * lanes], top))
+                if near or far:
+                    early = first if near else jnp.logical_not(first)
+                    start = pl.multiple_of(base + jnp.where(early, 3, 5) * lanes, lanes)
+                    ref = refs[2] if near else refs[0]
+                    rows = [[window(ref, i, part, early)] for part in range(2)]
+                    columns.append((left[:, pl.ds(start, 3 * lanes)], rows))
+                for lhs, rows in columns:
+                    rhs = jnp.concatenate([jnp.concatenate(r, 0) for r in rows], 1)
+                    term = jnp.dot(lhs, rhs, preferred_element_type=jnp.float32)
+                    both = term if both is None else both + term
+            real = both[:half, :lanes] - both[half:, lanes:]
+            imag = both[:half, lanes:] + both[half:, :lanes]
+            if far:
+                real, imag = refs[1 + t][0] + real, refs[1 + t][1] + imag
+            out[0] = real
+            out[1] = imag
 
     vmem = pl.BlockSpec(memory_space=pltpu.VMEM)
     result = jax.ShapeDtypeStruct((2, half, lanes), jnp.float32)
     return pl.pallas_call(
         kernel,
         out_shape=(result,) * 4,
-        in_specs=[pl.BlockSpec(memory_space=pltpu.SMEM)] + [vmem] * 8,
+        in_specs=[pl.BlockSpec(memory_space=pltpu.SMEM)] + [vmem] * (4 + len(operands)),
         out_specs=(vmem,) * 4,
         scratch_shapes=[pltpu.VMEM((2 * half, depth), jnp.bfloat16)],
         cost_estimate=pl.CostEstimate(
             flops=2 * 2 * half * depth * 8 * lanes, bytes_accessed=7 << 20, transcendentals=0
         ),
         compiler_params=pltpu.CompilerParams(vmem_limit_bytes=40 << 20),
-    )(place, *turned, a_own, a_peer, b_own, b_peer)
+    )(place, *turned, *operands)
 
 
 def finish(odd, wavelet, *blocks):
@@ -176,10 +198,11 @@
             for t, block in enumerate(blocks)
         ]
 
-    blocks = []
-    for g in range(2):
-        partial = contract(g, place, turned[g], a_own, a_peer, b_own[g], b_peer[g])
-        blocks.append(homeward(partial))
+    partial = contract(0, place, turned[0], a_own, a_peer, b_own[0], b_peer[0])
+    blocks = [homeward(partial)]
+    partial = contract(1, place, turned[1], a_own, a_peer, b_own[1], None, near=True)
+    partial = contract(1, place, turned[1], None, None, None, b_peer[1], far=partial)
+    blocks.append(homeward(partial))
     return finish(jnp.stack([x % 2]).astype(jnp.int32), wavelet, *blocks[0], *blocks[1])
 
 

time: 191 us -> 192 us (level)
  the two profiles are of different devices: /device:TPU:213 before, /device:TPU:35 now
where the time goes in v8:
time: 192 us; the launch traced here: 191 us
  starting transfers between devices  68.6 us (36%)
  waiting for transfers between devices  67.1 us (35%)
  blocking collectives  20 us (10%)
  Pallas kernels  14 us (7%)
  local copies, waits for them, and re-layouts  13.6 us (7%)
  other arithmetic  7.21 us (4%)
    ppermute x14, starting transfers between devices, send(): return lax.ppermute(value, AXES, moved(target))  40.9 us
    ppermute x14, waiting for transfers between devices, send(): return lax.ppermute(value, AXES, moved(target))  35.8 us
    all_to_all x1, blocking collectives, exchange(): lax.all_to_all(block, ('x', 'zr'), split_axis=0, concat_axis=0, tiled=True)  20 us
    all_to_all x2, waiting for transfers between devices, exchange(): lax.all_to_all(block, ('x', 'zr'), split_axis=0, concat_axis=0, tiled=True)  14.6 us
    ppermute x6, waiting for transfers between devices, turn(): lax.ppermute(pieces, 'y', [(i, (i + s) % 4) for i in range(4)])  13.7 us
    pallas_call x3, Pallas kernels, contract(): pl.pallas_call(kernel, out_shape=(result,) * 4, in_specs=[pl.BlockSpec(me...  11.7 us
    ppermute x6, starting transfers between devices, turn(): lax.ppermute(pieces, 'y', [(i, (i + s) % 4) for i in range(4)])  10.7 us
    all_to_all x2, starting transfers between devices, exchange(): lax.all_to_all(block, ('x', 'zr'), split_axis=0, concat_axis=0, tiled=True)  10.6 us
  transfers between devices with their start and end apart: 26, of which 12 were waited for; matrix products, arithmetic and copies ran while one was open for 4% of the time, Pallas kernels for 6%

profile of v8, /device:TPU:35, one launch (start us, length us, event | category | flops | bytes accessed | tf_op | source)
XLA Modules:
  0.0 190.8 jit_solution(18172692815861459212)
XLA Ops:
  2.3 3.0 %collective-permute-done = bf16[2,16,192,128]{3,2,1,0:T(8,128)(2,1)S(1)} collective-permute-done((bf16[2,16,192,128]{3,2,1,0:T(8,128)(2,1)S(1)}, bf16[2,16,192,128]{3,2,1,0:T(8,128)(2,1)S(1)}, u32[]{:S(2)}, u32[]{:S(2)}) %collective-permute-start) | collective-permute-done | bytes 1572896 | tf_op jit(solution)/shard_map/ppermute | solution.py:42
  8.2 5.2 %all-to-all-start = ((bf16[8,2,2,192,128]{4,3,2,1,0:T(8,128)(2,1)}), bf16[8,2,2,192,128]{4,3,2,1,0:T(8,128)(2,1)S(1)}, u32[]{:S(2)}, u32[]{:S(2)}) async-start(bf16[8,2,2,192,128]{4,3,2,1,0:T(8,128)(2,1)} %bitcast.7), calls=%async_computation | async-start | bytes 3145728 | tf_op jit(solution)/shard_map/all_to_all | solution.py:167
  14.6 2.7 %maximum_select_fusion = bf16[2,16,320,128]{3,2,1,0:T(8,128)(2,1)S(1)} fusion(bf16[2,16,192,128]{3,2,1,0:T(8,128)(2,1)S(1)} %collective-permute-done, bf16[2,16,128,128]{3,2,1,0:T(8,128)(2,1)S(1)} %slice-done, bf16[2,16,512,128]{3,2,1,0:T(8,128)(2,1)} %param.2, pred[]{:T(512)S(6)} %eq.12), kind=kLoop, calls=%fused_computation | loop fusion | flops 6553600 | bytes 7864321 | tf_op jit(solution)/shard_map/jit(_where)/select_n | solution.py:161
  18.8 14.6 %all-to-all-done.refs_0_ = bf16[8,2,2,192,128]{4,3,2,1,0:T(8,128)(2,1)S(1)} async-done(((bf16[8,2,2,192,128]{4,3,2,1,0:T(8,128)(2,1)}), bf16[8,2,2,192,128]{4,3,2,1,0:T(8,128)(2,1)S(1)}, u32[]{:S(2)}, u32[]{:S(2)}) %all-to-all-start) | async-done | bytes 1572896 | tf_op jit(solution)/shard_map/all_to_all | solution.py:167
  33.4 20.0 %all_to_all.15.refs_2_ = bf16[8,2,320,128]{3,2,1,0:T(8,128)(2,1)} all-to-all(bf16[8,2,320,128]{3,2,1,0:T(8,128)(2,1)S(1)} %bitcast.48), channel_id=1, replica_groups=mesh['zq'=2,'zr'=2,'core'=2,'x'=4,'y'=4,'zh'=2] {'x','zr'}, dimensions={0} | all-to-all | bytes 2621440 | tf_op jit(solution)/shard_map/all_to_all | solution.py:167
  53.4 5.5 %all-to-all-start.2 = ((bf16[8,2,320,128]{3,2,1,0:T(8,128)(2,1)}), bf16[8,2,320,128]{3,2,1,0:T(8,128)(2,1)}, u32[]{:S(2)}, u32[]{:S(2)}) async-start(bf16[8,2,320,128]{3,2,1,0:T(8,128)(2,1)} %bitcast.14), calls=%async_computation.2 | async-start | bytes 2621440 | tf_op jit(solution)/shard_map/all_to_all | solution.py:167
  58.9 2.5 %collective-permute-start.7 = (bf16[8,2,2,192,128]{4,3,2,1,0:T(8,128)(2,1)S(1)}, bf16[8,2,2,192,128]{4,3,2,1,0:T(8,128)(2,1)S(1)}, u32[]{:S(2)}, u32[]{:S(2)}) collective-permute-start(bf16[8,2,2,192,128]{4,3,2,1,0:T(8,128)(2,1)S(1)} %all-to-all-done.refs_0_), channel_id=1, source_target_pairs={{0,32},{32,0},{1,33},{33,1},{2,34},{34,2},{3,35},{35,3},{4,36},{36... | collective-permute-start | bytes 4718600 | tf_op jit(solution)/shard_map/ppermute | solution.py:42
  62.3 7.9 %collective-permute-start.1 = (bf16[2,2,192,128]{3,2,1,0:T(8,128)(2,1)S(1)}, bf16[2,2,192,128]{3,2,1,0:T(8,128)(2,1)}, u32[]{:S(2)}, u32[]{:S(2)}) collective-permute-start(bf16[2,2,192,128]{3,2,1,0:T(8,128)(2,1)S(1)} %get-tuple-element.33), channel_id=1, source_target_pairs={{0,1},{1,0},{2,3},{3,2},{4,5},{5,4},{6,7},{7,6},{8,9},{9,8},{10,11... | collective-permute-start | bytes 589832 | tf_op jit(solution)/shard_map/ppermute | solution.py:38
  70.2 2.0 %collective-permute-start.2 = (bf16[2,2,192,128]{3,2,1,0:T(8,128)(2,1)S(1)}, bf16[2,2,192,128]{3,2,1,0:T(8,128)(2,1)}, u32[]{:S(2)}, u32[]{:S(2)}) collective-permute-start(bf16[2,2,192,128]{3,2,1,0:T(8,128)(2,1)S(1)} %get-tuple-element.59), channel_id=1, source_target_pairs={{0,128},{1,129},{2,130},{3,131},{4,132},{5,133},{6,134},{7,135},{8... | collective-permute-start | bytes 589832 | tf_op jit(solution)/shard_map/ppermute | solution.py:38
  72.1 2.0 %collective-permute-start.3 = (bf16[2,2,192,128]{3,2,1,0:T(8,128)(2,1)S(1)}, bf16[2,2,192,128]{3,2,1,0:T(8,128)(2,1)}, u32[]{:S(2)}, u32[]{:S(2)}) collective-permute-start(bf16[2,2,192,128]{3,2,1,0:T(8,128)(2,1)S(1)} %get-tuple-element.59), channel_id=1, source_target_pairs={{0,129},{1,128},{2,131},{3,130},{4,133},{5,132},{6,135},{7,134},{8... | collective-permute-start | bytes 589832 | tf_op jit(solution)/shard_map/ppermute | solution.py:38
  74.1 3.1 %collective-permute-start.13 = (bf16[2,2,192,128]{3,2,1,0:T(8,128)(2,1)}, bf16[2,2,192,128]{3,2,1,0:T(8,128)(2,1)}, u32[]{:S(2)}, u32[]{:S(2)}) collective-permute-start(bf16[2,2,192,128]{3,2,1,0:T(8,128)(2,1)} %get-tuple-element.42), channel_id=1, source_target_pairs={{0,1},{1,0},{2,3},{3,2},{4,5},{5,4},{6,7},{7,6},{8,9},{9,8},{10,11... | collective-permute-start | bytes 589832 | tf_op jit(solution)/shard_map/ppermute | solution.py:38
  77.3 4.5 %collective-permute-done.1 = bf16[2,2,192,128]{3,2,1,0:T(8,128)(2,1)} collective-permute-done((bf16[2,2,192,128]{3,2,1,0:T(8,128)(2,1)S(1)}, bf16[2,2,192,128]{3,2,1,0:T(8,128)(2,1)}, u32[]{:S(2)}, u32[]{:S(2)}) %collective-permute-start.1) | collective-permute-done | bytes 196640 | tf_op jit(solution)/shard_map/ppermute | solution.py:38
  81.8 2.0 %collective-permute-start.14 = (bf16[2,2,192,128]{3,2,1,0:T(8,128)(2,1)}, bf16[2,2,192,128]{3,2,1,0:T(8,128)(2,1)}, u32[]{:S(2)}, u32[]{:S(2)}) collective-permute-start(bf16[2,2,192,128]{3,2,1,0:T(8,128)(2,1)} %get-tuple-element.57), channel_id=1, source_target_pairs={{0,128},{1,129},{2,130},{3,131},{4,132},{5,133},{6,134},{7,135},{8... | collective-permute-start | bytes 589832 | tf_op jit(solution)/shard_map/ppermute | solution.py:38
  83.7 6.5 %collective-permute-done.2 = bf16[2,2,192,128]{3,2,1,0:T(8,128)(2,1)} collective-permute-done((bf16[2,2,192,128]{3,2,1,0:T(8,128)(2,1)S(1)}, bf16[2,2,192,128]{3,2,1,0:T(8,128)(2,1)}, u32[]{:S(2)}, u32[]{:S(2)}) %collective-permute-start.2) | collective-permute-done | bytes 196640 | tf_op jit(solution)/shard_map/ppermute | solution.py:38
  90.3 2.8 %collective-permute-start.8 = (bf16[8,2,320,128]{3,2,1,0:T(8,128)(2,1)}, bf16[8,2,320,128]{3,2,1,0:T(8,128)(2,1)}, u32[]{:S(2)}, u32[]{:S(2)}) collective-permute-start(bf16[8,2,320,128]{3,2,1,0:T(8,128)(2,1)} %all_to_all.15.refs_2_), channel_id=1, source_target_pairs={{0,32},{32,0},{1,33},{33,1},{2,34},{34,2},{3,35},{35,3},{4,36},{36... | collective-permute-start | bytes 3932168 | tf_op jit(solution)/shard_map/ppermute | solution.py:42
  96.7 7.0 %collective-permute-start.15 = (bf16[2,2,192,128]{3,2,1,0:T(8,128)(2,1)}, bf16[2,2,192,128]{3,2,1,0:T(8,128)(2,1)S(1)}, u32[]{:S(2)}, u32[]{:S(2)}) collective-permute-start(bf16[2,2,192,128]{3,2,1,0:T(8,128)(2,1)} %get-tuple-element.57), channel_id=1, source_target_pairs={{0,129},{1,128},{2,131},{3,130},{4,133},{5,132},{6,135},{7,134},{8... | collective-permute-start | bytes 589832 | tf_op jit(solution)/shard_map/ppermute | solution.py:38
  103.7 4.1 %collective-permute-done.15 = bf16[2,2,192,128]{3,2,1,0:T(8,128)(2,1)S(1)} collective-permute-done((bf16[2,2,192,128]{3,2,1,0:T(8,128)(2,1)}, bf16[2,2,192,128]{3,2,1,0:T(8,128)(2,1)S(1)}, u32[]{:S(2)}, u32[]{:S(2)}) %collective-permute-start.15) | collective-permute-done | bytes 196640 | tf_op jit(solution)/shard_map/ppermute | solution.py:38
  107.8 2.9 %collective-permute-start.5 = (bf16[2,2,2,192,128]{4,3,2,1,0:T(8,128)(2,1)}, bf16[2,2,2,192,128]{4,3,2,1,0:T(8,128)(2,1)S(1)}, u32[]{:S(2)}, u32[]{:S(2)}) collective-permute-start(bf16[2,2,2,192,128]{4,3,2,1,0:T(8,128)(2,1)} %pad_maximum_fusion.u0), channel_id=1, source_target_pairs={{0,4},{2,6},{4,0},{6,2},{1,5},{3,7},{5,1},{7,3},{8,12},{10,14},{12... | collective-permute-start | bytes 1179656 | tf_op jit(solution)/shard_map/ppermute | solution.py:186
  112.6 6.2 %collective-permute-done.5.u2 = bf16[2,2,2,192,128]{4,3,2,1,0:T(8,128)(2,1)S(1)} collective-permute-done((bf16[2,2,2,192,128]{4,3,2,1,0:T(8,128)(2,1)}, bf16[2,2,2,192,128]{4,3,2,1,0:T(8,128)(2,1)S(1)}, u32[]{:S(2)}, u32[]{:S(2)}) %collective-permute-start.5) | collective-permute-done | bytes 393248 | tf_op jit(solution)/shard_map/ppermute | solution.py:186
  120.9 7.5 %collective-permute-done.6.u3 = bf16[2,2,2,192,128]{4,3,2,1,0:T(8,128)(2,1)S(1)} collective-permute-done((bf16[2,2,2,192,128]{4,3,2,1,0:T(8,128)(2,1)}, bf16[2,2,2,192,128]{4,3,2,1,0:T(8,128)(2,1)S(1)}, u32[]{:S(2)}, u32[]{:S(2)}) %collective-permute-start.6) | collective-permute-done | bytes 393248 | tf_op jit(solution)/shard_map/ppermute | solution.py:186
  130.8 2.8 %collective-permute-start.18 = (bf16[2,2,2,192,128]{4,3,2,1,0:T(8,128)(2,1)S(1)}, bf16[2,2,2,192,128]{4,3,2,1,0:T(8,128)(2,1)}, u32[]{:S(2)}, u32[]{:S(2)}) collective-permute-start(bf16[2,2,2,192,128]{4,3,2,1,0:T(8,128)(2,1)S(1)} %pad_maximum_fusion.1.u0), channel_id=1, source_target_pairs={{0,6},{2,0},{4,2},{6,4},{1,7},{3,1},{5,3},{7,5},{8,14},{10,8},{12,... | collective-permute-start | bytes 1179656 | tf_op jit(solution)/shard_map/ppermute | solution.py:186
  138.0 4.5 %shard_map.28 = (f32[2,192,128]{2,1,0:T(8,128)S(1)}, f32[2,192,128]{2,1,0:T(8,128)S(1)}, f32[2,192,128]{2,1,0:T(8,128)S(1)}, f32[2,192,128]{2,1,0:T(8,128)}) custom-call(s32[4]{0:T(128)S(1)} %pad_add_fusion.place_ref, bf16[2,2,2,192,128]{4,3,2,1,0:T(8,128)(2,1)} %pad_maximum_fusion.u0, bf16[2,2,2,192,128]{4,3,2,1,0:T(8,128)(2,1)S(1)} %copy-done.2, ...), custom_call_target="tpu_custom_call" | custom-call | flops 1610612736 | bytes 7340032 | tf_op jit(solution)/shard_map/pallas_call | solution.py:110
  144.7 6.3 %collective-permute-start.11 = (f32[2,192,128]{2,1,0:T(8,128)S(1)}, f32[2,192,128]{2,1,0:T(8,128)S(1)}, u32[]{:S(2)}, u32[]{:S(2)}) collective-permute-start(f32[2,192,128]{2,1,0:T(8,128)S(1)} %get-tuple-element.40), channel_id=1, source_target_pairs={{0,16},{1,17},{2,18},{3,19},{4,20},{5,21},{6,22},{7,23},{8,48},{9,... | collective-permute-start | bytes 589832 | tf_op jit(solution)/shard_map/ppermute | solution.py:38
  151.0 4.0 %shard_map.29 = (f32[2,192,128]{2,1,0:T(8,128)S(1)}, f32[2,192,128]{2,1,0:T(8,128)S(1)}, f32[2,192,128]{2,1,0:T(8,128)S(1)}, f32[2,192,128]{2,1,0:T(8,128)S(1)}) custom-call(s32[4]{0:T(128)S(1)} %pad_add_fusion.place_ref, bf16[2,2,2,192,128]{4,3,2,1,0:T(8,128)(2,1)S(1)} %pad_maximum_fusion.1.u0, bf16[2,2,2,192,128]{4,3,2,1,0:T(8,128)(2,1)} %collective-permute-done.16.u1, ...), custom_call_target="tpu_custom_call" | custom-call | flops 1610612736 | bytes 7340032 | tf_op jit(solution)/shard_map/pallas_call | solution.py:110
  155.1 3.1 %shard_map.30 = (f32[2,192,128]{2,1,0:T(8,128)S(1)}, f32[2,192,128]{2,1,0:T(8,128)S(1)}, f32[2,192,128]{2,1,0:T(8,128)S(1)}, f32[2,192,128]{2,1,0:T(8,128)S(1)}) custom-call(s32[4]{0:T(128)S(1)} %pad_add_fusion.place_ref, bf16[2,2,2,192,128]{4,3,2,1,0:T(8,128)(2,1)S(1)} %pad_maximum_fusion.1.u0, bf16[2,2,2,192,128]{4,3,2,1,0:T(8,128)(2,1)} %collective-permute-done.16.u1, ...), custom_call_target="tpu_custom_call" | custom-call | flops 1610612736 | bytes 7340032 | tf_op jit(solution)/shard_map/pallas_call | solution.py:110
  158.3 1.9 %collective-permute-start.20 = (f32[2,192,128]{2,1,0:T(8,128)S(1)}, f32[2,192,128]{2,1,0:T(8,128)S(1)}, u32[]{:S(2)}, u32[]{:S(2)}) collective-permute-start(f32[2,192,128]{2,1,0:T(8,128)S(1)} %get-tuple-element.51), channel_id=1, source_target_pairs={{0,0},{1,1},{2,2},{3,3},{4,4},{5,5},{6,6},{7,7},{8,32},{9,33},{10,... | collective-permute-start | bytes 589832 | tf_op jit(solution)/shard_map/ppermute | solution.py:38
  160.2 4.5 %collective-permute-start.21 = (f32[2,192,128]{2,1,0:T(8,128)S(1)}, f32[2,192,128]{2,1,0:T(8,128)S(1)}, u32[]{:S(2)}, u32[]{:S(2)}) collective-permute-start(f32[2,192,128]{2,1,0:T(8,128)S(1)} %get-tuple-element.52), channel_id=1, source_target_pairs={{0,8},{1,9},{2,10},{3,11},{4,12},{5,13},{6,14},{7,15},{8,40},{9,41... | collective-permute-start | bytes 589832 | tf_op jit(solution)/shard_map/ppermute | solution.py:38
  167.4 4.1 %collective-permute-done.20.refs_4_ = f32[2,192,128]{2,1,0:T(8,128)S(1)} collective-permute-done((f32[2,192,128]{2,1,0:T(8,128)S(1)}, f32[2,192,128]{2,1,0:T(8,128)S(1)}, u32[]{:S(2)}, u32[]{:S(2)}) %collective-permute-start.20) | collective-permute-done | bytes 196640 | tf_op jit(solution)/shard_map/ppermute | solution.py:38
  171.5 4.1 %collective-permute-done.21.refs_5_ = f32[2,192,128]{2,1,0:T(8,128)S(1)} collective-permute-done((f32[2,192,128]{2,1,0:T(8,128)S(1)}, f32[2,192,128]{2,1,0:T(8,128)S(1)}, u32[]{:S(2)}, u32[]{:S(2)}) %collective-permute-start.21) | collective-permute-done | bytes 196640 | tf_op jit(solution)/shard_map/ppermute | solution.py:38
  175.5 4.0 %collective-permute-done.22.refs_6_ = f32[2,192,128]{2,1,0:T(8,128)S(1)} collective-permute-done((f32[2,192,128]{2,1,0:T(8,128)S(1)}, f32[2,192,128]{2,1,0:T(8,128)S(1)}, u32[]{:S(2)}, u32[]{:S(2)}) %collective-permute-start.22) | collective-permute-done | bytes 196640 | tf_op jit(solution)/shard_map/ppermute | solution.py:38
  179.5 8.3 %collective-permute-done.23.refs_7_ = f32[2,192,128]{2,1,0:T(8,128)S(1)} collective-permute-done((f32[2,192,128]{2,1,0:T(8,128)S(1)}, f32[2,192,128]{2,1,0:T(8,128)S(1)}, u32[]{:S(2)}, u32[]{:S(2)}) %collective-permute-start.23) | collective-permute-done | bytes 196640 | tf_op jit(solution)/shard_map/ppermute | solution.py:38
  188.5 2.4 %shard_map.31 = bf16[2,2,384,128]{3,2,1,0:T(8,128)(2,1)} custom-call(s32[1]{0:T(128)} %bitcast.odd_ref, f32[2,2]{1,0:T(2,128)} %wave_ref.1, f32[2,192,128]{2,1,0:T(8,128)} %copy-done.7, f32[2,192,128]{2,1,0:T(8,128)} %copy-done.8, f32[2,192,128]{2,1,0:T(8,128)} %copy-done.9, f32[2,192,128]{2,1,0:T(8,128)} %copy-done.10, f32[2,192,128]{2,1,0:T(8,128)} %copy-done.11, ...), custom_call_target="tpu_custom_call" | custom-call | flops 786432 | bytes 2097152 | tf_op jit(solution)/shard_map/pallas_call | solution.py:137
  (70 shorter events, 28.7 us)
Async XLA Ops:
  1.5 3.8 %collective-permute-start = (bf16[2,16,192,128]{3,2,1,0:T(8,128)(2,1)S(1)}, bf16[2,16,192,128]{3,2,1,0:T(8,128)(2,1)S(1)}, u32[]{:S(2)}, u32[]{:S(2)}) collective-permute-start(bf16[2,16,192,128]{3,2,1,0:T(8,128)(2,1)S(1)} %constant_dynamic-slice_fusion), channel_id=1, source_target_pairs={{0,32},{32,0},{1,33},{33,1},{2,34},{34,2},{3,35},{35,3},{4,36},{36... | collective-permute-start | bytes 4718600 | tf_op jit(solution)/shard_map/ppermute | solution.py:42
  8.2 25.2 %all-to-all-start = ((bf16[8,2,2,192,128]{4,3,2,1,0:T(8,128)(2,1)}), bf16[8,2,2,192,128]{4,3,2,1,0:T(8,128)(2,1)S(1)}, u32[]{:S(2)}, u32[]{:S(2)}) async-start(bf16[8,2,2,192,128]{4,3,2,1,0:T(8,128)(2,1)} %bitcast.7), calls=%async_computation | async-start | bytes 3145728 | tf_op jit(solution)/shard_map/all_to_all | solution.py:167
  53.4 42.7 %all-to-all-start.2 = ((bf16[8,2,320,128]{3,2,1,0:T(8,128)(2,1)}), bf16[8,2,320,128]{3,2,1,0:T(8,128)(2,1)}, u32[]{:S(2)}, u32[]{:S(2)}) async-start(bf16[8,2,320,128]{3,2,1,0:T(8,128)(2,1)} %bitcast.14), calls=%async_computation.2 | async-start | bytes 2621440 | tf_op jit(solution)/shard_map/all_to_all | solution.py:167
  58.9 71.9 %collective-permute-start.7 = (bf16[8,2,2,192,128]{4,3,2,1,0:T(8,128)(2,1)S(1)}, bf16[8,2,2,192,128]{4,3,2,1,0:T(8,128)(2,1)S(1)}, u32[]{:S(2)}, u32[]{:S(2)}) collective-permute-start(bf16[8,2,2,192,128]{4,3,2,1,0:T(8,128)(2,1)S(1)} %all-to-all-done.refs_0_), channel_id=1, source_target_pairs={{0,32},{32,0},{1,33},{33,1},{2,34},{34,2},{3,35},{35,3},{4,36},{36... | collective-permute-start | bytes 4718600 | tf_op jit(solution)/shard_map/ppermute | solution.py:42
  62.3 19.5 %collective-permute-start.1 = (bf16[2,2,192,128]{3,2,1,0:T(8,128)(2,1)S(1)}, bf16[2,2,192,128]{3,2,1,0:T(8,128)(2,1)}, u32[]{:S(2)}, u32[]{:S(2)}) collective-permute-start(bf16[2,2,192,128]{3,2,1,0:T(8,128)(2,1)S(1)} %get-tuple-element.33), channel_id=1, source_target_pairs={{0,1},{1,0},{2,3},{3,2},{4,5},{5,4},{6,7},{7,6},{8,9},{9,8},{10,11... | collective-permute-start | bytes 589832 | tf_op jit(solution)/shard_map/ppermute | solution.py:38
  70.2 20.1 %collective-permute-start.2 = (bf16[2,2,192,128]{3,2,1,0:T(8,128)(2,1)S(1)}, bf16[2,2,192,128]{3,2,1,0:T(8,128)(2,1)}, u32[]{:S(2)}, u32[]{:S(2)}) collective-permute-start(bf16[2,2,192,128]{3,2,1,0:T(8,128)(2,1)S(1)} %get-tuple-element.59), channel_id=1, source_target_pairs={{0,128},{1,129},{2,130},{3,131},{4,132},{5,133},{6,134},{7,135},{8... | collective-permute-start | bytes 589832 | tf_op jit(solution)/shard_map/ppermute | solution.py:38
  72.1 18.1 %collective-permute-start.3 = (bf16[2,2,192,128]{3,2,1,0:T(8,128)(2,1)S(1)}, bf16[2,2,192,128]{3,2,1,0:T(8,128)(2,1)}, u32[]{:S(2)}, u32[]{:S(2)}) collective-permute-start(bf16[2,2,192,128]{3,2,1,0:T(8,128)(2,1)S(1)} %get-tuple-element.59), channel_id=1, source_target_pairs={{0,129},{1,128},{2,131},{3,130},{4,133},{5,132},{6,135},{7,134},{8... | collective-permute-start | bytes 589832 | tf_op jit(solution)/shard_map/ppermute | solution.py:38
  74.1 22.0 %collective-permute-start.13 = (bf16[2,2,192,128]{3,2,1,0:T(8,128)(2,1)}, bf16[2,2,192,128]{3,2,1,0:T(8,128)(2,1)}, u32[]{:S(2)}, u32[]{:S(2)}) collective-permute-start(bf16[2,2,192,128]{3,2,1,0:T(8,128)(2,1)} %get-tuple-element.42), channel_id=1, source_target_pairs={{0,1},{1,0},{2,3},{3,2},{4,5},{5,4},{6,7},{7,6},{8,9},{9,8},{10,11... | collective-permute-start | bytes 589832 | tf_op jit(solution)/shard_map/ppermute | solution.py:38
  81.8 14.9 %collective-permute-start.14 = (bf16[2,2,192,128]{3,2,1,0:T(8,128)(2,1)}, bf16[2,2,192,128]{3,2,1,0:T(8,128)(2,1)}, u32[]{:S(2)}, u32[]{:S(2)}) collective-permute-start(bf16[2,2,192,128]{3,2,1,0:T(8,128)(2,1)} %get-tuple-element.57), channel_id=1, source_target_pairs={{0,128},{1,129},{2,130},{3,131},{4,132},{5,133},{6,134},{7,135},{8... | collective-permute-start | bytes 589832 | tf_op jit(solution)/shard_map/ppermute | solution.py:38
  90.3 43.4 %collective-permute-start.8 = (bf16[8,2,320,128]{3,2,1,0:T(8,128)(2,1)}, bf16[8,2,320,128]{3,2,1,0:T(8,128)(2,1)}, u32[]{:S(2)}, u32[]{:S(2)}) collective-permute-start(bf16[8,2,320,128]{3,2,1,0:T(8,128)(2,1)} %all_to_all.15.refs_2_), channel_id=1, source_target_pairs={{0,32},{32,0},{1,33},{33,1},{2,34},{34,2},{3,35},{35,3},{4,36},{36... | collective-permute-start | bytes 3932168 | tf_op jit(solution)/shard_map/ppermute | solution.py:42
  94.9 15.9 %collective-permute-start.4 = (bf16[2,2,2,192,128]{4,3,2,1,0:T(8,128)(2,1)}, bf16[2,2,2,192,128]{4,3,2,1,0:T(8,128)(2,1)S(1)}, u32[]{:S(2)}, u32[]{:S(2)}) collective-permute-start(bf16[2,2,2,192,128]{4,3,2,1,0:T(8,128)(2,1)} %pad_maximum_fusion.u0), channel_id=1, source_target_pairs={{0,2},{2,4},{4,6},{6,0},{1,3},{3,5},{5,7},{7,1},{8,10},{10,12},{12... | collective-permute-start | bytes 1179656 | tf_op jit(solution)/shard_map/ppermute | solution.py:186
  96.2 59.0 %collective-permute-start.19 = (bf16[8,2,320,128]{3,2,1,0:T(8,128)(2,1)}, bf16[8,2,320,128]{3,2,1,0:T(8,128)(2,1)}, u32[]{:S(2)}, u32[]{:S(2)}) collective-permute-start(bf16[8,2,320,128]{3,2,1,0:T(8,128)(2,1)} %all-to-all-done.2.refs_2_), channel_id=1, source_target_pairs={{0,32},{32,0},{1,33},{33,1},{2,34},{34,2},{3,35},{35,3},{4,36},{36... | collective-permute-start | bytes 3932168 | tf_op jit(solution)/shard_map/ppermute | solution.py:42
  96.7 11.1 %collective-permute-start.15 = (bf16[2,2,192,128]{3,2,1,0:T(8,128)(2,1)}, bf16[2,2,192,128]{3,2,1,0:T(8,128)(2,1)S(1)}, u32[]{:S(2)}, u32[]{:S(2)}) collective-permute-start(bf16[2,2,192,128]{3,2,1,0:T(8,128)(2,1)} %get-tuple-element.57), channel_id=1, source_target_pairs={{0,129},{1,128},{2,131},{3,130},{4,133},{5,132},{6,135},{7,134},{8... | collective-permute-start | bytes 589832 | tf_op jit(solution)/shard_map/ppermute | solution.py:38
  107.8 11.0 %collective-permute-start.5 = (bf16[2,2,2,192,128]{4,3,2,1,0:T(8,128)(2,1)}, bf16[2,2,2,192,128]{4,3,2,1,0:T(8,128)(2,1)S(1)}, u32[]{:S(2)}, u32[]{:S(2)}) collective-permute-start(bf16[2,2,2,192,128]{4,3,2,1,0:T(8,128)(2,1)} %pad_maximum_fusion.u0), channel_id=1, source_target_pairs={{0,4},{2,6},{4,0},{6,2},{1,5},{3,7},{5,1},{7,3},{8,12},{10,14},{12... | collective-permute-start | bytes 1179656 | tf_op jit(solution)/shard_map/ppermute | solution.py:186
  110.7 1.9 copy-start.1
  110.7 17.7 %collective-permute-start.6 = (bf16[2,2,2,192,128]{4,3,2,1,0:T(8,128)(2,1)}, bf16[2,2,2,192,128]{4,3,2,1,0:T(8,128)(2,1)S(1)}, u32[]{:S(2)}, u32[]{:S(2)}) collective-permute-start(bf16[2,2,2,192,128]{4,3,2,1,0:T(8,128)(2,1)} %pad_maximum_fusion.u0), channel_id=1, source_target_pairs={{0,6},{2,0},{4,2},{6,4},{1,7},{3,1},{5,3},{7,5},{8,14},{10,8},{12,... | collective-permute-start | bytes 1179656 | tf_op jit(solution)/shard_map/ppermute | solution.py:186
  119.6 24.8 %collective-permute-start.16 = (bf16[2,2,2,192,128]{4,3,2,1,0:T(8,128)(2,1)S(1)}, bf16[2,2,2,192,128]{4,3,2,1,0:T(8,128)(2,1)}, u32[]{:S(2)}, u32[]{:S(2)}) collective-permute-start(bf16[2,2,2,192,128]{4,3,2,1,0:T(8,128)(2,1)S(1)} %pad_maximum_fusion.1.u0), channel_id=1, source_target_pairs={{0,2},{2,4},{4,6},{6,0},{1,3},{3,5},{5,7},{7,1},{8,10},{10,12},{12... | collective-permute-start | bytes 1179656 | tf_op jit(solution)/shard_map/ppermute | solution.py:186
  129.2 15.5 %collective-permute-start.17 = (bf16[2,2,2,192,128]{4,3,2,1,0:T(8,128)(2,1)S(1)}, bf16[2,2,2,192,128]{4,3,2,1,0:T(8,128)(2,1)}, u32[]{:S(2)}, u32[]{:S(2)}) collective-permute-start(bf16[2,2,2,192,128]{4,3,2,1,0:T(8,128)(2,1)S(1)} %pad_maximum_fusion.1.u0), channel_id=1, source_target_pairs={{0,4},{2,6},{4,0},{6,2},{1,5},{3,7},{5,1},{7,3},{8,12},{10,14},{12... | collective-permute-start | bytes 1179656 | tf_op jit(solution)/shard_map/ppermute | solution.py:186
  130.8 20.3 %collective-permute-start.18 = (bf16[2,2,2,192,128]{4,3,2,1,0:T(8,128)(2,1)S(1)}, bf16[2,2,2,192,128]{4,3,2,1,0:T(8,128)(2,1)}, u32[]{:S(2)}, u32[]{:S(2)}) collective-permute-start(bf16[2,2,2,192,128]{4,3,2,1,0:T(8,128)(2,1)S(1)} %pad_maximum_fusion.1.u0), channel_id=1, source_target_pairs={{0,6},{2,0},{4,2},{6,4},{1,7},{3,1},{5,3},{7,5},{8,14},{10,8},{12,... | collective-permute-start | bytes 1179656 | tf_op jit(solution)/shard_map/ppermute | solution.py:186
  142.5 17.7 %collective-permute-start.9 = (f32[2,192,128]{2,1,0:T(8,128)S(1)}, f32[2,192,128]{2,1,0:T(8,128)S(1)}, u32[]{:S(2)}, u32[]{:S(2)}) collective-permute-start(f32[2,192,128]{2,1,0:T(8,128)S(1)} %get-tuple-element.38), channel_id=1, source_target_pairs={{0,0},{1,1},{2,2},{3,3},{4,4},{5,5},{6,6},{7,7},{8,32},{9,33},{10,... | collective-permute-start | bytes 589832 | tf_op jit(solution)/shard_map/ppermute | solution.py:38
  144.4 20.3 %collective-permute-start.10 = (f32[2,192,128]{2,1,0:T(8,128)S(1)}, f32[2,192,128]{2,1,0:T(8,128)S(1)}, u32[]{:S(2)}, u32[]{:S(2)}) collective-permute-start(f32[2,192,128]{2,1,0:T(8,128)S(1)} %get-tuple-element.39), channel_id=1, source_target_pairs={{0,8},{1,9},{2,10},{3,11},{4,12},{5,13},{6,14},{7,15},{8,40},{9,41... | collective-permute-start | bytes 589832 | tf_op jit(solution)/shard_map/ppermute | solution.py:38
  144.7 21.5 %collective-permute-start.11 = (f32[2,192,128]{2,1,0:T(8,128)S(1)}, f32[2,192,128]{2,1,0:T(8,128)S(1)}, u32[]{:S(2)}, u32[]{:S(2)}) collective-permute-start(f32[2,192,128]{2,1,0:T(8,128)S(1)} %get-tuple-element.40), channel_id=1, source_target_pairs={{0,16},{1,17},{2,18},{3,19},{4,20},{5,21},{6,22},{7,23},{8,48},{9,... | collective-permute-start | bytes 589832 | tf_op jit(solution)/shard_map/ppermute | solution.py:38
  155.0 12.3 %collective-permute-start.12 = (f32[2,192,128]{2,1,0:T(8,128)}, f32[2,192,128]{2,1,0:T(8,128)S(1)}, u32[]{:S(2)}, u32[]{:S(2)}) collective-permute-start(f32[2,192,128]{2,1,0:T(8,128)} %get-tuple-element.41), channel_id=1, source_target_pairs={{0,24},{1,25},{2,26},{3,27},{4,28},{5,29},{6,30},{7,31},{8,56},{9,... | collective-permute-start | bytes 589832 | tf_op jit(solution)/shard_map/ppermute | solution.py:38
  158.3 13.2 %collective-permute-start.20 = (f32[2,192,128]{2,1,0:T(8,128)S(1)}, f32[2,192,128]{2,1,0:T(8,128)S(1)}, u32[]{:S(2)}, u32[]{:S(2)}) collective-permute-start(f32[2,192,128]{2,1,0:T(8,128)S(1)} %get-tuple-element.51), channel_id=1, source_target_pairs={{0,0},{1,1},{2,2},{3,3},{4,4},{5,5},{6,6},{7,7},{8,32},{9,33},{10,... | collective-permute-start | bytes 589832 | tf_op jit(solution)/shard_map/ppermute | solution.py:38
  160.2 6.0 %copy-start.7 = (f32[2,192,128]{2,1,0:T(8,128)}, f32[2,192,128]{2,1,0:T(8,128)S(1)}, u32[]{:S(2)}) copy-start(f32[2,192,128]{2,1,0:T(8,128)S(1)} %collective-permute-done.9.refs_0_) | copy-start | bytes 589828
  160.2 15.3 %collective-permute-start.21 = (f32[2,192,128]{2,1,0:T(8,128)S(1)}, f32[2,192,128]{2,1,0:T(8,128)S(1)}, u32[]{:S(2)}, u32[]{:S(2)}) collective-permute-start(f32[2,192,128]{2,1,0:T(8,128)S(1)} %get-tuple-element.52), channel_id=1, source_target_pairs={{0,8},{1,9},{2,10},{3,11},{4,12},{5,13},{6,14},{7,15},{8,40},{9,41... | collective-permute-start | bytes 589832 | tf_op jit(solution)/shard_map/ppermute | solution.py:38
  164.7 14.8 %collective-permute-start.22 = (f32[2,192,128]{2,1,0:T(8,128)S(1)}, f32[2,192,128]{2,1,0:T(8,128)S(1)}, u32[]{:S(2)}, u32[]{:S(2)}) collective-permute-start(f32[2,192,128]{2,1,0:T(8,128)S(1)} %get-tuple-element.53), channel_id=1, source_target_pairs={{0,16},{1,17},{2,18},{3,19},{4,20},{5,21},{6,22},{7,23},{8,48},{9,... | collective-permute-start | bytes 589832 | tf_op jit(solution)/shard_map/ppermute | solution.py:38
  166.9 20.9 %collective-permute-start.23 = (f32[2,192,128]{2,1,0:T(8,128)S(1)}, f32[2,192,128]{2,1,0:T(8,128)S(1)}, u32[]{:S(2)}, u32[]{:S(2)}) collective-permute-start(f32[2,192,128]{2,1,0:T(8,128)S(1)} %get-tuple-element.54), channel_id=1, source_target_pairs={{0,24},{1,25},{2,26},{3,27},{4,28},{5,29},{6,30},{7,31},{8,56},{9,... | collective-permute-start | bytes 589832 | tf_op jit(solution)/shard_map/ppermute | solution.py:38
  167.4 20.4 %copy-start.10 = (f32[2,192,128]{2,1,0:T(8,128)}, f32[2,192,128]{2,1,0:T(8,128)S(1)}, u32[]{:S(2)}) copy-start(f32[2,192,128]{2,1,0:T(8,128)S(1)} %collective-permute-done.12.refs_3_) | copy-start | bytes 589828
  171.5 16.3 %copy-start.11 = (f32[2,192,128]{2,1,0:T(8,128)}, f32[2,192,128]{2,1,0:T(8,128)S(1)}, u32[]{:S(2)}) copy-start(f32[2,192,128]{2,1,0:T(8,128)S(1)} %collective-permute-done.20.refs_4_) | copy-start | bytes 589828
  175.5 12.3 %copy-start.12 = (f32[2,192,128]{2,1,0:T(8,128)}, f32[2,192,128]{2,1,0:T(8,128)S(1)}, u32[]{:S(2)}) copy-start(f32[2,192,128]{2,1,0:T(8,128)S(1)} %collective-permute-done.21.refs_5_) | copy-start | bytes 589828
  179.5 8.3 %copy-start.13 = (f32[2,192,128]{2,1,0:T(8,128)}, f32[2,192,128]{2,1,0:T(8,128)S(1)}, u32[]{:S(2)}) copy-start(f32[2,192,128]{2,1,0:T(8,128)S(1)} %collective-permute-done.22.refs_6_) | copy-start | bytes 589828
  (10 other events, 10.0 us)

commit v9 on v7

--- a/solution.py
+++ b/solution.py
@@ -42,11 +42,11 @@
     return lax.ppermute(value, "core", [(0, 1), (1, 0)])
 
 
-def contract(g, place, turned, a_own, a_peer, b_own, b_peer):
+def contract(g, k, place, turned, a_own, a_peer, b_own, b_peer):
     half, lanes = turned[0].shape[-2:]
     depth = 16 * lanes
 
-    def kernel(place_ref, u0, u1, u2, u3, ao_ref, ap_ref, bo_ref, bp_ref, o0, o1, o2, o3, left):
+    def kernel(place_ref, u0, u1, u2, u3, ao_ref, ap_ref, bo_ref, bp_ref, o0, o1, left):
         core, zh, zq, y = place_ref[0], place_ref[1], place_ref[2], place_ref[3]
         for step, u_ref in enumerate((u0, u1, u2, u3)):
             ys = (y + 4 - step) % 4
@@ -57,7 +57,7 @@
                         left[part * half : (part + 1) * half, pl.ds(start, lanes)] = u_ref[piece, xl, part]
 
         first = core == 0
-        for t, out in enumerate((o0, o1, o2, o3)):
+        for t, out in ((k, o0), (k + 2, o1)):
             x = (2 * zq + core) ^ t
             rows = []
             for zr in range(2):
@@ -87,38 +87,41 @@
     result = jax.ShapeDtypeStruct((2, half, lanes), jnp.float32)
     return pl.pallas_call(
         kernel,
-        out_shape=(result,) * 4,
+        out_shape=(result,) * 2,
         in_specs=[pl.BlockSpec(memory_space=pltpu.SMEM)] + [vmem] * 8,
-        out_specs=(vmem,) * 4,
+        out_specs=(vmem,) * 2,
         scratch_shapes=[pltpu.VMEM((2 * half, depth), jnp.bfloat16)],
         cost_estimate=pl.CostEstimate(
-            flops=2 * 2 * half * depth * 8 * lanes, bytes_accessed=7 << 20, transcendentals=0
+            flops=2 * 2 * half * depth * 4 * lanes, bytes_accessed=7 << 20, transcendentals=0
         ),
         compiler_params=pltpu.CompilerParams(vmem_limit_bytes=40 << 20),
     )(place, *turned, a_own, a_peer, b_own, b_peer)
 
 
-def finish(odd, wavelet, *blocks):
+def finish(g, k, odd, wavelet, blocks, prior=()):
     half, lanes = blocks[0].shape[1:]
 
-    def kernel(odd_ref, wave_ref, *refs):
-        for g in range(2):
-            wave_real, wave_imag = wave_ref[0, g], wave_ref[1, g]
-            for t in range(2):
-                start = pl.multiple_of((odd_ref[0] ^ t) * half, half)
-                one, two = refs[4 * g + t], refs[4 * g + t + 2]
-                real, imag = one[0] + two[0], one[1] + two[1]
-                refs[8][0, g, pl.ds(start, half)] = (-(wave_real * real - wave_imag * imag)).astype(jnp.bfloat16)
-                refs[8][1, g, pl.ds(start, half)] = (-(wave_real * imag + wave_imag * real)).astype(jnp.bfloat16)
-
-    smem, vmem = pl.BlockSpec(memory_space=pltpu.SMEM), pl.BlockSpec(memory_space=pltpu.VMEM)
+    def kernel(odd_ref, wave_ref, one, two, *refs):
+        wave_real, wave_imag = wave_ref[0, g], wave_ref[1, g]
+        out = refs[-1]
+        real, imag = one[0] + two[0], one[1] + two[1]
+        out[0, 0] = (-(wave_real * real - wave_imag * imag)).astype(jnp.bfloat16)
+        out[1, 0] = (-(wave_real * imag + wave_imag * real)).astype(jnp.bfloat16)
+
+    whole = pl.BlockSpec((2, half, lanes), lambda i, odd_ref: (0, 0, 0))
     return pl.pallas_call(
         kernel,
+        grid_spec=pltpu.PrefetchScalarGridSpec(
+            num_scalar_prefetch=1,
+            grid=(1,),
+            in_specs=[pl.BlockSpec(memory_space=pltpu.SMEM), whole, whole]
+            + [pl.BlockSpec(memory_space=pl.ANY)] * len(prior),
+            out_specs=pl.BlockSpec((2, 1, half, lanes), lambda i, odd_ref: (0, g, odd_ref[0] ^ k, 0)),
+        ),
         out_shape=jax.ShapeDtypeStruct((2, 2, 2 * half, lanes), jnp.bfloat16),
-        in_specs=[smem, smem] + [vmem] * 8,
-        out_specs=vmem,
-        cost_estimate=pl.CostEstimate(flops=8 * 4 * half * lanes, bytes_accessed=2 << 20, transcendentals=0),
-    )(odd, wavelet, *blocks)
+        input_output_aliases={4: 0} if prior else {},
+        cost_estimate=pl.CostEstimate(flops=8 * half * lanes, bytes_accessed=1 << 20, transcendentals=0),
+    )(odd, wavelet, *blocks, *prior)
 
 
 def step(spectra, wavelet):
@@ -167,20 +170,22 @@
 
     turned = [turn(g) for g in range(2)]
 
-    def homeward(blocks):
+    def homeward(k, blocks):
         return [
-            send(
-                block,
-                lambda q, r, c, x, y, h: (r, x // 2, x % 2, (2 * q + c) ^ t, y, h),
-            )
-            for t, block in enumerate(blocks)
+            send(block, lambda q, r, c, x, y, h: (r, x // 2, x % 2, (2 * q + c) ^ t, y, h))
+            for t, block in zip((k, k + 2), blocks)
         ]
 
-    blocks = []
+    arrived = []
     for g in range(2):
-        partial = contract(g, place, turned[g], a_own, a_peer, b_own[g], b_peer[g])
-        blocks.append(homeward(partial))
-    return finish(jnp.stack([x % 2]).astype(jnp.int32), wavelet, *blocks[0], *blocks[1])
+        for k in range(2):
+            partial = contract(g, k, place, turned[g], a_own, a_peer, b_own[g], b_peer[g])
+            arrived.append((g, k, homeward(k, partial)))
+    odd = jnp.stack([x % 2]).astype(jnp.int32)
+    result = ()
+    for g, k, blocks in arrived:
+        result = (finish(g, k, odd, wavelet, blocks, result),)
+    return result[0]
 
 
 def solution(mesh):

time: 191 us -> 195 us (1.021)
  the two profiles are of different devices: /device:TPU:213 before, /device:TPU:66 now
where the time goes in v9:
time: 195 us; the launch traced here: 194 us
  waiting for transfers between devices  64 us (33%)
  starting transfers between devices  62.1 us (32%)
  Pallas kernels  21.9 us (11%)
  blocking collectives  21.3 us (11%)
  local copies, waits for them, and re-layouts  16 us (8%)
  other arithmetic  8.24 us (4%)
    ppermute x14, waiting for transfers between devices, send(): return lax.ppermute(value, AXES, moved(target))  41 us
    ppermute x14, starting transfers between devices, send(): return lax.ppermute(value, AXES, moved(target))  34.1 us
    all_to_all x1, blocking collectives, exchange(): lax.all_to_all(block, ('x', 'zr'), split_axis=0, concat_axis=0, tiled=True)  21.3 us
    ppermute x6, starting transfers between devices, turn(): lax.ppermute(pieces, 'y', [(i, (i + s) % 4) for i in range(4)])  15.2 us
    pallas_call x4, Pallas kernels, contract(): pl.pallas_call(kernel, out_shape=(result,) * 2, in_specs=[pl.BlockSpec(me...  15.1 us
    all_to_all x2, waiting for transfers between devices, exchange(): lax.all_to_all(block, ('x', 'zr'), split_axis=0, concat_axis=0, tiled=True)  14.5 us
    all_to_all x2, starting transfers between devices, exchange(): lax.all_to_all(block, ('x', 'zr'), split_axis=0, concat_axis=0, tiled=True)  12.1 us
    unnamed x32, local copies, waits for them, and re-layouts  10.9 us
  transfers between devices with their start and end apart: 26, of which 9 were waited for; matrix products, arithmetic and copies ran while one was open for 5% of the time, Pallas kernels for 10%

profile of v9, /device:TPU:66, one launch (start us, length us, event | category | flops | bytes accessed | tf_op | source)
XLA Modules:
  0.0 193.7 jit_solution(12671912580167224951)
XLA Ops:
  1.6 3.4 %collective-permute-done = bf16[2,16,192,128]{3,2,1,0:T(8,128)(2,1)S(1)} collective-permute-done((bf16[2,16,192,128]{3,2,1,0:T(8,128)(2,1)S(1)}, bf16[2,16,192,128]{3,2,1,0:T(8,128)(2,1)S(1)}, u32[]{:S(2)}, u32[]{:S(2)}) %collective-permute-start) | collective-permute-done | bytes 1572896 | tf_op jit(solution)/shard_map/ppermute | solution.py:42
  7.9 6.2 %all-to-all-start = ((bf16[8,2,2,192,128]{4,3,2,1,0:T(8,128)(2,1)}), bf16[8,2,2,192,128]{4,3,2,1,0:T(8,128)(2,1)S(1)}, u32[]{:S(2)}, u32[]{:S(2)}) async-start(bf16[8,2,2,192,128]{4,3,2,1,0:T(8,128)(2,1)} %bitcast.7), calls=%async_computation | async-start | bytes 3145728 | tf_op jit(solution)/shard_map/all_to_all | solution.py:148
  15.3 2.7 %maximum_select_fusion = bf16[2,16,320,128]{3,2,1,0:T(8,128)(2,1)S(1)} fusion(bf16[2,16,192,128]{3,2,1,0:T(8,128)(2,1)S(1)} %collective-permute-done, bf16[2,16,128,128]{3,2,1,0:T(8,128)(2,1)S(1)} %slice-done, bf16[2,16,512,128]{3,2,1,0:T(8,128)(2,1)} %param.2, pred[]{:T(512)S(6)} %eq.12), kind=kLoop, calls=%fused_computation | loop fusion | flops 6553600 | bytes 7864321 | tf_op jit(solution)/shard_map/jit(_where)/select_n | solution.py:142
  19.5 14.5 %all-to-all-done.ao_ref = bf16[8,2,2,192,128]{4,3,2,1,0:T(8,128)(2,1)S(1)} async-done(((bf16[8,2,2,192,128]{4,3,2,1,0:T(8,128)(2,1)}), bf16[8,2,2,192,128]{4,3,2,1,0:T(8,128)(2,1)S(1)}, u32[]{:S(2)}, u32[]{:S(2)}) %all-to-all-start) | async-done | bytes 1572896 | tf_op jit(solution)/shard_map/all_to_all | solution.py:148
  34.0 21.3 %all_to_all.15.bo_ref = bf16[8,2,320,128]{3,2,1,0:T(8,128)(2,1)} all-to-all(bf16[8,2,320,128]{3,2,1,0:T(8,128)(2,1)S(1)} %bitcast.48), channel_id=1, replica_groups=mesh['zq'=2,'zr'=2,'core'=2,'x'=4,'y'=4,'zh'=2] {'x','zr'}, dimensions={0} | all-to-all | bytes 2621440 | tf_op jit(solution)/shard_map/all_to_all | solution.py:148
  55.3 5.9 %all-to-all-start.1 = ((bf16[8,2,320,128]{3,2,1,0:T(8,128)(2,1)}), bf16[8,2,320,128]{3,2,1,0:T(8,128)(2,1)}, u32[]{:S(2)}, u32[]{:S(2)}) async-start(bf16[8,2,320,128]{3,2,1,0:T(8,128)(2,1)} %bitcast.14), calls=%async_computation.1 | async-start | bytes 2621440 | tf_op jit(solution)/shard_map/all_to_all | solution.py:148
  68.6 16.5 %collective-permute-done.14 = bf16[2,2,192,128]{3,2,1,0:T(8,128)(2,1)} collective-permute-done((bf16[2,2,192,128]{3,2,1,0:T(8,128)(2,1)}, bf16[2,2,192,128]{3,2,1,0:T(8,128)(2,1)}, u32[]{:S(2)}, u32[]{:S(2)}) %collective-permute-start.14) | collective-permute-done | bytes 196640 | tf_op jit(solution)/shard_map/ppermute | solution.py:38
  85.1 1.8 select_bitcast_fusion
  88.5 1.7 collective-permute-start.16
  90.2 2.6 %collective-permute-done.2 = bf16[2,2,192,128]{3,2,1,0:T(8,128)(2,1)} collective-permute-done((bf16[2,2,192,128]{3,2,1,0:T(8,128)(2,1)}, bf16[2,2,192,128]{3,2,1,0:T(8,128)(2,1)}, u32[]{:S(2)}, u32[]{:S(2)}) %collective-permute-start.2) | collective-permute-done | bytes 196640 | tf_op jit(solution)/shard_map/ppermute | solution.py:38
  94.0 8.6 %collective-permute-done.3 = bf16[2,2,192,128]{3,2,1,0:T(8,128)(2,1)S(1)} collective-permute-done((bf16[2,2,192,128]{3,2,1,0:T(8,128)(2,1)}, bf16[2,2,192,128]{3,2,1,0:T(8,128)(2,1)S(1)}, u32[]{:S(2)}, u32[]{:S(2)}) %collective-permute-start.3) | collective-permute-done | bytes 196640 | tf_op jit(solution)/shard_map/ppermute | solution.py:38
  102.6 3.2 %collective-permute-start.17 = (bf16[2,2,2,192,128]{4,3,2,1,0:T(8,128)(2,1)S(1)}, bf16[2,2,2,192,128]{4,3,2,1,0:T(8,128)(2,1)S(1)}, u32[]{:S(2)}, u32[]{:S(2)}) collective-permute-start(bf16[2,2,2,192,128]{4,3,2,1,0:T(8,128)(2,1)S(1)} %pad_maximum_fusion.1.u0), channel_id=1, source_target_pairs={{0,4},{2,6},{4,0},{6,2},{1,5},{3,7},{5,1},{7,3},{8,12},{10,14},{12... | collective-permute-start | bytes 1179656 | tf_op jit(solution)/shard_map/ppermute | solution.py:167
  108.7 4.2 %collective-permute-done.17.u2 = bf16[2,2,2,192,128]{4,3,2,1,0:T(8,128)(2,1)S(1)} collective-permute-done((bf16[2,2,2,192,128]{4,3,2,1,0:T(8,128)(2,1)S(1)}, bf16[2,2,2,192,128]{4,3,2,1,0:T(8,128)(2,1)S(1)}, u32[]{:S(2)}, u32[]{:S(2)}) %collective-permute-start.17) | collective-permute-done | bytes 393248 | tf_op jit(solution)/shard_map/ppermute | solution.py:167
  113.6 4.2 %collective-permute-start.4 = (bf16[2,2,2,192,128]{4,3,2,1,0:T(8,128)(2,1)S(1)}, bf16[2,2,2,192,128]{4,3,2,1,0:T(8,128)(2,1)}, u32[]{:S(2)}, u32[]{:S(2)}) collective-permute-start(bf16[2,2,2,192,128]{4,3,2,1,0:T(8,128)(2,1)S(1)} %pad_maximum_fusion.u0), channel_id=1, source_target_pairs={{0,2},{2,4},{4,6},{6,0},{1,3},{3,5},{5,7},{7,1},{8,10},{10,12},{12... | collective-permute-start | bytes 1179656 | tf_op jit(solution)/shard_map/ppermute | solution.py:167
  119.5 3.1 %collective-permute-start.5 = (bf16[2,2,2,192,128]{4,3,2,1,0:T(8,128)(2,1)S(1)}, bf16[2,2,2,192,128]{4,3,2,1,0:T(8,128)(2,1)}, u32[]{:S(2)}, u32[]{:S(2)}) collective-permute-start(bf16[2,2,2,192,128]{4,3,2,1,0:T(8,128)(2,1)S(1)} %pad_maximum_fusion.u0), channel_id=1, source_target_pairs={{0,4},{2,6},{4,0},{6,2},{1,5},{3,7},{5,1},{7,3},{8,12},{10,14},{12... | collective-permute-start | bytes 1179656 | tf_op jit(solution)/shard_map/ppermute | solution.py:167
  122.6 2.0 %collective-permute-start.6 = (bf16[2,2,2,192,128]{4,3,2,1,0:T(8,128)(2,1)S(1)}, bf16[2,2,2,192,128]{4,3,2,1,0:T(8,128)(2,1)}, u32[]{:S(2)}, u32[]{:S(2)}) collective-permute-start(bf16[2,2,2,192,128]{4,3,2,1,0:T(8,128)(2,1)S(1)} %pad_maximum_fusion.u0), channel_id=1, source_target_pairs={{0,6},{2,0},{4,2},{6,4},{1,7},{3,1},{5,3},{7,5},{8,14},{10,8},{12,... | collective-permute-start | bytes 1179656 | tf_op jit(solution)/shard_map/ppermute | solution.py:167
  130.0 2.8 %shard_map.31 = (f32[2,192,128]{2,1,0:T(8,128)S(1)}, f32[2,192,128]{2,1,0:T(8,128)S(1)}) custom-call(s32[4]{0:T(128)S(1)} %pad_add_fusion.place_ref, bf16[2,2,2,192,128]{4,3,2,1,0:T(8,128)(2,1)S(1)} %copy-done.2, bf16[2,2,2,192,128]{4,3,2,1,0:T(8,128)(2,1)S(1)} %copy-done.4, bf16[2,2,2,192,128]{4,3,2,1,0:T(8,128)(2,1)S(1)} %copy-done.6, ...), custom_call_target="tpu_custom_call" | custom-call | flops 805306368 | bytes 7340032 | tf_op jit(solution)/shard_map/pallas_call | solution.py:88
  132.8 6.5 %collective-permute-start.22 = (f32[2,192,128]{2,1,0:T(8,128)S(1)}, f32[2,192,128]{2,1,0:T(8,128)S(1)}, u32[]{:S(2)}, u32[]{:S(2)}) collective-permute-start(f32[2,192,128]{2,1,0:T(8,128)S(1)} %get-tuple-element.45), channel_id=1, source_target_pairs={{0,0},{1,1},{2,2},{3,3},{4,4},{5,5},{6,6},{7,7},{8,32},{9,33},{10,... | collective-permute-start | bytes 589832 | tf_op jit(solution)/shard_map/ppermute | solution.py:38
  139.4 3.6 %shard_map.30 = (f32[2,192,128]{2,1,0:T(8,128)S(1)}, f32[2,192,128]{2,1,0:T(8,128)}) custom-call(s32[4]{0:T(128)S(1)} %pad_add_fusion.place_ref, bf16[2,2,2,192,128]{4,3,2,1,0:T(8,128)(2,1)S(1)} %copy-done.2, bf16[2,2,2,192,128]{4,3,2,1,0:T(8,128)(2,1)S(1)} %copy-done.4, bf16[2,2,2,192,128]{4,3,2,1,0:T(8,128)(2,1)S(1)} %copy-done.6, ...), custom_call_target="tpu_custom_call" | custom-call | flops 805306368 | bytes 7340032 | tf_op jit(solution)/shard_map/pallas_call | solution.py:88
  143.0 2.5 %collective-permute-start.23 = (f32[2,192,128]{2,1,0:T(8,128)S(1)}, f32[2,192,128]{2,1,0:T(8,128)S(1)}, u32[]{:S(2)}, u32[]{:S(2)}) collective-permute-start(f32[2,192,128]{2,1,0:T(8,128)S(1)} %get-tuple-element.46), channel_id=1, source_target_pairs={{0,16},{1,17},{2,18},{3,19},{4,20},{5,21},{6,22},{7,23},{8,48},{9,... | collective-permute-start | bytes 589832 | tf_op jit(solution)/shard_map/ppermute | solution.py:38
  145.5 7.7 %collective-permute-start.20 = (f32[2,192,128]{2,1,0:T(8,128)S(1)}, f32[2,192,128]{2,1,0:T(8,128)S(1)}, u32[]{:S(2)}, u32[]{:S(2)}) collective-permute-start(f32[2,192,128]{2,1,0:T(8,128)S(1)} %get-tuple-element.43), channel_id=1, source_target_pairs={{0,8},{1,9},{2,10},{3,11},{4,12},{5,13},{6,14},{7,15},{8,40},{9,41... | collective-permute-start | bytes 589832 | tf_op jit(solution)/shard_map/ppermute | solution.py:38
  153.1 4.4 %shard_map.29 = (f32[2,192,128]{2,1,0:T(8,128)}, f32[2,192,128]{2,1,0:T(8,128)}) custom-call(s32[4]{0:T(128)S(1)} %pad_add_fusion.place_ref, bf16[2,2,2,192,128]{4,3,2,1,0:T(8,128)(2,1)S(1)} %pad_maximum_fusion.u0, bf16[2,2,2,192,128]{4,3,2,1,0:T(8,128)(2,1)} %collective-permute-done.4.u1, bf16[2,2,2,192,128]{4,3,2,1,0:T(8,128)(2,1)} %collective-permute-done.5.u2, ...), custom_call_target="tpu_custom_call" | custom-call | flops 805306368 | bytes 7340032 | tf_op jit(solution)/shard_map/pallas_call | solution.py:88
  157.5 2.7 %collective-permute-start.11 = (f32[2,192,128]{2,1,0:T(8,128)}, f32[2,192,128]{2,1,0:T(8,128)}, u32[]{:S(2)}, u32[]{:S(2)}) collective-permute-start(f32[2,192,128]{2,1,0:T(8,128)} %get-tuple-element.36), channel_id=1, source_target_pairs={{0,0},{1,1},{2,2},{3,3},{4,4},{5,5},{6,6},{7,7},{8,32},{9,33},{10,... | collective-permute-start | bytes 589832 | tf_op jit(solution)/shard_map/ppermute | solution.py:38
  160.2 4.3 %shard_map.28 = (f32[2,192,128]{2,1,0:T(8,128)}, f32[2,192,128]{2,1,0:T(8,128)}) custom-call(s32[4]{0:T(128)S(1)} %pad_add_fusion.place_ref, bf16[2,2,2,192,128]{4,3,2,1,0:T(8,128)(2,1)S(1)} %pad_maximum_fusion.u0, bf16[2,2,2,192,128]{4,3,2,1,0:T(8,128)(2,1)} %collective-permute-done.4.u1, bf16[2,2,2,192,128]{4,3,2,1,0:T(8,128)(2,1)} %collective-permute-done.5.u2, ...), custom_call_target="tpu_custom_call" | custom-call | flops 805306368 | bytes 7340032 | tf_op jit(solution)/shard_map/pallas_call | solution.py:88
  165.9 1.7 collective-permute-start.10
  168.3 3.8 %collective-permute-start.9 = (f32[2,192,128]{2,1,0:T(8,128)}, f32[2,192,128]{2,1,0:T(8,128)S(1)}, u32[]{:S(2)}, u32[]{:S(2)}) collective-permute-start(f32[2,192,128]{2,1,0:T(8,128)} %get-tuple-element.34), channel_id=1, source_target_pairs={{0,8},{1,9},{2,10},{3,11},{4,12},{5,13},{6,14},{7,15},{8,40},{9,41... | collective-permute-start | bytes 589832 | tf_op jit(solution)/shard_map/ppermute | solution.py:38
  172.1 1.7 shard_map.32.refs_0_
  173.9 1.7 shard_map.33.refs_0_
  176.3 1.7 shard_map.34.refs_0_
  178.0 5.1 %collective-permute-done.10.two = f32[2,192,128]{2,1,0:T(8,128)S(1)} collective-permute-done((f32[2,192,128]{2,1,0:T(8,128)}, f32[2,192,128]{2,1,0:T(8,128)S(1)}, u32[]{:S(2)}, u32[]{:S(2)}) %collective-permute-start.10) | collective-permute-done | bytes 196640 | tf_op jit(solution)/shard_map/ppermute | solution.py:38
  183.1 8.2 %collective-permute-done.9.one = f32[2,192,128]{2,1,0:T(8,128)S(1)} collective-permute-done((f32[2,192,128]{2,1,0:T(8,128)}, f32[2,192,128]{2,1,0:T(8,128)S(1)}, u32[]{:S(2)}, u32[]{:S(2)}) %collective-permute-start.9) | collective-permute-done | bytes 196640 | tf_op jit(solution)/shard_map/ppermute | solution.py:38
  191.9 1.7 shard_map.35
  (74 shorter events, 31.4 us)
Async XLA Ops:
  1.5 3.5 %collective-permute-start = (bf16[2,16,192,128]{3,2,1,0:T(8,128)(2,1)S(1)}, bf16[2,16,192,128]{3,2,1,0:T(8,128)(2,1)S(1)}, u32[]{:S(2)}, u32[]{:S(2)}) collective-permute-start(bf16[2,16,192,128]{3,2,1,0:T(8,128)(2,1)S(1)} %constant_dynamic-slice_fusion), channel_id=1, source_target_pairs={{0,32},{32,0},{1,33},{33,1},{2,34},{34,2},{3,35},{35,3},{4,36},{36... | collective-permute-start | bytes 4718600 | tf_op jit(solution)/shard_map/ppermute | solution.py:42
  7.9 26.1 %all-to-all-start = ((bf16[8,2,2,192,128]{4,3,2,1,0:T(8,128)(2,1)}), bf16[8,2,2,192,128]{4,3,2,1,0:T(8,128)(2,1)S(1)}, u32[]{:S(2)}, u32[]{:S(2)}) async-start(bf16[8,2,2,192,128]{4,3,2,1,0:T(8,128)(2,1)} %bitcast.7), calls=%async_computation | async-start | bytes 3145728 | tf_op jit(solution)/shard_map/all_to_all | solution.py:148
  14.1 1.2 slice-start
  55.3 31.7 %all-to-all-start.1 = ((bf16[8,2,320,128]{3,2,1,0:T(8,128)(2,1)}), bf16[8,2,320,128]{3,2,1,0:T(8,128)(2,1)}, u32[]{:S(2)}, u32[]{:S(2)}) async-start(bf16[8,2,320,128]{3,2,1,0:T(8,128)(2,1)} %bitcast.14), calls=%async_computation.1 | async-start | bytes 2621440 | tf_op jit(solution)/shard_map/all_to_all | solution.py:148
  61.2 61.4 %collective-permute-start.7 = (bf16[8,2,2,192,128]{4,3,2,1,0:T(8,128)(2,1)S(1)}, bf16[8,2,2,192,128]{4,3,2,1,0:T(8,128)(2,1)S(1)}, u32[]{:S(2)}, u32[]{:S(2)}) collective-permute-start(bf16[8,2,2,192,128]{4,3,2,1,0:T(8,128)(2,1)S(1)} %all-to-all-done.ao_ref), channel_id=1, source_target_pairs={{0,32},{32,0},{1,33},{33,1},{2,34},{34,2},{3,35},{35,3},{4,36},{36... | collective-permute-start | bytes 4718600 | tf_op jit(solution)/shard_map/ppermute | solution.py:42
  62.0 5.3 %collective-permute-start.13 = (bf16[2,2,192,128]{3,2,1,0:T(8,128)(2,1)S(1)}, bf16[2,2,192,128]{3,2,1,0:T(8,128)(2,1)}, u32[]{:S(2)}, u32[]{:S(2)}) collective-permute-start(bf16[2,2,192,128]{3,2,1,0:T(8,128)(2,1)S(1)} %get-tuple-element.38), channel_id=1, source_target_pairs={{0,1},{1,0},{2,3},{3,2},{4,5},{5,4},{6,7},{7,6},{8,9},{9,8},{10,11... | collective-permute-start | bytes 589832 | tf_op jit(solution)/shard_map/ppermute | solution.py:38
  63.4 21.7 %collective-permute-start.14 = (bf16[2,2,192,128]{3,2,1,0:T(8,128)(2,1)}, bf16[2,2,192,128]{3,2,1,0:T(8,128)(2,1)}, u32[]{:S(2)}, u32[]{:S(2)}) collective-permute-start(bf16[2,2,192,128]{3,2,1,0:T(8,128)(2,1)} %get-tuple-element.49), channel_id=1, source_target_pairs={{0,128},{1,129},{2,130},{3,131},{4,132},{5,133},{6,134},{7,135},{8... | collective-permute-start | bytes 589832 | tf_op jit(solution)/shard_map/ppermute | solution.py:38
  64.6 20.5 %collective-permute-start.15 = (bf16[2,2,192,128]{3,2,1,0:T(8,128)(2,1)}, bf16[2,2,192,128]{3,2,1,0:T(8,128)(2,1)}, u32[]{:S(2)}, u32[]{:S(2)}) collective-permute-start(bf16[2,2,192,128]{3,2,1,0:T(8,128)(2,1)} %get-tuple-element.49), channel_id=1, source_target_pairs={{0,129},{1,128},{2,131},{3,130},{4,133},{5,132},{6,135},{7,134},{8... | collective-permute-start | bytes 589832 | tf_op jit(solution)/shard_map/ppermute | solution.py:38
  66.0 22.5 %collective-permute-start.1 = (bf16[2,2,192,128]{3,2,1,0:T(8,128)(2,1)S(1)}, bf16[2,2,192,128]{3,2,1,0:T(8,128)(2,1)}, u32[]{:S(2)}, u32[]{:S(2)}) collective-permute-start(bf16[2,2,192,128]{3,2,1,0:T(8,128)(2,1)S(1)} %get-tuple-element.29), channel_id=1, source_target_pairs={{0,1},{1,0},{2,3},{3,2},{4,5},{5,4},{6,7},{7,6},{8,9},{9,8},{10,11... | collective-permute-start | bytes 589832 | tf_op jit(solution)/shard_map/ppermute | solution.py:38
  67.3 25.4 %collective-permute-start.2 = (bf16[2,2,192,128]{3,2,1,0:T(8,128)(2,1)}, bf16[2,2,192,128]{3,2,1,0:T(8,128)(2,1)}, u32[]{:S(2)}, u32[]{:S(2)}) collective-permute-start(bf16[2,2,192,128]{3,2,1,0:T(8,128)(2,1)} %get-tuple-element.51), channel_id=1, source_target_pairs={{0,128},{1,129},{2,130},{3,131},{4,132},{5,133},{6,134},{7,135},{8... | collective-permute-start | bytes 589832 | tf_op jit(solution)/shard_map/ppermute | solution.py:38
  85.1 39.6 %collective-permute-start.19 = (bf16[8,2,320,128]{3,2,1,0:T(8,128)(2,1)}, bf16[8,2,320,128]{3,2,1,0:T(8,128)(2,1)}, u32[]{:S(2)}, u32[]{:S(2)}) collective-permute-start(bf16[8,2,320,128]{3,2,1,0:T(8,128)(2,1)} %all_to_all.15.bo_ref), channel_id=1, source_target_pairs={{0,32},{32,0},{1,33},{33,1},{2,34},{34,2},{3,35},{35,3},{4,36},{36... | collective-permute-start | bytes 3932168 | tf_op jit(solution)/shard_map/ppermute | solution.py:42
  86.9 66.2 %collective-permute-start.8 = (bf16[8,2,320,128]{3,2,1,0:T(8,128)(2,1)}, bf16[8,2,320,128]{3,2,1,0:T(8,128)(2,1)}, u32[]{:S(2)}, u32[]{:S(2)}) collective-permute-start(bf16[8,2,320,128]{3,2,1,0:T(8,128)(2,1)} %all-to-all-done.1.bo_ref), channel_id=1, source_target_pairs={{0,32},{32,0},{1,33},{33,1},{2,34},{34,2},{3,35},{35,3},{4,36},{36... | collective-permute-start | bytes 3932168 | tf_op jit(solution)/shard_map/ppermute | solution.py:42
  88.5 34.1 %copy-start.1 = (bf16[2,2,2,192,128]{4,3,2,1,0:T(8,128)(2,1)}, bf16[2,2,2,192,128]{4,3,2,1,0:T(8,128)(2,1)S(1)}, u32[]{:S(2)}) copy-start(bf16[2,2,2,192,128]{4,3,2,1,0:T(8,128)(2,1)S(1)} %pad_maximum_fusion.1.u0) | copy-start | bytes 1179652
  88.5 17.3 %collective-permute-start.16 = (bf16[2,2,2,192,128]{4,3,2,1,0:T(8,128)(2,1)S(1)}, bf16[2,2,2,192,128]{4,3,2,1,0:T(8,128)(2,1)S(1)}, u32[]{:S(2)}, u32[]{:S(2)}) collective-permute-start(bf16[2,2,2,192,128]{4,3,2,1,0:T(8,128)(2,1)S(1)} %pad_maximum_fusion.1.u0), channel_id=1, source_target_pairs={{0,2},{2,4},{4,6},{6,0},{1,3},{3,5},{5,7},{7,1},{8,10},{10,12},{12... | collective-permute-start | bytes 1179656 | tf_op jit(solution)/shard_map/ppermute | solution.py:167
  92.7 9.9 %collective-permute-start.3 = (bf16[2,2,192,128]{3,2,1,0:T(8,128)(2,1)}, bf16[2,2,192,128]{3,2,1,0:T(8,128)(2,1)S(1)}, u32[]{:S(2)}, u32[]{:S(2)}) collective-permute-start(bf16[2,2,192,128]{3,2,1,0:T(8,128)(2,1)} %get-tuple-element.51), channel_id=1, source_target_pairs={{0,129},{1,128},{2,131},{3,130},{4,133},{5,132},{6,135},{7,134},{8... | collective-permute-start | bytes 589832 | tf_op jit(solution)/shard_map/ppermute | solution.py:38
  102.6 10.3 %collective-permute-start.17 = (bf16[2,2,2,192,128]{4,3,2,1,0:T(8,128)(2,1)S(1)}, bf16[2,2,2,192,128]{4,3,2,1,0:T(8,128)(2,1)S(1)}, u32[]{:S(2)}, u32[]{:S(2)}) collective-permute-start(bf16[2,2,2,192,128]{4,3,2,1,0:T(8,128)(2,1)S(1)} %pad_maximum_fusion.1.u0), channel_id=1, source_target_pairs={{0,4},{2,6},{4,0},{6,2},{1,5},{3,7},{5,1},{7,3},{8,12},{10,14},{12... | collective-permute-start | bytes 1179656 | tf_op jit(solution)/shard_map/ppermute | solution.py:167
  106.6 12.1 %collective-permute-start.18 = (bf16[2,2,2,192,128]{4,3,2,1,0:T(8,128)(2,1)S(1)}, bf16[2,2,2,192,128]{4,3,2,1,0:T(8,128)(2,1)S(1)}, u32[]{:S(2)}, u32[]{:S(2)}) collective-permute-start(bf16[2,2,2,192,128]{4,3,2,1,0:T(8,128)(2,1)S(1)} %pad_maximum_fusion.1.u0), channel_id=1, source_target_pairs={{0,6},{2,0},{4,2},{6,4},{1,7},{3,1},{5,3},{7,5},{8,14},{10,8},{12,... | collective-permute-start | bytes 1179656 | tf_op jit(solution)/shard_map/ppermute | solution.py:167
  113.6 29.3 %collective-permute-start.4 = (bf16[2,2,2,192,128]{4,3,2,1,0:T(8,128)(2,1)S(1)}, bf16[2,2,2,192,128]{4,3,2,1,0:T(8,128)(2,1)}, u32[]{:S(2)}, u32[]{:S(2)}) collective-permute-start(bf16[2,2,2,192,128]{4,3,2,1,0:T(8,128)(2,1)S(1)} %pad_maximum_fusion.u0), channel_id=1, source_target_pairs={{0,2},{2,4},{4,6},{6,0},{1,3},{3,5},{5,7},{7,1},{8,10},{10,12},{12... | collective-permute-start | bytes 1179656 | tf_op jit(solution)/shard_map/ppermute | solution.py:167
  119.5 26.0 %collective-permute-start.5 = (bf16[2,2,2,192,128]{4,3,2,1,0:T(8,128)(2,1)S(1)}, bf16[2,2,2,192,128]{4,3,2,1,0:T(8,128)(2,1)}, u32[]{:S(2)}, u32[]{:S(2)}) collective-permute-start(bf16[2,2,2,192,128]{4,3,2,1,0:T(8,128)(2,1)S(1)} %pad_maximum_fusion.u0), channel_id=1, source_target_pairs={{0,4},{2,6},{4,0},{6,2},{1,5},{3,7},{5,1},{7,3},{8,12},{10,14},{12... | collective-permute-start | bytes 1179656 | tf_op jit(solution)/shard_map/ppermute | solution.py:167
  122.6 30.5 %collective-permute-start.6 = (bf16[2,2,2,192,128]{4,3,2,1,0:T(8,128)(2,1)S(1)}, bf16[2,2,2,192,128]{4,3,2,1,0:T(8,128)(2,1)}, u32[]{:S(2)}, u32[]{:S(2)}) collective-permute-start(bf16[2,2,2,192,128]{4,3,2,1,0:T(8,128)(2,1)S(1)} %pad_maximum_fusion.u0), channel_id=1, source_target_pairs={{0,6},{2,0},{4,2},{6,4},{1,7},{3,1},{5,3},{7,5},{8,14},{10,8},{12,... | collective-permute-start | bytes 1179656 | tf_op jit(solution)/shard_map/ppermute | solution.py:167
  124.7 1.3 copy-start
  132.8 31.7 %collective-permute-start.22 = (f32[2,192,128]{2,1,0:T(8,128)S(1)}, f32[2,192,128]{2,1,0:T(8,128)S(1)}, u32[]{:S(2)}, u32[]{:S(2)}) collective-permute-start(f32[2,192,128]{2,1,0:T(8,128)S(1)} %get-tuple-element.45), channel_id=1, source_target_pairs={{0,0},{1,1},{2,2},{3,3},{4,4},{5,5},{6,6},{7,7},{8,32},{9,33},{10,... | collective-permute-start | bytes 589832 | tf_op jit(solution)/shard_map/ppermute | solution.py:38
  143.0 22.9 %collective-permute-start.23 = (f32[2,192,128]{2,1,0:T(8,128)S(1)}, f32[2,192,128]{2,1,0:T(8,128)S(1)}, u32[]{:S(2)}, u32[]{:S(2)}) collective-permute-start(f32[2,192,128]{2,1,0:T(8,128)S(1)} %get-tuple-element.46), channel_id=1, source_target_pairs={{0,16},{1,17},{2,18},{3,19},{4,20},{5,21},{6,22},{7,23},{8,48},{9,... | collective-permute-start | bytes 589832 | tf_op jit(solution)/shard_map/ppermute | solution.py:38
  145.5 22.1 %collective-permute-start.20 = (f32[2,192,128]{2,1,0:T(8,128)S(1)}, f32[2,192,128]{2,1,0:T(8,128)S(1)}, u32[]{:S(2)}, u32[]{:S(2)}) collective-permute-start(f32[2,192,128]{2,1,0:T(8,128)S(1)} %get-tuple-element.43), channel_id=1, source_target_pairs={{0,8},{1,9},{2,10},{3,11},{4,12},{5,13},{6,14},{7,15},{8,40},{9,41... | collective-permute-start | bytes 589832 | tf_op jit(solution)/shard_map/ppermute | solution.py:38
  153.1 20.7 %collective-permute-start.21 = (f32[2,192,128]{2,1,0:T(8,128)}, f32[2,192,128]{2,1,0:T(8,128)}, u32[]{:S(2)}, u32[]{:S(2)}) collective-permute-start(f32[2,192,128]{2,1,0:T(8,128)} %get-tuple-element.44), channel_id=1, source_target_pairs={{0,24},{1,25},{2,26},{3,27},{4,28},{5,29},{6,30},{7,31},{8,56},{9,... | collective-permute-start | bytes 589832 | tf_op jit(solution)/shard_map/ppermute | solution.py:38
  157.5 18.1 %collective-permute-start.11 = (f32[2,192,128]{2,1,0:T(8,128)}, f32[2,192,128]{2,1,0:T(8,128)}, u32[]{:S(2)}, u32[]{:S(2)}) collective-permute-start(f32[2,192,128]{2,1,0:T(8,128)} %get-tuple-element.36), channel_id=1, source_target_pairs={{0,0},{1,1},{2,2},{3,3},{4,4},{5,5},{6,6},{7,7},{8,32},{9,33},{10,... | collective-permute-start | bytes 589832 | tf_op jit(solution)/shard_map/ppermute | solution.py:38
  164.6 3.7 %copy-start.13 = (f32[2,192,128]{2,1,0:T(8,128)}, f32[2,192,128]{2,1,0:T(8,128)S(1)}, u32[]{:S(2)}) copy-start(f32[2,192,128]{2,1,0:T(8,128)S(1)} %collective-permute-done.22.one) | copy-start | bytes 589828
  164.6 11.0 %collective-permute-start.12 = (f32[2,192,128]{2,1,0:T(8,128)}, f32[2,192,128]{2,1,0:T(8,128)S(1)}, u32[]{:S(2)}, u32[]{:S(2)}) collective-permute-start(f32[2,192,128]{2,1,0:T(8,128)} %get-tuple-element.37), channel_id=1, source_target_pairs={{0,16},{1,17},{2,18},{3,19},{4,20},{5,21},{6,22},{7,23},{8,48},{9,... | collective-permute-start | bytes 589832 | tf_op jit(solution)/shard_map/ppermute | solution.py:38
  165.9 2.4 %copy-start.14 = (f32[2,192,128]{2,1,0:T(8,128)}, f32[2,192,128]{2,1,0:T(8,128)S(1)}, u32[]{:S(2)}) copy-start(f32[2,192,128]{2,1,0:T(8,128)S(1)} %collective-permute-done.23.two) | copy-start | bytes 589828
  165.9 17.2 %collective-permute-start.10 = (f32[2,192,128]{2,1,0:T(8,128)}, f32[2,192,128]{2,1,0:T(8,128)S(1)}, u32[]{:S(2)}, u32[]{:S(2)}) collective-permute-start(f32[2,192,128]{2,1,0:T(8,128)} %get-tuple-element.35), channel_id=1, source_target_pairs={{0,24},{1,25},{2,26},{3,27},{4,28},{5,29},{6,30},{7,31},{8,56},{9,... | collective-permute-start | bytes 589832 | tf_op jit(solution)/shard_map/ppermute | solution.py:38
  168.3 23.0 %collective-permute-start.9 = (f32[2,192,128]{2,1,0:T(8,128)}, f32[2,192,128]{2,1,0:T(8,128)S(1)}, u32[]{:S(2)}, u32[]{:S(2)}) collective-permute-start(f32[2,192,128]{2,1,0:T(8,128)} %get-tuple-element.34), channel_id=1, source_target_pairs={{0,8},{1,9},{2,10},{3,11},{4,12},{5,13},{6,14},{7,15},{8,40},{9,41... | collective-permute-start | bytes 589832 | tf_op jit(solution)/shard_map/ppermute | solution.py:38
  183.1 8.2 %copy-start.10 = (f32[2,192,128]{2,1,0:T(8,128)}, f32[2,192,128]{2,1,0:T(8,128)S(1)}, u32[]{:S(2)}) copy-start(f32[2,192,128]{2,1,0:T(8,128)S(1)} %collective-permute-done.10.two) | copy-start | bytes 589828
  (10 other events, 8.3 us)

commit v10 on v7

v10 whole, which is shorter than its diff:
```python
import jax
import jax.numpy as jnp
from jax import lax
from jax.experimental import pallas as pl
from jax.experimental.pallas import tpu as pltpu
from jax.sharding import Mesh, PartitionSpec as P


NOUT = 384
AXES = ("zq", "zr", "core", "x", "y", "zh")
SIZES = (2, 2, 2, 4, 4, 2)


def coordinates():
    out = [()]
    for size in SIZES:
        out = [c + (i,) for c in out for i in range(size)]
    return out


def flat(c):
    index = 0
    for i, size in zip(c, SIZES):
        index = index * size + i
    return index


def moved(target):
    pairs = []
    for c in coordinates():
        t = target(*c)
        if t is not None:
            pairs.append((flat(c), flat(t)))
    return pairs


def send(value, target):
    return lax.ppermute(value, AXES, moved(target))


def swap_core(value):
    return lax.ppermute(value, "core", [(0, 1), (1, 0)])


def contract(g, place, turned, a_own, a_peer, b_own, b_peer):
    half, lanes = turned[0].shape[-2:]
    depth = 16 * lanes

    def kernel(place_ref, u0, u1, u2, u3, ao_ref, ap_ref, bo_ref, bp_ref, o0, o1, o2, o3, left):
        core, zh, y = place_ref[0], place_ref[1], place_ref[3]
        t = pl.program_id(0)

        @pl.when(t == 0)
        def _():
            for step, u_ref in enumerate((u0, u1, u2, u3)):
                ys = (y + 4 - step) % 4
                for xl in range(2):
                    for piece in range(2):
                        start = pl.multiple_of(((xl * 4 + ys) * 2 + (piece ^ zh)) * lanes, lanes)
                        for part in range(2):
                            left[part * half : (part + 1) * half, pl.ds(start, lanes)] = u_ref[piece, xl, part]

        first = core == 0
        rows = []
        for zr in range(2):
            parts = []
            for part in range(2):
                ao, ap = ao_ref[zr, 0, part], ap_ref[zr, 0, part]
                bo, bp = bo_ref[zr, part], bp_ref[zr, part]
                parts.append(
                    jnp.concatenate(
                        [
                            jnp.where(first, ao, ap),
                            jnp.where(first, ap, ao),
                            jnp.where(first, bo, bp),
                            jnp.where(first, bp, bo),
                        ],
                        0,
                    )
                )
            rows.append(jnp.concatenate(parts, 1))
        right = jnp.concatenate(rows, 0)
        both = jnp.dot(left[...], right, preferred_element_type=jnp.float32)
        real = both[:half, :lanes] - both[half:, lanes:]
        imag = both[:half, lanes:] + both[half:, :lanes]
        for i, out in enumerate((o0, o1, o2, o3)):

            @pl.when(t == i)
            def _():
                out[0] = real
                out[1] = imag

    def column(t, place_ref):
        return (2 * place_ref[2] + place_ref[0]) ^ t

    a_spec = pl.BlockSpec((2, 1, 2, half, lanes), lambda t, p: (column(t, p), g, 0, 0, 0))
    b_spec = pl.BlockSpec((2,) + b_own.shape[1:], lambda t, p: (column(t, p), 0, 0, 0))
    u_spec = pl.BlockSpec(turned[0].shape, lambda t, p: (0, 0, 0, 0, 0))
    result = jax.ShapeDtypeStruct((2, half, lanes), jnp.float32)
    return pl.pallas_call(
        kernel,
        out_shape=(result,) * 4,
        grid_spec=pltpu.PrefetchScalarGridSpec(
            num_scalar_prefetch=1,
            grid=(4,),
            in_specs=[u_spec] * 4 + [a_spec, a_spec, b_spec, b_spec],
            out_specs=(pl.BlockSpec((2, half, lanes), lambda t, p: (0, 0, 0)),) * 4,
            scratch_shapes=[pltpu.VMEM((2 * half, depth), jnp.bfloat16)],
        ),
        cost_estimate=pl.CostEstimate(
            flops=2 * 2 * half * depth * 8 * lanes, bytes_accessed=7 << 20, transcendentals=0
        ),
        compiler_params=pltpu.CompilerParams(vmem_limit_bytes=40 << 20),
    )(place, *turned, a_own, a_peer, b_own, b_peer)


def arrange(core, spectra, passed):
    half, lanes = passed.shape[2:]

    def kernel(core_ref, low_ref, passed_ref, out_ref):
        first = core_ref[0] == 0
        pair = 8 * pl.program_id(1) + 2 * pl.program_id(0)
        for g in range(2):
            for part in range(2):
                out_ref[0, g, part] = jnp.where(first, low_ref[part, g], passed_ref[part, pair + g])

    spec = pl.BlockSpec((2, 2, half, lanes), lambda x, zr, c: (0, 4 * zr + x, 0, 0))
    return pl.pallas_call(
        kernel,
        out_shape=jax.ShapeDtypeStruct((8, 2, 2, half, lanes), jnp.bfloat16),
        grid_spec=pltpu.PrefetchScalarGridSpec(
            num_scalar_prefetch=1,
            grid=(4, 2),
            in_specs=[spec, pl.BlockSpec(memory_space=pltpu.VMEM)],
            out_specs=pl.BlockSpec((1, 2, 2, half, lanes), lambda x, zr, c: (2 * x + zr, 0, 0, 0, 0)),
        ),
        cost_estimate=pl.CostEstimate(flops=0, bytes_accessed=5 << 20, transcendentals=0),
    )(core, spectra, passed)


def finish(g, odd, wavelet, blocks, prior=()):
    half, lanes = blocks[0].shape[1:]

    def kernel(odd_ref, wave_ref, *refs):
        wave_real, wave_imag = wave_ref[0, g], wave_ref[1, g]
        out = refs[-1]
        for t in range(2):
            start = pl.multiple_of((odd_ref[0] ^ t) * half, half)
            one, two = refs[t], refs[t + 2]
            real, imag = one[0] + two[0], one[1] + two[1]
            out[0, 0, pl.ds(start, half)] = (-(wave_real * real - wave_imag * imag)).astype(jnp.bfloat16)
            out[1, 0, pl.ds(start, half)] = (-(wave_real * imag + wave_imag * real)).astype(jnp.bfloat16)

    smem, vmem = pl.BlockSpec(memory_space=pltpu.SMEM), pl.BlockSpec(memory_space=pltpu.VMEM)
    return pl.pallas_call(
        kernel,
        grid=(1,),
        out_shape=jax.ShapeDtypeStruct((2, 2, 2 * half, lanes), jnp.bfloat16),
        in_specs=[smem, smem] + [vmem] * 4 + [pl.BlockSpec(memory_space=pl.ANY)] * len(prior),
        out_specs=pl.BlockSpec((2, 1, 2 * half, lanes), lambda i: (0, g, 0, 0)),
        input_output_aliases={6: 0} if prior else {},
        cost_estimate=pl.CostEstimate(flops=8 * 2 * half * lanes, bytes_accessed=1 << 20, transcendentals=0),
    )(odd, wavelet, *blocks, *prior)


def step(spectra, wavelet):
    zq, core, x = lax.axis_index("zq"), lax.axis_index("core"), lax.axis_index("x")
    y, zh = lax.axis_index("y"), lax.axis_index("zh")
    place = jnp.stack([core, zh, zq, y]).astype(jnp.int32)
    rows, _ = spectra.shape[2:]
    window = NOUT * rows // 512
    half = window // 2
    first = core == 0

    def ordered(block):
        return block.reshape((2, 2, 4, 2) + block.shape[2:])

    passed = swap_core(lax.dynamic_slice_in_dim(spectra, (1 - core) * half, half, 2))
    a = arrange(place, spectra, passed)
    b = jnp.where(first, jnp.concatenate([spectra[:, :, window:], passed], 2), spectra[:, :, half:])
    b = [ordered(b)[:, :, :, g].transpose(2, 1, 0, 3, 4) for g in range(2)]
    b = [b[g].reshape((8, 2) + b[g].shape[3:]) for g in range(2)]
    b = lax.optimization_barrier(b)

    def exchange(block):
        return lax.all_to_all(block, ("x", "zr"), split_axis=0, concat_axis=0, tiled=True)

    a_own = exchange(a)
    a_own, *b = lax.optimization_barrier((a_own, *b))
    a_peer = swap_core(a_own)
    b_own, b_peer = [], []
    for g in range(2):
        b_own.append(exchange(b[g]))
        b_peer.append(swap_core(b_own[g]))

    def turn(g):
        shots = a_own.reshape((4, 2) + a_own.shape[1:])[:, 0, g]
        near, far = shots[:2], shots[2:]
        across = send(near, lambda q, r, c, x, y, h: (0, r, c, x, y, 1 - h) if q == 0 else None)
        up = send(far, lambda q, r, c, x, y, h: (1, r, c, x, y, h) if q == 0 else None)
        down = send(far, lambda q, r, c, x, y, h: (1, r, c, x, y, 1 - h) if q == 0 else None)
        mine, across, up, down = lax.optimization_barrier((near, across, up, down))
        pieces = jnp.stack([jnp.where(zq == 0, mine, up), jnp.where(zq == 0, across, down)])
        plus, minus, two = (
            lax.ppermute(pieces, "y", [(i, (i + s) % 4) for i in range(4)]) for s in (1, 3, 2)
        )
        return pieces, plus, two, minus

    turned = [turn(g) for g in range(2)]

    def homeward(blocks):
        return [
            send(
                block,
                lambda q, r, c, x, y, h: (r, x // 2, x % 2, (2 * q + c) ^ t, y, h),
            )
            for t, block in enumerate(blocks)
        ]

    blocks = []
    for g in range(2):
        partial = contract(g, place, turned[g], a_own, a_peer, b_own[g], b_peer[g])
        blocks.append(homeward(partial))
    odd = jnp.stack([x % 2]).astype(jnp.int32)
    early = finish(0, odd, wavelet, blocks[0])
    return finish(1, odd, wavelet, blocks[1], (early,))


def solution(mesh):
    fine = Mesh(mesh.devices.reshape(SIZES), AXES)
    freq, col = AXES[:3], AXES[3:]
    return jax.shard_map(
        step,
        mesh=fine,
        in_specs=(P(None, None, freq, col), P(None, freq)),
        out_specs=P(None, freq, None, col),
        check_vma=False,
    )
```

time: 191 us -> 191 us (level)
  the two profiles are of different devices: /device:TPU:213 before, /device:TPU:197 now
where the time goes in v10:
time: 191 us; the launch traced here: 190 us
  waiting for transfers between devices  70.8 us (37%)
  starting transfers between devices  61.5 us (32%)
  Pallas kernels  21.8 us (11%)
  blocking collectives  20.6 us (11%)
  other arithmetic  7.75 us (4%)
  local copies, waits for them, and re-layouts  7.54 us (4%)
    ppermute x14, waiting for transfers between devices, send(): return lax.ppermute(value, AXES, moved(target))  45.3 us
    ppermute x14, starting transfers between devices, send(): return lax.ppermute(value, AXES, moved(target))  33.6 us
    all_to_all x1, blocking collectives, exchange(): lax.all_to_all(block, ('x', 'zr'), split_axis=0, concat_axis=0, tiled=True)  20.6 us
    ppermute x6, starting transfers between devices, turn(): lax.ppermute(pieces, 'y', [(i, (i + s) % 4) for i in range(4)])  12.7 us
    all_to_all x2, waiting for transfers between devices, exchange(): lax.all_to_all(block, ('x', 'zr'), split_axis=0, concat_axis=0, tiled=True)  12.6 us
    all_to_all x2, starting transfers between devices, exchange(): lax.all_to_all(block, ('x', 'zr'), split_axis=0, concat_axis=0, tiled=True)  11.2 us
    pallas_call x2, Pallas kernels, contract(): pl.pallas_call(kernel, out_shape=(result,) * 4, grid_spec=pltpu.PrefetchS...  11 us
    ppermute x6, waiting for transfers between devices, turn(): lax.ppermute(pieces, 'y', [(i, (i + s) % 4) for i in range(4)])  10.6 us
  transfers between devices with their start and end apart: 26, of which 11 were waited for; matrix products, arithmetic and copies ran while one was open for 5% of the time, Pallas kernels for 7%

profile of v10, /device:TPU:197, one launch (start us, length us, event | category | flops | bytes accessed | tf_op | source)
XLA Modules:
  0.0 190.3 jit_solution(5028265208296542757)
XLA Ops:
  0.0 1.5 constant_dynamic-slice_fusion
  2.9 2.4 %collective-permute-done.passed_ref = bf16[2,16,192,128]{3,2,1,0:T(8,128)(2,1)S(1)} collective-permute-done((bf16[2,16,192,128]{3,2,1,0:T(8,128)(2,1)S(1)}, bf16[2,16,192,128]{3,2,1,0:T(8,128)(2,1)S(1)}, u32[]{:S(2)}, u32[]{:S(2)}) %collective-permute-start) | collective-permute-done | bytes 1572896 | tf_op jit(solution)/shard_map/ppermute | solution.py:42
  6.5 6.9 %shard_map.28 = bf16[8,2,2,192,128]{4,3,2,1,0:T(8,128)(2,1)} custom-call(s32[4]{0:T(128)} %pad_add_fusion.core_ref.place_ref, bf16[2,16,512,128]{3,2,1,0:T(8,128)(2,1)} %low_ref.1, bf16[2,16,192,128]{3,2,1,0:T(8,128)(2,1)} %copy-done.2), custom_call_target="tpu_custom_call" | custom-call | bytes 5242880 | tf_op jit(solution)/shard_map/pallas_call | solution.py:128
  13.4 4.7 %all-to-all-start = ((bf16[8,2,2,192,128]{4,3,2,1,0:T(8,128)(2,1)}), bf16[8,2,2,192,128]{4,3,2,1,0:T(8,128)(2,1)S(1)}, u32[]{:S(2)}, u32[]{:S(2)}) async-start(bf16[8,2,2,192,128]{4,3,2,1,0:T(8,128)(2,1)} %shard_map.28), calls=%async_computation | async-start | bytes 3145728 | tf_op jit(solution)/shard_map/all_to_all | solution.py:186
  19.3 3.2 %maximum_select_fusion = bf16[2,16,320,128]{3,2,1,0:T(8,128)(2,1)S(1)} fusion(bf16[2,16,192,128]{3,2,1,0:T(8,128)(2,1)} %copy-done.2, bf16[2,16,128,128]{3,2,1,0:T(8,128)(2,1)S(1)} %slice-done, bf16[2,16,512,128]{3,2,1,0:T(8,128)(2,1)} %low_ref.1, pred[]{:T(512)S(6)} %eq.12), kind=kLoop, calls=%fused_computation | loop fusion | flops 6553600 | bytes 7864321 | tf_op jit(solution)/shard_map/jit(_where)/select_n | solution.py:180
  23.9 12.6 %all-to-all-done.ao_ref = bf16[8,2,2,192,128]{4,3,2,1,0:T(8,128)(2,1)S(1)} async-done(((bf16[8,2,2,192,128]{4,3,2,1,0:T(8,128)(2,1)}), bf16[8,2,2,192,128]{4,3,2,1,0:T(8,128)(2,1)S(1)}, u32[]{:S(2)}, u32[]{:S(2)}) %all-to-all-start) | async-done | bytes 1572896 | tf_op jit(solution)/shard_map/all_to_all | solution.py:186
  36.5 20.6 %all_to_all.15.bo_ref = bf16[8,2,320,128]{3,2,1,0:T(8,128)(2,1)} all-to-all(bf16[8,2,320,128]{3,2,1,0:T(8,128)(2,1)S(1)} %bitcast.43), channel_id=1, replica_groups=mesh['zq'=2,'zr'=2,'core'=2,'x'=4,'y'=4,'zh'=2] {'x','zr'}, dimensions={0} | all-to-all | bytes 2621440 | tf_op jit(solution)/shard_map/all_to_all | solution.py:186
  57.1 6.5 %all-to-all-start.1 = ((bf16[8,2,320,128]{3,2,1,0:T(8,128)(2,1)}), bf16[8,2,320,128]{3,2,1,0:T(8,128)(2,1)}, u32[]{:S(2)}, u32[]{:S(2)}) async-start(bf16[8,2,320,128]{3,2,1,0:T(8,128)(2,1)} %bitcast.11), calls=%async_computation.1 | async-start | bytes 2621440 | tf_op jit(solution)/shard_map/all_to_all | solution.py:186
  63.6 2.5 %collective-permute-start.7 = (bf16[8,2,2,192,128]{4,3,2,1,0:T(8,128)(2,1)S(1)}, bf16[8,2,2,192,128]{4,3,2,1,0:T(8,128)(2,1)S(1)}, u32[]{:S(2)}, u32[]{:S(2)}) collective-permute-start(bf16[8,2,2,192,128]{4,3,2,1,0:T(8,128)(2,1)S(1)} %all-to-all-done.ao_ref), channel_id=1, source_target_pairs={{0,32},{32,0},{1,33},{33,1},{2,34},{34,2},{3,35},{35,3},{4,36},{36... | collective-permute-start | bytes 4718600 | tf_op jit(solution)/shard_map/ppermute | solution.py:42
  73.5 12.7 %collective-permute-done.14 = bf16[2,2,192,128]{3,2,1,0:T(8,128)(2,1)} collective-permute-done((bf16[2,2,192,128]{3,2,1,0:T(8,128)(2,1)}, bf16[2,2,192,128]{3,2,1,0:T(8,128)(2,1)}, u32[]{:S(2)}, u32[]{:S(2)}) %collective-permute-start.14) | collective-permute-done | bytes 196640 | tf_op jit(solution)/shard_map/ppermute | solution.py:38
  86.2 7.4 %collective-permute-done.15 = bf16[2,2,192,128]{3,2,1,0:T(8,128)(2,1)} collective-permute-done((bf16[2,2,192,128]{3,2,1,0:T(8,128)(2,1)}, bf16[2,2,192,128]{3,2,1,0:T(8,128)(2,1)}, u32[]{:S(2)}, u32[]{:S(2)}) %collective-permute-start.15) | collective-permute-done | bytes 196640 | tf_op jit(solution)/shard_map/ppermute | solution.py:38
  94.2 1.8 select_bitcast_fusion
  100.0 8.7 %collective-permute-done.3 = bf16[2,2,192,128]{3,2,1,0:T(8,128)(2,1)S(1)} collective-permute-done((bf16[2,2,192,128]{3,2,1,0:T(8,128)(2,1)}, bf16[2,2,192,128]{3,2,1,0:T(8,128)(2,1)S(1)}, u32[]{:S(2)}, u32[]{:S(2)}) %collective-permute-start.3) | collective-permute-done | bytes 196640 | tf_op jit(solution)/shard_map/ppermute | solution.py:38
  108.7 2.6 %collective-permute-start.17 = (bf16[2,2,2,192,128]{4,3,2,1,0:T(8,128)(2,1)S(1)}, bf16[2,2,2,192,128]{4,3,2,1,0:T(8,128)(2,1)S(1)}, u32[]{:S(2)}, u32[]{:S(2)}) collective-permute-start(bf16[2,2,2,192,128]{4,3,2,1,0:T(8,128)(2,1)S(1)} %pad_maximum_fusion.1.u0), channel_id=1, source_target_pairs={{0,4},{2,6},{4,0},{6,2},{1,5},{3,7},{5,1},{7,3},{8,12},{10,14},{12... | collective-permute-start | bytes 1179656 | tf_op jit(solution)/shard_map/ppermute | solution.py:205
  113.4 3.4 %collective-permute-done.17.u2 = bf16[2,2,2,192,128]{4,3,2,1,0:T(8,128)(2,1)S(1)} collective-permute-done((bf16[2,2,2,192,128]{4,3,2,1,0:T(8,128)(2,1)S(1)}, bf16[2,2,2,192,128]{4,3,2,1,0:T(8,128)(2,1)S(1)}, u32[]{:S(2)}, u32[]{:S(2)}) %collective-permute-start.17) | collective-permute-done | bytes 393248 | tf_op jit(solution)/shard_map/ppermute | solution.py:205
  116.8 1.4 collective-permute-start.4
  118.2 7.2 %collective-permute-done.18.u3 = bf16[2,2,2,192,128]{4,3,2,1,0:T(8,128)(2,1)S(1)} collective-permute-done((bf16[2,2,2,192,128]{4,3,2,1,0:T(8,128)(2,1)S(1)}, bf16[2,2,2,192,128]{4,3,2,1,0:T(8,128)(2,1)S(1)}, u32[]{:S(2)}, u32[]{:S(2)}) %collective-permute-start.18) | collective-permute-done | bytes 393248 | tf_op jit(solution)/shard_map/ppermute | solution.py:205
  125.4 3.4 %collective-permute-start.5 = (bf16[2,2,2,192,128]{4,3,2,1,0:T(8,128)(2,1)S(1)}, bf16[2,2,2,192,128]{4,3,2,1,0:T(8,128)(2,1)S(1)}, u32[]{:S(2)}, u32[]{:S(2)}) collective-permute-start(bf16[2,2,2,192,128]{4,3,2,1,0:T(8,128)(2,1)S(1)} %pad_maximum_fusion.u0), channel_id=1, source_target_pairs={{0,4},{2,6},{4,0},{6,2},{1,5},{3,7},{5,1},{7,3},{8,12},{10,14},{12... | collective-permute-start | bytes 1179656 | tf_op jit(solution)/shard_map/ppermute | solution.py:205
  128.8 2.8 %collective-permute-start.6 = (bf16[2,2,2,192,128]{4,3,2,1,0:T(8,128)(2,1)S(1)}, bf16[2,2,2,192,128]{4,3,2,1,0:T(8,128)(2,1)S(1)}, u32[]{:S(2)}, u32[]{:S(2)}) collective-permute-start(bf16[2,2,2,192,128]{4,3,2,1,0:T(8,128)(2,1)S(1)} %pad_maximum_fusion.u0), channel_id=1, source_target_pairs={{0,6},{2,0},{4,2},{6,4},{1,7},{3,1},{5,3},{7,5},{8,14},{10,8},{12,... | collective-permute-start | bytes 1179656 | tf_op jit(solution)/shard_map/ppermute | solution.py:205
  131.6 5.1 %shard_map.30 = (f32[2,192,128]{2,1,0:T(8,128)S(1)}, f32[2,192,128]{2,1,0:T(8,128)S(1)}, f32[2,192,128]{2,1,0:T(8,128)S(1)}, f32[2,192,128]{2,1,0:T(8,128)S(1)}) custom-call(s32[4]{0:T(128)S(1)} %copy-done.1, bf16[2,2,2,192,128]{4,3,2,1,0:T(8,128)(2,1)S(1)} %pad_maximum_fusion.1.u0, bf16[2,2,2,192,128]{4,3,2,1,0:T(8,128)(2,1)S(1)} %collective-permute-done.16.u1, ...), custom_call_target="tpu_custom_call" | custom-call | flops 1610612736 | bytes 7340032 | tf_op jit(solution)/shard_map/pallas_call | solution.py:100
  136.7 5.9 %collective-permute-start.20 = (f32[2,192,128]{2,1,0:T(8,128)S(1)}, f32[2,192,128]{2,1,0:T(8,128)S(1)}, u32[]{:S(2)}, u32[]{:S(2)}) collective-permute-start(f32[2,192,128]{2,1,0:T(8,128)S(1)} %get-tuple-element.43), channel_id=1, source_target_pairs={{0,0},{1,1},{2,2},{3,3},{4,4},{5,5},{6,6},{7,7},{8,32},{9,33},{10,... | collective-permute-start | bytes 589832 | tf_op jit(solution)/shard_map/ppermute | solution.py:38
  142.7 4.0 %collective-permute-start.21 = (f32[2,192,128]{2,1,0:T(8,128)S(1)}, f32[2,192,128]{2,1,0:T(8,128)S(1)}, u32[]{:S(2)}, u32[]{:S(2)}) collective-permute-start(f32[2,192,128]{2,1,0:T(8,128)S(1)} %get-tuple-element.44), channel_id=1, source_target_pairs={{0,8},{1,9},{2,10},{3,11},{4,12},{5,13},{6,14},{7,15},{8,40},{9,41... | collective-permute-start | bytes 589832 | tf_op jit(solution)/shard_map/ppermute | solution.py:38
  146.7 4.8 %collective-permute-start.23 = (f32[2,192,128]{2,1,0:T(8,128)S(1)}, f32[2,192,128]{2,1,0:T(8,128)}, u32[]{:S(2)}, u32[]{:S(2)}) collective-permute-start(f32[2,192,128]{2,1,0:T(8,128)S(1)} %get-tuple-element.46), channel_id=1, source_target_pairs={{0,24},{1,25},{2,26},{3,27},{4,28},{5,29},{6,30},{7,31},{8,56},{9,... | collective-permute-start | bytes 589832 | tf_op jit(solution)/shard_map/ppermute | solution.py:38
  151.5 5.9 %shard_map.29 = (f32[2,192,128]{2,1,0:T(8,128)S(1)}, f32[2,192,128]{2,1,0:T(8,128)}, f32[2,192,128]{2,1,0:T(8,128)}, f32[2,192,128]{2,1,0:T(8,128)}) custom-call(s32[4]{0:T(128)S(1)} %copy-done.1, bf16[2,2,2,192,128]{4,3,2,1,0:T(8,128)(2,1)S(1)} %pad_maximum_fusion.u0, bf16[2,2,2,192,128]{4,3,2,1,0:T(8,128)(2,1)S(1)} %collective-permute-done.4.u1, ...), custom_call_target="tpu_custom_call" | custom-call | flops 1610612736 | bytes 7340032 | tf_op jit(solution)/shard_map/pallas_call | solution.py:100
  157.4 6.0 %collective-permute-start.10 = (f32[2,192,128]{2,1,0:T(8,128)}, f32[2,192,128]{2,1,0:T(8,128)S(1)}, u32[]{:S(2)}, u32[]{:S(2)}) collective-permute-start(f32[2,192,128]{2,1,0:T(8,128)} %get-tuple-element.35), channel_id=1, source_target_pairs={{0,8},{1,9},{2,10},{3,11},{4,12},{5,13},{6,14},{7,15},{8,40},{9,41... | collective-permute-start | bytes 589832 | tf_op jit(solution)/shard_map/ppermute | solution.py:38
  163.4 3.2 %collective-permute-start.12 = (f32[2,192,128]{2,1,0:T(8,128)}, f32[2,192,128]{2,1,0:T(8,128)S(1)}, u32[]{:S(2)}, u32[]{:S(2)}) collective-permute-start(f32[2,192,128]{2,1,0:T(8,128)} %get-tuple-element.37), channel_id=1, source_target_pairs={{0,24},{1,25},{2,26},{3,27},{4,28},{5,29},{6,30},{7,31},{8,56},{9,... | collective-permute-start | bytes 589832 | tf_op jit(solution)/shard_map/ppermute | solution.py:38
  167.3 1.9 %collective-permute-start.9 = (f32[2,192,128]{2,1,0:T(8,128)S(1)}, f32[2,192,128]{2,1,0:T(8,128)S(1)}, u32[]{:S(2)}, u32[]{:S(2)}) collective-permute-start(f32[2,192,128]{2,1,0:T(8,128)S(1)} %get-tuple-element.34), channel_id=1, source_target_pairs={{0,0},{1,1},{2,2},{3,3},{4,4},{5,5},{6,6},{7,7},{8,32},{9,33},{10,... | collective-permute-start | bytes 589832 | tf_op jit(solution)/shard_map/ppermute | solution.py:38
  169.2 2.0 %shard_map.31.refs_4_ = bf16[2,2,384,128]{3,2,1,0:T(8,128)(2,1)} custom-call(s32[1]{0:T(128)} %bitcast.odd_ref, f32[2,2]{1,0:T(2,128)} %wave_ref.3, f32[2,192,128]{2,1,0:T(8,128)} %copy-done.3, f32[2,192,128]{2,1,0:T(8,128)} %copy-done.4, f32[2,192,128]{2,1,0:T(8,128)} %copy-done.5, f32[2,192,128]{2,1,0:T(8,128)} %collective-permute-done.23.refs_3_), custom_call_target="tpu_custom_call" | custom-call | flops 393216 | bytes 1048576 | tf_op jit(solution)/shard_map/pallas_call | solution.py:155
  172.3 3.0 %collective-permute-done.11.refs_2_ = f32[2,192,128]{2,1,0:T(8,128)S(1)} collective-permute-done((f32[2,192,128]{2,1,0:T(8,128)}, f32[2,192,128]{2,1,0:T(8,128)S(1)}, u32[]{:S(2)}, u32[]{:S(2)}) %collective-permute-start.11) | collective-permute-done | bytes 196640 | tf_op jit(solution)/shard_map/ppermute | solution.py:38
  175.3 3.3 %collective-permute-done.12.refs_3_ = f32[2,192,128]{2,1,0:T(8,128)S(1)} collective-permute-done((f32[2,192,128]{2,1,0:T(8,128)}, f32[2,192,128]{2,1,0:T(8,128)S(1)}, u32[]{:S(2)}, u32[]{:S(2)}) %collective-permute-start.12) | collective-permute-done | bytes 196640 | tf_op jit(solution)/shard_map/ppermute | solution.py:38
  178.6 9.1 %collective-permute-done.9.refs_0_ = f32[2,192,128]{2,1,0:T(8,128)S(1)} collective-permute-done((f32[2,192,128]{2,1,0:T(8,128)S(1)}, f32[2,192,128]{2,1,0:T(8,128)S(1)}, u32[]{:S(2)}, u32[]{:S(2)}) %collective-permute-start.9) | collective-permute-done | bytes 196640 | tf_op jit(solution)/shard_map/ppermute | solution.py:38
  188.3 2.0 %shard_map.32 = bf16[2,2,384,128]{3,2,1,0:T(8,128)(2,1)} custom-call(s32[1]{0:T(128)} %bitcast.odd_ref, f32[2,2]{1,0:T(2,128)} %wave_ref.3, f32[2,192,128]{2,1,0:T(8,128)} %copy-done.9, f32[2,192,128]{2,1,0:T(8,128)} %copy-done.6, f32[2,192,128]{2,1,0:T(8,128)} %copy-done.7, f32[2,192,128]{2,1,0:T(8,128)} %copy-done.8, ...), custom_call_target="tpu_custom_call", output_to_operand_aliasing={{}: (6, {})} | custom-call | flops 393216 | bytes 1048576 | tf_op jit(solution)/shard_map/pallas_call | solution.py:155
  (59 shorter events, 21.6 us)
Async XLA Ops:
  1.5 3.8 %collective-permute-start = (bf16[2,16,192,128]{3,2,1,0:T(8,128)(2,1)S(1)}, bf16[2,16,192,128]{3,2,1,0:T(8,128)(2,1)S(1)}, u32[]{:S(2)}, u32[]{:S(2)}) collective-permute-start(bf16[2,16,192,128]{3,2,1,0:T(8,128)(2,1)S(1)} %constant_dynamic-slice_fusion), channel_id=1, source_target_pairs={{0,32},{32,0},{1,33},{33,1},{2,34},{34,2},{3,35},{35,3},{4,36},{36... | collective-permute-start | bytes 4718600 | tf_op jit(solution)/shard_map/ppermute | solution.py:42
  13.4 23.1 %all-to-all-start = ((bf16[8,2,2,192,128]{4,3,2,1,0:T(8,128)(2,1)}), bf16[8,2,2,192,128]{4,3,2,1,0:T(8,128)(2,1)S(1)}, u32[]{:S(2)}, u32[]{:S(2)}) async-start(bf16[8,2,2,192,128]{4,3,2,1,0:T(8,128)(2,1)} %shard_map.28), calls=%async_computation | async-start | bytes 3145728 | tf_op jit(solution)/shard_map/all_to_all | solution.py:186
  57.1 39.0 %all-to-all-start.1 = ((bf16[8,2,320,128]{3,2,1,0:T(8,128)(2,1)}), bf16[8,2,320,128]{3,2,1,0:T(8,128)(2,1)}, u32[]{:S(2)}, u32[]{:S(2)}) async-start(bf16[8,2,320,128]{3,2,1,0:T(8,128)(2,1)} %bitcast.11), calls=%async_computation.1 | async-start | bytes 2621440 | tf_op jit(solution)/shard_map/all_to_all | solution.py:186
  63.6 65.2 %collective-permute-start.7 = (bf16[8,2,2,192,128]{4,3,2,1,0:T(8,128)(2,1)S(1)}, bf16[8,2,2,192,128]{4,3,2,1,0:T(8,128)(2,1)S(1)}, u32[]{:S(2)}, u32[]{:S(2)}) collective-permute-start(bf16[8,2,2,192,128]{4,3,2,1,0:T(8,128)(2,1)S(1)} %all-to-all-done.ao_ref), channel_id=1, source_target_pairs={{0,32},{32,0},{1,33},{33,1},{2,34},{34,2},{3,35},{35,3},{4,36},{36... | collective-permute-start | bytes 4718600 | tf_op jit(solution)/shard_map/ppermute | solution.py:42
  66.9 5.3 %collective-permute-start.13 = (bf16[2,2,192,128]{3,2,1,0:T(8,128)(2,1)S(1)}, bf16[2,2,192,128]{3,2,1,0:T(8,128)(2,1)}, u32[]{:S(2)}, u32[]{:S(2)}) collective-permute-start(bf16[2,2,192,128]{3,2,1,0:T(8,128)(2,1)S(1)} %get-tuple-element.38), channel_id=1, source_target_pairs={{0,1},{1,0},{2,3},{3,2},{4,5},{5,4},{6,7},{7,6},{8,9},{9,8},{10,11... | collective-permute-start | bytes 589832 | tf_op jit(solution)/shard_map/ppermute | solution.py:38
  68.2 17.9 %collective-permute-start.14 = (bf16[2,2,192,128]{3,2,1,0:T(8,128)(2,1)}, bf16[2,2,192,128]{3,2,1,0:T(8,128)(2,1)}, u32[]{:S(2)}, u32[]{:S(2)}) collective-permute-start(bf16[2,2,192,128]{3,2,1,0:T(8,128)(2,1)} %get-tuple-element.49), channel_id=1, source_target_pairs={{0,128},{1,129},{2,130},{3,131},{4,132},{5,133},{6,134},{7,135},{8... | collective-permute-start | bytes 589832 | tf_op jit(solution)/shard_map/ppermute | solution.py:38
  69.5 24.1 %collective-permute-start.15 = (bf16[2,2,192,128]{3,2,1,0:T(8,128)(2,1)}, bf16[2,2,192,128]{3,2,1,0:T(8,128)(2,1)}, u32[]{:S(2)}, u32[]{:S(2)}) collective-permute-start(bf16[2,2,192,128]{3,2,1,0:T(8,128)(2,1)} %get-tuple-element.49), channel_id=1, source_target_pairs={{0,129},{1,128},{2,131},{3,130},{4,133},{5,132},{6,135},{7,134},{8... | collective-permute-start | bytes 589832 | tf_op jit(solution)/shard_map/ppermute | solution.py:38
  70.8 26.5 %collective-permute-start.1 = (bf16[2,2,192,128]{3,2,1,0:T(8,128)(2,1)S(1)}, bf16[2,2,192,128]{3,2,1,0:T(8,128)(2,1)}, u32[]{:S(2)}, u32[]{:S(2)}) collective-permute-start(bf16[2,2,192,128]{3,2,1,0:T(8,128)(2,1)S(1)} %get-tuple-element.29), channel_id=1, source_target_pairs={{0,1},{1,0},{2,3},{3,2},{4,5},{5,4},{6,7},{7,6},{8,9},{9,8},{10,11... | collective-permute-start | bytes 589832 | tf_op jit(solution)/shard_map/ppermute | solution.py:38
  72.2 26.5 %collective-permute-start.2 = (bf16[2,2,192,128]{3,2,1,0:T(8,128)(2,1)}, bf16[2,2,192,128]{3,2,1,0:T(8,128)(2,1)}, u32[]{:S(2)}, u32[]{:S(2)}) collective-permute-start(bf16[2,2,192,128]{3,2,1,0:T(8,128)(2,1)} %get-tuple-element.51), channel_id=1, source_target_pairs={{0,128},{1,129},{2,130},{3,131},{4,132},{5,133},{6,134},{7,135},{8... | collective-permute-start | bytes 589832 | tf_op jit(solution)/shard_map/ppermute | solution.py:38
  93.6 38.0 %collective-permute-start.19 = (bf16[8,2,320,128]{3,2,1,0:T(8,128)(2,1)}, bf16[8,2,320,128]{3,2,1,0:T(8,128)(2,1)}, u32[]{:S(2)}, u32[]{:S(2)}) collective-permute-start(bf16[8,2,320,128]{3,2,1,0:T(8,128)(2,1)} %all_to_all.15.bo_ref), channel_id=1, source_target_pairs={{0,32},{32,0},{1,33},{33,1},{2,34},{34,2},{3,35},{35,3},{4,36},{36... | collective-permute-start | bytes 3932168 | tf_op jit(solution)/shard_map/ppermute | solution.py:42
  96.1 35.5 %copy-start.1 = (s32[4]{0:T(128)S(1)}, s32[4]{0:T(128)}, u32[]{:S(2)}) copy-start(s32[4]{0:T(128)} %pad_add_fusion.core_ref.place_ref) | copy-start | bytes 52
  96.1 35.5 %copy-start = (bf16[8,2,320,128]{3,2,1,0:T(8,128)(2,1)S(1)}, bf16[8,2,320,128]{3,2,1,0:T(8,128)(2,1)}, u32[]{:S(2)}) copy-start(bf16[8,2,320,128]{3,2,1,0:T(8,128)(2,1)} %all_to_all.15.bo_ref) | copy-start | bytes 3932164
  96.1 55.5 %collective-permute-start.8 = (bf16[8,2,320,128]{3,2,1,0:T(8,128)(2,1)}, bf16[8,2,320,128]{3,2,1,0:T(8,128)(2,1)S(1)}, u32[]{:S(2)}, u32[]{:S(2)}) collective-permute-start(bf16[8,2,320,128]{3,2,1,0:T(8,128)(2,1)} %all-to-all-done.1.bo_ref), channel_id=1, source_target_pairs={{0,32},{32,0},{1,33},{33,1},{2,34},{34,2},{3,35},{35,3},{4,36},{36... | collective-permute-start | bytes 3932168 | tf_op jit(solution)/shard_map/ppermute | solution.py:42
  97.3 14.0 %collective-permute-start.16 = (bf16[2,2,2,192,128]{4,3,2,1,0:T(8,128)(2,1)S(1)}, bf16[2,2,2,192,128]{4,3,2,1,0:T(8,128)(2,1)S(1)}, u32[]{:S(2)}, u32[]{:S(2)}) collective-permute-start(bf16[2,2,2,192,128]{4,3,2,1,0:T(8,128)(2,1)S(1)} %pad_maximum_fusion.1.u0), channel_id=1, source_target_pairs={{0,2},{2,4},{4,6},{6,0},{1,3},{3,5},{5,7},{7,1},{8,10},{10,12},{12... | collective-permute-start | bytes 1179656 | tf_op jit(solution)/shard_map/ppermute | solution.py:205
  98.7 10.0 %collective-permute-start.3 = (bf16[2,2,192,128]{3,2,1,0:T(8,128)(2,1)}, bf16[2,2,192,128]{3,2,1,0:T(8,128)(2,1)S(1)}, u32[]{:S(2)}, u32[]{:S(2)}) collective-permute-start(bf16[2,2,192,128]{3,2,1,0:T(8,128)(2,1)} %get-tuple-element.51), channel_id=1, source_target_pairs={{0,129},{1,128},{2,131},{3,130},{4,133},{5,132},{6,135},{7,134},{8... | collective-permute-start | bytes 589832 | tf_op jit(solution)/shard_map/ppermute | solution.py:38
  108.7 8.1 %collective-permute-start.17 = (bf16[2,2,2,192,128]{4,3,2,1,0:T(8,128)(2,1)S(1)}, bf16[2,2,2,192,128]{4,3,2,1,0:T(8,128)(2,1)S(1)}, u32[]{:S(2)}, u32[]{:S(2)}) collective-permute-start(bf16[2,2,2,192,128]{4,3,2,1,0:T(8,128)(2,1)S(1)} %pad_maximum_fusion.1.u0), channel_id=1, source_target_pairs={{0,4},{2,6},{4,0},{6,2},{1,5},{3,7},{5,1},{7,3},{8,12},{10,14},{12... | collective-permute-start | bytes 1179656 | tf_op jit(solution)/shard_map/ppermute | solution.py:205
  111.3 14.1 %collective-permute-start.18 = (bf16[2,2,2,192,128]{4,3,2,1,0:T(8,128)(2,1)S(1)}, bf16[2,2,2,192,128]{4,3,2,1,0:T(8,128)(2,1)S(1)}, u32[]{:S(2)}, u32[]{:S(2)}) collective-permute-start(bf16[2,2,2,192,128]{4,3,2,1,0:T(8,128)(2,1)S(1)} %pad_maximum_fusion.1.u0), channel_id=1, source_target_pairs={{0,6},{2,0},{4,2},{6,4},{1,7},{3,1},{5,3},{7,5},{8,14},{10,8},{12,... | collective-permute-start | bytes 1179656 | tf_op jit(solution)/shard_map/ppermute | solution.py:205
  116.8 25.9 %collective-permute-start.4 = (bf16[2,2,2,192,128]{4,3,2,1,0:T(8,128)(2,1)S(1)}, bf16[2,2,2,192,128]{4,3,2,1,0:T(8,128)(2,1)S(1)}, u32[]{:S(2)}, u32[]{:S(2)}) collective-permute-start(bf16[2,2,2,192,128]{4,3,2,1,0:T(8,128)(2,1)S(1)} %pad_maximum_fusion.u0), channel_id=1, source_target_pairs={{0,2},{2,4},{4,6},{6,0},{1,3},{3,5},{5,7},{7,1},{8,10},{10,12},{12... | collective-permute-start | bytes 1179656 | tf_op jit(solution)/shard_map/ppermute | solution.py:205
  125.4 21.3 %collective-permute-start.5 = (bf16[2,2,2,192,128]{4,3,2,1,0:T(8,128)(2,1)S(1)}, bf16[2,2,2,192,128]{4,3,2,1,0:T(8,128)(2,1)S(1)}, u32[]{:S(2)}, u32[]{:S(2)}) collective-permute-start(bf16[2,2,2,192,128]{4,3,2,1,0:T(8,128)(2,1)S(1)} %pad_maximum_fusion.u0), channel_id=1, source_target_pairs={{0,4},{2,6},{4,0},{6,2},{1,5},{3,7},{5,1},{7,3},{8,12},{10,14},{12... | collective-permute-start | bytes 1179656 | tf_op jit(solution)/shard_map/ppermute | solution.py:205
  128.8 17.9 %collective-permute-start.6 = (bf16[2,2,2,192,128]{4,3,2,1,0:T(8,128)(2,1)S(1)}, bf16[2,2,2,192,128]{4,3,2,1,0:T(8,128)(2,1)S(1)}, u32[]{:S(2)}, u32[]{:S(2)}) collective-permute-start(bf16[2,2,2,192,128]{4,3,2,1,0:T(8,128)(2,1)S(1)} %pad_maximum_fusion.u0), channel_id=1, source_target_pairs={{0,6},{2,0},{4,2},{6,4},{1,7},{3,1},{5,3},{7,5},{8,14},{10,8},{12,... | collective-permute-start | bytes 1179656 | tf_op jit(solution)/shard_map/ppermute | solution.py:205
  136.7 26.7 %collective-permute-start.20 = (f32[2,192,128]{2,1,0:T(8,128)S(1)}, f32[2,192,128]{2,1,0:T(8,128)S(1)}, u32[]{:S(2)}, u32[]{:S(2)}) collective-permute-start(f32[2,192,128]{2,1,0:T(8,128)S(1)} %get-tuple-element.43), channel_id=1, source_target_pairs={{0,0},{1,1},{2,2},{3,3},{4,4},{5,5},{6,6},{7,7},{8,32},{9,33},{10,... | collective-permute-start | bytes 589832 | tf_op jit(solution)/shard_map/ppermute | solution.py:38
  142.7 20.8 %collective-permute-start.21 = (f32[2,192,128]{2,1,0:T(8,128)S(1)}, f32[2,192,128]{2,1,0:T(8,128)S(1)}, u32[]{:S(2)}, u32[]{:S(2)}) collective-permute-start(f32[2,192,128]{2,1,0:T(8,128)S(1)} %get-tuple-element.44), channel_id=1, source_target_pairs={{0,8},{1,9},{2,10},{3,11},{4,12},{5,13},{6,14},{7,15},{8,40},{9,41... | collective-permute-start | bytes 589832 | tf_op jit(solution)/shard_map/ppermute | solution.py:38
  146.7 19.9 %collective-permute-start.22 = (f32[2,192,128]{2,1,0:T(8,128)S(1)}, f32[2,192,128]{2,1,0:T(8,128)S(1)}, u32[]{:S(2)}, u32[]{:S(2)}) collective-permute-start(f32[2,192,128]{2,1,0:T(8,128)S(1)} %get-tuple-element.45), channel_id=1, source_target_pairs={{0,16},{1,17},{2,18},{3,19},{4,20},{5,21},{6,22},{7,23},{8,48},{9,... | collective-permute-start | bytes 589832 | tf_op jit(solution)/shard_map/ppermute | solution.py:38
  146.7 22.5 %collective-permute-start.23 = (f32[2,192,128]{2,1,0:T(8,128)S(1)}, f32[2,192,128]{2,1,0:T(8,128)}, u32[]{:S(2)}, u32[]{:S(2)}) collective-permute-start(f32[2,192,128]{2,1,0:T(8,128)S(1)} %get-tuple-element.46), channel_id=1, source_target_pairs={{0,24},{1,25},{2,26},{3,27},{4,28},{5,29},{6,30},{7,31},{8,56},{9,... | collective-permute-start | bytes 589832 | tf_op jit(solution)/shard_map/ppermute | solution.py:38
  157.4 14.8 %collective-permute-start.10 = (f32[2,192,128]{2,1,0:T(8,128)}, f32[2,192,128]{2,1,0:T(8,128)S(1)}, u32[]{:S(2)}, u32[]{:S(2)}) collective-permute-start(f32[2,192,128]{2,1,0:T(8,128)} %get-tuple-element.35), channel_id=1, source_target_pairs={{0,8},{1,9},{2,10},{3,11},{4,12},{5,13},{6,14},{7,15},{8,40},{9,41... | collective-permute-start | bytes 589832 | tf_op jit(solution)/shard_map/ppermute | solution.py:38
  163.4 3.2 %copy-start.3 = (f32[2,192,128]{2,1,0:T(8,128)}, f32[2,192,128]{2,1,0:T(8,128)S(1)}, u32[]{:S(2)}) copy-start(f32[2,192,128]{2,1,0:T(8,128)S(1)} %collective-permute-done.20.refs_0_) | copy-start | bytes 589828
  163.4 11.9 %collective-permute-start.11 = (f32[2,192,128]{2,1,0:T(8,128)}, f32[2,192,128]{2,1,0:T(8,128)S(1)}, u32[]{:S(2)}, u32[]{:S(2)}) collective-permute-start(f32[2,192,128]{2,1,0:T(8,128)} %get-tuple-element.36), channel_id=1, source_target_pairs={{0,16},{1,17},{2,18},{3,19},{4,20},{5,21},{6,22},{7,23},{8,48},{9,... | collective-permute-start | bytes 589832 | tf_op jit(solution)/shard_map/ppermute | solution.py:38
  163.4 15.1 %collective-permute-start.12 = (f32[2,192,128]{2,1,0:T(8,128)}, f32[2,192,128]{2,1,0:T(8,128)S(1)}, u32[]{:S(2)}, u32[]{:S(2)}) collective-permute-start(f32[2,192,128]{2,1,0:T(8,128)} %get-tuple-element.37), channel_id=1, source_target_pairs={{0,24},{1,25},{2,26},{3,27},{4,28},{5,29},{6,30},{7,31},{8,56},{9,... | collective-permute-start | bytes 589832 | tf_op jit(solution)/shard_map/ppermute | solution.py:38
  167.3 20.3 %collective-permute-start.9 = (f32[2,192,128]{2,1,0:T(8,128)S(1)}, f32[2,192,128]{2,1,0:T(8,128)S(1)}, u32[]{:S(2)}, u32[]{:S(2)}) collective-permute-start(f32[2,192,128]{2,1,0:T(8,128)S(1)} %get-tuple-element.34), channel_id=1, source_target_pairs={{0,0},{1,1},{2,2},{3,3},{4,4},{5,5},{6,6},{7,7},{8,32},{9,33},{10,... | collective-permute-start | bytes 589832 | tf_op jit(solution)/shard_map/ppermute | solution.py:38
  172.3 15.4 %copy-start.6 = (f32[2,192,128]{2,1,0:T(8,128)}, f32[2,192,128]{2,1,0:T(8,128)S(1)}, u32[]{:S(2)}) copy-start(f32[2,192,128]{2,1,0:T(8,128)S(1)} %collective-permute-done.10.refs_1_) | copy-start | bytes 589828
  175.3 12.4 %copy-start.7 = (f32[2,192,128]{2,1,0:T(8,128)}, f32[2,192,128]{2,1,0:T(8,128)S(1)}, u32[]{:S(2)}) copy-start(f32[2,192,128]{2,1,0:T(8,128)S(1)} %collective-permute-done.11.refs_2_) | copy-start | bytes 589828
  178.6 9.1 %copy-start.8 = (f32[2,192,128]{2,1,0:T(8,128)}, f32[2,192,128]{2,1,0:T(8,128)S(1)}, u32[]{:S(2)}) copy-start(f32[2,192,128]{2,1,0:T(8,128)S(1)} %collective-permute-done.12.refs_3_) | copy-start | bytes 589828
  (5 other events, 7.0 us)

commit v11 on v7

--- a/solution.py
+++ b/solution.py
@@ -98,27 +98,29 @@
     )(place, *turned, a_own, a_peer, b_own, b_peer)
 
 
-def finish(odd, wavelet, *blocks):
+def finish(g, odd, wavelet, blocks, prior=()):
     half, lanes = blocks[0].shape[1:]
 
     def kernel(odd_ref, wave_ref, *refs):
-        for g in range(2):
-            wave_real, wave_imag = wave_ref[0, g], wave_ref[1, g]
-            for t in range(2):
-                start = pl.multiple_of((odd_ref[0] ^ t) * half, half)
-                one, two = refs[4 * g + t], refs[4 * g + t + 2]
-                real, imag = one[0] + two[0], one[1] + two[1]
-                refs[8][0, g, pl.ds(start, half)] = (-(wave_real * real - wave_imag * imag)).astype(jnp.bfloat16)
-                refs[8][1, g, pl.ds(start, half)] = (-(wave_real * imag + wave_imag * real)).astype(jnp.bfloat16)
+        wave_real, wave_imag = wave_ref[0, g], wave_ref[1, g]
+        out = refs[-1]
+        for t in range(2):
+            start = pl.multiple_of((odd_ref[0] ^ t) * half, half)
+            one, two = refs[t], refs[t + 2]
+            real, imag = one[0] + two[0], one[1] + two[1]
+            out[0, 0, pl.ds(start, half)] = (-(wave_real * real - wave_imag * imag)).astype(jnp.bfloat16)
+            out[1, 0, pl.ds(start, half)] = (-(wave_real * imag + wave_imag * real)).astype(jnp.bfloat16)
 
     smem, vmem = pl.BlockSpec(memory_space=pltpu.SMEM), pl.BlockSpec(memory_space=pltpu.VMEM)
     return pl.pallas_call(
         kernel,
+        grid=(1,),
         out_shape=jax.ShapeDtypeStruct((2, 2, 2 * half, lanes), jnp.bfloat16),
-        in_specs=[smem, smem] + [vmem] * 8,
-        out_specs=vmem,
-        cost_estimate=pl.CostEstimate(flops=8 * 4 * half * lanes, bytes_accessed=2 << 20, transcendentals=0),
-    )(odd, wavelet, *blocks)
+        in_specs=[smem, smem] + [vmem] * 4 + [pl.BlockSpec(memory_space=pl.ANY)] * len(prior),
+        out_specs=pl.BlockSpec((2, 1, 2 * half, lanes), lambda i: (0, g, 0, 0)),
+        input_output_aliases={6: 0} if prior else {},
+        cost_estimate=pl.CostEstimate(flops=8 * 2 * half * lanes, bytes_accessed=1 << 20, transcendentals=0),
+    )(odd, wavelet, *blocks, *prior)
 
 
 def step(spectra, wavelet):
@@ -168,19 +170,20 @@
     turned = [turn(g) for g in range(2)]
 
     def homeward(blocks):
-        return [
-            send(
-                block,
-                lambda q, r, c, x, y, h: (r, x // 2, x % 2, (2 * q + c) ^ t, y, h),
+        moved_on = []
+        for t, block in enumerate(blocks):
+            moved_on.append(
+                send(block, lambda q, r, c, x, y, h: (r, x // 2, x % 2, (2 * q + c) ^ t, y, h))
             )
-            for t, block in enumerate(blocks)
-        ]
+        return moved_on
 
     blocks = []
     for g in range(2):
         partial = contract(g, place, turned[g], a_own, a_peer, b_own[g], b_peer[g])
         blocks.append(homeward(partial))
-    return finish(jnp.stack([x % 2]).astype(jnp.int32), wavelet, *blocks[0], *blocks[1])
+    odd = jnp.stack([x % 2]).astype(jnp.int32)
+    early = finish(0, odd, wavelet, blocks[0])
+    return finish(1, odd, wavelet, blocks[1], (early,))
 
 
 def solution(mesh):

time: 191 us -> 191 us (level)
  waiting for transfers between devices: 82.9 us -> 80.9 us
    ppermute x14, waiting for transfers between devices: 53 us -> 51 us  [send(): return lax.ppermute(value, AXES, moved(target))]
    pallas_call x1 -> x2, Pallas kernels: 2.36 us -> 3.97 us  [finish(): pl.pallas_call(kernel, grid=(1,), out_shape=jax.ShapeDtypeStruct((2, 2, 2...]
  transfers between devices with their start and end apart: 26 -> 26, of which waited for: 10 -> 10; matrix products, arithmetic and copies ran while one was open for 5% -> 5% of each run, Pallas kernels for 5% -> 6%
where the time goes in v11:
time: 191 us; the launch traced here: 190 us
  waiting for transfers between devices  80.9 us (42%)
  starting transfers between devices  51.2 us (27%)
  blocking collectives  20.6 us (11%)
  local copies, waits for them, and re-layouts  15.3 us (8%)
  Pallas kernels  13.6 us (7%)
  other arithmetic  8.23 us (4%)
    ppermute x14, waiting for transfers between devices, send(): return lax.ppermute(value, AXES, moved(target))  51 us
    ppermute x14, starting transfers between devices, send(): return lax.ppermute(value, AXES, moved(target))  31.2 us
    all_to_all x1, blocking collectives, exchange(): lax.all_to_all(block, ('x', 'zr'), split_axis=0, concat_axis=0, tiled=True)  20.6 us
    ppermute x6, waiting for transfers between devices, turn(): lax.ppermute(pieces, 'y', [(i, (i + s) % 4) for i in range(4)])  13.9 us
    all_to_all x2, waiting for transfers between devices, exchange(): lax.all_to_all(block, ('x', 'zr'), split_axis=0, concat_axis=0, tiled=True)  13 us
    all_to_all x2, starting transfers between devices, exchange(): lax.all_to_all(block, ('x', 'zr'), split_axis=0, concat_axis=0, tiled=True)  11.2 us
    unnamed x34, local copies, waits for them, and re-layouts  10.2 us
    pallas_call x2, Pallas kernels, contract(): pl.pallas_call(kernel, out_shape=(result,) * 4, in_specs=[pl.BlockSpec(me...  9.59 us
  transfers between devices with their start and end apart: 26, of which 10 were waited for; matrix products, arithmetic and copies ran while one was open for 5% of the time, Pallas kernels for 6%

profile of v11, /device:TPU:213, one launch (start us, length us, event | category | flops | bytes accessed | tf_op | source)
XLA Modules:
  0.0 190.1 jit_solution(4629663433536481777)
XLA Ops:
  0.0 1.5 constant_dynamic-slice_fusion
  2.3 3.0 %collective-permute-done = bf16[2,16,192,128]{3,2,1,0:T(8,128)(2,1)S(1)} collective-permute-done((bf16[2,16,192,128]{3,2,1,0:T(8,128)(2,1)S(1)}, bf16[2,16,192,128]{3,2,1,0:T(8,128)(2,1)S(1)}, u32[]{:S(2)}, u32[]{:S(2)}) %collective-permute-start) | collective-permute-done | bytes 1572896 | tf_op jit(solution)/shard_map/ppermute | solution.py:42
  5.3 1.6 slice_select_fusion
  6.9 1.3 copy.4
  8.2 4.7 %all-to-all-start = ((bf16[8,2,2,192,128]{4,3,2,1,0:T(8,128)(2,1)}), bf16[8,2,2,192,128]{4,3,2,1,0:T(8,128)(2,1)S(1)}, u32[]{:S(2)}, u32[]{:S(2)}) async-start(bf16[8,2,2,192,128]{4,3,2,1,0:T(8,128)(2,1)} %bitcast.7), calls=%async_computation | async-start | bytes 3145728 | tf_op jit(solution)/shard_map/all_to_all | solution.py:147
  14.1 2.7 %maximum_select_fusion = bf16[2,16,320,128]{3,2,1,0:T(8,128)(2,1)S(1)} fusion(bf16[2,16,192,128]{3,2,1,0:T(8,128)(2,1)S(1)} %collective-permute-done, bf16[2,16,128,128]{3,2,1,0:T(8,128)(2,1)S(1)} %slice-done, bf16[2,16,512,128]{3,2,1,0:T(8,128)(2,1)} %param.2, pred[]{:T(512)S(6)} %eq.12), kind=kLoop, calls=%fused_computation | loop fusion | flops 6553600 | bytes 7864321 | tf_op jit(solution)/shard_map/jit(_where)/select_n | solution.py:141
  18.3 13.0 %all-to-all-done.ao_ref = bf16[8,2,2,192,128]{4,3,2,1,0:T(8,128)(2,1)S(1)} async-done(((bf16[8,2,2,192,128]{4,3,2,1,0:T(8,128)(2,1)}), bf16[8,2,2,192,128]{4,3,2,1,0:T(8,128)(2,1)S(1)}, u32[]{:S(2)}, u32[]{:S(2)}) %all-to-all-start) | async-done | bytes 1572896 | tf_op jit(solution)/shard_map/all_to_all | solution.py:147
  31.3 20.6 %all_to_all.15.bo_ref = bf16[8,2,320,128]{3,2,1,0:T(8,128)(2,1)} all-to-all(bf16[8,2,320,128]{3,2,1,0:T(8,128)(2,1)S(1)} %bitcast.48), channel_id=1, replica_groups=mesh['zq'=2,'zr'=2,'core'=2,'x'=4,'y'=4,'zh'=2] {'x','zr'}, dimensions={0} | all-to-all | bytes 2621440 | tf_op jit(solution)/shard_map/all_to_all | solution.py:147
  52.0 6.5 %all-to-all-start.1 = ((bf16[8,2,320,128]{3,2,1,0:T(8,128)(2,1)}), bf16[8,2,320,128]{3,2,1,0:T(8,128)(2,1)}, u32[]{:S(2)}, u32[]{:S(2)}) async-start(bf16[8,2,320,128]{3,2,1,0:T(8,128)(2,1)} %bitcast.14), calls=%async_computation.1 | async-start | bytes 2621440 | tf_op jit(solution)/shard_map/all_to_all | solution.py:147
  58.4 2.5 %collective-permute-start.7 = (bf16[8,2,2,192,128]{4,3,2,1,0:T(8,128)(2,1)S(1)}, bf16[8,2,2,192,128]{4,3,2,1,0:T(8,128)(2,1)S(1)}, u32[]{:S(2)}, u32[]{:S(2)}) collective-permute-start(bf16[8,2,2,192,128]{4,3,2,1,0:T(8,128)(2,1)S(1)} %all-to-all-done.ao_ref), channel_id=1, source_target_pairs={{0,32},{32,0},{1,33},{33,1},{2,34},{34,2},{3,35},{35,3},{4,36},{36... | collective-permute-start | bytes 4718600 | tf_op jit(solution)/shard_map/ppermute | solution.py:42
  61.8 1.3 collective-permute-start.13
  65.7 1.3 collective-permute-start.1
  68.3 12.7 %collective-permute-done.14 = bf16[2,2,192,128]{3,2,1,0:T(8,128)(2,1)} collective-permute-done((bf16[2,2,192,128]{3,2,1,0:T(8,128)(2,1)}, bf16[2,2,192,128]{3,2,1,0:T(8,128)(2,1)}, u32[]{:S(2)}, u32[]{:S(2)}) %collective-permute-start.14) | collective-permute-done | bytes 196640 | tf_op jit(solution)/shard_map/ppermute | solution.py:38
  81.0 7.4 %collective-permute-done.15 = bf16[2,2,192,128]{3,2,1,0:T(8,128)(2,1)} collective-permute-done((bf16[2,2,192,128]{3,2,1,0:T(8,128)(2,1)}, bf16[2,2,192,128]{3,2,1,0:T(8,128)(2,1)}, u32[]{:S(2)}, u32[]{:S(2)}) %collective-permute-start.15) | collective-permute-done | bytes 196640 | tf_op jit(solution)/shard_map/ppermute | solution.py:38
  89.1 1.8 select_bitcast_fusion
  94.4 8.6 %collective-permute-done.3 = bf16[2,2,192,128]{3,2,1,0:T(8,128)(2,1)S(1)} collective-permute-done((bf16[2,2,192,128]{3,2,1,0:T(8,128)(2,1)}, bf16[2,2,192,128]{3,2,1,0:T(8,128)(2,1)S(1)}, u32[]{:S(2)}, u32[]{:S(2)}) %collective-permute-start.3) | collective-permute-done | bytes 196640 | tf_op jit(solution)/shard_map/ppermute | solution.py:38
  106.1 5.0 %collective-permute-done.17.u2 = bf16[2,2,2,192,128]{4,3,2,1,0:T(8,128)(2,1)S(1)} collective-permute-done((bf16[2,2,2,192,128]{4,3,2,1,0:T(8,128)(2,1)S(1)}, bf16[2,2,2,192,128]{4,3,2,1,0:T(8,128)(2,1)S(1)}, u32[]{:S(2)}, u32[]{:S(2)}) %collective-permute-start.17) | collective-permute-done | bytes 393248 | tf_op jit(solution)/shard_map/ppermute | solution.py:166
  112.1 8.9 %collective-permute-done.18.u3 = bf16[2,2,2,192,128]{4,3,2,1,0:T(8,128)(2,1)S(1)} collective-permute-done((bf16[2,2,2,192,128]{4,3,2,1,0:T(8,128)(2,1)S(1)}, bf16[2,2,2,192,128]{4,3,2,1,0:T(8,128)(2,1)S(1)}, u32[]{:S(2)}, u32[]{:S(2)}) %collective-permute-start.18) | collective-permute-done | bytes 393248 | tf_op jit(solution)/shard_map/ppermute | solution.py:166
  121.7 2.3 %collective-permute-start.6 = (bf16[2,2,2,192,128]{4,3,2,1,0:T(8,128)(2,1)S(1)}, bf16[2,2,2,192,128]{4,3,2,1,0:T(8,128)(2,1)}, u32[]{:S(2)}, u32[]{:S(2)}) collective-permute-start(bf16[2,2,2,192,128]{4,3,2,1,0:T(8,128)(2,1)S(1)} %pad_maximum_fusion.u0), channel_id=1, source_target_pairs={{0,6},{2,0},{4,2},{6,4},{1,7},{3,1},{5,3},{7,5},{8,14},{10,8},{12,... | collective-permute-start | bytes 1179656 | tf_op jit(solution)/shard_map/ppermute | solution.py:166
  129.4 4.4 %shard_map.29 = (f32[2,192,128]{2,1,0:T(8,128)S(1)}, f32[2,192,128]{2,1,0:T(8,128)S(1)}, f32[2,192,128]{2,1,0:T(8,128)S(1)}, f32[2,192,128]{2,1,0:T(8,128)}) custom-call(s32[4]{0:T(128)S(1)} %pad_add_fusion.place_ref, bf16[2,2,2,192,128]{4,3,2,1,0:T(8,128)(2,1)S(1)} %copy-done.2, bf16[2,2,2,192,128]{4,3,2,1,0:T(8,128)(2,1)S(1)} %copy-done.4, ...), custom_call_target="tpu_custom_call" | custom-call | flops 1610612736 | bytes 7340032 | tf_op jit(solution)/shard_map/pallas_call | solution.py:88
  133.8 7.1 %collective-permute-start.20 = (f32[2,192,128]{2,1,0:T(8,128)S(1)}, f32[2,192,128]{2,1,0:T(8,128)S(1)}, u32[]{:S(2)}, u32[]{:S(2)}) collective-permute-start(f32[2,192,128]{2,1,0:T(8,128)S(1)} %get-tuple-element.43), channel_id=1, source_target_pairs={{0,0},{1,1},{2,2},{3,3},{4,4},{5,5},{6,6},{7,7},{8,32},{9,33},{10,... | collective-permute-start | bytes 589832 | tf_op jit(solution)/shard_map/ppermute | solution.py:38
  141.0 4.7 %collective-permute-start.21 = (f32[2,192,128]{2,1,0:T(8,128)S(1)}, f32[2,192,128]{2,1,0:T(8,128)S(1)}, u32[]{:S(2)}, u32[]{:S(2)}) collective-permute-start(f32[2,192,128]{2,1,0:T(8,128)S(1)} %get-tuple-element.44), channel_id=1, source_target_pairs={{0,8},{1,9},{2,10},{3,11},{4,12},{5,13},{6,14},{7,15},{8,40},{9,41... | collective-permute-start | bytes 589832 | tf_op jit(solution)/shard_map/ppermute | solution.py:38
  145.6 4.1 %collective-permute-start.23 = (f32[2,192,128]{2,1,0:T(8,128)}, f32[2,192,128]{2,1,0:T(8,128)}, u32[]{:S(2)}, u32[]{:S(2)}) collective-permute-start(f32[2,192,128]{2,1,0:T(8,128)} %get-tuple-element.46), channel_id=1, source_target_pairs={{0,24},{1,25},{2,26},{3,27},{4,28},{5,29},{6,30},{7,31},{8,56},{9,... | collective-permute-start | bytes 589832 | tf_op jit(solution)/shard_map/ppermute | solution.py:38
  149.7 5.2 %shard_map.28 = (f32[2,192,128]{2,1,0:T(8,128)}, f32[2,192,128]{2,1,0:T(8,128)}, f32[2,192,128]{2,1,0:T(8,128)}, f32[2,192,128]{2,1,0:T(8,128)}) custom-call(s32[4]{0:T(128)S(1)} %pad_add_fusion.place_ref, bf16[2,2,2,192,128]{4,3,2,1,0:T(8,128)(2,1)S(1)} %pad_maximum_fusion.u0, bf16[2,2,2,192,128]{4,3,2,1,0:T(8,128)(2,1)} %collective-permute-done.4.u1, ...), custom_call_target="tpu_custom_call" | custom-call | flops 1610612736 | bytes 7340032 | tf_op jit(solution)/shard_map/pallas_call | solution.py:88
  154.9 2.3 %collective-permute-start.10 = (f32[2,192,128]{2,1,0:T(8,128)}, f32[2,192,128]{2,1,0:T(8,128)S(1)}, u32[]{:S(2)}, u32[]{:S(2)}) collective-permute-start(f32[2,192,128]{2,1,0:T(8,128)} %get-tuple-element.35), channel_id=1, source_target_pairs={{0,8},{1,9},{2,10},{3,11},{4,12},{5,13},{6,14},{7,15},{8,40},{9,41... | collective-permute-start | bytes 589832 | tf_op jit(solution)/shard_map/ppermute | solution.py:38
  157.3 3.3 %collective-permute-start.12 = (f32[2,192,128]{2,1,0:T(8,128)}, f32[2,192,128]{2,1,0:T(8,128)S(1)}, u32[]{:S(2)}, u32[]{:S(2)}) collective-permute-start(f32[2,192,128]{2,1,0:T(8,128)} %get-tuple-element.37), channel_id=1, source_target_pairs={{0,24},{1,25},{2,26},{3,27},{4,28},{5,29},{6,30},{7,31},{8,56},{9,... | collective-permute-start | bytes 589832 | tf_op jit(solution)/shard_map/ppermute | solution.py:38
  161.3 1.9 %collective-permute-start.9 = (f32[2,192,128]{2,1,0:T(8,128)}, f32[2,192,128]{2,1,0:T(8,128)S(1)}, u32[]{:S(2)}, u32[]{:S(2)}) collective-permute-start(f32[2,192,128]{2,1,0:T(8,128)} %get-tuple-element.34), channel_id=1, source_target_pairs={{0,0},{1,1},{2,2},{3,3},{4,4},{5,5},{6,6},{7,7},{8,32},{9,33},{10,... | collective-permute-start | bytes 589832 | tf_op jit(solution)/shard_map/ppermute | solution.py:38
  163.2 2.0 %shard_map.30.refs_4_ = bf16[2,2,384,128]{3,2,1,0:T(8,128)(2,1)} custom-call(s32[1]{0:T(128)} %bitcast.odd_ref, f32[2,2]{1,0:T(2,128)} %wave_ref.3, f32[2,192,128]{2,1,0:T(8,128)} %copy-done.9, f32[2,192,128]{2,1,0:T(8,128)} %copy-done.10, f32[2,192,128]{2,1,0:T(8,128)} %copy-done.11, f32[2,192,128]{2,1,0:T(8,128)} %collective-permute-done.23.refs_3_), custom_call_target="tpu_custom_call" | custom-call | flops 393216 | bytes 1048576 | tf_op jit(solution)/shard_map/pallas_call | solution.py:115
  165.2 6.3 %collective-permute-done.10.refs_1_ = f32[2,192,128]{2,1,0:T(8,128)S(1)} collective-permute-done((f32[2,192,128]{2,1,0:T(8,128)}, f32[2,192,128]{2,1,0:T(8,128)S(1)}, u32[]{:S(2)}, u32[]{:S(2)}) %collective-permute-start.10) | collective-permute-done | bytes 196640 | tf_op jit(solution)/shard_map/ppermute | solution.py:38
  171.5 5.5 %collective-permute-done.12.refs_3_ = f32[2,192,128]{2,1,0:T(8,128)S(1)} collective-permute-done((f32[2,192,128]{2,1,0:T(8,128)}, f32[2,192,128]{2,1,0:T(8,128)S(1)}, u32[]{:S(2)}, u32[]{:S(2)}) %collective-permute-start.12) | collective-permute-done | bytes 196640 | tf_op jit(solution)/shard_map/ppermute | solution.py:38
  177.0 10.4 %collective-permute-done.9.refs_0_ = f32[2,192,128]{2,1,0:T(8,128)S(1)} collective-permute-done((f32[2,192,128]{2,1,0:T(8,128)}, f32[2,192,128]{2,1,0:T(8,128)S(1)}, u32[]{:S(2)}, u32[]{:S(2)}) %collective-permute-start.9) | collective-permute-done | bytes 196640 | tf_op jit(solution)/shard_map/ppermute | solution.py:38
  188.1 2.0 %shard_map.31 = bf16[2,2,384,128]{3,2,1,0:T(8,128)(2,1)} custom-call(s32[1]{0:T(128)} %bitcast.odd_ref, f32[2,2]{1,0:T(2,128)} %wave_ref.3, f32[2,192,128]{2,1,0:T(8,128)} %copy-done.15, f32[2,192,128]{2,1,0:T(8,128)} %copy-done.12, f32[2,192,128]{2,1,0:T(8,128)} %copy-done.13, f32[2,192,128]{2,1,0:T(8,128)} %copy-done.14, ...), custom_call_target="tpu_custom_call", output_to_operand_aliasing={{}: (6, {})} | custom-call | flops 393216 | bytes 1048576 | tf_op jit(solution)/shard_map/pallas_call | solution.py:115
  (72 shorter events, 23.8 us)
Async XLA Ops:
  1.5 3.8 %collective-permute-start = (bf16[2,16,192,128]{3,2,1,0:T(8,128)(2,1)S(1)}, bf16[2,16,192,128]{3,2,1,0:T(8,128)(2,1)S(1)}, u32[]{:S(2)}, u32[]{:S(2)}) collective-permute-start(bf16[2,16,192,128]{3,2,1,0:T(8,128)(2,1)S(1)} %constant_dynamic-slice_fusion), channel_id=1, source_target_pairs={{0,32},{32,0},{1,33},{33,1},{2,34},{34,2},{3,35},{35,3},{4,36},{36... | collective-permute-start | bytes 4718600 | tf_op jit(solution)/shard_map/ppermute | solution.py:42
  8.2 23.1 %all-to-all-start = ((bf16[8,2,2,192,128]{4,3,2,1,0:T(8,128)(2,1)}), bf16[8,2,2,192,128]{4,3,2,1,0:T(8,128)(2,1)S(1)}, u32[]{:S(2)}, u32[]{:S(2)}) async-start(bf16[8,2,2,192,128]{4,3,2,1,0:T(8,128)(2,1)} %bitcast.7), calls=%async_computation | async-start | bytes 3145728 | tf_op jit(solution)/shard_map/all_to_all | solution.py:147
  52.0 39.0 %all-to-all-start.1 = ((bf16[8,2,320,128]{3,2,1,0:T(8,128)(2,1)}), bf16[8,2,320,128]{3,2,1,0:T(8,128)(2,1)}, u32[]{:S(2)}, u32[]{:S(2)}) async-start(bf16[8,2,320,128]{3,2,1,0:T(8,128)(2,1)} %bitcast.14), calls=%async_computation.1 | async-start | bytes 2621440 | tf_op jit(solution)/shard_map/all_to_all | solution.py:147
  58.4 63.3 %collective-permute-start.7 = (bf16[8,2,2,192,128]{4,3,2,1,0:T(8,128)(2,1)S(1)}, bf16[8,2,2,192,128]{4,3,2,1,0:T(8,128)(2,1)S(1)}, u32[]{:S(2)}, u32[]{:S(2)}) collective-permute-start(bf16[8,2,2,192,128]{4,3,2,1,0:T(8,128)(2,1)S(1)} %all-to-all-done.ao_ref), channel_id=1, source_target_pairs={{0,32},{32,0},{1,33},{33,1},{2,34},{34,2},{3,35},{35,3},{4,36},{36... | collective-permute-start | bytes 4718600 | tf_op jit(solution)/shard_map/ppermute | solution.py:42
  61.8 5.3 %collective-permute-start.13 = (bf16[2,2,192,128]{3,2,1,0:T(8,128)(2,1)S(1)}, bf16[2,2,192,128]{3,2,1,0:T(8,128)(2,1)}, u32[]{:S(2)}, u32[]{:S(2)}) collective-permute-start(bf16[2,2,192,128]{3,2,1,0:T(8,128)(2,1)S(1)} %get-tuple-element.38), channel_id=1, source_target_pairs={{0,1},{1,0},{2,3},{3,2},{4,5},{5,4},{6,7},{7,6},{8,9},{9,8},{10,11... | collective-permute-start | bytes 589832 | tf_op jit(solution)/shard_map/ppermute | solution.py:38
  63.1 17.9 %collective-permute-start.14 = (bf16[2,2,192,128]{3,2,1,0:T(8,128)(2,1)}, bf16[2,2,192,128]{3,2,1,0:T(8,128)(2,1)}, u32[]{:S(2)}, u32[]{:S(2)}) collective-permute-start(bf16[2,2,192,128]{3,2,1,0:T(8,128)(2,1)} %get-tuple-element.49), channel_id=1, source_target_pairs={{0,128},{1,129},{2,130},{3,131},{4,132},{5,133},{6,134},{7,135},{8... | collective-permute-start | bytes 589832 | tf_op jit(solution)/shard_map/ppermute | solution.py:38
  64.4 24.1 %collective-permute-start.15 = (bf16[2,2,192,128]{3,2,1,0:T(8,128)(2,1)}, bf16[2,2,192,128]{3,2,1,0:T(8,128)(2,1)}, u32[]{:S(2)}, u32[]{:S(2)}) collective-permute-start(bf16[2,2,192,128]{3,2,1,0:T(8,128)(2,1)} %get-tuple-element.49), channel_id=1, source_target_pairs={{0,129},{1,128},{2,131},{3,130},{4,133},{5,132},{6,135},{7,134},{8... | collective-permute-start | bytes 589832 | tf_op jit(solution)/shard_map/ppermute | solution.py:38
  65.7 26.3 %collective-permute-start.1 = (bf16[2,2,192,128]{3,2,1,0:T(8,128)(2,1)S(1)}, bf16[2,2,192,128]{3,2,1,0:T(8,128)(2,1)}, u32[]{:S(2)}, u32[]{:S(2)}) collective-permute-start(bf16[2,2,192,128]{3,2,1,0:T(8,128)(2,1)S(1)} %get-tuple-element.29), channel_id=1, source_target_pairs={{0,1},{1,0},{2,3},{3,2},{4,5},{5,4},{6,7},{7,6},{8,9},{9,8},{10,11... | collective-permute-start | bytes 589832 | tf_op jit(solution)/shard_map/ppermute | solution.py:38
  67.0 26.0 %collective-permute-start.2 = (bf16[2,2,192,128]{3,2,1,0:T(8,128)(2,1)}, bf16[2,2,192,128]{3,2,1,0:T(8,128)(2,1)}, u32[]{:S(2)}, u32[]{:S(2)}) collective-permute-start(bf16[2,2,192,128]{3,2,1,0:T(8,128)(2,1)} %get-tuple-element.51), channel_id=1, source_target_pairs={{0,128},{1,129},{2,130},{3,131},{4,132},{5,133},{6,134},{7,135},{8... | collective-permute-start | bytes 589832 | tf_op jit(solution)/shard_map/ppermute | solution.py:38
  88.5 35.6 %collective-permute-start.19 = (bf16[8,2,320,128]{3,2,1,0:T(8,128)(2,1)}, bf16[8,2,320,128]{3,2,1,0:T(8,128)(2,1)}, u32[]{:S(2)}, u32[]{:S(2)}) collective-permute-start(bf16[8,2,320,128]{3,2,1,0:T(8,128)(2,1)} %all_to_all.15.bo_ref), channel_id=1, source_target_pairs={{0,32},{32,0},{1,33},{33,1},{2,34},{34,2},{3,35},{35,3},{4,36},{36... | collective-permute-start | bytes 3932168 | tf_op jit(solution)/shard_map/ppermute | solution.py:42
  90.9 58.8 %collective-permute-start.8 = (bf16[8,2,320,128]{3,2,1,0:T(8,128)(2,1)}, bf16[8,2,320,128]{3,2,1,0:T(8,128)(2,1)}, u32[]{:S(2)}, u32[]{:S(2)}) collective-permute-start(bf16[8,2,320,128]{3,2,1,0:T(8,128)(2,1)} %all-to-all-done.1.bo_ref), channel_id=1, source_target_pairs={{0,32},{32,0},{1,33},{33,1},{2,34},{34,2},{3,35},{35,3},{4,36},{36... | collective-permute-start | bytes 3932168 | tf_op jit(solution)/shard_map/ppermute | solution.py:42
  92.0 29.7 %copy-start.1 = (bf16[2,2,2,192,128]{4,3,2,1,0:T(8,128)(2,1)}, bf16[2,2,2,192,128]{4,3,2,1,0:T(8,128)(2,1)S(1)}, u32[]{:S(2)}) copy-start(bf16[2,2,2,192,128]{4,3,2,1,0:T(8,128)(2,1)S(1)} %pad_maximum_fusion.1.u0) | copy-start | bytes 1179652
  92.0 11.3 %collective-permute-start.16 = (bf16[2,2,2,192,128]{4,3,2,1,0:T(8,128)(2,1)S(1)}, bf16[2,2,2,192,128]{4,3,2,1,0:T(8,128)(2,1)S(1)}, u32[]{:S(2)}, u32[]{:S(2)}) collective-permute-start(bf16[2,2,2,192,128]{4,3,2,1,0:T(8,128)(2,1)S(1)} %pad_maximum_fusion.1.u0), channel_id=1, source_target_pairs={{0,2},{2,4},{4,6},{6,0},{1,3},{3,5},{5,7},{7,1},{8,10},{10,12},{12... | collective-permute-start | bytes 1179656 | tf_op jit(solution)/shard_map/ppermute | solution.py:166
  93.1 9.9 %collective-permute-start.3 = (bf16[2,2,192,128]{3,2,1,0:T(8,128)(2,1)}, bf16[2,2,192,128]{3,2,1,0:T(8,128)(2,1)S(1)}, u32[]{:S(2)}, u32[]{:S(2)}) collective-permute-start(bf16[2,2,192,128]{3,2,1,0:T(8,128)(2,1)} %get-tuple-element.51), channel_id=1, source_target_pairs={{0,129},{1,128},{2,131},{3,130},{4,133},{5,132},{6,135},{7,134},{8... | collective-permute-start | bytes 589832 | tf_op jit(solution)/shard_map/ppermute | solution.py:38
  103.0 8.1 %collective-permute-start.17 = (bf16[2,2,2,192,128]{4,3,2,1,0:T(8,128)(2,1)S(1)}, bf16[2,2,2,192,128]{4,3,2,1,0:T(8,128)(2,1)S(1)}, u32[]{:S(2)}, u32[]{:S(2)}) collective-permute-start(bf16[2,2,2,192,128]{4,3,2,1,0:T(8,128)(2,1)S(1)} %pad_maximum_fusion.1.u0), channel_id=1, source_target_pairs={{0,4},{2,6},{4,0},{6,2},{1,5},{3,7},{5,1},{7,3},{8,12},{10,14},{12... | collective-permute-start | bytes 1179656 | tf_op jit(solution)/shard_map/ppermute | solution.py:166
  104.1 16.9 %collective-permute-start.18 = (bf16[2,2,2,192,128]{4,3,2,1,0:T(8,128)(2,1)S(1)}, bf16[2,2,2,192,128]{4,3,2,1,0:T(8,128)(2,1)S(1)}, u32[]{:S(2)}, u32[]{:S(2)}) collective-permute-start(bf16[2,2,2,192,128]{4,3,2,1,0:T(8,128)(2,1)S(1)} %pad_maximum_fusion.1.u0), channel_id=1, source_target_pairs={{0,6},{2,0},{4,2},{6,4},{1,7},{3,1},{5,3},{7,5},{8,14},{10,8},{12,... | collective-permute-start | bytes 1179656 | tf_op jit(solution)/shard_map/ppermute | solution.py:166
  111.9 29.1 %collective-permute-start.4 = (bf16[2,2,2,192,128]{4,3,2,1,0:T(8,128)(2,1)S(1)}, bf16[2,2,2,192,128]{4,3,2,1,0:T(8,128)(2,1)}, u32[]{:S(2)}, u32[]{:S(2)}) collective-permute-start(bf16[2,2,2,192,128]{4,3,2,1,0:T(8,128)(2,1)S(1)} %pad_maximum_fusion.u0), channel_id=1, source_target_pairs={{0,2},{2,4},{4,6},{6,0},{1,3},{3,5},{5,7},{7,1},{8,10},{10,12},{12... | collective-permute-start | bytes 1179656 | tf_op jit(solution)/shard_map/ppermute | solution.py:166
  121.7 23.9 %collective-permute-start.5 = (bf16[2,2,2,192,128]{4,3,2,1,0:T(8,128)(2,1)S(1)}, bf16[2,2,2,192,128]{4,3,2,1,0:T(8,128)(2,1)}, u32[]{:S(2)}, u32[]{:S(2)}) collective-permute-start(bf16[2,2,2,192,128]{4,3,2,1,0:T(8,128)(2,1)S(1)} %pad_maximum_fusion.u0), channel_id=1, source_target_pairs={{0,4},{2,6},{4,0},{6,2},{1,5},{3,7},{5,1},{7,3},{8,12},{10,14},{12... | collective-permute-start | bytes 1179656 | tf_op jit(solution)/shard_map/ppermute | solution.py:166
  121.7 23.9 %collective-permute-start.6 = (bf16[2,2,2,192,128]{4,3,2,1,0:T(8,128)(2,1)S(1)}, bf16[2,2,2,192,128]{4,3,2,1,0:T(8,128)(2,1)}, u32[]{:S(2)}, u32[]{:S(2)}) collective-permute-start(bf16[2,2,2,192,128]{4,3,2,1,0:T(8,128)(2,1)S(1)} %pad_maximum_fusion.u0), channel_id=1, source_target_pairs={{0,6},{2,0},{4,2},{6,4},{1,7},{3,1},{5,3},{7,5},{8,14},{10,8},{12,... | collective-permute-start | bytes 1179656 | tf_op jit(solution)/shard_map/ppermute | solution.py:166
  133.8 23.5 %collective-permute-start.20 = (f32[2,192,128]{2,1,0:T(8,128)S(1)}, f32[2,192,128]{2,1,0:T(8,128)S(1)}, u32[]{:S(2)}, u32[]{:S(2)}) collective-permute-start(f32[2,192,128]{2,1,0:T(8,128)S(1)} %get-tuple-element.43), channel_id=1, source_target_pairs={{0,0},{1,1},{2,2},{3,3},{4,4},{5,5},{6,6},{7,7},{8,32},{9,33},{10,... | collective-permute-start | bytes 589832 | tf_op jit(solution)/shard_map/ppermute | solution.py:38
  141.0 16.3 %collective-permute-start.21 = (f32[2,192,128]{2,1,0:T(8,128)S(1)}, f32[2,192,128]{2,1,0:T(8,128)S(1)}, u32[]{:S(2)}, u32[]{:S(2)}) collective-permute-start(f32[2,192,128]{2,1,0:T(8,128)S(1)} %get-tuple-element.44), channel_id=1, source_target_pairs={{0,8},{1,9},{2,10},{3,11},{4,12},{5,13},{6,14},{7,15},{8,40},{9,41... | collective-permute-start | bytes 589832 | tf_op jit(solution)/shard_map/ppermute | solution.py:38
  145.6 14.9 %collective-permute-start.22 = (f32[2,192,128]{2,1,0:T(8,128)S(1)}, f32[2,192,128]{2,1,0:T(8,128)S(1)}, u32[]{:S(2)}, u32[]{:S(2)}) collective-permute-start(f32[2,192,128]{2,1,0:T(8,128)S(1)} %get-tuple-element.45), channel_id=1, source_target_pairs={{0,16},{1,17},{2,18},{3,19},{4,20},{5,21},{6,22},{7,23},{8,48},{9,... | collective-permute-start | bytes 589832 | tf_op jit(solution)/shard_map/ppermute | solution.py:38
  145.6 17.5 %collective-permute-start.23 = (f32[2,192,128]{2,1,0:T(8,128)}, f32[2,192,128]{2,1,0:T(8,128)}, u32[]{:S(2)}, u32[]{:S(2)}) collective-permute-start(f32[2,192,128]{2,1,0:T(8,128)} %get-tuple-element.46), channel_id=1, source_target_pairs={{0,24},{1,25},{2,26},{3,27},{4,28},{5,29},{6,30},{7,31},{8,56},{9,... | collective-permute-start | bytes 589832 | tf_op jit(solution)/shard_map/ppermute | solution.py:38
  154.9 16.6 %collective-permute-start.10 = (f32[2,192,128]{2,1,0:T(8,128)}, f32[2,192,128]{2,1,0:T(8,128)S(1)}, u32[]{:S(2)}, u32[]{:S(2)}) collective-permute-start(f32[2,192,128]{2,1,0:T(8,128)} %get-tuple-element.35), channel_id=1, source_target_pairs={{0,8},{1,9},{2,10},{3,11},{4,12},{5,13},{6,14},{7,15},{8,40},{9,41... | collective-permute-start | bytes 589832 | tf_op jit(solution)/shard_map/ppermute | solution.py:38
  157.3 3.3 %copy-start.9 = (f32[2,192,128]{2,1,0:T(8,128)}, f32[2,192,128]{2,1,0:T(8,128)S(1)}, u32[]{:S(2)}) copy-start(f32[2,192,128]{2,1,0:T(8,128)S(1)} %collective-permute-done.20.refs_0_) | copy-start | bytes 589828
  157.3 14.3 %collective-permute-start.11 = (f32[2,192,128]{2,1,0:T(8,128)}, f32[2,192,128]{2,1,0:T(8,128)S(1)}, u32[]{:S(2)}, u32[]{:S(2)}) collective-permute-start(f32[2,192,128]{2,1,0:T(8,128)} %get-tuple-element.36), channel_id=1, source_target_pairs={{0,16},{1,17},{2,18},{3,19},{4,20},{5,21},{6,22},{7,23},{8,48},{9,... | collective-permute-start | bytes 589832 | tf_op jit(solution)/shard_map/ppermute | solution.py:38
  157.3 3.3 %copy-start.10 = (f32[2,192,128]{2,1,0:T(8,128)}, f32[2,192,128]{2,1,0:T(8,128)S(1)}, u32[]{:S(2)}) copy-start(f32[2,192,128]{2,1,0:T(8,128)S(1)} %collective-permute-done.21.refs_1_) | copy-start | bytes 589828
  157.3 19.7 %collective-permute-start.12 = (f32[2,192,128]{2,1,0:T(8,128)}, f32[2,192,128]{2,1,0:T(8,128)S(1)}, u32[]{:S(2)}, u32[]{:S(2)}) collective-permute-start(f32[2,192,128]{2,1,0:T(8,128)} %get-tuple-element.37), channel_id=1, source_target_pairs={{0,24},{1,25},{2,26},{3,27},{4,28},{5,29},{6,30},{7,31},{8,56},{9,... | collective-permute-start | bytes 589832 | tf_op jit(solution)/shard_map/ppermute | solution.py:38
  161.3 26.2 %collective-permute-start.9 = (f32[2,192,128]{2,1,0:T(8,128)}, f32[2,192,128]{2,1,0:T(8,128)S(1)}, u32[]{:S(2)}, u32[]{:S(2)}) collective-permute-start(f32[2,192,128]{2,1,0:T(8,128)} %get-tuple-element.34), channel_id=1, source_target_pairs={{0,0},{1,1},{2,2},{3,3},{4,4},{5,5},{6,6},{7,7},{8,32},{9,33},{10,... | collective-permute-start | bytes 589832 | tf_op jit(solution)/shard_map/ppermute | solution.py:38
  171.5 15.9 %copy-start.12 = (f32[2,192,128]{2,1,0:T(8,128)}, f32[2,192,128]{2,1,0:T(8,128)S(1)}, u32[]{:S(2)}) copy-start(f32[2,192,128]{2,1,0:T(8,128)S(1)} %collective-permute-done.10.refs_1_) | copy-start | bytes 589828
  171.5 15.9 %copy-start.13 = (f32[2,192,128]{2,1,0:T(8,128)}, f32[2,192,128]{2,1,0:T(8,128)S(1)}, u32[]{:S(2)}) copy-start(f32[2,192,128]{2,1,0:T(8,128)S(1)} %collective-permute-done.11.refs_2_) | copy-start | bytes 589828
  177.0 10.4 %copy-start.14 = (f32[2,192,128]{2,1,0:T(8,128)}, f32[2,192,128]{2,1,0:T(8,128)S(1)}, u32[]{:S(2)}) copy-start(f32[2,192,128]{2,1,0:T(8,128)S(1)} %collective-permute-done.12.refs_3_) | copy-start | bytes 589828
  (11 other events, 10.2 us)

commit v12 on v11

--- a/solution.py
+++ b/solution.py
@@ -42,7 +42,7 @@
     return lax.ppermute(value, "core", [(0, 1), (1, 0)])
 
 
-def contract(g, place, turned, a_own, a_peer, b_own, b_peer):
+def contract(place, turned, a_own, a_peer, b_own, b_peer):
     half, lanes = turned[0].shape[-2:]
     depth = 16 * lanes
 
@@ -64,7 +64,7 @@
                 i = 2 * x + zr
                 parts = []
                 for part in range(2):
-                    ao, ap = ao_ref[i, g, part], ap_ref[i, g, part]
+                    ao, ap = ao_ref[i, part], ap_ref[i, part]
                     bo, bp = bo_ref[i, part], bp_ref[i, part]
                     parts.append(
                         jnp.concatenate(
@@ -136,8 +136,8 @@
         return block.reshape((2, 2, 4, 2) + block.shape[2:])
 
     passed = swap_core(lax.dynamic_slice_in_dim(spectra, (1 - core) * half, half, 2))
-    a = ordered(jnp.where(first, spectra[:, :, :half], passed)).transpose(2, 1, 3, 0, 4, 5)
-    a = a.reshape((8, 2, 2) + a.shape[4:])
+    a = ordered(jnp.where(first, spectra[:, :, :half], passed)).transpose(3, 2, 1, 0, 4, 5)
+    a = a.reshape((2, 8, 2) + a.shape[4:])
     b = jnp.where(first, jnp.concatenate([spectra[:, :, window:], passed], 2), spectra[:, :, half:])
     b = [ordered(b)[:, :, :, g].transpose(2, 1, 0, 3, 4) for g in range(2)]
     b = [b[g].reshape((8, 2) + b[g].shape[3:]) for g in range(2)]
@@ -146,16 +146,20 @@
     def exchange(block):
         return lax.all_to_all(block, ("x", "zr"), split_axis=0, concat_axis=0, tiled=True)
 
-    a_own = exchange(a)
-    a_own, *b = lax.optimization_barrier((a_own, *b))
-    a_peer = swap_core(a_own)
+    a_own, a_peer = [], []
+    for g in range(2):
+        a_own.append(exchange(a[g]))
+    a_sent = list(a_own)
+    *a_own, b[0], b[1] = lax.optimization_barrier((*a_own, *b))
+    for g in range(2):
+        a_peer.append(swap_core(a_own[g]))
     b_own, b_peer = [], []
     for g in range(2):
         b_own.append(exchange(b[g]))
         b_peer.append(swap_core(b_own[g]))
 
     def turn(g):
-        shots = a_own.reshape((4, 2) + a_own.shape[1:])[:, 0, g]
+        shots = a_sent[g].reshape((4, 2) + a_sent[g].shape[1:])[:, 0]
         near, far = shots[:2], shots[2:]
         across = send(near, lambda q, r, c, x, y, h: (0, r, c, x, y, 1 - h) if q == 0 else None)
         up = send(far, lambda q, r, c, x, y, h: (1, r, c, x, y, h) if q == 0 else None)
@@ -170,16 +174,17 @@
     turned = [turn(g) for g in range(2)]
 
     def homeward(blocks):
-        moved_on = []
-        for t, block in enumerate(blocks):
-            moved_on.append(
-                send(block, lambda q, r, c, x, y, h: (r, x // 2, x % 2, (2 * q + c) ^ t, y, h))
+        return [
+            send(
+                block,
+                lambda q, r, c, x, y, h: (r, x // 2, x % 2, (2 * q + c) ^ t, y, h),
             )
-        return moved_on
+            for t, block in enumerate(blocks)
+        ]
 
     blocks = []
     for g in range(2):
-        partial = contract(g, place, turned[g], a_own, a_peer, b_own[g], b_peer[g])
+        partial = contract(place, turned[g], a_own[g], a_peer[g], b_own[g], b_peer[g])
         blocks.append(homeward(partial))
     odd = jnp.stack([x % 2]).astype(jnp.int32)
     early = finish(0, odd, wavelet, blocks[0])

time: 191 us -> 199 us (1.042)
  the two profiles are of different devices: /device:TPU:213 before, /device:TPU:4 now
where the time goes in v12:
time: 199 us; the launch traced here: 195 us
  starting transfers between devices  63.2 us (32%)
  waiting for transfers between devices  57.2 us (29%)
  blocking collectives  36.9 us (19%)
  local copies, waits for them, and re-layouts  16.3 us (8%)
  Pallas kernels  12.8 us (6%)
  other arithmetic  8.54 us (4%)
    ppermute x14, waiting for transfers between devices, send(): return lax.ppermute(value, AXES, moved(target))  38.8 us
    all_to_all x2, blocking collectives, exchange(): lax.all_to_all(block, ('x', 'zr'), split_axis=0, concat_axis=0, tiled=True)  36.9 us
    ppermute x14, starting transfers between devices, send(): return lax.ppermute(value, AXES, moved(target))  34.9 us
    ppermute x6, starting transfers between devices, turn(): lax.ppermute(pieces, 'y', [(i, (i + s) % 4) for i in range(4)])  16.1 us
    unnamed x38, local copies, waits for them, and re-layouts  12.7 us
    all_to_all x2, starting transfers between devices, exchange(): lax.all_to_all(block, ('x', 'zr'), split_axis=0, concat_axis=0, tiled=True)  11.9 us
    ppermute x6, waiting for transfers between devices, turn(): lax.ppermute(pieces, 'y', [(i, (i + s) % 4) for i in range(4)])  11.2 us
    pallas_call x2, Pallas kernels, contract(): pl.pallas_call(kernel, out_shape=(result,) * 4, in_specs=[pl.BlockSpec(me...  8.84 us
  transfers between devices with their start and end apart: 27, of which 11 were waited for; matrix products, arithmetic and copies ran while one was open for 4% of the time, Pallas kernels for 6%

profile of v12, /device:TPU:4, one launch (start us, length us, event | category | flops | bytes accessed | tf_op | source)
XLA Modules:
  0.0 195.2 jit_solution(1804739306990142263)
XLA Ops:
  1.6 3.4 %collective-permute-done = bf16[2,16,192,128]{3,2,1,0:T(8,128)(2,1)S(1)} collective-permute-done((bf16[2,16,192,128]{3,2,1,0:T(8,128)(2,1)S(1)}, bf16[2,16,192,128]{3,2,1,0:T(8,128)(2,1)S(1)}, u32[]{:S(2)}, u32[]{:S(2)}) %collective-permute-start) | collective-permute-done | bytes 1572896 | tf_op jit(solution)/shard_map/ppermute | solution.py:42
  5.0 2.1 %slice_select_fusion = bf16[2,16,192,128]{3,2,1,0:T(8,128)(2,1)S(1)} fusion(bf16[2,16,192,128]{3,2,1,0:T(8,128)(2,1)S(1)} %collective-permute-done, bf16[2,16,512,128]{3,2,1,0:T(8,128)(2,1)} %param.2, pred[]{:T(512)S(6)} %eq.12), kind=kLoop, calls=%fused_computation.2 | loop fusion | flops 786432 | bytes 4718593 | tf_op jit(solution)/shard_map/jit(_where)/select_n | solution.py:139
  8.3 16.7 %all_to_all.20.ao_ref = bf16[8,2,192,128]{3,2,1,0:T(8,128)(2,1)S(1)} all-to-all(bf16[8,2,192,128]{3,2,1,0:T(8,128)(2,1)S(1)} %bitcast.55), channel_id=1, replica_groups=mesh['zq'=2,'zr'=2,'core'=2,'x'=4,'y'=4,'zh'=2] {'x','zr'}, dimensions={0} | all-to-all | bytes 1572864 | tf_op jit(solution)/shard_map/all_to_all | solution.py:147
  25.0 6.0 %all-to-all-start = ((bf16[8,2,192,128]{3,2,1,0:T(8,128)(2,1)}), bf16[8,2,192,128]{3,2,1,0:T(8,128)(2,1)S(1)}, u32[]{:S(2)}, u32[]{:S(2)}) async-start(bf16[8,2,192,128]{3,2,1,0:T(8,128)(2,1)} %bitcast.7), calls=%async_computation | async-start | bytes 1572864 | tf_op jit(solution)/shard_map/all_to_all | solution.py:147
  32.5 2.7 %maximum_select_fusion = bf16[2,16,320,128]{3,2,1,0:T(8,128)(2,1)S(1)} fusion(bf16[2,16,192,128]{3,2,1,0:T(8,128)(2,1)S(1)} %copy-done.10, bf16[2,16,128,128]{3,2,1,0:T(8,128)(2,1)S(1)} %slice-done, bf16[2,16,512,128]{3,2,1,0:T(8,128)(2,1)} %param.2, pred[]{:T(512)S(6)} %eq.12), kind=kLoop, calls=%fused_computation | loop fusion | flops 6553600 | bytes 7864321 | tf_op jit(solution)/shard_map/jit(_where)/select_n | solution.py:141
  36.6 3.9 %all-to-all-done.ao_ref = bf16[8,2,192,128]{3,2,1,0:T(8,128)(2,1)S(1)} async-done(((bf16[8,2,192,128]{3,2,1,0:T(8,128)(2,1)}), bf16[8,2,192,128]{3,2,1,0:T(8,128)(2,1)S(1)}, u32[]{:S(2)}, u32[]{:S(2)}) %all-to-all-start) | async-done | bytes 786464 | tf_op jit(solution)/shard_map/all_to_all | solution.py:147
  40.5 20.2 %all_to_all.21.bo_ref = bf16[8,2,320,128]{3,2,1,0:T(8,128)(2,1)} all-to-all(bf16[8,2,320,128]{3,2,1,0:T(8,128)(2,1)S(1)} %bitcast.54), channel_id=1, replica_groups=mesh['zq'=2,'zr'=2,'core'=2,'x'=4,'y'=4,'zh'=2] {'x','zr'}, dimensions={0} | all-to-all | bytes 2621440 | tf_op jit(solution)/shard_map/all_to_all | solution.py:147
  60.7 5.9 %all-to-all-start.2 = ((bf16[8,2,320,128]{3,2,1,0:T(8,128)(2,1)}), bf16[8,2,320,128]{3,2,1,0:T(8,128)(2,1)S(1)}, u32[]{:S(2)}, u32[]{:S(2)}) async-start(bf16[8,2,320,128]{3,2,1,0:T(8,128)(2,1)} %bitcast.53), calls=%async_computation.2 | async-start | bytes 2621440 | tf_op jit(solution)/shard_map/all_to_all | solution.py:147
  66.6 5.2 %collective-permute-start.14 = (bf16[2,2,192,128]{3,2,1,0:T(8,128)(2,1)S(1)}, bf16[2,2,192,128]{3,2,1,0:T(8,128)(2,1)S(1)}, u32[]{:S(2)}, u32[]{:S(2)}) collective-permute-start(bf16[2,2,192,128]{3,2,1,0:T(8,128)(2,1)S(1)} %get-tuple-element.53), channel_id=1, source_target_pairs={{0,128},{1,129},{2,130},{3,131},{4,132},{5,133},{6,134},{7,135},{8... | collective-permute-start | bytes 589832 | tf_op jit(solution)/shard_map/ppermute | solution.py:38
  71.8 3.4 %collective-permute-start.15 = (bf16[2,2,192,128]{3,2,1,0:T(8,128)(2,1)S(1)}, bf16[2,2,192,128]{3,2,1,0:T(8,128)(2,1)S(1)}, u32[]{:S(2)}, u32[]{:S(2)}) collective-permute-start(bf16[2,2,192,128]{3,2,1,0:T(8,128)(2,1)S(1)} %get-tuple-element.53), channel_id=1, source_target_pairs={{0,129},{1,128},{2,131},{3,130},{4,133},{5,132},{6,135},{7,134},{8... | collective-permute-start | bytes 589832 | tf_op jit(solution)/shard_map/ppermute | solution.py:38
  75.3 4.3 %collective-permute-start.13 = (bf16[2,2,192,128]{3,2,1,0:T(8,128)(2,1)S(1)}, bf16[2,2,192,128]{3,2,1,0:T(8,128)(2,1)S(1)}, u32[]{:S(2)}, u32[]{:S(2)}) collective-permute-start(bf16[2,2,192,128]{3,2,1,0:T(8,128)(2,1)S(1)} %get-tuple-element.39), channel_id=1, source_target_pairs={{0,1},{1,0},{2,3},{3,2},{4,5},{5,4},{6,7},{7,6},{8,9},{9,8},{10,11... | collective-permute-start | bytes 589832 | tf_op jit(solution)/shard_map/ppermute | solution.py:38
  80.4 2.0 %collective-permute-start.2 = (bf16[2,2,192,128]{3,2,1,0:T(8,128)(2,1)}, bf16[2,2,192,128]{3,2,1,0:T(8,128)(2,1)}, u32[]{:S(2)}, u32[]{:S(2)}) collective-permute-start(bf16[2,2,192,128]{3,2,1,0:T(8,128)(2,1)} %get-tuple-element.55), channel_id=1, source_target_pairs={{0,128},{1,129},{2,130},{3,131},{4,132},{5,133},{6,134},{7,135},{8... | collective-permute-start | bytes 589832 | tf_op jit(solution)/shard_map/ppermute | solution.py:38
  82.3 13.0 %collective-permute-done.13 = bf16[2,2,192,128]{3,2,1,0:T(8,128)(2,1)S(1)} collective-permute-done((bf16[2,2,192,128]{3,2,1,0:T(8,128)(2,1)S(1)}, bf16[2,2,192,128]{3,2,1,0:T(8,128)(2,1)S(1)}, u32[]{:S(2)}, u32[]{:S(2)}) %collective-permute-start.13) | collective-permute-done | bytes 196640 | tf_op jit(solution)/shard_map/ppermute | solution.py:38
  95.4 2.0 %collective-permute-start.3 = (bf16[2,2,192,128]{3,2,1,0:T(8,128)(2,1)}, bf16[2,2,192,128]{3,2,1,0:T(8,128)(2,1)}, u32[]{:S(2)}, u32[]{:S(2)}) collective-permute-start(bf16[2,2,192,128]{3,2,1,0:T(8,128)(2,1)} %get-tuple-element.55), channel_id=1, source_target_pairs={{0,129},{1,128},{2,131},{3,130},{4,133},{5,132},{6,135},{7,134},{8... | collective-permute-start | bytes 589832 | tf_op jit(solution)/shard_map/ppermute | solution.py:38
  101.2 7.7 %collective-permute-done.1 = bf16[2,2,192,128]{3,2,1,0:T(8,128)(2,1)} collective-permute-done((bf16[2,2,192,128]{3,2,1,0:T(8,128)(2,1)S(1)}, bf16[2,2,192,128]{3,2,1,0:T(8,128)(2,1)}, u32[]{:S(2)}, u32[]{:S(2)}) %collective-permute-start.1) | collective-permute-done | bytes 196640 | tf_op jit(solution)/shard_map/ppermute | solution.py:38
  110.5 3.0 %collective-permute-start.17 = (bf16[2,2,2,192,128]{4,3,2,1,0:T(8,128)(2,1)S(1)}, bf16[2,2,2,192,128]{4,3,2,1,0:T(8,128)(2,1)S(1)}, u32[]{:S(2)}, u32[]{:S(2)}) collective-permute-start(bf16[2,2,2,192,128]{4,3,2,1,0:T(8,128)(2,1)S(1)} %pad_maximum_fusion.1.u0), channel_id=1, source_target_pairs={{0,4},{2,6},{4,0},{6,2},{1,5},{3,7},{5,1},{7,3},{8,12},{10,14},{12... | collective-permute-start | bytes 1179656 | tf_op jit(solution)/shard_map/ppermute | solution.py:170
  113.5 7.2 %collective-permute-done.16.u1 = bf16[2,2,2,192,128]{4,3,2,1,0:T(8,128)(2,1)S(1)} collective-permute-done((bf16[2,2,2,192,128]{4,3,2,1,0:T(8,128)(2,1)S(1)}, bf16[2,2,2,192,128]{4,3,2,1,0:T(8,128)(2,1)S(1)}, u32[]{:S(2)}, u32[]{:S(2)}) %collective-permute-start.16) | collective-permute-done | bytes 393248 | tf_op jit(solution)/shard_map/ppermute | solution.py:170
  121.4 3.0 %collective-permute-start.18 = (bf16[2,2,2,192,128]{4,3,2,1,0:T(8,128)(2,1)S(1)}, bf16[2,2,2,192,128]{4,3,2,1,0:T(8,128)(2,1)S(1)}, u32[]{:S(2)}, u32[]{:S(2)}) collective-permute-start(bf16[2,2,2,192,128]{4,3,2,1,0:T(8,128)(2,1)S(1)} %pad_maximum_fusion.1.u0), channel_id=1, source_target_pairs={{0,6},{2,0},{4,2},{6,4},{1,7},{3,1},{5,3},{7,5},{8,14},{10,8},{12,... | collective-permute-start | bytes 1179656 | tf_op jit(solution)/shard_map/ppermute | solution.py:170
  124.5 3.1 %collective-permute-done.17.u2 = bf16[2,2,2,192,128]{4,3,2,1,0:T(8,128)(2,1)S(1)} collective-permute-done((bf16[2,2,2,192,128]{4,3,2,1,0:T(8,128)(2,1)S(1)}, bf16[2,2,2,192,128]{4,3,2,1,0:T(8,128)(2,1)S(1)}, u32[]{:S(2)}, u32[]{:S(2)}) %collective-permute-start.17) | collective-permute-done | bytes 393248 | tf_op jit(solution)/shard_map/ppermute | solution.py:170
  131.8 3.8 %collective-permute-start.4 = (bf16[2,2,2,192,128]{4,3,2,1,0:T(8,128)(2,1)}, bf16[2,2,2,192,128]{4,3,2,1,0:T(8,128)(2,1)}, u32[]{:S(2)}, u32[]{:S(2)}) collective-permute-start(bf16[2,2,2,192,128]{4,3,2,1,0:T(8,128)(2,1)} %pad_maximum_fusion.u0), channel_id=1, source_target_pairs={{0,2},{2,4},{4,6},{6,0},{1,3},{3,5},{5,7},{7,1},{8,10},{10,12},{12... | collective-permute-start | bytes 1179656 | tf_op jit(solution)/shard_map/ppermute | solution.py:170
  136.5 2.1 %collective-permute-start.5 = (bf16[2,2,2,192,128]{4,3,2,1,0:T(8,128)(2,1)}, bf16[2,2,2,192,128]{4,3,2,1,0:T(8,128)(2,1)}, u32[]{:S(2)}, u32[]{:S(2)}) collective-permute-start(bf16[2,2,2,192,128]{4,3,2,1,0:T(8,128)(2,1)} %pad_maximum_fusion.u0), channel_id=1, source_target_pairs={{0,4},{2,6},{4,0},{6,2},{1,5},{3,7},{5,1},{7,3},{8,12},{10,14},{12... | collective-permute-start | bytes 1179656 | tf_op jit(solution)/shard_map/ppermute | solution.py:170
  138.5 2.6 %collective-permute-start.6 = (bf16[2,2,2,192,128]{4,3,2,1,0:T(8,128)(2,1)}, bf16[2,2,2,192,128]{4,3,2,1,0:T(8,128)(2,1)}, u32[]{:S(2)}, u32[]{:S(2)}) collective-permute-start(bf16[2,2,2,192,128]{4,3,2,1,0:T(8,128)(2,1)} %pad_maximum_fusion.u0), channel_id=1, source_target_pairs={{0,6},{2,0},{4,2},{6,4},{1,7},{3,1},{5,3},{7,5},{8,14},{10,8},{12,... | collective-permute-start | bytes 1179656 | tf_op jit(solution)/shard_map/ppermute | solution.py:170
  146.7 3.8 %shard_map.29 = (f32[2,192,128]{2,1,0:T(8,128)S(1)}, f32[2,192,128]{2,1,0:T(8,128)S(1)}, f32[2,192,128]{2,1,0:T(8,128)S(1)}, f32[2,192,128]{2,1,0:T(8,128)S(1)}) custom-call(s32[4]{0:T(128)S(1)} %pad_add_fusion.place_ref, bf16[2,2,2,192,128]{4,3,2,1,0:T(8,128)(2,1)S(1)} %pad_maximum_fusion.1.u0, bf16[2,2,2,192,128]{4,3,2,1,0:T(8,128)(2,1)S(1)} %copy-done.4, ...), custom_call_target="tpu_custom_call" | custom-call | flops 1610612736 | bytes 7340032 | tf_op jit(solution)/shard_map/pallas_call | solution.py:88
  150.5 3.4 %collective-permute-start.21 = (f32[2,192,128]{2,1,0:T(8,128)S(1)}, f32[2,192,128]{2,1,0:T(8,128)S(1)}, u32[]{:S(2)}, u32[]{:S(2)}) collective-permute-start(f32[2,192,128]{2,1,0:T(8,128)S(1)} %get-tuple-element.45), channel_id=1, source_target_pairs={{0,0},{1,1},{2,2},{3,3},{4,4},{5,5},{6,6},{7,7},{8,32},{9,33},{10,... | collective-permute-start | bytes 589832 | tf_op jit(solution)/shard_map/ppermute | solution.py:38
  155.9 5.1 %shard_map.28 = (f32[2,192,128]{2,1,0:T(8,128)S(1)}, f32[2,192,128]{2,1,0:T(8,128)}, f32[2,192,128]{2,1,0:T(8,128)}, f32[2,192,128]{2,1,0:T(8,128)S(1)}) custom-call(s32[4]{0:T(128)S(1)} %pad_add_fusion.place_ref, bf16[2,2,2,192,128]{4,3,2,1,0:T(8,128)(2,1)} %pad_maximum_fusion.u0, bf16[2,2,2,192,128]{4,3,2,1,0:T(8,128)(2,1)} %collective-permute-done.4.u1, ...), custom_call_target="tpu_custom_call" | custom-call | flops 1610612736 | bytes 7340032 | tf_op jit(solution)/shard_map/pallas_call | solution.py:88
  160.9 6.1 %collective-permute-start.10 = (f32[2,192,128]{2,1,0:T(8,128)}, f32[2,192,128]{2,1,0:T(8,128)S(1)}, u32[]{:S(2)}, u32[]{:S(2)}) collective-permute-start(f32[2,192,128]{2,1,0:T(8,128)} %get-tuple-element.36), channel_id=1, source_target_pairs={{0,8},{1,9},{2,10},{3,11},{4,12},{5,13},{6,14},{7,15},{8,40},{9,41... | collective-permute-start | bytes 589832 | tf_op jit(solution)/shard_map/ppermute | solution.py:38
  167.8 3.9 %collective-permute-done.23.refs_2_ = f32[2,192,128]{2,1,0:T(8,128)S(1)} collective-permute-done((f32[2,192,128]{2,1,0:T(8,128)S(1)}, f32[2,192,128]{2,1,0:T(8,128)S(1)}, u32[]{:S(2)}, u32[]{:S(2)}) %collective-permute-start.23) | collective-permute-done | bytes 196640 | tf_op jit(solution)/shard_map/ppermute | solution.py:38
  172.4 4.0 %collective-permute-start.9 = (f32[2,192,128]{2,1,0:T(8,128)S(1)}, f32[2,192,128]{2,1,0:T(8,128)S(1)}, u32[]{:S(2)}, u32[]{:S(2)}) collective-permute-start(f32[2,192,128]{2,1,0:T(8,128)S(1)} %get-tuple-element.35), channel_id=1, source_target_pairs={{0,0},{1,1},{2,2},{3,3},{4,4},{5,5},{6,6},{7,7},{8,32},{9,33},{10,... | collective-permute-start | bytes 589832 | tf_op jit(solution)/shard_map/ppermute | solution.py:38
  176.5 2.0 %shard_map.30.refs_4_ = bf16[2,2,384,128]{3,2,1,0:T(8,128)(2,1)} custom-call(s32[1]{0:T(128)} %bitcast.odd_ref, f32[2,2]{1,0:T(2,128)} %wave_ref.3, f32[2,192,128]{2,1,0:T(8,128)} %copy-done.11, f32[2,192,128]{2,1,0:T(8,128)} %copy-done.12, f32[2,192,128]{2,1,0:T(8,128)} %copy-done.13, f32[2,192,128]{2,1,0:T(8,128)} %collective-permute-done.24.refs_3_), custom_call_target="tpu_custom_call" | custom-call | flops 393216 | bytes 1048576 | tf_op jit(solution)/shard_map/pallas_call | solution.py:115
  179.1 8.4 %collective-permute-done.11.refs_2_ = f32[2,192,128]{2,1,0:T(8,128)S(1)} collective-permute-done((f32[2,192,128]{2,1,0:T(8,128)}, f32[2,192,128]{2,1,0:T(8,128)S(1)}, u32[]{:S(2)}, u32[]{:S(2)}) %collective-permute-start.11) | collective-permute-done | bytes 196640 | tf_op jit(solution)/shard_map/ppermute | solution.py:38
  187.5 5.0 %collective-permute-done.9.refs_0_ = f32[2,192,128]{2,1,0:T(8,128)S(1)} collective-permute-done((f32[2,192,128]{2,1,0:T(8,128)S(1)}, f32[2,192,128]{2,1,0:T(8,128)S(1)}, u32[]{:S(2)}, u32[]{:S(2)}) %collective-permute-start.9) | collective-permute-done | bytes 196640 | tf_op jit(solution)/shard_map/ppermute | solution.py:38
  193.2 2.0 %shard_map.31 = bf16[2,2,384,128]{3,2,1,0:T(8,128)(2,1)} custom-call(s32[1]{0:T(128)} %bitcast.odd_ref, f32[2,2]{1,0:T(2,128)} %wave_ref.3, f32[2,192,128]{2,1,0:T(8,128)} %copy-done.17, f32[2,192,128]{2,1,0:T(8,128)} %copy-done.14, f32[2,192,128]{2,1,0:T(8,128)} %copy-done.15, f32[2,192,128]{2,1,0:T(8,128)} %copy-done.16, ...), custom_call_target="tpu_custom_call", output_to_operand_aliasing={{}: (6, {})} | custom-call | flops 393216 | bytes 1048576 | tf_op jit(solution)/shard_map/pallas_call | solution.py:115
  (81 shorter events, 27.8 us)
Async XLA Ops:
  1.5 3.5 %collective-permute-start = (bf16[2,16,192,128]{3,2,1,0:T(8,128)(2,1)S(1)}, bf16[2,16,192,128]{3,2,1,0:T(8,128)(2,1)S(1)}, u32[]{:S(2)}, u32[]{:S(2)}) collective-permute-start(bf16[2,16,192,128]{3,2,1,0:T(8,128)(2,1)S(1)} %constant_dynamic-slice_fusion), channel_id=1, source_target_pairs={{0,32},{32,0},{1,33},{33,1},{2,34},{34,2},{3,35},{35,3},{4,36},{36... | collective-permute-start | bytes 4718600 | tf_op jit(solution)/shard_map/ppermute | solution.py:42
  25.0 6.0 %slice-start = ((bf16[2,16,512,128]{3,2,1,0:T(8,128)(2,1)}), bf16[2,16,128,128]{3,2,1,0:T(8,128)(2,1)S(1)}, s32[]{:S(2)}) async-start(bf16[2,16,512,128]{3,2,1,0:T(8,128)(2,1)} %param.2), calls=%async_computation.4 | async-start | bytes 2097152 | tf_op jit(solution)/shard_map/slice | solution.py:141
  25.0 15.5 %all-to-all-start = ((bf16[8,2,192,128]{3,2,1,0:T(8,128)(2,1)}), bf16[8,2,192,128]{3,2,1,0:T(8,128)(2,1)S(1)}, u32[]{:S(2)}, u32[]{:S(2)}) async-start(bf16[8,2,192,128]{3,2,1,0:T(8,128)(2,1)} %bitcast.7), calls=%async_computation | async-start | bytes 1572864 | tf_op jit(solution)/shard_map/all_to_all | solution.py:147
  60.7 39.4 %all-to-all-start.2 = ((bf16[8,2,320,128]{3,2,1,0:T(8,128)(2,1)}), bf16[8,2,320,128]{3,2,1,0:T(8,128)(2,1)S(1)}, u32[]{:S(2)}, u32[]{:S(2)}) async-start(bf16[8,2,320,128]{3,2,1,0:T(8,128)(2,1)} %bitcast.53), calls=%async_computation.2 | async-start | bytes 2621440 | tf_op jit(solution)/shard_map/all_to_all | solution.py:147
  66.6 30.7 %collective-permute-start.14 = (bf16[2,2,192,128]{3,2,1,0:T(8,128)(2,1)S(1)}, bf16[2,2,192,128]{3,2,1,0:T(8,128)(2,1)S(1)}, u32[]{:S(2)}, u32[]{:S(2)}) collective-permute-start(bf16[2,2,192,128]{3,2,1,0:T(8,128)(2,1)S(1)} %get-tuple-element.53), channel_id=1, source_target_pairs={{0,128},{1,129},{2,130},{3,131},{4,132},{5,133},{6,134},{7,135},{8... | collective-permute-start | bytes 589832 | tf_op jit(solution)/shard_map/ppermute | solution.py:38
  71.8 27.4 %collective-permute-start.15 = (bf16[2,2,192,128]{3,2,1,0:T(8,128)(2,1)S(1)}, bf16[2,2,192,128]{3,2,1,0:T(8,128)(2,1)S(1)}, u32[]{:S(2)}, u32[]{:S(2)}) collective-permute-start(bf16[2,2,192,128]{3,2,1,0:T(8,128)(2,1)S(1)} %get-tuple-element.53), channel_id=1, source_target_pairs={{0,129},{1,128},{2,131},{3,130},{4,133},{5,132},{6,135},{7,134},{8... | collective-permute-start | bytes 589832 | tf_op jit(solution)/shard_map/ppermute | solution.py:38
  75.3 20.1 %collective-permute-start.13 = (bf16[2,2,192,128]{3,2,1,0:T(8,128)(2,1)S(1)}, bf16[2,2,192,128]{3,2,1,0:T(8,128)(2,1)S(1)}, u32[]{:S(2)}, u32[]{:S(2)}) collective-permute-start(bf16[2,2,192,128]{3,2,1,0:T(8,128)(2,1)S(1)} %get-tuple-element.39), channel_id=1, source_target_pairs={{0,1},{1,0},{2,3},{3,2},{4,5},{5,4},{6,7},{7,6},{8,9},{9,8},{10,11... | collective-permute-start | bytes 589832 | tf_op jit(solution)/shard_map/ppermute | solution.py:38
  79.5 59.0 %collective-permute-start.20 = (bf16[8,2,320,128]{3,2,1,0:T(8,128)(2,1)}, bf16[8,2,320,128]{3,2,1,0:T(8,128)(2,1)}, u32[]{:S(2)}, u32[]{:S(2)}) collective-permute-start(bf16[8,2,320,128]{3,2,1,0:T(8,128)(2,1)} %all_to_all.21.bo_ref), channel_id=1, source_target_pairs={{0,32},{32,0},{1,33},{33,1},{2,34},{34,2},{3,35},{35,3},{4,36},{36... | collective-permute-start | bytes 3932168 | tf_op jit(solution)/shard_map/ppermute | solution.py:42
  80.4 30.1 %collective-permute-start.2 = (bf16[2,2,192,128]{3,2,1,0:T(8,128)(2,1)}, bf16[2,2,192,128]{3,2,1,0:T(8,128)(2,1)}, u32[]{:S(2)}, u32[]{:S(2)}) collective-permute-start(bf16[2,2,192,128]{3,2,1,0:T(8,128)(2,1)} %get-tuple-element.55), channel_id=1, source_target_pairs={{0,128},{1,129},{2,130},{3,131},{4,132},{5,133},{6,134},{7,135},{8... | collective-permute-start | bytes 589832 | tf_op jit(solution)/shard_map/ppermute | solution.py:38
  95.4 15.1 %collective-permute-start.3 = (bf16[2,2,192,128]{3,2,1,0:T(8,128)(2,1)}, bf16[2,2,192,128]{3,2,1,0:T(8,128)(2,1)}, u32[]{:S(2)}, u32[]{:S(2)}) collective-permute-start(bf16[2,2,192,128]{3,2,1,0:T(8,128)(2,1)} %get-tuple-element.55), channel_id=1, source_target_pairs={{0,129},{1,128},{2,131},{3,130},{4,133},{5,132},{6,135},{7,134},{8... | collective-permute-start | bytes 589832 | tf_op jit(solution)/shard_map/ppermute | solution.py:38
  97.3 11.6 %collective-permute-start.1 = (bf16[2,2,192,128]{3,2,1,0:T(8,128)(2,1)S(1)}, bf16[2,2,192,128]{3,2,1,0:T(8,128)(2,1)}, u32[]{:S(2)}, u32[]{:S(2)}) collective-permute-start(bf16[2,2,192,128]{3,2,1,0:T(8,128)(2,1)S(1)} %get-tuple-element.27), channel_id=1, source_target_pairs={{0,1},{1,0},{2,3},{3,2},{4,5},{5,4},{6,7},{7,6},{8,9},{9,8},{10,11... | collective-permute-start | bytes 589832 | tf_op jit(solution)/shard_map/ppermute | solution.py:38
  100.1 55.8 %collective-permute-start.8 = (bf16[8,2,320,128]{3,2,1,0:T(8,128)(2,1)S(1)}, bf16[8,2,320,128]{3,2,1,0:T(8,128)(2,1)}, u32[]{:S(2)}, u32[]{:S(2)}) collective-permute-start(bf16[8,2,320,128]{3,2,1,0:T(8,128)(2,1)S(1)} %all-to-all-done.2.bo_ref), channel_id=1, source_target_pairs={{0,32},{32,0},{1,33},{33,1},{2,34},{34,2},{3,35},{35,3},{4,36},{36... | collective-permute-start | bytes 3932168 | tf_op jit(solution)/shard_map/ppermute | solution.py:42
  108.9 11.8 %collective-permute-start.16 = (bf16[2,2,2,192,128]{4,3,2,1,0:T(8,128)(2,1)S(1)}, bf16[2,2,2,192,128]{4,3,2,1,0:T(8,128)(2,1)S(1)}, u32[]{:S(2)}, u32[]{:S(2)}) collective-permute-start(bf16[2,2,2,192,128]{4,3,2,1,0:T(8,128)(2,1)S(1)} %pad_maximum_fusion.1.u0), channel_id=1, source_target_pairs={{0,2},{2,4},{4,6},{6,0},{1,3},{3,5},{5,7},{7,1},{8,10},{10,12},{12... | collective-permute-start | bytes 1179656 | tf_op jit(solution)/shard_map/ppermute | solution.py:170
  110.5 25.1 %collective-permute-start.19 = (bf16[8,2,192,128]{3,2,1,0:T(8,128)(2,1)S(1)}, bf16[8,2,192,128]{3,2,1,0:T(8,128)(2,1)S(1)}, u32[]{:S(2)}, u32[]{:S(2)}) collective-permute-start(bf16[8,2,192,128]{3,2,1,0:T(8,128)(2,1)S(1)} %all_to_all.20.ao_ref), channel_id=1, source_target_pairs={{0,32},{32,0},{1,33},{33,1},{2,34},{34,2},{3,35},{35,3},{4,36},{36... | collective-permute-start | bytes 2359304 | tf_op jit(solution)/shard_map/ppermute | solution.py:42
  110.5 17.1 %collective-permute-start.17 = (bf16[2,2,2,192,128]{4,3,2,1,0:T(8,128)(2,1)S(1)}, bf16[2,2,2,192,128]{4,3,2,1,0:T(8,128)(2,1)S(1)}, u32[]{:S(2)}, u32[]{:S(2)}) collective-permute-start(bf16[2,2,2,192,128]{4,3,2,1,0:T(8,128)(2,1)S(1)} %pad_maximum_fusion.1.u0), channel_id=1, source_target_pairs={{0,4},{2,6},{4,0},{6,2},{1,5},{3,7},{5,1},{7,3},{8,12},{10,14},{12... | collective-permute-start | bytes 1179656 | tf_op jit(solution)/shard_map/ppermute | solution.py:170
  121.4 9.6 %collective-permute-start.18 = (bf16[2,2,2,192,128]{4,3,2,1,0:T(8,128)(2,1)S(1)}, bf16[2,2,2,192,128]{4,3,2,1,0:T(8,128)(2,1)S(1)}, u32[]{:S(2)}, u32[]{:S(2)}) collective-permute-start(bf16[2,2,2,192,128]{4,3,2,1,0:T(8,128)(2,1)S(1)} %pad_maximum_fusion.1.u0), channel_id=1, source_target_pairs={{0,6},{2,0},{4,2},{6,4},{1,7},{3,1},{5,3},{7,5},{8,14},{10,8},{12,... | collective-permute-start | bytes 1179656 | tf_op jit(solution)/shard_map/ppermute | solution.py:170
  128.3 26.9 %collective-permute-start.7 = (bf16[8,2,192,128]{3,2,1,0:T(8,128)(2,1)S(1)}, bf16[8,2,192,128]{3,2,1,0:T(8,128)(2,1)}, u32[]{:S(2)}, u32[]{:S(2)}) collective-permute-start(bf16[8,2,192,128]{3,2,1,0:T(8,128)(2,1)S(1)} %all-to-all-done.ao_ref), channel_id=1, source_target_pairs={{0,32},{32,0},{1,33},{33,1},{2,34},{34,2},{3,35},{35,3},{4,36},{36... | collective-permute-start | bytes 2359304 | tf_op jit(solution)/shard_map/ppermute | solution.py:42
  131.8 18.7 %collective-permute-start.4 = (bf16[2,2,2,192,128]{4,3,2,1,0:T(8,128)(2,1)}, bf16[2,2,2,192,128]{4,3,2,1,0:T(8,128)(2,1)}, u32[]{:S(2)}, u32[]{:S(2)}) collective-permute-start(bf16[2,2,2,192,128]{4,3,2,1,0:T(8,128)(2,1)} %pad_maximum_fusion.u0), channel_id=1, source_target_pairs={{0,2},{2,4},{4,6},{6,0},{1,3},{3,5},{5,7},{7,1},{8,10},{10,12},{12... | collective-permute-start | bytes 1179656 | tf_op jit(solution)/shard_map/ppermute | solution.py:170
  136.5 17.4 %collective-permute-start.5 = (bf16[2,2,2,192,128]{4,3,2,1,0:T(8,128)(2,1)}, bf16[2,2,2,192,128]{4,3,2,1,0:T(8,128)(2,1)}, u32[]{:S(2)}, u32[]{:S(2)}) collective-permute-start(bf16[2,2,2,192,128]{4,3,2,1,0:T(8,128)(2,1)} %pad_maximum_fusion.u0), channel_id=1, source_target_pairs={{0,4},{2,6},{4,0},{6,2},{1,5},{3,7},{5,1},{7,3},{8,12},{10,14},{12... | collective-permute-start | bytes 1179656 | tf_op jit(solution)/shard_map/ppermute | solution.py:170
  138.5 15.5 %collective-permute-start.6 = (bf16[2,2,2,192,128]{4,3,2,1,0:T(8,128)(2,1)}, bf16[2,2,2,192,128]{4,3,2,1,0:T(8,128)(2,1)}, u32[]{:S(2)}, u32[]{:S(2)}) collective-permute-start(bf16[2,2,2,192,128]{4,3,2,1,0:T(8,128)(2,1)} %pad_maximum_fusion.u0), channel_id=1, source_target_pairs={{0,6},{2,0},{4,2},{6,4},{1,7},{3,1},{5,3},{7,5},{8,14},{10,8},{12,... | collective-permute-start | bytes 1179656 | tf_op jit(solution)/shard_map/ppermute | solution.py:170
  150.5 16.6 %collective-permute-start.21 = (f32[2,192,128]{2,1,0:T(8,128)S(1)}, f32[2,192,128]{2,1,0:T(8,128)S(1)}, u32[]{:S(2)}, u32[]{:S(2)}) collective-permute-start(f32[2,192,128]{2,1,0:T(8,128)S(1)} %get-tuple-element.45), channel_id=1, source_target_pairs={{0,0},{1,1},{2,2},{3,3},{4,4},{5,5},{6,6},{7,7},{8,32},{9,33},{10,... | collective-permute-start | bytes 589832 | tf_op jit(solution)/shard_map/ppermute | solution.py:38
  153.9 13.1 %collective-permute-start.22 = (f32[2,192,128]{2,1,0:T(8,128)S(1)}, f32[2,192,128]{2,1,0:T(8,128)S(1)}, u32[]{:S(2)}, u32[]{:S(2)}) collective-permute-start(f32[2,192,128]{2,1,0:T(8,128)S(1)} %get-tuple-element.46), channel_id=1, source_target_pairs={{0,8},{1,9},{2,10},{3,11},{4,12},{5,13},{6,14},{7,15},{8,40},{9,41... | collective-permute-start | bytes 589832 | tf_op jit(solution)/shard_map/ppermute | solution.py:38
  154.0 17.7 %collective-permute-start.23 = (f32[2,192,128]{2,1,0:T(8,128)S(1)}, f32[2,192,128]{2,1,0:T(8,128)S(1)}, u32[]{:S(2)}, u32[]{:S(2)}) collective-permute-start(f32[2,192,128]{2,1,0:T(8,128)S(1)} %get-tuple-element.47), channel_id=1, source_target_pairs={{0,16},{1,17},{2,18},{3,19},{4,20},{5,21},{6,22},{7,23},{8,48},{9,... | collective-permute-start | bytes 589832 | tf_op jit(solution)/shard_map/ppermute | solution.py:38
  155.3 21.2 %collective-permute-start.24 = (f32[2,192,128]{2,1,0:T(8,128)S(1)}, f32[2,192,128]{2,1,0:T(8,128)}, u32[]{:S(2)}, u32[]{:S(2)}) collective-permute-start(f32[2,192,128]{2,1,0:T(8,128)S(1)} %get-tuple-element.48), channel_id=1, source_target_pairs={{0,24},{1,25},{2,26},{3,27},{4,28},{5,29},{6,30},{7,31},{8,56},{9,... | collective-permute-start | bytes 589832 | tf_op jit(solution)/shard_map/ppermute | solution.py:38
  160.9 18.2 %collective-permute-start.10 = (f32[2,192,128]{2,1,0:T(8,128)}, f32[2,192,128]{2,1,0:T(8,128)S(1)}, u32[]{:S(2)}, u32[]{:S(2)}) collective-permute-start(f32[2,192,128]{2,1,0:T(8,128)} %get-tuple-element.36), channel_id=1, source_target_pairs={{0,8},{1,9},{2,10},{3,11},{4,12},{5,13},{6,14},{7,15},{8,40},{9,41... | collective-permute-start | bytes 589832 | tf_op jit(solution)/shard_map/ppermute | solution.py:38
  167.0 9.5 %copy-start.11 = (f32[2,192,128]{2,1,0:T(8,128)}, f32[2,192,128]{2,1,0:T(8,128)S(1)}, u32[]{:S(2)}) copy-start(f32[2,192,128]{2,1,0:T(8,128)S(1)} %collective-permute-done.21.refs_0_) | copy-start | bytes 589828
  167.0 20.5 %collective-permute-start.11 = (f32[2,192,128]{2,1,0:T(8,128)}, f32[2,192,128]{2,1,0:T(8,128)S(1)}, u32[]{:S(2)}, u32[]{:S(2)}) collective-permute-start(f32[2,192,128]{2,1,0:T(8,128)} %get-tuple-element.37), channel_id=1, source_target_pairs={{0,16},{1,17},{2,18},{3,19},{4,20},{5,21},{6,22},{7,23},{8,48},{9,... | collective-permute-start | bytes 589832 | tf_op jit(solution)/shard_map/ppermute | solution.py:38
  167.0 9.4 %copy-start.12 = (f32[2,192,128]{2,1,0:T(8,128)}, f32[2,192,128]{2,1,0:T(8,128)S(1)}, u32[]{:S(2)}) copy-start(f32[2,192,128]{2,1,0:T(8,128)S(1)} %collective-permute-done.22.refs_1_) | copy-start | bytes 589828
  167.0 20.4 %collective-permute-start.12 = (f32[2,192,128]{2,1,0:T(8,128)S(1)}, f32[2,192,128]{2,1,0:T(8,128)S(1)}, u32[]{:S(2)}, u32[]{:S(2)}) collective-permute-start(f32[2,192,128]{2,1,0:T(8,128)S(1)} %get-tuple-element.38), channel_id=1, source_target_pairs={{0,24},{1,25},{2,26},{3,27},{4,28},{5,29},{6,30},{7,31},{8,56},{9,... | collective-permute-start | bytes 589832 | tf_op jit(solution)/shard_map/ppermute | solution.py:38
  172.4 20.1 %collective-permute-start.9 = (f32[2,192,128]{2,1,0:T(8,128)S(1)}, f32[2,192,128]{2,1,0:T(8,128)S(1)}, u32[]{:S(2)}, u32[]{:S(2)}) collective-permute-start(f32[2,192,128]{2,1,0:T(8,128)S(1)} %get-tuple-element.35), channel_id=1, source_target_pairs={{0,0},{1,1},{2,2},{3,3},{4,4},{5,5},{6,6},{7,7},{8,32},{9,33},{10,... | collective-permute-start | bytes 589832 | tf_op jit(solution)/shard_map/ppermute | solution.py:38
  179.1 13.4 %copy-start.14 = (f32[2,192,128]{2,1,0:T(8,128)}, f32[2,192,128]{2,1,0:T(8,128)S(1)}, u32[]{:S(2)}) copy-start(f32[2,192,128]{2,1,0:T(8,128)S(1)} %collective-permute-done.10.refs_1_) | copy-start | bytes 589828
  187.5 5.1 %copy-start.15 = (f32[2,192,128]{2,1,0:T(8,128)}, f32[2,192,128]{2,1,0:T(8,128)S(1)}, u32[]{:S(2)}) copy-start(f32[2,192,128]{2,1,0:T(8,128)S(1)} %collective-permute-done.11.refs_2_) | copy-start | bytes 589828
  (14 other events, 18.6 us)

commit v13 on v11

--- a/solution.py
+++ b/solution.py
@@ -170,12 +170,13 @@
     turned = [turn(g) for g in range(2)]
 
     def homeward(blocks):
-        moved_on = []
-        for t, block in enumerate(blocks):
-            moved_on.append(
-                send(block, lambda q, r, c, x, y, h: (r, x // 2, x % 2, (2 * q + c) ^ t, y, h))
+        return [
+            send(
+                block,
+                lambda q, r, c, x, y, h: (r, x // 2, x % 2, (2 * q + c) ^ t, y, h),
             )
-        return moved_on
+            for t, block in enumerate(blocks)
+        ]
 
     blocks = []
     for g in range(2):

time: 191 us -> 191 us (level)
  no operation moved by 1% of the time
where the time goes in v13:
time: 191 us; the launch traced here: 190 us
  waiting for transfers between devices  80.9 us (42%)
  starting transfers between devices  51.2 us (27%)
  blocking collectives  20.6 us (11%)
  local copies, waits for them, and re-layouts  15.3 us (8%)
  Pallas kernels  13.6 us (7%)
  other arithmetic  8.23 us (4%)
    ppermute x14, waiting for transfers between devices, send(): return lax.ppermute(value, AXES, moved(target))  51 us
    ppermute x14, starting transfers between devices, send(): return lax.ppermute(value, AXES, moved(target))  31.2 us
    all_to_all x1, blocking collectives, exchange(): lax.all_to_all(block, ('x', 'zr'), split_axis=0, concat_axis=0, tiled=True)  20.6 us
    ppermute x6, waiting for transfers between devices, turn(): lax.ppermute(pieces, 'y', [(i, (i + s) % 4) for i in range(4)])  13.9 us
    all_to_all x2, waiting for transfers between devices, exchange(): lax.all_to_all(block, ('x', 'zr'), split_axis=0, concat_axis=0, tiled=True)  13 us
    all_to_all x2, starting transfers between devices, exchange(): lax.all_to_all(block, ('x', 'zr'), split_axis=0, concat_axis=0, tiled=True)  11.2 us
    unnamed x34, local copies, waits for them, and re-layouts  10.2 us
    pallas_call x2, Pallas kernels, contract(): pl.pallas_call(kernel, out_shape=(result,) * 4, in_specs=[pl.BlockSpec(me...  9.59 us
  transfers between devices with their start and end apart: 26, of which 10 were waited for; matrix products, arithmetic and copies ran while one was open for 5% of the time, Pallas kernels for 6%

profile of v13, /device:TPU:213, one launch (start us, length us, event | category | flops | bytes accessed | tf_op | source)
XLA Modules:
  0.0 190.1 jit_solution(4629663433536481777)
XLA Ops:
  0.0 1.5 constant_dynamic-slice_fusion
  2.3 3.0 %collective-permute-done = bf16[2,16,192,128]{3,2,1,0:T(8,128)(2,1)S(1)} collective-permute-done((bf16[2,16,192,128]{3,2,1,0:T(8,128)(2,1)S(1)}, bf16[2,16,192,128]{3,2,1,0:T(8,128)(2,1)S(1)}, u32[]{:S(2)}, u32[]{:S(2)}) %collective-permute-start) | collective-permute-done | bytes 1572896 | tf_op jit(solution)/shard_map/ppermute | solution.py:42
  5.3 1.6 slice_select_fusion
  6.9 1.3 copy.4
  8.2 4.7 %all-to-all-start = ((bf16[8,2,2,192,128]{4,3,2,1,0:T(8,128)(2,1)}), bf16[8,2,2,192,128]{4,3,2,1,0:T(8,128)(2,1)S(1)}, u32[]{:S(2)}, u32[]{:S(2)}) async-start(bf16[8,2,2,192,128]{4,3,2,1,0:T(8,128)(2,1)} %bitcast.7), calls=%async_computation | async-start | bytes 3145728 | tf_op jit(solution)/shard_map/all_to_all | solution.py:147
  14.1 2.7 %maximum_select_fusion = bf16[2,16,320,128]{3,2,1,0:T(8,128)(2,1)S(1)} fusion(bf16[2,16,192,128]{3,2,1,0:T(8,128)(2,1)S(1)} %collective-permute-done, bf16[2,16,128,128]{3,2,1,0:T(8,128)(2,1)S(1)} %slice-done, bf16[2,16,512,128]{3,2,1,0:T(8,128)(2,1)} %param.2, pred[]{:T(512)S(6)} %eq.12), kind=kLoop, calls=%fused_computation | loop fusion | flops 6553600 | bytes 7864321 | tf_op jit(solution)/shard_map/jit(_where)/select_n | solution.py:141
  18.3 13.0 %all-to-all-done.ao_ref = bf16[8,2,2,192,128]{4,3,2,1,0:T(8,128)(2,1)S(1)} async-done(((bf16[8,2,2,192,128]{4,3,2,1,0:T(8,128)(2,1)}), bf16[8,2,2,192,128]{4,3,2,1,0:T(8,128)(2,1)S(1)}, u32[]{:S(2)}, u32[]{:S(2)}) %all-to-all-start) | async-done | bytes 1572896 | tf_op jit(solution)/shard_map/all_to_all | solution.py:147
  31.3 20.6 %all_to_all.15.bo_ref = bf16[8,2,320,128]{3,2,1,0:T(8,128)(2,1)} all-to-all(bf16[8,2,320,128]{3,2,1,0:T(8,128)(2,1)S(1)} %bitcast.48), channel_id=1, replica_groups=mesh['zq'=2,'zr'=2,'core'=2,'x'=4,'y'=4,'zh'=2] {'x','zr'}, dimensions={0} | all-to-all | bytes 2621440 | tf_op jit(solution)/shard_map/all_to_all | solution.py:147
  52.0 6.5 %all-to-all-start.1 = ((bf16[8,2,320,128]{3,2,1,0:T(8,128)(2,1)}), bf16[8,2,320,128]{3,2,1,0:T(8,128)(2,1)}, u32[]{:S(2)}, u32[]{:S(2)}) async-start(bf16[8,2,320,128]{3,2,1,0:T(8,128)(2,1)} %bitcast.14), calls=%async_computation.1 | async-start | bytes 2621440 | tf_op jit(solution)/shard_map/all_to_all | solution.py:147
  58.4 2.5 %collective-permute-start.7 = (bf16[8,2,2,192,128]{4,3,2,1,0:T(8,128)(2,1)S(1)}, bf16[8,2,2,192,128]{4,3,2,1,0:T(8,128)(2,1)S(1)}, u32[]{:S(2)}, u32[]{:S(2)}) collective-permute-start(bf16[8,2,2,192,128]{4,3,2,1,0:T(8,128)(2,1)S(1)} %all-to-all-done.ao_ref), channel_id=1, source_target_pairs={{0,32},{32,0},{1,33},{33,1},{2,34},{34,2},{3,35},{35,3},{4,36},{36... | collective-permute-start | bytes 4718600 | tf_op jit(solution)/shard_map/ppermute | solution.py:42
  61.8 1.3 collective-permute-start.13
  65.7 1.3 collective-permute-start.1
  68.3 12.7 %collective-permute-done.14 = bf16[2,2,192,128]{3,2,1,0:T(8,128)(2,1)} collective-permute-done((bf16[2,2,192,128]{3,2,1,0:T(8,128)(2,1)}, bf16[2,2,192,128]{3,2,1,0:T(8,128)(2,1)}, u32[]{:S(2)}, u32[]{:S(2)}) %collective-permute-start.14) | collective-permute-done | bytes 196640 | tf_op jit(solution)/shard_map/ppermute | solution.py:38
  81.0 7.4 %collective-permute-done.15 = bf16[2,2,192,128]{3,2,1,0:T(8,128)(2,1)} collective-permute-done((bf16[2,2,192,128]{3,2,1,0:T(8,128)(2,1)}, bf16[2,2,192,128]{3,2,1,0:T(8,128)(2,1)}, u32[]{:S(2)}, u32[]{:S(2)}) %collective-permute-start.15) | collective-permute-done | bytes 196640 | tf_op jit(solution)/shard_map/ppermute | solution.py:38
  89.1 1.8 select_bitcast_fusion
  94.4 8.6 %collective-permute-done.3 = bf16[2,2,192,128]{3,2,1,0:T(8,128)(2,1)S(1)} collective-permute-done((bf16[2,2,192,128]{3,2,1,0:T(8,128)(2,1)}, bf16[2,2,192,128]{3,2,1,0:T(8,128)(2,1)S(1)}, u32[]{:S(2)}, u32[]{:S(2)}) %collective-permute-start.3) | collective-permute-done | bytes 196640 | tf_op jit(solution)/shard_map/ppermute | solution.py:38
  106.1 5.0 %collective-permute-done.17.u2 = bf16[2,2,2,192,128]{4,3,2,1,0:T(8,128)(2,1)S(1)} collective-permute-done((bf16[2,2,2,192,128]{4,3,2,1,0:T(8,128)(2,1)S(1)}, bf16[2,2,2,192,128]{4,3,2,1,0:T(8,128)(2,1)S(1)}, u32[]{:S(2)}, u32[]{:S(2)}) %collective-permute-start.17) | collective-permute-done | bytes 393248 | tf_op jit(solution)/shard_map/ppermute | solution.py:166
  112.1 8.9 %collective-permute-done.18.u3 = bf16[2,2,2,192,128]{4,3,2,1,0:T(8,128)(2,1)S(1)} collective-permute-done((bf16[2,2,2,192,128]{4,3,2,1,0:T(8,128)(2,1)S(1)}, bf16[2,2,2,192,128]{4,3,2,1,0:T(8,128)(2,1)S(1)}, u32[]{:S(2)}, u32[]{:S(2)}) %collective-permute-start.18) | collective-permute-done | bytes 393248 | tf_op jit(solution)/shard_map/ppermute | solution.py:166
  121.7 2.3 %collective-permute-start.6 = (bf16[2,2,2,192,128]{4,3,2,1,0:T(8,128)(2,1)S(1)}, bf16[2,2,2,192,128]{4,3,2,1,0:T(8,128)(2,1)}, u32[]{:S(2)}, u32[]{:S(2)}) collective-permute-start(bf16[2,2,2,192,128]{4,3,2,1,0:T(8,128)(2,1)S(1)} %pad_maximum_fusion.u0), channel_id=1, source_target_pairs={{0,6},{2,0},{4,2},{6,4},{1,7},{3,1},{5,3},{7,5},{8,14},{10,8},{12,... | collective-permute-start | bytes 1179656 | tf_op jit(solution)/shard_map/ppermute | solution.py:166
  129.4 4.4 %shard_map.29 = (f32[2,192,128]{2,1,0:T(8,128)S(1)}, f32[2,192,128]{2,1,0:T(8,128)S(1)}, f32[2,192,128]{2,1,0:T(8,128)S(1)}, f32[2,192,128]{2,1,0:T(8,128)}) custom-call(s32[4]{0:T(128)S(1)} %pad_add_fusion.place_ref, bf16[2,2,2,192,128]{4,3,2,1,0:T(8,128)(2,1)S(1)} %copy-done.2, bf16[2,2,2,192,128]{4,3,2,1,0:T(8,128)(2,1)S(1)} %copy-done.4, ...), custom_call_target="tpu_custom_call" | custom-call | flops 1610612736 | bytes 7340032 | tf_op jit(solution)/shard_map/pallas_call | solution.py:88
  133.8 7.1 %collective-permute-start.20 = (f32[2,192,128]{2,1,0:T(8,128)S(1)}, f32[2,192,128]{2,1,0:T(8,128)S(1)}, u32[]{:S(2)}, u32[]{:S(2)}) collective-permute-start(f32[2,192,128]{2,1,0:T(8,128)S(1)} %get-tuple-element.43), channel_id=1, source_target_pairs={{0,0},{1,1},{2,2},{3,3},{4,4},{5,5},{6,6},{7,7},{8,32},{9,33},{10,... | collective-permute-start | bytes 589832 | tf_op jit(solution)/shard_map/ppermute | solution.py:38
  141.0 4.7 %collective-permute-start.21 = (f32[2,192,128]{2,1,0:T(8,128)S(1)}, f32[2,192,128]{2,1,0:T(8,128)S(1)}, u32[]{:S(2)}, u32[]{:S(2)}) collective-permute-start(f32[2,192,128]{2,1,0:T(8,128)S(1)} %get-tuple-element.44), channel_id=1, source_target_pairs={{0,8},{1,9},{2,10},{3,11},{4,12},{5,13},{6,14},{7,15},{8,40},{9,41... | collective-permute-start | bytes 589832 | tf_op jit(solution)/shard_map/ppermute | solution.py:38
  145.6 4.1 %collective-permute-start.23 = (f32[2,192,128]{2,1,0:T(8,128)}, f32[2,192,128]{2,1,0:T(8,128)}, u32[]{:S(2)}, u32[]{:S(2)}) collective-permute-start(f32[2,192,128]{2,1,0:T(8,128)} %get-tuple-element.46), channel_id=1, source_target_pairs={{0,24},{1,25},{2,26},{3,27},{4,28},{5,29},{6,30},{7,31},{8,56},{9,... | collective-permute-start | bytes 589832 | tf_op jit(solution)/shard_map/ppermute | solution.py:38
  149.7 5.2 %shard_map.28 = (f32[2,192,128]{2,1,0:T(8,128)}, f32[2,192,128]{2,1,0:T(8,128)}, f32[2,192,128]{2,1,0:T(8,128)}, f32[2,192,128]{2,1,0:T(8,128)}) custom-call(s32[4]{0:T(128)S(1)} %pad_add_fusion.place_ref, bf16[2,2,2,192,128]{4,3,2,1,0:T(8,128)(2,1)S(1)} %pad_maximum_fusion.u0, bf16[2,2,2,192,128]{4,3,2,1,0:T(8,128)(2,1)} %collective-permute-done.4.u1, ...), custom_call_target="tpu_custom_call" | custom-call | flops 1610612736 | bytes 7340032 | tf_op jit(solution)/shard_map/pallas_call | solution.py:88
  154.9 2.3 %collective-permute-start.10 = (f32[2,192,128]{2,1,0:T(8,128)}, f32[2,192,128]{2,1,0:T(8,128)S(1)}, u32[]{:S(2)}, u32[]{:S(2)}) collective-permute-start(f32[2,192,128]{2,1,0:T(8,128)} %get-tuple-element.35), channel_id=1, source_target_pairs={{0,8},{1,9},{2,10},{3,11},{4,12},{5,13},{6,14},{7,15},{8,40},{9,41... | collective-permute-start | bytes 589832 | tf_op jit(solution)/shard_map/ppermute | solution.py:38
  157.3 3.3 %collective-permute-start.12 = (f32[2,192,128]{2,1,0:T(8,128)}, f32[2,192,128]{2,1,0:T(8,128)S(1)}, u32[]{:S(2)}, u32[]{:S(2)}) collective-permute-start(f32[2,192,128]{2,1,0:T(8,128)} %get-tuple-element.37), channel_id=1, source_target_pairs={{0,24},{1,25},{2,26},{3,27},{4,28},{5,29},{6,30},{7,31},{8,56},{9,... | collective-permute-start | bytes 589832 | tf_op jit(solution)/shard_map/ppermute | solution.py:38
  161.3 1.9 %collective-permute-start.9 = (f32[2,192,128]{2,1,0:T(8,128)}, f32[2,192,128]{2,1,0:T(8,128)S(1)}, u32[]{:S(2)}, u32[]{:S(2)}) collective-permute-start(f32[2,192,128]{2,1,0:T(8,128)} %get-tuple-element.34), channel_id=1, source_target_pairs={{0,0},{1,1},{2,2},{3,3},{4,4},{5,5},{6,6},{7,7},{8,32},{9,33},{10,... | collective-permute-start | bytes 589832 | tf_op jit(solution)/shard_map/ppermute | solution.py:38
  163.2 2.0 %shard_map.30.refs_4_ = bf16[2,2,384,128]{3,2,1,0:T(8,128)(2,1)} custom-call(s32[1]{0:T(128)} %bitcast.odd_ref, f32[2,2]{1,0:T(2,128)} %wave_ref.3, f32[2,192,128]{2,1,0:T(8,128)} %copy-done.9, f32[2,192,128]{2,1,0:T(8,128)} %copy-done.10, f32[2,192,128]{2,1,0:T(8,128)} %copy-done.11, f32[2,192,128]{2,1,0:T(8,128)} %collective-permute-done.23.refs_3_), custom_call_target="tpu_custom_call" | custom-call | flops 393216 | bytes 1048576 | tf_op jit(solution)/shard_map/pallas_call | solution.py:115
  165.2 6.3 %collective-permute-done.10.refs_1_ = f32[2,192,128]{2,1,0:T(8,128)S(1)} collective-permute-done((f32[2,192,128]{2,1,0:T(8,128)}, f32[2,192,128]{2,1,0:T(8,128)S(1)}, u32[]{:S(2)}, u32[]{:S(2)}) %collective-permute-start.10) | collective-permute-done | bytes 196640 | tf_op jit(solution)/shard_map/ppermute | solution.py:38
  171.5 5.5 %collective-permute-done.12.refs_3_ = f32[2,192,128]{2,1,0:T(8,128)S(1)} collective-permute-done((f32[2,192,128]{2,1,0:T(8,128)}, f32[2,192,128]{2,1,0:T(8,128)S(1)}, u32[]{:S(2)}, u32[]{:S(2)}) %collective-permute-start.12) | collective-permute-done | bytes 196640 | tf_op jit(solution)/shard_map/ppermute | solution.py:38
  177.0 10.4 %collective-permute-done.9.refs_0_ = f32[2,192,128]{2,1,0:T(8,128)S(1)} collective-permute-done((f32[2,192,128]{2,1,0:T(8,128)}, f32[2,192,128]{2,1,0:T(8,128)S(1)}, u32[]{:S(2)}, u32[]{:S(2)}) %collective-permute-start.9) | collective-permute-done | bytes 196640 | tf_op jit(solution)/shard_map/ppermute | solution.py:38
  188.1 2.0 %shard_map.31 = bf16[2,2,384,128]{3,2,1,0:T(8,128)(2,1)} custom-call(s32[1]{0:T(128)} %bitcast.odd_ref, f32[2,2]{1,0:T(2,128)} %wave_ref.3, f32[2,192,128]{2,1,0:T(8,128)} %copy-done.15, f32[2,192,128]{2,1,0:T(8,128)} %copy-done.12, f32[2,192,128]{2,1,0:T(8,128)} %copy-done.13, f32[2,192,128]{2,1,0:T(8,128)} %copy-done.14, ...), custom_call_target="tpu_custom_call", output_to_operand_aliasing={{}: (6, {})} | custom-call | flops 393216 | bytes 1048576 | tf_op jit(solution)/shard_map/pallas_call | solution.py:115
  (72 shorter events, 23.8 us)
Async XLA Ops:
  1.5 3.8 %collective-permute-start = (bf16[2,16,192,128]{3,2,1,0:T(8,128)(2,1)S(1)}, bf16[2,16,192,128]{3,2,1,0:T(8,128)(2,1)S(1)}, u32[]{:S(2)}, u32[]{:S(2)}) collective-permute-start(bf16[2,16,192,128]{3,2,1,0:T(8,128)(2,1)S(1)} %constant_dynamic-slice_fusion), channel_id=1, source_target_pairs={{0,32},{32,0},{1,33},{33,1},{2,34},{34,2},{3,35},{35,3},{4,36},{36... | collective-permute-start | bytes 4718600 | tf_op jit(solution)/shard_map/ppermute | solution.py:42
  8.2 23.1 %all-to-all-start = ((bf16[8,2,2,192,128]{4,3,2,1,0:T(8,128)(2,1)}), bf16[8,2,2,192,128]{4,3,2,1,0:T(8,128)(2,1)S(1)}, u32[]{:S(2)}, u32[]{:S(2)}) async-start(bf16[8,2,2,192,128]{4,3,2,1,0:T(8,128)(2,1)} %bitcast.7), calls=%async_computation | async-start | bytes 3145728 | tf_op jit(solution)/shard_map/all_to_all | solution.py:147
  52.0 39.0 %all-to-all-start.1 = ((bf16[8,2,320,128]{3,2,1,0:T(8,128)(2,1)}), bf16[8,2,320,128]{3,2,1,0:T(8,128)(2,1)}, u32[]{:S(2)}, u32[]{:S(2)}) async-start(bf16[8,2,320,128]{3,2,1,0:T(8,128)(2,1)} %bitcast.14), calls=%async_computation.1 | async-start | bytes 2621440 | tf_op jit(solution)/shard_map/all_to_all | solution.py:147
  58.4 63.3 %collective-permute-start.7 = (bf16[8,2,2,192,128]{4,3,2,1,0:T(8,128)(2,1)S(1)}, bf16[8,2,2,192,128]{4,3,2,1,0:T(8,128)(2,1)S(1)}, u32[]{:S(2)}, u32[]{:S(2)}) collective-permute-start(bf16[8,2,2,192,128]{4,3,2,1,0:T(8,128)(2,1)S(1)} %all-to-all-done.ao_ref), channel_id=1, source_target_pairs={{0,32},{32,0},{1,33},{33,1},{2,34},{34,2},{3,35},{35,3},{4,36},{36... | collective-permute-start | bytes 4718600 | tf_op jit(solution)/shard_map/ppermute | solution.py:42
  61.8 5.3 %collective-permute-start.13 = (bf16[2,2,192,128]{3,2,1,0:T(8,128)(2,1)S(1)}, bf16[2,2,192,128]{3,2,1,0:T(8,128)(2,1)}, u32[]{:S(2)}, u32[]{:S(2)}) collective-permute-start(bf16[2,2,192,128]{3,2,1,0:T(8,128)(2,1)S(1)} %get-tuple-element.38), channel_id=1, source_target_pairs={{0,1},{1,0},{2,3},{3,2},{4,5},{5,4},{6,7},{7,6},{8,9},{9,8},{10,11... | collective-permute-start | bytes 589832 | tf_op jit(solution)/shard_map/ppermute | solution.py:38
  63.1 17.9 %collective-permute-start.14 = (bf16[2,2,192,128]{3,2,1,0:T(8,128)(2,1)}, bf16[2,2,192,128]{3,2,1,0:T(8,128)(2,1)}, u32[]{:S(2)}, u32[]{:S(2)}) collective-permute-start(bf16[2,2,192,128]{3,2,1,0:T(8,128)(2,1)} %get-tuple-element.49), channel_id=1, source_target_pairs={{0,128},{1,129},{2,130},{3,131},{4,132},{5,133},{6,134},{7,135},{8... | collective-permute-start | bytes 589832 | tf_op jit(solution)/shard_map/ppermute | solution.py:38
  64.4 24.1 %collective-permute-start.15 = (bf16[2,2,192,128]{3,2,1,0:T(8,128)(2,1)}, bf16[2,2,192,128]{3,2,1,0:T(8,128)(2,1)}, u32[]{:S(2)}, u32[]{:S(2)}) collective-permute-start(bf16[2,2,192,128]{3,2,1,0:T(8,128)(2,1)} %get-tuple-element.49), channel_id=1, source_target_pairs={{0,129},{1,128},{2,131},{3,130},{4,133},{5,132},{6,135},{7,134},{8... | collective-permute-start | bytes 589832 | tf_op jit(solution)/shard_map/ppermute | solution.py:38
  65.7 26.3 %collective-permute-start.1 = (bf16[2,2,192,128]{3,2,1,0:T(8,128)(2,1)S(1)}, bf16[2,2,192,128]{3,2,1,0:T(8,128)(2,1)}, u32[]{:S(2)}, u32[]{:S(2)}) collective-permute-start(bf16[2,2,192,128]{3,2,1,0:T(8,128)(2,1)S(1)} %get-tuple-element.29), channel_id=1, source_target_pairs={{0,1},{1,0},{2,3},{3,2},{4,5},{5,4},{6,7},{7,6},{8,9},{9,8},{10,11... | collective-permute-start | bytes 589832 | tf_op jit(solution)/shard_map/ppermute | solution.py:38
  67.0 26.0 %collective-permute-start.2 = (bf16[2,2,192,128]{3,2,1,0:T(8,128)(2,1)}, bf16[2,2,192,128]{3,2,1,0:T(8,128)(2,1)}, u32[]{:S(2)}, u32[]{:S(2)}) collective-permute-start(bf16[2,2,192,128]{3,2,1,0:T(8,128)(2,1)} %get-tuple-element.51), channel_id=1, source_target_pairs={{0,128},{1,129},{2,130},{3,131},{4,132},{5,133},{6,134},{7,135},{8... | collective-permute-start | bytes 589832 | tf_op jit(solution)/shard_map/ppermute | solution.py:38
  88.5 35.6 %collective-permute-start.19 = (bf16[8,2,320,128]{3,2,1,0:T(8,128)(2,1)}, bf16[8,2,320,128]{3,2,1,0:T(8,128)(2,1)}, u32[]{:S(2)}, u32[]{:S(2)}) collective-permute-start(bf16[8,2,320,128]{3,2,1,0:T(8,128)(2,1)} %all_to_all.15.bo_ref), channel_id=1, source_target_pairs={{0,32},{32,0},{1,33},{33,1},{2,34},{34,2},{3,35},{35,3},{4,36},{36... | collective-permute-start | bytes 3932168 | tf_op jit(solution)/shard_map/ppermute | solution.py:42
  90.9 58.8 %collective-permute-start.8 = (bf16[8,2,320,128]{3,2,1,0:T(8,128)(2,1)}, bf16[8,2,320,128]{3,2,1,0:T(8,128)(2,1)}, u32[]{:S(2)}, u32[]{:S(2)}) collective-permute-start(bf16[8,2,320,128]{3,2,1,0:T(8,128)(2,1)} %all-to-all-done.1.bo_ref), channel_id=1, source_target_pairs={{0,32},{32,0},{1,33},{33,1},{2,34},{34,2},{3,35},{35,3},{4,36},{36... | collective-permute-start | bytes 3932168 | tf_op jit(solution)/shard_map/ppermute | solution.py:42
  92.0 29.7 %copy-start.1 = (bf16[2,2,2,192,128]{4,3,2,1,0:T(8,128)(2,1)}, bf16[2,2,2,192,128]{4,3,2,1,0:T(8,128)(2,1)S(1)}, u32[]{:S(2)}) copy-start(bf16[2,2,2,192,128]{4,3,2,1,0:T(8,128)(2,1)S(1)} %pad_maximum_fusion.1.u0) | copy-start | bytes 1179652
  92.0 11.3 %collective-permute-start.16 = (bf16[2,2,2,192,128]{4,3,2,1,0:T(8,128)(2,1)S(1)}, bf16[2,2,2,192,128]{4,3,2,1,0:T(8,128)(2,1)S(1)}, u32[]{:S(2)}, u32[]{:S(2)}) collective-permute-start(bf16[2,2,2,192,128]{4,3,2,1,0:T(8,128)(2,1)S(1)} %pad_maximum_fusion.1.u0), channel_id=1, source_target_pairs={{0,2},{2,4},{4,6},{6,0},{1,3},{3,5},{5,7},{7,1},{8,10},{10,12},{12... | collective-permute-start | bytes 1179656 | tf_op jit(solution)/shard_map/ppermute | solution.py:166
  93.1 9.9 %collective-permute-start.3 = (bf16[2,2,192,128]{3,2,1,0:T(8,128)(2,1)}, bf16[2,2,192,128]{3,2,1,0:T(8,128)(2,1)S(1)}, u32[]{:S(2)}, u32[]{:S(2)}) collective-permute-start(bf16[2,2,192,128]{3,2,1,0:T(8,128)(2,1)} %get-tuple-element.51), channel_id=1, source_target_pairs={{0,129},{1,128},{2,131},{3,130},{4,133},{5,132},{6,135},{7,134},{8... | collective-permute-start | bytes 589832 | tf_op jit(solution)/shard_map/ppermute | solution.py:38
  103.0 8.1 %collective-permute-start.17 = (bf16[2,2,2,192,128]{4,3,2,1,0:T(8,128)(2,1)S(1)}, bf16[2,2,2,192,128]{4,3,2,1,0:T(8,128)(2,1)S(1)}, u32[]{:S(2)}, u32[]{:S(2)}) collective-permute-start(bf16[2,2,2,192,128]{4,3,2,1,0:T(8,128)(2,1)S(1)} %pad_maximum_fusion.1.u0), channel_id=1, source_target_pairs={{0,4},{2,6},{4,0},{6,2},{1,5},{3,7},{5,1},{7,3},{8,12},{10,14},{12... | collective-permute-start | bytes 1179656 | tf_op jit(solution)/shard_map/ppermute | solution.py:166
  104.1 16.9 %collective-permute-start.18 = (bf16[2,2,2,192,128]{4,3,2,1,0:T(8,128)(2,1)S(1)}, bf16[2,2,2,192,128]{4,3,2,1,0:T(8,128)(2,1)S(1)}, u32[]{:S(2)}, u32[]{:S(2)}) collective-permute-start(bf16[2,2,2,192,128]{4,3,2,1,0:T(8,128)(2,1)S(1)} %pad_maximum_fusion.1.u0), channel_id=1, source_target_pairs={{0,6},{2,0},{4,2},{6,4},{1,7},{3,1},{5,3},{7,5},{8,14},{10,8},{12,... | collective-permute-start | bytes 1179656 | tf_op jit(solution)/shard_map/ppermute | solution.py:166
  111.9 29.1 %collective-permute-start.4 = (bf16[2,2,2,192,128]{4,3,2,1,0:T(8,128)(2,1)S(1)}, bf16[2,2,2,192,128]{4,3,2,1,0:T(8,128)(2,1)}, u32[]{:S(2)}, u32[]{:S(2)}) collective-permute-start(bf16[2,2,2,192,128]{4,3,2,1,0:T(8,128)(2,1)S(1)} %pad_maximum_fusion.u0), channel_id=1, source_target_pairs={{0,2},{2,4},{4,6},{6,0},{1,3},{3,5},{5,7},{7,1},{8,10},{10,12},{12... | collective-permute-start | bytes 1179656 | tf_op jit(solution)/shard_map/ppermute | solution.py:166
  121.7 23.9 %collective-permute-start.5 = (bf16[2,2,2,192,128]{4,3,2,1,0:T(8,128)(2,1)S(1)}, bf16[2,2,2,192,128]{4,3,2,1,0:T(8,128)(2,1)}, u32[]{:S(2)}, u32[]{:S(2)}) collective-permute-start(bf16[2,2,2,192,128]{4,3,2,1,0:T(8,128)(2,1)S(1)} %pad_maximum_fusion.u0), channel_id=1, source_target_pairs={{0,4},{2,6},{4,0},{6,2},{1,5},{3,7},{5,1},{7,3},{8,12},{10,14},{12... | collective-permute-start | bytes 1179656 | tf_op jit(solution)/shard_map/ppermute | solution.py:166
  121.7 23.9 %collective-permute-start.6 = (bf16[2,2,2,192,128]{4,3,2,1,0:T(8,128)(2,1)S(1)}, bf16[2,2,2,192,128]{4,3,2,1,0:T(8,128)(2,1)}, u32[]{:S(2)}, u32[]{:S(2)}) collective-permute-start(bf16[2,2,2,192,128]{4,3,2,1,0:T(8,128)(2,1)S(1)} %pad_maximum_fusion.u0), channel_id=1, source_target_pairs={{0,6},{2,0},{4,2},{6,4},{1,7},{3,1},{5,3},{7,5},{8,14},{10,8},{12,... | collective-permute-start | bytes 1179656 | tf_op jit(solution)/shard_map/ppermute | solution.py:166
  133.8 23.5 %collective-permute-start.20 = (f32[2,192,128]{2,1,0:T(8,128)S(1)}, f32[2,192,128]{2,1,0:T(8,128)S(1)}, u32[]{:S(2)}, u32[]{:S(2)}) collective-permute-start(f32[2,192,128]{2,1,0:T(8,128)S(1)} %get-tuple-element.43), channel_id=1, source_target_pairs={{0,0},{1,1},{2,2},{3,3},{4,4},{5,5},{6,6},{7,7},{8,32},{9,33},{10,... | collective-permute-start | bytes 589832 | tf_op jit(solution)/shard_map/ppermute | solution.py:38
  141.0 16.3 %collective-permute-start.21 = (f32[2,192,128]{2,1,0:T(8,128)S(1)}, f32[2,192,128]{2,1,0:T(8,128)S(1)}, u32[]{:S(2)}, u32[]{:S(2)}) collective-permute-start(f32[2,192,128]{2,1,0:T(8,128)S(1)} %get-tuple-element.44), channel_id=1, source_target_pairs={{0,8},{1,9},{2,10},{3,11},{4,12},{5,13},{6,14},{7,15},{8,40},{9,41... | collective-permute-start | bytes 589832 | tf_op jit(solution)/shard_map/ppermute | solution.py:38
  145.6 14.9 %collective-permute-start.22 = (f32[2,192,128]{2,1,0:T(8,128)S(1)}, f32[2,192,128]{2,1,0:T(8,128)S(1)}, u32[]{:S(2)}, u32[]{:S(2)}) collective-permute-start(f32[2,192,128]{2,1,0:T(8,128)S(1)} %get-tuple-element.45), channel_id=1, source_target_pairs={{0,16},{1,17},{2,18},{3,19},{4,20},{5,21},{6,22},{7,23},{8,48},{9,... | collective-permute-start | bytes 589832 | tf_op jit(solution)/shard_map/ppermute | solution.py:38
  145.6 17.5 %collective-permute-start.23 = (f32[2,192,128]{2,1,0:T(8,128)}, f32[2,192,128]{2,1,0:T(8,128)}, u32[]{:S(2)}, u32[]{:S(2)}) collective-permute-start(f32[2,192,128]{2,1,0:T(8,128)} %get-tuple-element.46), channel_id=1, source_target_pairs={{0,24},{1,25},{2,26},{3,27},{4,28},{5,29},{6,30},{7,31},{8,56},{9,... | collective-permute-start | bytes 589832 | tf_op jit(solution)/shard_map/ppermute | solution.py:38
  154.9 16.6 %collective-permute-start.10 = (f32[2,192,128]{2,1,0:T(8,128)}, f32[2,192,128]{2,1,0:T(8,128)S(1)}, u32[]{:S(2)}, u32[]{:S(2)}) collective-permute-start(f32[2,192,128]{2,1,0:T(8,128)} %get-tuple-element.35), channel_id=1, source_target_pairs={{0,8},{1,9},{2,10},{3,11},{4,12},{5,13},{6,14},{7,15},{8,40},{9,41... | collective-permute-start | bytes 589832 | tf_op jit(solution)/shard_map/ppermute | solution.py:38
  157.3 3.3 %copy-start.9 = (f32[2,192,128]{2,1,0:T(8,128)}, f32[2,192,128]{2,1,0:T(8,128)S(1)}, u32[]{:S(2)}) copy-start(f32[2,192,128]{2,1,0:T(8,128)S(1)} %collective-permute-done.20.refs_0_) | copy-start | bytes 589828
  157.3 14.3 %collective-permute-start.11 = (f32[2,192,128]{2,1,0:T(8,128)}, f32[2,192,128]{2,1,0:T(8,128)S(1)}, u32[]{:S(2)}, u32[]{:S(2)}) collective-permute-start(f32[2,192,128]{2,1,0:T(8,128)} %get-tuple-element.36), channel_id=1, source_target_pairs={{0,16},{1,17},{2,18},{3,19},{4,20},{5,21},{6,22},{7,23},{8,48},{9,... | collective-permute-start | bytes 589832 | tf_op jit(solution)/shard_map/ppermute | solution.py:38
  157.3 3.3 %copy-start.10 = (f32[2,192,128]{2,1,0:T(8,128)}, f32[2,192,128]{2,1,0:T(8,128)S(1)}, u32[]{:S(2)}) copy-start(f32[2,192,128]{2,1,0:T(8,128)S(1)} %collective-permute-done.21.refs_1_) | copy-start | bytes 589828
  157.3 19.7 %collective-permute-start.12 = (f32[2,192,128]{2,1,0:T(8,128)}, f32[2,192,128]{2,1,0:T(8,128)S(1)}, u32[]{:S(2)}, u32[]{:S(2)}) collective-permute-start(f32[2,192,128]{2,1,0:T(8,128)} %get-tuple-element.37), channel_id=1, source_target_pairs={{0,24},{1,25},{2,26},{3,27},{4,28},{5,29},{6,30},{7,31},{8,56},{9,... | collective-permute-start | bytes 589832 | tf_op jit(solution)/shard_map/ppermute | solution.py:38
  161.3 26.2 %collective-permute-start.9 = (f32[2,192,128]{2,1,0:T(8,128)}, f32[2,192,128]{2,1,0:T(8,128)S(1)}, u32[]{:S(2)}, u32[]{:S(2)}) collective-permute-start(f32[2,192,128]{2,1,0:T(8,128)} %get-tuple-element.34), channel_id=1, source_target_pairs={{0,0},{1,1},{2,2},{3,3},{4,4},{5,5},{6,6},{7,7},{8,32},{9,33},{10,... | collective-permute-start | bytes 589832 | tf_op jit(solution)/shard_map/ppermute | solution.py:38
  171.5 15.9 %copy-start.12 = (f32[2,192,128]{2,1,0:T(8,128)}, f32[2,192,128]{2,1,0:T(8,128)S(1)}, u32[]{:S(2)}) copy-start(f32[2,192,128]{2,1,0:T(8,128)S(1)} %collective-permute-done.10.refs_1_) | copy-start | bytes 589828
  171.5 15.9 %copy-start.13 = (f32[2,192,128]{2,1,0:T(8,128)}, f32[2,192,128]{2,1,0:T(8,128)S(1)}, u32[]{:S(2)}) copy-start(f32[2,192,128]{2,1,0:T(8,128)S(1)} %collective-permute-done.11.refs_2_) | copy-start | bytes 589828
  177.0 10.4 %copy-start.14 = (f32[2,192,128]{2,1,0:T(8,128)}, f32[2,192,128]{2,1,0:T(8,128)S(1)}, u32[]{:S(2)}) copy-start(f32[2,192,128]{2,1,0:T(8,128)S(1)} %collective-permute-done.12.refs_3_) | copy-start | bytes 589828
  (11 other events, 10.2 us)
